TPU v7x, 128 devices: a whole 4x4x4 slice. The times are simulated.
128 devices in a mesh: row: 8 (over x_lo, z), col: 16 (over y, x_hi, core).
Axes of the slice: x: 4 (x_hi: 2, x_lo: 2; x = x_hi * 2 + x_lo), y: 4, z: 4, core: 2. Of those that a mesh axis runs over, the one named last changes fastest.
Arguments:
- grad: bfloat16 [16384, 26624], P(('row', 'col')), may hold values from -6 to 6
- basis_new: bfloat16 [16384, 512], P('row'), may hold values from -0.046875 to 0.046875
- basis_old: bfloat16 [16384, 512], P('row'), may hold values from -0.046875 to 0.046875
- moment_first: float32 [512, 26624], P('row', 'col'), may hold values from -18 to 18
- moment_second: float32 [512, 26624], P('row', 'col'), may hold values from 0.5 to 8
Outputs:
- update: bfloat16 [16384, 26624], P(('row', 'col'))
- first_new: float32 [512, 26624], P('row', 'col')
- second_new: float32 [512, 26624], P('row', 'col')
All inputs are finite; a program needn't handle non-finite values.
Results may differ from a plain program's by a relative error of at most 0.0049.
Values may be sent and summed in bfloat16 or wider, within the bound.
No kernel may reach another device: no remote copies, remote signals or barrier semaphores. Data moves between devices by JAX's collectives and lax.ppermute only.
A program may use at most 128 MiB of HBM per device.

v0:
```python
import functools
import itertools

import jax
import jax.numpy as jnp
from jax import lax
from jax.experimental import pallas as pl
from jax.experimental.pallas import tpu as pltpu
from jax.sharding import Mesh, PartitionSpec as P


STEP = 10
BF, F32 = jnp.bfloat16, jnp.float32
NAMES = ("xl", "z", "y", "xh", "core")
SIZES = (2, 4, 4, 2, 2)
ROW = ("xl", "z")
ANY = pl.BlockSpec(memory_space=pl.ANY)
SMEM = pl.BlockSpec(memory_space=pltpu.SMEM)
VMEM = pl.BlockSpec(memory_space=pltpu.VMEM)
DMA = pltpu.SemaphoreType.DMA
STEPS = (0, 2, 1, 3)
WIDTH = {"y": 2048, "z": 2048, "x": 2560}
GROUPS = ((2048, 128), (1280, 80))
TILE = (512, 640)
SLOT = {"x": 0, "y": 1, "z": 2, "core": 3, "xh": 4, "u0": 5, "v0": 6, "u1": 2, "v1": 1}
SPOTS = [dict(zip(NAMES, spot)) for spot in itertools.product(*(range(n) for n in SIZES))]


def place(where, axis):
    return where[SLOT[axis]]


def ring_shift(spot, ring, step):
    spot = dict(spot)
    if ring == "x":
        x = (spot["xh"] * 2 + spot["xl"] + step) % 4
        spot["xh"], spot["xl"] = x // 2, x % 2
    elif ring == "core":
        spot["core"] = 1 - spot["core"]
    else:
        spot[ring] = (spot[ring] + step) % 4
    return spot


def shift(array, rings, step):
    pairs = []
    for spot in SPOTS:
        target = ring_shift(spot, rings[spot["core"]], step)
        pairs.append((SPOTS.index(spot), SPOTS.index(target)))
    return lax.ppermute(array, NAMES, pairs)


RINGS = {ring: (ring, ring) for ring in ("x", "y", "z", "core")}
U = (("x", "y"), ("z", "z"))
V = (("z", "x"), ("y", "y"))


def runs(ring, at):
    out, done = [], 0
    if ring == "y":
        for xh in range(2):
            out.append((done, (at * 4 + xh * 2) * 1664, 1024))
            done += 1024
    elif ring == "z":
        for y, xh, xl in itertools.product(range(4), range(2), range(2)):
            out.append((done, (y * 4 + xh * 2 + 1) * 1664 + (xl * 4 + at) * 128, 128))
            done += 128
    else:
        xh, xl = at // 2, at % 2
        for core, y in itertools.product(range(2), range(4)):
            out.append((core * 1280 + y * 256, (y * 4 + xh * 2 + core) * 1664 + (8 + 2 * xl) * 128, 256))
    return out


def pieces(group, u_at):
    if group == 0:
        return [(u_at * 512, 512)]
    return [one for v in range(4) for one in ((v * 256 + u_at * 64, 64), (1024 + v * 64 + u_at * 16, 16))]


def rows_at(first, count):
    return pl.ds(pl.multiple_of(first, 16), count)


def estimate(flops, size):
    return pl.CostEstimate(flops=flops, bytes_accessed=size, transcendentals=0)


def start_all(copies):
    for copy in copies:
        copy.start()
    return copies


def wait_all(copies):
    for copy in copies:
        copy.wait()


def turned(tile):
    return pltpu.roll(tile.astype(F32), 64, 1).astype(BF)


def pack_kernel(ring, where, grad, *refs):
    outs, (held, in_sem, out_sem), more = refs[:4], refs[4:7], refs[7:]
    loads = [
        [
            pltpu.make_async_copy(grad.at[:, pl.ds(source, count)], held.at[at, :, pl.ds(to, count)], in_sem.at[at, j])
            for j, (to, source, count) in enumerate(runs(ring, at))
        ]
        for at in range(4)
    ]
    for copies in loads:
        start_all(copies)
    if ring == "x":
        ends, end_sem = more
        copies = start_all(
            [pltpu.make_async_copy(grad.at[:, pl.ds(b * 1664 + 1536, 128)], ends.at[b], end_sem.at[b]) for b in range(16)]
        )
        wait_all(copies)
        left = lax.broadcasted_iota(jnp.int32, (128, 128), 1) < 64
        for xh, core, pair in itertools.product(range(2), range(2), range(2)):
            one, two = (ends[(2 * pair + i) * 4 + xh * 2 + core] for i in range(2))
            columns = pl.ds(core * 1280 + 1024 + pair * 128, 128)
            held[xh * 2, :, columns] = jnp.where(left, one, turned(two))
            held[xh * 2 + 1, :, columns] = jnp.where(left, turned(one), two)
    for copies in loads:
        wait_all(copies)
    t = place(where, ring)
    wait_all(
        start_all([pltpu.make_async_copy(held.at[(t + step) % 4], outs[k], out_sem.at[k]) for k, step in enumerate(STEPS)])
    )


def pack(ring, where, grad):
    width = WIDTH[ring]
    return pl.pallas_call(
        functools.partial(pack_kernel, ring),
        out_shape=[jax.ShapeDtypeStruct((128, width), BF)] * 4,
        in_specs=[SMEM, ANY],
        out_specs=[ANY] * 4,
        scratch_shapes=[pltpu.VMEM((4, 128, width), BF), DMA((4, 16)), DMA((4,))]
        + ([pltpu.VMEM((16, 128, 128), BF), DMA((16,))] if ring == "x" else []),
        cost_estimate=estimate(0, 4 * 128 * width * 4),
    )(where, grad)


def unpack_kernel(ring, where, *refs):
    blocks = refs[:4]
    if ring == "x":
        out, held, in_sem, out_sem, ends, end_sem = refs[-6:]
    else:
        out, held, in_sem, out_sem = refs[-4:]
    t = place(where, ring)
    wait_all(
        start_all(
            [
                pltpu.make_async_copy(blocks[k], held.at[(t + 4 - step) % 4], in_sem.at[k])
                for k, step in enumerate(STEPS)
            ]
        )
    )
    stores = [
        pltpu.make_async_copy(held.at[at, :, pl.ds(to, count)], out.at[:, pl.ds(source, count)], out_sem.at[at, j])
        for at in range(4)
        for j, (to, source, count) in enumerate(runs(ring, at))
    ]
    start_all(stores)
    if ring == "x":
        left = lax.broadcasted_iota(jnp.int32, (128, 128), 1) < 64
        for xh, core, pair in itertools.product(range(2), range(2), range(2)):
            columns = pl.ds(core * 1280 + 1024 + pair * 128, 128)
            one, two = held[xh * 2, :, columns], held[xh * 2 + 1, :, columns]
            block = 2 * pair * 4 + xh * 2 + core
            ends[block] = jnp.where(left, one, turned(two))
            ends[block + 4] = jnp.where(left, turned(one), two)
        wait_all(
            start_all(
                [pltpu.make_async_copy(ends.at[b], out.at[:, pl.ds(b * 1664 + 1536, 128)], end_sem.at[b]) for b in range(16)]
            )
        )
    wait_all(stores)


def unpack(ring, where, blocks, before, columns):
    width = WIDTH[ring]
    more = [] if before is None else [before]
    return pl.pallas_call(
        functools.partial(unpack_kernel, ring),
        out_shape=jax.ShapeDtypeStruct((128, columns), BF),
        in_specs=[SMEM] + [ANY] * (4 + len(more)),
        out_specs=ANY,
        scratch_shapes=[pltpu.VMEM((4, 128, width), BF), DMA((4,)), DMA((4, 16))]
        + ([pltpu.VMEM((16, 128, 128), BF), DMA((16,))] if ring == "x" else []),
        input_output_aliases={5: 0} if more else {},
        cost_estimate=estimate(0, 4 * 128 * width * 4),
    )(where, *blocks, *more)


def basis_rows(ring, where, step, bases):
    y, xh, core = place(where, "y"), place(where, "xh"), place(where, "core")
    base = bases[0]
    if ring == "y":
        first = ((y + step) % 4) * 4 + xh * 2 + core
    elif ring == "z":
        first = y * 4 + xh * 2 + core
        if step % 4:
            base, first = bases[step % 4], 0
    else:
        at = (place(where, "x") + step) % 4
        first = y * 4 + (at // 2) * 2 + core
        if step % 2:
            base, first = bases[4], at // 2
    return base.at[pl.ds(pl.multiple_of(first * 128, 128), 128), :]


def load_blocks(ring, where, blocks, columns, bases, held, base, in_sem, base_sem):
    copies = []
    for k, step in enumerate(STEPS):
        rows = pl.ds(k * 128, 128)
        copies.append(pltpu.make_async_copy(blocks[k].at[:, columns], held.at[rows, :], in_sem.at[k]))
        source = basis_rows(ring, where, 4 - step, bases)
        copies.append(pltpu.make_async_copy(source, base.at[rows, :], base_sem.at[k]))
    return copies


def project_kernel(group, own, where, *refs):
    count = 8 if group == 0 else 4
    blocks, bases, refs = refs[:count], refs[count : count + 5], refs[count + 5 :]
    if own:
        other, outs, (held, base, total, in_sem, base_sem, other_sem, out_sem) = refs[0], refs[1:5], refs[5:]
    else:
        out, held, base, total, in_sem, base_sem, out_sem = refs
    chunk = GROUPS[group][0]
    core = place(where, "core")
    scratch = (bases, held, base, in_sem, base_sem)
    if own:
        copy = pltpu.make_async_copy(other, total, other_sem)
        copy.start()
    if group == 0:
        on_y = core == (0 if own else 1)
        for ring, mine, chosen in (("y", blocks[:4], on_y), ("z", blocks[4:], jnp.logical_not(on_y))):

            @pl.when(chosen)
            def _():
                wait_all(start_all(load_blocks(ring, where, mine, pl.ds(0, chunk), *scratch)))

    else:
        first = (core if own else 1 - core) * chunk
        columns = pl.ds(pl.multiple_of(first, 128), chunk)
        wait_all(start_all(load_blocks("x", where, blocks, columns, *scratch)))
    if own:
        copy.wait()

    tile = TILE[group]

    @pl.loop(0, chunk // tile)
    def _(i):
        some = pl.ds(pl.multiple_of(i * tile, tile), tile)
        product = lax.dot_general(held[:, some], base[...], (((0,), (0,)), ((), ())), preferred_element_type=F32)
        if own:
            product = product + total[some, :].astype(F32)
        total[some, :] = product.astype(BF)

    if not own:
        wait_all(start_all([pltpu.make_async_copy(total, out, out_sem)]))
        return
    stores = []
    for j in range(4):
        done = 0
        for i, (first, size) in enumerate(pieces(group, (place(where, "u%d" % group) + j) % 4)):
            stores.append(
                pltpu.make_async_copy(
                    total.at[rows_at(first, size), :], outs[j].at[pl.ds(done, size), :], out_sem.at[j, i]
                )
            )
            done += size
    wait_all(start_all(stores))


def project(group, where, blocks, bases, other=None):
    chunk = GROUPS[group][0]
    own = other is not None
    shapes = [jax.ShapeDtypeStruct((chunk // 4, 512), BF)] * 4 if own else jax.ShapeDtypeStruct((chunk, 512), BF)
    return pl.pallas_call(
        functools.partial(project_kernel, group, own),
        out_shape=shapes,
        in_specs=[SMEM] + [ANY] * (len(blocks) + len(bases) + own),
        out_specs=[ANY] * 4 if own else ANY,
        scratch_shapes=[
            pltpu.VMEM((512, chunk), BF),
            pltpu.VMEM((512, 512), BF),
            pltpu.VMEM((chunk, 512), BF),
            DMA((4,)),
            DMA((4,)),
        ]
        + ([DMA, DMA((4, 8))] if own else [DMA]),
        cost_estimate=estimate(2 * 512 * 512 * chunk, 512 * chunk * 2 + 512 * 1024 + chunk * 1024),
    )(where, *blocks, *bases, *([other] if own else []))


def add_kernel(group, where, a, b, c, d, *refs):
    outs, total = refs[:4], refs[4]
    piece = GROUPS[group][1]
    total[...] = (
        (a[...].astype(F32) + b[...].astype(F32)) + (c[...].astype(F32) + d[...].astype(F32))
    ).astype(BF)
    for j in range(4):
        at = (place(where, "v%d" % group) + j) % 4
        outs[j][...] = total[rows_at(at * piece, piece), :]


def add_up(group, where, arrays):
    chunk, piece = GROUPS[group]
    return pl.pallas_call(
        functools.partial(add_kernel, group),
        out_shape=[jax.ShapeDtypeStruct((piece, 512), BF)] * 4,
        in_specs=[SMEM] + [VMEM] * 4,
        out_specs=[VMEM] * 4,
        scratch_shapes=[pltpu.VMEM((chunk // 4, 512), BF)],
        cost_estimate=estimate(3 * chunk * 128, 5 * chunk * 256),
    )(where, *arrays)


def step_kernel(where, *refs):
    sums, (own, other, one, one_low, two), lows = refs[:8], refs[8:13], refs[13:15]
    first_out, second_out, margin = refs[15:]
    core = place(where, "core")
    margin[rows_at(core * 256, 256), :] = own[...]
    margin[rows_at(256 - core * 256, 256), :] = other[...]
    projected = jnp.concatenate(
        [sum(ref[...].astype(F32) for ref in sums[4 * g : 4 * g + 4]) for g in range(2)], axis=0
    )
    contract = (((0,), (1,)), ((), ()))
    rotated_one = lax.dot_general(one[...], margin[...], contract, preferred_element_type=F32)
    rotated_one = rotated_one + lax.dot_general(one_low[...], margin[...], contract, preferred_element_type=F32)
    wide = margin[...].astype(F32)
    rotated_two = lax.dot_general(two[...], (wide * wide).astype(BF), contract, preferred_element_type=F32)
    first_new = 0.9 * rotated_one + 0.1 * projected
    second_new = 0.999 * rotated_two + 0.001 * projected * projected
    low_step = (
        first_new / (1.0 - 0.9**STEP) / (jnp.sqrt(second_new / (1.0 - 0.999**STEP)) + 1e-08)
    ).astype(BF)
    begin = 0
    for ref in lows:
        ref[...] = low_step[begin : begin + ref.shape[0], :]
        begin += ref.shape[0]
    first_out[...] = first_new
    second_out[...] = second_new


def take_step(where, sums, *rest):
    return pl.pallas_call(
        step_kernel,
        out_shape=[jax.ShapeDtypeStruct((piece, 512), BF) for _, piece in GROUPS]
        + [jax.ShapeDtypeStruct((208, 512), F32)] * 2,
        in_specs=[SMEM] + [VMEM] * 13,
        out_specs=[VMEM] * 4,
        scratch_shapes=[pltpu.VMEM((512, 512), BF)],
        cost_estimate=estimate(6 * 208 * 512 * 512, 4 * 2**20),
        name="step",
    )(where, *sums, *rest)


def join_kernel(group, where, *refs):
    arrays, out = refs[:4], refs[4]
    piece = GROUPS[group][1]
    for j in range(4):
        at = (place(where, "v%d" % group) + 4 - j) % 4
        out[rows_at(at * piece, piece), :] = arrays[j][...]


def join(group, where, arrays):
    chunk = GROUPS[group][0]
    return pl.pallas_call(
        functools.partial(join_kernel, group),
        out_shape=jax.ShapeDtypeStruct((chunk // 4, 512), BF),
        in_specs=[SMEM] + [VMEM] * 4,
        out_specs=VMEM,
        cost_estimate=estimate(0, chunk * 512),
    )(where, *arrays)


def low_copies(group, where, arrays, begin, low, in_sem, core_of_arrays):
    if group == 0:
        u = jnp.where(core_of_arrays == 0, place(where, "x"), place(where, "y"))
    else:
        u = place(where, "u1")
    copies = []
    for j in range(4):
        done = 0
        for i, (first, size) in enumerate(pieces(group, (u + 4 - j) % 4)):
            copies.append(
                pltpu.make_async_copy(
                    arrays[j].at[pl.ds(done, size), :], low.at[rows_at(begin + first, size), :], in_sem.at[j, i]
                )
            )
            done += size
    return copies


def update_kernel(ring, where, *refs):
    own, other, bases, outs = refs[:4], refs[4:8], refs[8:13], refs[13:17]
    low, base, held, in_sem, other_sem, base_sem, out_sem = refs[17:]
    core = place(where, "core")
    width = WIDTH[ring]
    copies = []
    for k, step in enumerate(STEPS):
        source = basis_rows(ring, where, step, bases)
        copies.append(pltpu.make_async_copy(source, base.at[pl.ds(k * 128, 128), :], base_sem.at[k]))
    start_all(copies)
    if ring == "x":
        more = low_copies(1, where, own, core * 1280, low, in_sem, core)
        more += low_copies(1, where, other, (1 - core) * 1280, low, other_sem, 1 - core)
        wait_all(start_all(more))
    else:
        part_core = 0 if ring == "y" else 1
        for arrays, chosen in ((own, core == part_core), (other, core != part_core)):

            @pl.when(chosen)
            def _():
                wait_all(start_all(low_copies(0, where, arrays, 0, low, in_sem, jnp.int32(part_core))))

    wait_all(copies)

    @pl.loop(0, width // 512)
    def _(i):
        columns = pl.ds(pl.multiple_of(i * 512, 512), 512)
        product = lax.dot_general(base[...], low[columns, :], (((1,), (1,)), ((), ())), preferred_element_type=F32)
        held[:, columns] = (8.0 * product).astype(BF)

    wait_all(
        start_all([pltpu.make_async_copy(held.at[pl.ds(k * 128, 128), :], outs[k], out_sem.at[k]) for k in range(4)])
    )


def update_blocks(ring, where, arrays, bases):
    width = WIDTH[ring]
    return pl.pallas_call(
        functools.partial(update_kernel, ring),
        out_shape=[jax.ShapeDtypeStruct((128, width), BF)] * 4,
        in_specs=[SMEM] + [ANY] * (8 + len(bases)),
        out_specs=[ANY] * 4,
        scratch_shapes=[
            pltpu.VMEM((width, 512), BF),
            pltpu.VMEM((512, 512), BF),
            pltpu.VMEM((512, width), BF),
            DMA((4, 8)),
            DMA((4, 8)),
            DMA((4,)),
            DMA((4,)),
        ],
        cost_estimate=estimate(2 * 512 * 512 * width, 512 * width * 2 + 512 * 1024 + width * 1024),
    )(where, *arrays, *bases)


def spread(moment):
    own = moment.shape[0]
    parts = [moment[:, :1024].reshape(own, 8, 128), moment[:, 1024:1536].reshape(own, 8, 64), moment[:, 1536:].reshape(own, 8, 16)]
    return jnp.concatenate(parts, axis=-1).transpose(1, 0, 2)


def gather_back(moment):
    own = moment.shape[1]
    moment = moment.transpose(1, 0, 2)
    parts = [moment[:, :, :128].reshape(own, 1024), moment[:, :, 128:192].reshape(own, 512), moment[:, :, 192:].reshape(own, 128)]
    return jnp.concatenate(parts, axis=-1)


def exchange(blocks, rings):
    return [blocks[0]] + [shift(block, rings, step) for block, step in zip(blocks[1:], STEPS[1:])]


def compute(grad, basis_new, basis_old, moment_first, moment_second):
    xl, z, y, xh, core = (lax.axis_index(name).astype(jnp.int32) for name in NAMES)
    x = xh * 2 + xl
    spot = lax.broadcasted_iota(jnp.int32, (8,), 0)
    where = jnp.zeros((8,), jnp.int32)
    for i, value in enumerate((x, y, z, core, xh, jnp.where(core == 0, x, y), jnp.where(core == 0, z, x))):
        where = jnp.where(spot == i, value, where)

    arrived = {}
    for ring in ("x", "y", "z"):
        blocks = pack(ring, where, grad)
        arrived[ring] = exchange(blocks, RINGS[ring])
    by_core = basis_new.reshape(4, 2, 2, 128, 512)
    by_x = lax.dynamic_index_in_dim(lax.dynamic_index_in_dim(by_core, core, 2, False), y, 0, False)
    by_z = lax.dynamic_index_in_dim(by_x, xh, 0, False)
    bases = [basis_new] + [shift(by_z, RINGS["z"], 4 - step) for step in range(1, 4)]
    bases.append(lax.ppermute(by_x.reshape(256, 512), "xl", [(0, 1), (1, 0)]))

    half = lax.dynamic_slice_in_dim(basis_new, core * 256, 256, 1)
    margin = jnp.dot(half.T, basis_old, preferred_element_type=F32).astype(BF).reshape(8, 32, 512)
    margin = jnp.pad(margin, ((0, 0), (0, 0), (0, 112))).reshape(8, 32, 3, 208).transpose(0, 2, 1, 3)
    first = spread(moment_first)
    first_high = first.astype(BF)
    first_low = (first - first_high.astype(F32)).astype(BF)
    moments = jnp.concatenate(
        [first_high, first_low, spread(moment_second).astype(BF), margin.reshape(8, 96, 208)], axis=1
    )
    moments = lax.all_to_all(moments, ROW, 0, 0, tiled=True)
    one, one_low, two = (moments[:, i * 64 : i * 64 + 64].reshape(512, 208) for i in range(3))
    margin = jnp.sum(moments[:, 192:].astype(F32), axis=0).astype(BF)
    margin = margin.reshape(3, 32, 208).transpose(1, 0, 2).reshape(32, 624)[:, :512]
    margin = jnp.broadcast_to(margin, (8, 32, 512))
    margin = lax.all_to_all(margin, ROW, 0, 0, tiled=True).reshape(256, 512)
    margin_other = shift(margin, RINGS["core"], 1)

    totals = {}
    for group, blocks in ((1, arrived["x"]), (0, arrived["y"] + arrived["z"])):
        other = project(group, where, blocks, bases)
        other = shift(other, RINGS["core"], 1)
        partial = project(group, where, blocks, bases, other)
        halves = [partial[0]] + [shift(partial[j], U[group], j) for j in (2, 1, 3)]
        rest = add_up(group, where, halves)
        totals[group] = [rest[0]] + [shift(rest[j], V[group], j) for j in (2, 1, 3)]

    *lows, first_new, second_new = take_step(
        where, totals[0] + totals[1], margin, margin_other, one, one_low, two
    )

    sent = {}
    for group, rings in ((1, ("x",)), (0, ("y", "z"))):
        low = lows[group]
        quarters = [low] + [shift(low, V[group], j) for j in range(1, 4)]
        quarter = join(group, where, quarters)
        whole = [quarter] + [shift(quarter, U[group], j) for j in range(1, 4)]
        whole = whole + [shift(array, RINGS["core"], 1) for array in whole]
        for ring in rings:
            blocks = update_blocks(ring, where, whole, bases)
            sent[ring] = exchange(blocks, RINGS[ring])
    update = None
    for ring in ("x", "y", "z"):
        update = unpack(ring, where, sent[ring], update, grad.shape[1])

    new = jnp.stack([first_new.T.reshape(8, 64, 208), second_new.T.reshape(8, 64, 208)], axis=1).astype(BF)
    new = lax.all_to_all(new, ROW, 0, 0, tiled=True).astype(F32)
    return update, gather_back(new[:, 0]), gather_back(new[:, 1])


def solution(mesh):
    fine = Mesh(mesh.devices.reshape(SIZES), NAMES)
    col = ("y", "xh", "core")
    placed = (P(NAMES, None), P(ROW, None), P(ROW, None), P(ROW, col), P(ROW, col))
    return jax.shard_map(
        compute,
        mesh=fine,
        in_specs=placed,
        out_specs=(P(NAMES, None), P(ROW, col), P(ROW, col)),
        check_vma=False,
    )
```

profile of v0, /device:TPU:1, one launch (start us, length us, event | category | flops | bytes accessed | tf_op | source)
XLA Modules:
  0.0 289.6 jit_solution(9673283122178038517)
XLA Ops:
  1.3 4.2 %shard_map.76 = (bf16[128,2048]{1,0:T(8,128)(2,1)}, bf16[128,2048]{1,0:T(8,128)(2,1)}, bf16[128,2048]{1,0:T(8,128)(2,1)}, bf16[128,2048]{1,0:T(8,128)(2,1)}) custom-call(s32[8]{0:T(128)} %compare_select_fusion.6.where, bf16[128,26624]{1,0:T(8,128)(2,1)} %grad.5), custom_call_target="tpu_custom_call" | custom-call | bytes 4194304 | tf_op jit(solution)/shard_map/pallas_call | solution.py:137
  5.5 3.8 %collective-permute-start = (bf16[128,2048]{1,0:T(8,128)(2,1)}, bf16[128,2048]{1,0:T(8,128)(2,1)S(1)}, u32[]{:S(2)}, u32[]{:S(2)}) collective-permute-start(bf16[128,2048]{1,0:T(8,128)(2,1)} %get-tuple-element.48), channel_id=1, source_target_pairs={{0,8},{1,9},{2,10},{3,11},{4,12},{5,13},{6,14},{7,15},{8,0},{9,1},... | collective-permute-start | bytes 1572872 | tf_op jit(solution)/shard_map/ppermute | solution.py:50
  11.6 1.6 dynamic-slice_bitcast_fusion
  13.1 1.6 collective-permute-start.8
  14.8 3.3 %collective-permute-start.7 = (bf16[128,512]{1,0:T(8,128)(2,1)}, bf16[128,512]{1,0:T(8,128)(2,1)S(1)}, u32[]{:S(2)}, u32[]{:S(2)}) collective-permute-start(bf16[128,512]{1,0:T(8,128)(2,1)} %dynamic-slice_bitcast_fusion), channel_id=1, source_target_pairs={{0,32},{1,33},{2,34},{3,35},{4,36},{5,37},{6,38},{7,39},{8,40},{9,... | collective-permute-start | bytes 393224 | tf_op jit(solution)/shard_map/ppermute | solution.py:50
  18.8 4.2 %shard_map.77 = (bf16[128,2048]{1,0:T(8,128)(2,1)}, bf16[128,2048]{1,0:T(8,128)(2,1)}, bf16[128,2048]{1,0:T(8,128)(2,1)}, bf16[128,2048]{1,0:T(8,128)(2,1)}) custom-call(s32[8]{0:T(128)} %compare_select_fusion.6.where, bf16[128,26624]{1,0:T(8,128)(2,1)} %grad.5), custom_call_target="tpu_custom_call" | custom-call | bytes 4194304 | tf_op jit(solution)/shard_map/pallas_call | solution.py:137
  23.5 2.3 collective-permute-start.2
  26.8 2.3 collective-permute-start.5
  29.0 4.9 %shard_map.81 = (bf16[128,2560]{1,0:T(8,128)(2,1)}, bf16[128,2560]{1,0:T(8,128)(2,1)}, bf16[128,2560]{1,0:T(8,128)(2,1)}, bf16[128,2560]{1,0:T(8,128)(2,1)}) custom-call(s32[8]{0:T(128)} %compare_select_fusion.6.where, bf16[128,26624]{1,0:T(8,128)(2,1)} %grad.5), custom_call_target="tpu_custom_call" | custom-call | bytes 5242880 | tf_op jit(solution)/shard_map/pallas_call | solution.py:137
  34.0 2.0 collective-permute-done.1.refs_2_
  36.0 2.5 collective-permute-start.17
  38.5 2.6 collective-permute-start.19
  41.2 11.5 %collective-permute-done.4.refs_6_ = bf16[128,2048]{1,0:T(8,128)(2,1)} collective-permute-done((bf16[128,2048]{1,0:T(8,128)(2,1)}, bf16[128,2048]{1,0:T(8,128)(2,1)}, u32[]{:S(2)}, u32[]{:S(2)}) %collective-permute-start.4) | collective-permute-done | bytes 524320 | tf_op jit(solution)/shard_map/ppermute | solution.py:50
  52.7 5.8 %shard_map.78 = bf16[2048,512]{1,0:T(8,128)(2,1)} custom-call(s32[8]{0:T(128)} %compare_select_fusion.6.where, bf16[128,2048]{1,0:T(8,128)(2,1)} %get-tuple-element.47.refs_0_, bf16[128,2048]{1,0:T(8,128)(2,1)} %copy-done.11, bf16[128,2048]{1,0:T(8,128)(2,1)} %collective-permute-done.1.refs_2_, bf16[128,2048]{1,0:T(8,128)(2,1)} %collective-permute-done.2.refs_3_, ...), custom_call_target="tpu_custom_call" | custom-call | flops 1073741824 | bytes 4718592 | tf_op jit(solution)/shard_map/pallas_call | solution.py:285
  61.4 1.6 slice.61
  63.0 1.6 slice.79
  68.6 1.7 reshape.86
  70.3 1.7 copy.111
  72.1 1.7 copy.84
  73.8 1.7 copy.82
  75.5 1.9 convolution_convert_fusion
  79.1 4.4 %shard_map.82 = bf16[1280,512]{1,0:T(8,128)(2,1)} custom-call(s32[8]{0:T(128)} %compare_select_fusion.6.where, bf16[128,2560]{1,0:T(8,128)(2,1)} %get-tuple-element.63.refs_0_, bf16[128,2560]{1,0:T(8,128)(2,1)} %copy-done.7, bf16[128,2560]{1,0:T(8,128)(2,1)} %copy-done.8, bf16[128,2560]{1,0:T(8,128)(2,1)} %collective-permute-done.19.refs_3_, ...), custom_call_target="tpu_custom_call" | custom-call | flops 671088640 | bytes 3145728 | tf_op jit(solution)/shard_map/pallas_call | solution.py:285
  85.9 3.6 %all-to-all-start = ((bf16[8,288,208]{2,1,0:T(8,128)(2,1)}), bf16[8,288,208]{2,1,0:T(8,128)(2,1)S(1)}, u32[]{:S(2)}, u32[]{:S(2)}) async-start(bf16[8,288,208]{2,1,0:T(8,128)(2,1)} %pad_maximum_fusion), calls=%async_computation | async-start | bytes 2359296 | tf_op jit(solution)/shard_map/all_to_all | solution.py:501
  90.5 5.0 %shard_map.83 = (bf16[320,512]{1,0:T(8,128)(2,1)}, bf16[320,512]{1,0:T(8,128)(2,1)}, bf16[320,512]{1,0:T(8,128)(2,1)}, bf16[320,512]{1,0:T(8,128)(2,1)}) custom-call(s32[8]{0:T(128)} %compare_select_fusion.6.where, bf16[128,2560]{1,0:T(8,128)(2,1)} %get-tuple-element.63.refs_0_, bf16[128,2560]{1,0:T(8,128)(2,1)} %copy-done.7, bf16[128,2560]{1,0:T(8,128)(2,1)} %copy-done.8, ...), custom_call_target="tpu_custom_call" | custom-call | flops 671088640 | bytes 3145728 | tf_op jit(solution)/shard_map/pallas_call | solution.py:285
  95.4 2.9 %collective-permute-start.21 = (bf16[320,512]{1,0:T(8,128)(2,1)}, bf16[320,512]{1,0:T(8,128)(2,1)S(1)}, u32[]{:S(2)}, u32[]{:S(2)}) collective-permute-start(bf16[320,512]{1,0:T(8,128)(2,1)} %get-tuple-element.68), channel_id=1, source_target_pairs={{0,32},{1,33},{2,34},{3,35},{4,36},{5,37},{6,38},{7,39},{8,40},{9,... | collective-permute-start | bytes 983048 | tf_op jit(solution)/shard_map/ppermute | solution.py:50
  98.7 6.6 %shard_map.79 = (bf16[512,512]{1,0:T(8,128)(2,1)}, bf16[512,512]{1,0:T(8,128)(2,1)}, bf16[512,512]{1,0:T(8,128)(2,1)}, bf16[512,512]{1,0:T(8,128)(2,1)}) custom-call(s32[8]{0:T(128)} %compare_select_fusion.6.where, bf16[128,2048]{1,0:T(8,128)(2,1)} %get-tuple-element.47.refs_0_, bf16[128,2048]{1,0:T(8,128)(2,1)} %copy-done.11, ...), custom_call_target="tpu_custom_call" | custom-call | flops 1073741824 | bytes 4718592 | tf_op jit(solution)/shard_map/pallas_call | solution.py:285
  106.0 2.3 collective-permute-start.13
  109.2 4.6 %all-to-all-start.1 = ((bf16[8,32,512]{2,1,0:T(8,128)(2,1)}), bf16[8,32,512]{2,1,0:T(8,128)(2,1)S(1)}, u32[]{:S(2)}, u32[]{:S(2)}) async-start(bf16[8,32,512]{2,1,0:T(8,128)(2,1)} %broadcast_in_dim.32), calls=%async_computation.1 | async-start | bytes 524288 | tf_op jit(solution)/shard_map/all_to_all | solution.py:506
  113.9 2.7 collective-permute-start.23
  116.6 5.0 %all-to-all-done.1 = bf16[8,32,512]{2,1,0:T(8,128)(2,1)S(1)} async-done(((bf16[8,32,512]{2,1,0:T(8,128)(2,1)}), bf16[8,32,512]{2,1,0:T(8,128)(2,1)S(1)}, u32[]{:S(2)}, u32[]{:S(2)}) %all-to-all-start.1) | async-done | bytes 262176 | tf_op jit(solution)/shard_map/all_to_all | solution.py:506
  121.6 5.9 %collective-permute-start.27 = (bf16[256,512]{1,0:T(8,128)(2,1)S(1)}, bf16[256,512]{1,0:T(8,128)(2,1)}, u32[]{:S(2)}, u32[]{:S(2)}) collective-permute-start(bf16[256,512]{1,0:T(8,128)(2,1)S(1)} %bitcast.66), channel_id=1, source_target_pairs={{0,1},{1,0},{2,3},{3,2},{4,5},{5,4},{6,7},{7,6},{8,9},{9,8},{10,11... | collective-permute-start | bytes 786440 | tf_op jit(solution)/shard_map/ppermute | solution.py:50
  127.5 2.3 shard_map.84
  130.5 2.1 collective-permute-start.26
  133.4 2.8 shard_map.80
  136.2 1.7 collective-permute-start.14
  138.2 2.5 collective-permute-start.16
  141.7 1.7 collective-permute-done.15.refs_2_
  144.2 3.4 %step.1 = (bf16[128,512]{1,0:T(8,128)(2,1)}, bf16[80,512]{1,0:T(8,128)(2,1)}, f32[208,512]{1,0:T(8,128)}, f32[208,512]{1,0:T(8,128)}) custom-call(s32[8]{0:T(128)} %compare_select_fusion.6.where, bf16[128,512]{1,0:T(8,128)(2,1)} %get-tuple-element.59.refs_0_, bf16[128,512]{1,0:T(8,128)(2,1)} %copy-done.30, bf16[128,512]{1,0:T(8,128)(2,1)} %copy-done.31, ...), custom_call_target="tpu_custom_call" | custom-call | flops 327155712 | bytes 4194304 | tf_op jit(solution)/shard_map/step/pallas_call | solution.py:353
  151.1 2.1 collective-permute-done.45.refs_2_
  154.7 1.8 shard_map.88.refs_0_
  156.5 4.5 %collective-permute-start.50 = (bf16[320,512]{1,0:T(8,128)(2,1)}, bf16[320,512]{1,0:T(8,128)(2,1)S(1)}, u32[]{:S(2)}, u32[]{:S(2)}) collective-permute-start(bf16[320,512]{1,0:T(8,128)(2,1)} %shard_map.88.refs_0_), channel_id=1, source_target_pairs={{0,1},{1,0},{2,3},{3,2},{4,5},{5,4},{6,7},{7,6},{8,9},{9,8},{10,11... | collective-permute-start | bytes 983048 | tf_op jit(solution)/shard_map/ppermute | solution.py:50
  161.0 2.9 %collective-permute-start.49 = (bf16[320,512]{1,0:T(8,128)(2,1)}, bf16[320,512]{1,0:T(8,128)(2,1)S(1)}, u32[]{:S(2)}, u32[]{:S(2)}) collective-permute-start(bf16[320,512]{1,0:T(8,128)(2,1)} %shard_map.88.refs_0_), channel_id=1, source_target_pairs={{0,48},{1,49},{2,50},{3,51},{4,52},{5,53},{6,54},{7,55},{8,56},{9,... | collective-permute-start | bytes 983048 | tf_op jit(solution)/shard_map/ppermute | solution.py:50
  163.9 2.4 collective-permute-start.30
  167.2 2.8 collective-permute-done.30.refs_3_
  170.1 2.0 collective-permute-done.29.refs_2_
  174.0 1.9 shard_map.85.refs_0_
  175.9 1.7 collective-permute-start.33
  178.9 10.8 %collective-permute-start.53 = (bf16[320,512]{1,0:T(8,128)(2,1)S(1)}, bf16[320,512]{1,0:T(8,128)(2,1)}, u32[]{:S(2)}, u32[]{:S(2)}) collective-permute-start(bf16[320,512]{1,0:T(8,128)(2,1)S(1)} %collective-permute-done.49.refs_3_), channel_id=1, source_target_pairs={{0,1},{1,0},{2,3},{3,2},{4,5},{5,4},{6,7},{7,6},{8,9},{9,8},{10,11... | collective-permute-start | bytes 983048 | tf_op jit(solution)/shard_map/ppermute | solution.py:50
  192.3 8.6 %collective-permute-start.34 = (bf16[512,512]{1,0:T(8,128)(2,1)S(1)}, bf16[512,512]{1,0:T(8,128)(2,1)}, u32[]{:S(2)}, u32[]{:S(2)}) collective-permute-start(bf16[512,512]{1,0:T(8,128)(2,1)S(1)} %copy-done.6), channel_id=1, source_target_pairs={{0,1},{1,0},{2,3},{3,2},{4,5},{5,4},{6,7},{7,6},{8,9},{9,8},{10,11... | collective-permute-start | bytes 1572872 | tf_op jit(solution)/shard_map/ppermute | solution.py:50
  201.1 3.9 %collective-permute-start.36 = (bf16[512,512]{1,0:T(8,128)(2,1)S(1)}, bf16[512,512]{1,0:T(8,128)(2,1)}, u32[]{:S(2)}, u32[]{:S(2)}) collective-permute-start(bf16[512,512]{1,0:T(8,128)(2,1)S(1)} %collective-permute-done.32.refs_2_), channel_id=1, source_target_pairs={{0,1},{1,0},{2,3},{3,2},{4,5},{5,4},{6,7},{7,6},{8,9},{9,8},{10,11... | collective-permute-start | bytes 1572872 | tf_op jit(solution)/shard_map/ppermute | solution.py:50
  205.9 3.5 %all-to-all-start.2 = ((bf16[8,2,64,208]{3,2,1,0:T(8,128)(2,1)}), bf16[8,2,64,208]{3,2,1,0:T(8,128)(2,1)S(1)}, u32[]{:S(2)}, u32[]{:S(2)}) async-start(bf16[8,2,64,208]{3,2,1,0:T(8,128)(2,1)} %copy.93), calls=%async_computation.2 | async-start | bytes 1048576 | tf_op jit(solution)/shard_map/all_to_all | solution.py:537
  210.0 7.7 %all-to-all-done.2 = bf16[8,2,64,208]{3,2,1,0:T(8,128)(2,1)S(1)} async-done(((bf16[8,2,64,208]{3,2,1,0:T(8,128)(2,1)}), bf16[8,2,64,208]{3,2,1,0:T(8,128)(2,1)S(1)}, u32[]{:S(2)}, u32[]{:S(2)}) %all-to-all-start.2) | async-done | bytes 426016 | tf_op jit(solution)/shard_map/all_to_all | solution.py:537
  218.5 7.1 %shard_map.89 = (bf16[128,2560]{1,0:T(8,128)(2,1)}, bf16[128,2560]{1,0:T(8,128)(2,1)}, bf16[128,2560]{1,0:T(8,128)(2,1)}, bf16[128,2560]{1,0:T(8,128)(2,1)}) custom-call(s32[8]{0:T(128)} %compare_select_fusion.6.where, bf16[320,512]{1,0:T(8,128)(2,1)} %shard_map.88.refs_0_, bf16[320,512]{1,0:T(8,128)(2,1)} %copy-done.27, ...), custom_call_target="tpu_custom_call" | custom-call | flops 1342177280 | bytes 5767168 | tf_op jit(solution)/shard_map/pallas_call | solution.py:439
  226.3 1.8 collective-permute-start.55
  228.0 2.4 collective-permute-start.56
  230.4 6.4 %shard_map.87 = (bf16[128,2048]{1,0:T(8,128)(2,1)}, bf16[128,2048]{1,0:T(8,128)(2,1)}, bf16[128,2048]{1,0:T(8,128)(2,1)}, bf16[128,2048]{1,0:T(8,128)(2,1)}) custom-call(s32[8]{0:T(128)} %compare_select_fusion.6.where, bf16[512,512]{1,0:T(8,128)(2,1)} %shard_map.85.refs_0_, bf16[512,512]{1,0:T(8,128)(2,1)} %collective-permute-done.31.refs_1_, ...), custom_call_target="tpu_custom_call" | custom-call | flops 1073741824 | bytes 4718592 | tf_op jit(solution)/shard_map/pallas_call | solution.py:439
  239.4 6.3 %shard_map.86 = (bf16[128,2048]{1,0:T(8,128)(2,1)}, bf16[128,2048]{1,0:T(8,128)(2,1)}, bf16[128,2048]{1,0:T(8,128)(2,1)}, bf16[128,2048]{1,0:T(8,128)(2,1)}) custom-call(s32[8]{0:T(128)} %compare_select_fusion.6.where, bf16[512,512]{1,0:T(8,128)(2,1)} %shard_map.85.refs_0_, bf16[512,512]{1,0:T(8,128)(2,1)} %collective-permute-done.31.refs_1_, ...), custom_call_target="tpu_custom_call" | custom-call | flops 1073741824 | bytes 4718592 | tf_op jit(solution)/shard_map/pallas_call | solution.py:439
  247.1 11.2 %collective-permute-done.55.refs_2_ = bf16[128,2560]{1,0:T(8,128)(2,1)} collective-permute-done((bf16[128,2560]{1,0:T(8,128)(2,1)}, bf16[128,2560]{1,0:T(8,128)(2,1)}, u32[]{:S(2)}, u32[]{:S(2)}) %collective-permute-start.55) | collective-permute-done | bytes 655392 | tf_op jit(solution)/shard_map/ppermute | solution.py:50
  258.2 1.9 collective-permute-start.38
  260.5 2.3 collective-permute-start.40
  265.7 4.6 %shard_map.90.refs_4_ = bf16[128,26624]{1,0:T(8,128)(2,1)} custom-call(s32[8]{0:T(128)} %compare_select_fusion.6.where, bf16[128,2560]{1,0:T(8,128)(2,1)} %get-tuple-element.85.refs_0_, bf16[128,2560]{1,0:T(8,128)(2,1)} %collective-permute-done.54.refs_1_, bf16[128,2560]{1,0:T(8,128)(2,1)} %collective-permute-done.55.refs_2_, ...), custom_call_target="tpu_custom_call" | custom-call | bytes 5242880 | tf_op jit(solution)/shard_map/pallas_call | solution.py:188
  271.2 4.1 %shard_map.91.refs_4_ = bf16[128,26624]{1,0:T(8,128)(2,1)} custom-call(s32[8]{0:T(128)} %compare_select_fusion.6.where, bf16[128,2048]{1,0:T(8,128)(2,1)} %get-tuple-element.80.refs_0_, bf16[128,2048]{1,0:T(8,128)(2,1)} %copy-done.16, bf16[128,2048]{1,0:T(8,128)(2,1)} %copy-done.17, ...), custom_call_target="tpu_custom_call", output_to_operand_aliasing={{}: (5, {})} | custom-call | bytes 4194304 | tf_op jit(solution)/shard_map/pallas_call | solution.py:188
  275.3 9.8 %collective-permute-done.39.refs_2_ = bf16[128,2048]{1,0:T(8,128)(2,1)} collective-permute-done((bf16[128,2048]{1,0:T(8,128)(2,1)}, bf16[128,2048]{1,0:T(8,128)(2,1)}, u32[]{:S(2)}, u32[]{:S(2)}) %collective-permute-start.39) | collective-permute-done | bytes 524320 | tf_op jit(solution)/shard_map/ppermute | solution.py:50
  285.2 4.2 %shard_map.92 = bf16[128,26624]{1,0:T(8,128)(2,1)} custom-call(s32[8]{0:T(128)} %compare_select_fusion.6.where, bf16[128,2048]{1,0:T(8,128)(2,1)} %get-tuple-element.76.refs_0_, bf16[128,2048]{1,0:T(8,128)(2,1)} %copy-done.21, bf16[128,2048]{1,0:T(8,128)(2,1)} %collective-permute-done.39.refs_2_, ...), custom_call_target="tpu_custom_call", output_to_operand_aliasing={{}: (5, {})} | custom-call | bytes 4194304 | tf_op jit(solution)/shard_map/pallas_call | solution.py:188
  (217 shorter events, 45.0 us)
Async XLA Ops:
  0.6 74.9 %copy-start = (bf16[2048,512]{1,0:T(8,128)(2,1)S(1)}, bf16[2048,512]{1,0:T(8,128)(2,1)}, u32[]{:S(2)}) copy-start(bf16[2048,512]{1,0:T(8,128)(2,1)} %param.7) | copy-start | bytes 6291460
  5.5 21.3 %collective-permute-start = (bf16[128,2048]{1,0:T(8,128)(2,1)}, bf16[128,2048]{1,0:T(8,128)(2,1)S(1)}, u32[]{:S(2)}, u32[]{:S(2)}) collective-permute-start(bf16[128,2048]{1,0:T(8,128)(2,1)} %get-tuple-element.48), channel_id=1, source_target_pairs={{0,8},{1,9},{2,10},{3,11},{4,12},{5,13},{6,14},{7,15},{8,0},{9,1},... | collective-permute-start | bytes 1572872 | tf_op jit(solution)/shard_map/ppermute | solution.py:50
  10.3 16.0 %collective-permute-start.9 = (bf16[256,512]{1,0:T(8,128)(2,1)S(1)}, bf16[256,512]{1,0:T(8,128)(2,1)S(1)}, u32[]{:S(2)}, u32[]{:S(2)}) collective-permute-start(bf16[256,512]{1,0:T(8,128)(2,1)S(1)} %bitcast.78), channel_id=1, source_target_pairs={{0,64},{64,0},{1,65},{65,1},{2,66},{66,2},{3,67},{67,3},{4,68},{68... | collective-permute-start | bytes 786440 | tf_op jit(solution)/shard_map/ppermute | solution.py:490
  13.1 9.9 %collective-permute-start.8 = (bf16[128,512]{1,0:T(8,128)(2,1)}, bf16[128,512]{1,0:T(8,128)(2,1)S(1)}, u32[]{:S(2)}, u32[]{:S(2)}) collective-permute-start(bf16[128,512]{1,0:T(8,128)(2,1)} %dynamic-slice_bitcast_fusion), channel_id=1, source_target_pairs={{0,16},{1,17},{2,18},{3,19},{4,20},{5,21},{6,22},{7,23},{8,24},{9,... | collective-permute-start | bytes 393224 | tf_op jit(solution)/shard_map/ppermute | solution.py:50
  14.8 8.7 %collective-permute-start.7 = (bf16[128,512]{1,0:T(8,128)(2,1)}, bf16[128,512]{1,0:T(8,128)(2,1)S(1)}, u32[]{:S(2)}, u32[]{:S(2)}) collective-permute-start(bf16[128,512]{1,0:T(8,128)(2,1)} %dynamic-slice_bitcast_fusion), channel_id=1, source_target_pairs={{0,32},{1,33},{2,34},{3,35},{4,36},{5,37},{6,38},{7,39},{8,40},{9,... | collective-permute-start | bytes 393224 | tf_op jit(solution)/shard_map/ppermute | solution.py:50
  18.1 7.7 %collective-permute-start.6 = (bf16[128,512]{1,0:T(8,128)(2,1)}, bf16[128,512]{1,0:T(8,128)(2,1)S(1)}, u32[]{:S(2)}, u32[]{:S(2)}) collective-permute-start(bf16[128,512]{1,0:T(8,128)(2,1)} %dynamic-slice_bitcast_fusion), channel_id=1, source_target_pairs={{0,48},{1,49},{2,50},{3,51},{4,52},{5,53},{6,54},{7,55},{8,56},{9,... | collective-permute-start | bytes 393224 | tf_op jit(solution)/shard_map/ppermute | solution.py:50
  23.0 13.0 %collective-permute-start.1 = (bf16[128,2048]{1,0:T(8,128)(2,1)}, bf16[128,2048]{1,0:T(8,128)(2,1)}, u32[]{:S(2)}, u32[]{:S(2)}) collective-permute-start(bf16[128,2048]{1,0:T(8,128)(2,1)} %get-tuple-element.49), channel_id=1, source_target_pairs={{0,4},{1,5},{2,6},{3,7},{4,8},{5,9},{6,10},{7,11},{8,12},{9,13},{1... | collective-permute-start | bytes 1572872 | tf_op jit(solution)/shard_map/ppermute | solution.py:50
  23.5 15.0 %collective-permute-start.2 = (bf16[128,2048]{1,0:T(8,128)(2,1)}, bf16[128,2048]{1,0:T(8,128)(2,1)}, u32[]{:S(2)}, u32[]{:S(2)}) collective-permute-start(bf16[128,2048]{1,0:T(8,128)(2,1)} %get-tuple-element.50), channel_id=1, source_target_pairs={{0,12},{1,13},{2,14},{3,15},{4,0},{5,1},{6,2},{7,3},{8,4},{9,5},{1... | collective-permute-start | bytes 1572872 | tf_op jit(solution)/shard_map/ppermute | solution.py:50
  25.8 12.8 %collective-permute-start.3 = (bf16[128,2048]{1,0:T(8,128)(2,1)}, bf16[128,2048]{1,0:T(8,128)(2,1)}, u32[]{:S(2)}, u32[]{:S(2)}) collective-permute-start(bf16[128,2048]{1,0:T(8,128)(2,1)} %get-tuple-element.52), channel_id=1, source_target_pairs={{0,32},{1,33},{2,34},{3,35},{4,36},{5,37},{6,38},{7,39},{8,40},{9,... | collective-permute-start | bytes 1572872 | tf_op jit(solution)/shard_map/ppermute | solution.py:50
  26.3 26.4 %collective-permute-start.4 = (bf16[128,2048]{1,0:T(8,128)(2,1)}, bf16[128,2048]{1,0:T(8,128)(2,1)}, u32[]{:S(2)}, u32[]{:S(2)}) collective-permute-start(bf16[128,2048]{1,0:T(8,128)(2,1)} %get-tuple-element.53), channel_id=1, source_target_pairs={{0,16},{1,17},{2,18},{3,19},{4,20},{5,21},{6,22},{7,23},{8,24},{9,... | collective-permute-start | bytes 1572872 | tf_op jit(solution)/shard_map/ppermute | solution.py:50
  26.8 25.9 %collective-permute-start.5 = (bf16[128,2048]{1,0:T(8,128)(2,1)}, bf16[128,2048]{1,0:T(8,128)(2,1)}, u32[]{:S(2)}, u32[]{:S(2)}) collective-permute-start(bf16[128,2048]{1,0:T(8,128)(2,1)} %get-tuple-element.54), channel_id=1, source_target_pairs={{0,48},{1,49},{2,50},{3,51},{4,52},{5,53},{6,54},{7,55},{8,56},{9,... | collective-permute-start | bytes 1572872 | tf_op jit(solution)/shard_map/ppermute | solution.py:50
  36.0 41.8 %collective-permute-start.17 = (bf16[128,2560]{1,0:T(8,128)(2,1)}, bf16[128,2560]{1,0:T(8,128)(2,1)S(1)}, u32[]{:S(2)}, u32[]{:S(2)}) collective-permute-start(bf16[128,2560]{1,0:T(8,128)(2,1)} %get-tuple-element.64), channel_id=1, source_target_pairs={{0,2},{1,3},{2,0},{3,1},{4,6},{5,7},{6,4},{7,5},{8,10},{9,11},{10,... | collective-permute-start | bytes 1966088 | tf_op jit(solution)/shard_map/ppermute | solution.py:50
  38.5 39.4 %collective-permute-start.18 = (bf16[128,2560]{1,0:T(8,128)(2,1)}, bf16[128,2560]{1,0:T(8,128)(2,1)S(1)}, u32[]{:S(2)}, u32[]{:S(2)}) collective-permute-start(bf16[128,2560]{1,0:T(8,128)(2,1)} %get-tuple-element.65), channel_id=1, source_target_pairs={{0,64},{1,65},{2,66},{3,67},{4,68},{5,69},{6,70},{7,71},{8,72},{9,... | collective-permute-start | bytes 1966088 | tf_op jit(solution)/shard_map/ppermute | solution.py:50
  38.5 39.4 %collective-permute-start.19 = (bf16[128,2560]{1,0:T(8,128)(2,1)}, bf16[128,2560]{1,0:T(8,128)(2,1)}, u32[]{:S(2)}, u32[]{:S(2)}) collective-permute-start(bf16[128,2560]{1,0:T(8,128)(2,1)} %get-tuple-element.66), channel_id=1, source_target_pairs={{0,66},{1,67},{2,64},{3,65},{4,70},{5,71},{6,68},{7,69},{8,74},{9,... | collective-permute-start | bytes 1966088 | tf_op jit(solution)/shard_map/ppermute | solution.py:50
  58.5 40.2 %collective-permute-start.10 = (bf16[2048,512]{1,0:T(8,128)(2,1)}, bf16[2048,512]{1,0:T(8,128)(2,1)}, u32[]{:S(2)}, u32[]{:S(2)}) collective-permute-start(bf16[2048,512]{1,0:T(8,128)(2,1)} %shard_map.78), channel_id=1, source_target_pairs={{0,1},{1,0},{2,3},{3,2},{4,5},{5,4},{6,7},{7,6},{8,9},{9,8},{10,11... | collective-permute-start | bytes 6291464 | tf_op jit(solution)/shard_map/ppermute | solution.py:50
  83.5 5.9 %collective-permute-start.20 = (bf16[1280,512]{1,0:T(8,128)(2,1)}, bf16[1280,512]{1,0:T(8,128)(2,1)S(1)}, u32[]{:S(2)}, u32[]{:S(2)}) collective-permute-start(bf16[1280,512]{1,0:T(8,128)(2,1)} %shard_map.82), channel_id=1, source_target_pairs={{0,1},{1,0},{2,3},{3,2},{4,5},{5,4},{6,7},{7,6},{8,9},{9,8},{10,11... | collective-permute-start | bytes 3932168 | tf_op jit(solution)/shard_map/ppermute | solution.py:50
  85.9 22.4 %all-to-all-start = ((bf16[8,288,208]{2,1,0:T(8,128)(2,1)}), bf16[8,288,208]{2,1,0:T(8,128)(2,1)S(1)}, u32[]{:S(2)}, u32[]{:S(2)}) async-start(bf16[8,288,208]{2,1,0:T(8,128)(2,1)} %pad_maximum_fusion), calls=%async_computation | async-start | bytes 2359296 | tf_op jit(solution)/shard_map/all_to_all | solution.py:501
  95.4 18.4 %collective-permute-start.21 = (bf16[320,512]{1,0:T(8,128)(2,1)}, bf16[320,512]{1,0:T(8,128)(2,1)S(1)}, u32[]{:S(2)}, u32[]{:S(2)}) collective-permute-start(bf16[320,512]{1,0:T(8,128)(2,1)} %get-tuple-element.68), channel_id=1, source_target_pairs={{0,32},{1,33},{2,34},{3,35},{4,36},{5,37},{6,38},{7,39},{8,40},{9,... | collective-permute-start | bytes 983048 | tf_op jit(solution)/shard_map/ppermute | solution.py:50
  98.4 23.2 %collective-permute-start.22 = (bf16[320,512]{1,0:T(8,128)(2,1)}, bf16[320,512]{1,0:T(8,128)(2,1)}, u32[]{:S(2)}, u32[]{:S(2)}) collective-permute-start(bf16[320,512]{1,0:T(8,128)(2,1)} %get-tuple-element.69), channel_id=1, source_target_pairs={{0,16},{1,17},{2,18},{3,19},{4,20},{5,21},{6,22},{7,23},{8,24},{9,... | collective-permute-start | bytes 983048 | tf_op jit(solution)/shard_map/ppermute | solution.py:50
  105.3 24.6 %collective-permute-start.11 = (bf16[512,512]{1,0:T(8,128)(2,1)}, bf16[512,512]{1,0:T(8,128)(2,1)S(1)}, u32[]{:S(2)}, u32[]{:S(2)}) collective-permute-start(bf16[512,512]{1,0:T(8,128)(2,1)} %get-tuple-element.56), channel_id=1, source_target_pairs={{0,2},{1,9},{2,0},{3,11},{4,6},{5,13},{6,4},{7,15},{8,10},{9,1},{1... | collective-permute-start | bytes 1572872 | tf_op jit(solution)/shard_map/ppermute | solution.py:50
  105.3 25.2 %collective-permute-start.12 = (bf16[512,512]{1,0:T(8,128)(2,1)}, bf16[512,512]{1,0:T(8,128)(2,1)S(1)}, u32[]{:S(2)}, u32[]{:S(2)}) collective-permute-start(bf16[512,512]{1,0:T(8,128)(2,1)} %get-tuple-element.57), channel_id=1, source_target_pairs={{0,64},{1,5},{2,66},{3,7},{4,68},{5,9},{6,70},{7,11},{8,72},{9,13}... | collective-permute-start | bytes 1572872 | tf_op jit(solution)/shard_map/ppermute | solution.py:50
  106.0 26.6 %collective-permute-start.13 = (bf16[512,512]{1,0:T(8,128)(2,1)}, bf16[512,512]{1,0:T(8,128)(2,1)S(1)}, u32[]{:S(2)}, u32[]{:S(2)}) collective-permute-start(bf16[512,512]{1,0:T(8,128)(2,1)} %get-tuple-element.58), channel_id=1, source_target_pairs={{0,66},{1,13},{2,64},{3,15},{4,70},{5,1},{6,68},{7,3},{8,74},{9,5}... | collective-permute-start | bytes 1572872 | tf_op jit(solution)/shard_map/ppermute | solution.py:50
  109.2 12.4 %all-to-all-start.1 = ((bf16[8,32,512]{2,1,0:T(8,128)(2,1)}), bf16[8,32,512]{2,1,0:T(8,128)(2,1)S(1)}, u32[]{:S(2)}, u32[]{:S(2)}) async-start(bf16[8,32,512]{2,1,0:T(8,128)(2,1)} %broadcast_in_dim.32), calls=%async_computation.1 | async-start | bytes 524288 | tf_op jit(solution)/shard_map/all_to_all | solution.py:506
  113.9 13.7 %collective-permute-start.23 = (bf16[320,512]{1,0:T(8,128)(2,1)}, bf16[320,512]{1,0:T(8,128)(2,1)}, u32[]{:S(2)}, u32[]{:S(2)}) collective-permute-start(bf16[320,512]{1,0:T(8,128)(2,1)} %get-tuple-element.70), channel_id=1, source_target_pairs={{0,48},{1,49},{2,50},{3,51},{4,52},{5,53},{6,54},{7,55},{8,56},{9,... | collective-permute-start | bytes 983048 | tf_op jit(solution)/shard_map/ppermute | solution.py:50
  121.6 16.3 %collective-permute-start.27 = (bf16[256,512]{1,0:T(8,128)(2,1)S(1)}, bf16[256,512]{1,0:T(8,128)(2,1)}, u32[]{:S(2)}, u32[]{:S(2)}) collective-permute-start(bf16[256,512]{1,0:T(8,128)(2,1)S(1)} %bitcast.66), channel_id=1, source_target_pairs={{0,1},{1,0},{2,3},{3,2},{4,5},{5,4},{6,7},{7,6},{8,9},{9,8},{10,11... | collective-permute-start | bytes 786440 | tf_op jit(solution)/shard_map/ppermute | solution.py:50
  129.8 8.3 %collective-permute-start.24 = (bf16[80,512]{1,0:T(8,128)(2,1)}, bf16[80,512]{1,0:T(8,128)(2,1)S(1)}, u32[]{:S(2)}, u32[]{:S(2)}) collective-permute-start(bf16[80,512]{1,0:T(8,128)(2,1)} %get-tuple-element.72), channel_id=1, source_target_pairs={{0,8},{1,9},{2,10},{3,11},{4,12},{5,13},{6,14},{7,15},{8,0},{9,1},... | collective-permute-start | bytes 245768 | tf_op jit(solution)/shard_map/ppermute | solution.py:50
  129.8 11.7 %collective-permute-start.25 = (bf16[80,512]{1,0:T(8,128)(2,1)}, bf16[80,512]{1,0:T(8,128)(2,1)S(1)}, u32[]{:S(2)}, u32[]{:S(2)}) collective-permute-start(bf16[80,512]{1,0:T(8,128)(2,1)} %get-tuple-element.73), channel_id=1, source_target_pairs={{0,4},{1,5},{2,6},{3,7},{4,8},{5,9},{6,10},{7,11},{8,12},{9,13},{1... | collective-permute-start | bytes 245768 | tf_op jit(solution)/shard_map/ppermute | solution.py:50
  130.5 11.0 %collective-permute-start.26 = (bf16[80,512]{1,0:T(8,128)(2,1)}, bf16[80,512]{1,0:T(8,128)(2,1)S(1)}, u32[]{:S(2)}, u32[]{:S(2)}) collective-permute-start(bf16[80,512]{1,0:T(8,128)(2,1)} %get-tuple-element.74), channel_id=1, source_target_pairs={{0,12},{1,13},{2,14},{3,15},{4,0},{5,1},{6,2},{7,3},{8,4},{9,5},{1... | collective-permute-start | bytes 245768 | tf_op jit(solution)/shard_map/ppermute | solution.py:50
  136.2 5.5 %collective-permute-start.14 = (bf16[128,512]{1,0:T(8,128)(2,1)}, bf16[128,512]{1,0:T(8,128)(2,1)S(1)}, u32[]{:S(2)}, u32[]{:S(2)}) collective-permute-start(bf16[128,512]{1,0:T(8,128)(2,1)} %get-tuple-element.60), channel_id=1, source_target_pairs={{0,32},{1,3},{2,34},{3,1},{4,36},{5,7},{6,38},{7,5},{8,40},{9,11},... | collective-permute-start | bytes 393224 | tf_op jit(solution)/shard_map/ppermute | solution.py:50
  137.9 5.5 %collective-permute-start.15 = (bf16[128,512]{1,0:T(8,128)(2,1)}, bf16[128,512]{1,0:T(8,128)(2,1)S(1)}, u32[]{:S(2)}, u32[]{:S(2)}) collective-permute-start(bf16[128,512]{1,0:T(8,128)(2,1)} %get-tuple-element.61), channel_id=1, source_target_pairs={{0,16},{1,65},{2,18},{3,67},{4,20},{5,69},{6,22},{7,71},{8,24},{9,... | collective-permute-start | bytes 393224 | tf_op jit(solution)/shard_map/ppermute | solution.py:50
  138.2 5.3 %collective-permute-start.16 = (bf16[128,512]{1,0:T(8,128)(2,1)}, bf16[128,512]{1,0:T(8,128)(2,1)S(1)}, u32[]{:S(2)}, u32[]{:S(2)}) collective-permute-start(bf16[128,512]{1,0:T(8,128)(2,1)} %get-tuple-element.62), channel_id=1, source_target_pairs={{0,48},{1,67},{2,50},{3,65},{4,52},{5,71},{6,54},{7,69},{8,56},{9,... | collective-permute-start | bytes 393224 | tf_op jit(solution)/shard_map/ppermute | solution.py:50
  147.6 3.5 %collective-permute-start.46 = (bf16[80,512]{1,0:T(8,128)(2,1)}, bf16[80,512]{1,0:T(8,128)(2,1)S(1)}, u32[]{:S(2)}, u32[]{:S(2)}) collective-permute-start(bf16[80,512]{1,0:T(8,128)(2,1)} %get-tuple-element.84.refs_0_), channel_id=1, source_target_pairs={{0,12},{1,13},{2,14},{3,15},{4,0},{5,1},{6,2},{7,3},{8,4},{9,5},{1... | collective-permute-start | bytes 245768 | tf_op jit(solution)/shard_map/ppermute | solution.py:50
  148.2 5.0 %collective-permute-start.45 = (bf16[80,512]{1,0:T(8,128)(2,1)}, bf16[80,512]{1,0:T(8,128)(2,1)S(1)}, u32[]{:S(2)}, u32[]{:S(2)}) collective-permute-start(bf16[80,512]{1,0:T(8,128)(2,1)} %get-tuple-element.84.refs_0_), channel_id=1, source_target_pairs={{0,8},{1,9},{2,10},{3,11},{4,12},{5,13},{6,14},{7,15},{8,0},{9,1},... | collective-permute-start | bytes 245768 | tf_op jit(solution)/shard_map/ppermute | solution.py:50
  149.3 4.8 %collective-permute-start.44 = (bf16[80,512]{1,0:T(8,128)(2,1)}, bf16[80,512]{1,0:T(8,128)(2,1)S(1)}, u32[]{:S(2)}, u32[]{:S(2)}) collective-permute-start(bf16[80,512]{1,0:T(8,128)(2,1)} %get-tuple-element.84.refs_0_), channel_id=1, source_target_pairs={{0,4},{1,5},{2,6},{3,7},{4,8},{5,9},{6,10},{7,11},{8,12},{9,13},{1... | collective-permute-start | bytes 245768 | tf_op jit(solution)/shard_map/ppermute | solution.py:50
  156.5 21.1 %collective-permute-start.50 = (bf16[320,512]{1,0:T(8,128)(2,1)}, bf16[320,512]{1,0:T(8,128)(2,1)S(1)}, u32[]{:S(2)}, u32[]{:S(2)}) collective-permute-start(bf16[320,512]{1,0:T(8,128)(2,1)} %shard_map.88.refs_0_), channel_id=1, source_target_pairs={{0,1},{1,0},{2,3},{3,2},{4,5},{5,4},{6,7},{7,6},{8,9},{9,8},{10,11... | collective-permute-start | bytes 983048 | tf_op jit(solution)/shard_map/ppermute | solution.py:50
  161.0 17.9 %collective-permute-start.49 = (bf16[320,512]{1,0:T(8,128)(2,1)}, bf16[320,512]{1,0:T(8,128)(2,1)S(1)}, u32[]{:S(2)}, u32[]{:S(2)}) collective-permute-start(bf16[320,512]{1,0:T(8,128)(2,1)} %shard_map.88.refs_0_), channel_id=1, source_target_pairs={{0,48},{1,49},{2,50},{3,51},{4,52},{5,53},{6,54},{7,55},{8,56},{9,... | collective-permute-start | bytes 983048 | tf_op jit(solution)/shard_map/ppermute | solution.py:50
  163.9 6.1 %collective-permute-start.30 = (bf16[128,512]{1,0:T(8,128)(2,1)}, bf16[128,512]{1,0:T(8,128)(2,1)S(1)}, u32[]{:S(2)}, u32[]{:S(2)}) collective-permute-start(bf16[128,512]{1,0:T(8,128)(2,1)} %get-tuple-element.75.refs_0_), channel_id=1, source_target_pairs={{0,48},{1,67},{2,50},{3,65},{4,52},{5,71},{6,54},{7,69},{8,56},{9,... | collective-permute-start | bytes 393224 | tf_op jit(solution)/shard_map/ppermute | solution.py:50
  166.4 5.6 %collective-permute-start.29 = (bf16[128,512]{1,0:T(8,128)(2,1)}, bf16[128,512]{1,0:T(8,128)(2,1)S(1)}, u32[]{:S(2)}, u32[]{:S(2)}) collective-permute-start(bf16[128,512]{1,0:T(8,128)(2,1)} %get-tuple-element.75.refs_0_), channel_id=1, source_target_pairs={{0,32},{1,3},{2,34},{3,1},{4,36},{5,7},{6,38},{7,5},{8,40},{9,11},... | collective-permute-start | bytes 393224 | tf_op jit(solution)/shard_map/ppermute | solution.py:50
  166.9 6.4 %collective-permute-start.28 = (bf16[128,512]{1,0:T(8,128)(2,1)}, bf16[128,512]{1,0:T(8,128)(2,1)S(1)}, u32[]{:S(2)}, u32[]{:S(2)}) collective-permute-start(bf16[128,512]{1,0:T(8,128)(2,1)} %get-tuple-element.75.refs_0_), channel_id=1, source_target_pairs={{0,16},{1,65},{2,18},{3,67},{4,20},{5,69},{6,22},{7,71},{8,24},{9,... | collective-permute-start | bytes 393224 | tf_op jit(solution)/shard_map/ppermute | solution.py:50
  170.1 8.8 %collective-permute-start.48 = (bf16[320,512]{1,0:T(8,128)(2,1)}, bf16[320,512]{1,0:T(8,128)(2,1)}, u32[]{:S(2)}, u32[]{:S(2)}) collective-permute-start(bf16[320,512]{1,0:T(8,128)(2,1)} %shard_map.88.refs_0_), channel_id=1, source_target_pairs={{0,32},{1,33},{2,34},{3,35},{4,36},{5,37},{6,38},{7,39},{8,40},{9,... | collective-permute-start | bytes 983048 | tf_op jit(solution)/shard_map/ppermute | solution.py:50
  172.0 17.7 %collective-permute-start.47 = (bf16[320,512]{1,0:T(8,128)(2,1)}, bf16[320,512]{1,0:T(8,128)(2,1)S(1)}, u32[]{:S(2)}, u32[]{:S(2)}) collective-permute-start(bf16[320,512]{1,0:T(8,128)(2,1)} %shard_map.88.refs_0_), channel_id=1, source_target_pairs={{0,16},{1,17},{2,18},{3,19},{4,20},{5,21},{6,22},{7,23},{8,24},{9,... | collective-permute-start | bytes 983048 | tf_op jit(solution)/shard_map/ppermute | solution.py:50
  175.9 16.4 %collective-permute-start.33 = (bf16[512,512]{1,0:T(8,128)(2,1)}, bf16[512,512]{1,0:T(8,128)(2,1)S(1)}, u32[]{:S(2)}, u32[]{:S(2)}) collective-permute-start(bf16[512,512]{1,0:T(8,128)(2,1)} %shard_map.85.refs_0_), channel_id=1, source_target_pairs={{0,66},{1,13},{2,64},{3,15},{4,70},{5,1},{6,68},{7,3},{8,74},{9,5}... | collective-permute-start | bytes 1572872 | tf_op jit(solution)/shard_map/ppermute | solution.py:50
  177.6 28.2 %copy-start.25 = (bf16[320,512]{1,0:T(8,128)(2,1)}, bf16[320,512]{1,0:T(8,128)(2,1)S(1)}, u32[]{:S(2)}) copy-start(bf16[320,512]{1,0:T(8,128)(2,1)S(1)} %collective-permute-done.50.refs_4_) | copy-start | bytes 983044
  177.6 23.3 %collective-permute-start.32 = (bf16[512,512]{1,0:T(8,128)(2,1)}, bf16[512,512]{1,0:T(8,128)(2,1)S(1)}, u32[]{:S(2)}, u32[]{:S(2)}) collective-permute-start(bf16[512,512]{1,0:T(8,128)(2,1)} %shard_map.85.refs_0_), channel_id=1, source_target_pairs={{0,2},{1,9},{2,0},{3,11},{4,6},{5,13},{6,4},{7,15},{8,10},{9,1},{1... | collective-permute-start | bytes 1572872 | tf_op jit(solution)/shard_map/ppermute | solution.py:50
  178.9 27.0 %copy-start.26 = (bf16[320,512]{1,0:T(8,128)(2,1)}, bf16[320,512]{1,0:T(8,128)(2,1)S(1)}, u32[]{:S(2)}) copy-start(bf16[320,512]{1,0:T(8,128)(2,1)S(1)} %collective-permute-done.49.refs_3_) | copy-start | bytes 983044
  178.9 22.2 %collective-permute-start.31 = (bf16[512,512]{1,0:T(8,128)(2,1)}, bf16[512,512]{1,0:T(8,128)(2,1)}, u32[]{:S(2)}, u32[]{:S(2)}) collective-permute-start(bf16[512,512]{1,0:T(8,128)(2,1)} %shard_map.85.refs_0_), channel_id=1, source_target_pairs={{0,64},{1,5},{2,66},{3,7},{4,68},{5,9},{6,70},{7,11},{8,72},{9,13}... | collective-permute-start | bytes 1572872 | tf_op jit(solution)/shard_map/ppermute | solution.py:50
  178.9 26.0 %collective-permute-start.53 = (bf16[320,512]{1,0:T(8,128)(2,1)S(1)}, bf16[320,512]{1,0:T(8,128)(2,1)}, u32[]{:S(2)}, u32[]{:S(2)}) collective-permute-start(bf16[320,512]{1,0:T(8,128)(2,1)S(1)} %collective-permute-done.49.refs_3_), channel_id=1, source_target_pairs={{0,1},{1,0},{2,3},{3,2},{4,5},{5,4},{6,7},{7,6},{8,9},{9,8},{10,11... | collective-permute-start | bytes 983048 | tf_op jit(solution)/shard_map/ppermute | solution.py:50
  189.7 19.7 %collective-permute-start.52 = (bf16[320,512]{1,0:T(8,128)(2,1)}, bf16[320,512]{1,0:T(8,128)(2,1)}, u32[]{:S(2)}, u32[]{:S(2)}) collective-permute-start(bf16[320,512]{1,0:T(8,128)(2,1)} %collective-permute-done.48.refs_2_), channel_id=1, source_target_pairs={{0,1},{1,0},{2,3},{3,2},{4,5},{5,4},{6,7},{7,6},{8,9},{9,8},{10,11... | collective-permute-start | bytes 983048 | tf_op jit(solution)/shard_map/ppermute | solution.py:50
  192.3 25.4 %copy-start.12 = (bf16[512,512]{1,0:T(8,128)(2,1)}, bf16[512,512]{1,0:T(8,128)(2,1)S(1)}, u32[]{:S(2)}) copy-start(bf16[512,512]{1,0:T(8,128)(2,1)S(1)} %collective-permute-done.33.refs_3_) | copy-start | bytes 1572868
  192.3 33.9 %collective-permute-start.34 = (bf16[512,512]{1,0:T(8,128)(2,1)S(1)}, bf16[512,512]{1,0:T(8,128)(2,1)}, u32[]{:S(2)}, u32[]{:S(2)}) collective-permute-start(bf16[512,512]{1,0:T(8,128)(2,1)S(1)} %copy-done.6), channel_id=1, source_target_pairs={{0,1},{1,0},{2,3},{3,2},{4,5},{5,4},{6,7},{7,6},{8,9},{9,8},{10,11... | collective-permute-start | bytes 1572872 | tf_op jit(solution)/shard_map/ppermute | solution.py:50
  201.0 27.1 %collective-permute-start.37 = (bf16[512,512]{1,0:T(8,128)(2,1)S(1)}, bf16[512,512]{1,0:T(8,128)(2,1)}, u32[]{:S(2)}, u32[]{:S(2)}) collective-permute-start(bf16[512,512]{1,0:T(8,128)(2,1)S(1)} %collective-permute-done.33.refs_3_), channel_id=1, source_target_pairs={{0,1},{1,0},{2,3},{3,2},{4,5},{5,4},{6,7},{7,6},{8,9},{9,8},{10,11... | collective-permute-start | bytes 1572872 | tf_op jit(solution)/shard_map/ppermute | solution.py:50
  201.1 29.4 %collective-permute-start.36 = (bf16[512,512]{1,0:T(8,128)(2,1)S(1)}, bf16[512,512]{1,0:T(8,128)(2,1)}, u32[]{:S(2)}, u32[]{:S(2)}) collective-permute-start(bf16[512,512]{1,0:T(8,128)(2,1)S(1)} %collective-permute-done.32.refs_2_), channel_id=1, source_target_pairs={{0,1},{1,0},{2,3},{3,2},{4,5},{5,4},{6,7},{7,6},{8,9},{9,8},{10,11... | collective-permute-start | bytes 1572872 | tf_op jit(solution)/shard_map/ppermute | solution.py:50
  204.9 25.5 %collective-permute-start.35 = (bf16[512,512]{1,0:T(8,128)(2,1)}, bf16[512,512]{1,0:T(8,128)(2,1)}, u32[]{:S(2)}, u32[]{:S(2)}) collective-permute-start(bf16[512,512]{1,0:T(8,128)(2,1)} %collective-permute-done.31.refs_1_), channel_id=1, source_target_pairs={{0,1},{1,0},{2,3},{3,2},{4,5},{5,4},{6,7},{7,6},{8,9},{9,8},{10,11... | collective-permute-start | bytes 1572872 | tf_op jit(solution)/shard_map/ppermute | solution.py:50
  205.9 11.8 %all-to-all-start.2 = ((bf16[8,2,64,208]{3,2,1,0:T(8,128)(2,1)}), bf16[8,2,64,208]{3,2,1,0:T(8,128)(2,1)S(1)}, u32[]{:S(2)}, u32[]{:S(2)}) async-start(bf16[8,2,64,208]{3,2,1,0:T(8,128)(2,1)} %copy.93), calls=%async_computation.2 | async-start | bytes 1048576 | tf_op jit(solution)/shard_map/all_to_all | solution.py:537
  209.4 8.4 %collective-permute-start.51 = (bf16[320,512]{1,0:T(8,128)(2,1)}, bf16[320,512]{1,0:T(8,128)(2,1)S(1)}, u32[]{:S(2)}, u32[]{:S(2)}) collective-permute-start(bf16[320,512]{1,0:T(8,128)(2,1)} %copy-done.27), channel_id=1, source_target_pairs={{0,1},{1,0},{2,3},{3,2},{4,5},{5,4},{6,7},{7,6},{8,9},{9,8},{10,11... | collective-permute-start | bytes 983048 | tf_op jit(solution)/shard_map/ppermute | solution.py:50
  225.6 20.1 %collective-permute-start.54 = (bf16[128,2560]{1,0:T(8,128)(2,1)}, bf16[128,2560]{1,0:T(8,128)(2,1)}, u32[]{:S(2)}, u32[]{:S(2)}) collective-permute-start(bf16[128,2560]{1,0:T(8,128)(2,1)} %get-tuple-element.86), channel_id=1, source_target_pairs={{0,2},{1,3},{2,0},{3,1},{4,6},{5,7},{6,4},{7,5},{8,10},{9,11},{10,... | collective-permute-start | bytes 1966088 | tf_op jit(solution)/shard_map/ppermute | solution.py:50
  226.3 32.0 %collective-permute-start.55 = (bf16[128,2560]{1,0:T(8,128)(2,1)}, bf16[128,2560]{1,0:T(8,128)(2,1)}, u32[]{:S(2)}, u32[]{:S(2)}) collective-permute-start(bf16[128,2560]{1,0:T(8,128)(2,1)} %get-tuple-element.87), channel_id=1, source_target_pairs={{0,64},{1,65},{2,66},{3,67},{4,68},{5,69},{6,70},{7,71},{8,72},{9,... | collective-permute-start | bytes 1966088 | tf_op jit(solution)/shard_map/ppermute | solution.py:50
  228.0 32.1 %collective-permute-start.56 = (bf16[128,2560]{1,0:T(8,128)(2,1)}, bf16[128,2560]{1,0:T(8,128)(2,1)}, u32[]{:S(2)}, u32[]{:S(2)}) collective-permute-start(bf16[128,2560]{1,0:T(8,128)(2,1)} %get-tuple-element.88), channel_id=1, source_target_pairs={{0,66},{1,67},{2,64},{3,65},{4,70},{5,71},{6,68},{7,69},{8,74},{9,... | collective-permute-start | bytes 1966088 | tf_op jit(solution)/shard_map/ppermute | solution.py:50
  236.8 23.7 %collective-permute-start.41 = (bf16[128,2048]{1,0:T(8,128)(2,1)}, bf16[128,2048]{1,0:T(8,128)(2,1)S(1)}, u32[]{:S(2)}, u32[]{:S(2)}) collective-permute-start(bf16[128,2048]{1,0:T(8,128)(2,1)} %get-tuple-element.81), channel_id=1, source_target_pairs={{0,8},{1,9},{2,10},{3,11},{4,12},{5,13},{6,14},{7,15},{8,0},{9,1},... | collective-permute-start | bytes 1572872 | tf_op jit(solution)/shard_map/ppermute | solution.py:50
  237.9 32.4 %collective-permute-start.42 = (bf16[128,2048]{1,0:T(8,128)(2,1)}, bf16[128,2048]{1,0:T(8,128)(2,1)S(1)}, u32[]{:S(2)}, u32[]{:S(2)}) collective-permute-start(bf16[128,2048]{1,0:T(8,128)(2,1)} %get-tuple-element.82), channel_id=1, source_target_pairs={{0,4},{1,5},{2,6},{3,7},{4,8},{5,9},{6,10},{7,11},{8,12},{9,13},{1... | collective-permute-start | bytes 1572872 | tf_op jit(solution)/shard_map/ppermute | solution.py:50
  245.7 24.7 %collective-permute-start.43 = (bf16[128,2048]{1,0:T(8,128)(2,1)}, bf16[128,2048]{1,0:T(8,128)(2,1)}, u32[]{:S(2)}, u32[]{:S(2)}) collective-permute-start(bf16[128,2048]{1,0:T(8,128)(2,1)} %get-tuple-element.83), channel_id=1, source_target_pairs={{0,12},{1,13},{2,14},{3,15},{4,0},{5,1},{6,2},{7,3},{8,4},{9,5},{1... | collective-permute-start | bytes 1572872 | tf_op jit(solution)/shard_map/ppermute | solution.py:50
  258.2 17.1 %collective-permute-start.38 = (bf16[128,2048]{1,0:T(8,128)(2,1)}, bf16[128,2048]{1,0:T(8,128)(2,1)S(1)}, u32[]{:S(2)}, u32[]{:S(2)}) collective-permute-start(bf16[128,2048]{1,0:T(8,128)(2,1)} %get-tuple-element.77), channel_id=1, source_target_pairs={{0,32},{1,33},{2,34},{3,35},{4,36},{5,37},{6,38},{7,39},{8,40},{9,... | collective-permute-start | bytes 1572872 | tf_op jit(solution)/shard_map/ppermute | solution.py:50
  260.2 25.0 %collective-permute-start.39 = (bf16[128,2048]{1,0:T(8,128)(2,1)}, bf16[128,2048]{1,0:T(8,128)(2,1)}, u32[]{:S(2)}, u32[]{:S(2)}) collective-permute-start(bf16[128,2048]{1,0:T(8,128)(2,1)} %get-tuple-element.78), channel_id=1, source_target_pairs={{0,16},{1,17},{2,18},{3,19},{4,20},{5,21},{6,22},{7,23},{8,24},{9,... | collective-permute-start | bytes 1572872 | tf_op jit(solution)/shard_map/ppermute | solution.py:50
  260.5 24.6 %collective-permute-start.40 = (bf16[128,2048]{1,0:T(8,128)(2,1)}, bf16[128,2048]{1,0:T(8,128)(2,1)}, u32[]{:S(2)}, u32[]{:S(2)}) collective-permute-start(bf16[128,2048]{1,0:T(8,128)(2,1)} %get-tuple-element.79), channel_id=1, source_target_pairs={{0,48},{1,49},{2,50},{3,51},{4,52},{5,53},{6,54},{7,55},{8,56},{9,... | collective-permute-start | bytes 1572872 | tf_op jit(solution)/shard_map/ppermute | solution.py:50
  (39 other events, 189.6 us)
where the time goes:
time: 291 us; the launch traced here: 290 us
  starting transfers between devices  111 us (38%)
  Pallas kernels  80.2 us (28%)
  waiting for transfers between devices  59.3 us (20%)
  local copies, waits for them, and re-layouts  30.7 us (11%)
  other arithmetic  5.26 us (2%)
    ppermute x56, starting transfers between devices, shift(): return lax.ppermute(array, NAMES, pairs)  97.7 us
    ppermute x56, waiting for transfers between devices, shift(): return lax.ppermute(array, NAMES, pairs)  46.6 us
    pallas_call x4, Pallas kernels, project(): pl.pallas_call(functools.partial(project_kernel, group, own), out_shape=s...  21.7 us
    pallas_call x3, Pallas kernels, update_blocks(): pl.pallas_call(functools.partial(update_kernel, ring), out_shape=[jax.Sha...  19.9 us
    pallas_call x3, Pallas kernels, pack(): pl.pallas_call(functools.partial(pack_kernel, ring), out_shape=[jax.Shape...  13.4 us
    pallas_call x3, Pallas kernels, unpack(): pl.pallas_call(functools.partial(unpack_kernel, ring), out_shape=jax.Shap...  12.9 us
    unnamed x90, local copies, waits for them, and re-layouts  11.1 us
    all_to_all x1, waiting for transfers between devices, compute(): new = lax.all_to_all(new, ROW, 0, 0, tiled=True).astype(F32)  7.66 us
  transfers between devices with their start and end apart: 60, of which 15 were waited for; matrix products, arithmetic and copies ran while one was open for 10% of the time, Pallas kernels for 23%

commit v1 on v0

--- a/solution.py
+++ b/solution.py
@@ -18,7 +18,7 @@
 SMEM = pl.BlockSpec(memory_space=pltpu.SMEM)
 VMEM = pl.BlockSpec(memory_space=pltpu.VMEM)
 DMA = pltpu.SemaphoreType.DMA
-STEPS = (0, 2, 1, 3)
+STEPS = (0, 1, 3, 2)
 WIDTH = {"y": 2048, "z": 2048, "x": 2560}
 GROUPS = ((2048, 128), (1280, 80))
 TILE = (512, 640)
@@ -97,39 +97,47 @@
         copy.wait()
 
 
+def wait_for(ref, sem):
+    pltpu.make_async_copy(ref, ref, sem).wait()
+
+
 def turned(tile):
     return pltpu.roll(tile.astype(F32), 64, 1).astype(BF)
 
 
 def pack_kernel(ring, where, grad, *refs):
     outs, (held, in_sem, out_sem), more = refs[:4], refs[4:7], refs[7:]
-    loads = [
-        [
-            pltpu.make_async_copy(grad.at[:, pl.ds(source, count)], held.at[at, :, pl.ds(to, count)], in_sem.at[at, j])
-            for j, (to, source, count) in enumerate(runs(ring, at))
-        ]
-        for at in range(4)
-    ]
-    for copies in loads:
-        start_all(copies)
     if ring == "x":
         ends, end_sem = more
-        copies = start_all(
+        end_copies = start_all(
             [pltpu.make_async_copy(grad.at[:, pl.ds(b * 1664 + 1536, 128)], ends.at[b], end_sem.at[b]) for b in range(16)]
         )
-        wait_all(copies)
+    for at in range(4):
+        start_all(
+            [
+                pltpu.make_async_copy(grad.at[:, pl.ds(source, count)], held.at[at, :, pl.ds(to, count)], in_sem.at[at])
+                for to, source, count in runs(ring, at)
+            ]
+        )
+    whole = held
+    if ring == "x":
+        wait_all(end_copies)
         left = lax.broadcasted_iota(jnp.int32, (128, 128), 1) < 64
         for xh, core, pair in itertools.product(range(2), range(2), range(2)):
             one, two = (ends[(2 * pair + i) * 4 + xh * 2 + core] for i in range(2))
             columns = pl.ds(core * 1280 + 1024 + pair * 128, 128)
             held[xh * 2, :, columns] = jnp.where(left, one, turned(two))
             held[xh * 2 + 1, :, columns] = jnp.where(left, turned(one), two)
-    for copies in loads:
-        wait_all(copies)
+        whole = held.at[:, :, pl.ds(0, 2048)]
     t = place(where, ring)
-    wait_all(
-        start_all([pltpu.make_async_copy(held.at[(t + step) % 4], outs[k], out_sem.at[k]) for k, step in enumerate(STEPS)])
-    )
+    stores = []
+    for k, step in enumerate(STEPS):
+        at = (t + step) % 4
+        wait_for(whole.at[at], in_sem.at[at])
+        copy = pltpu.make_async_copy(held.at[at], outs[k], out_sem.at[k])
+        copy.start()
+        stores.append(copy)
+    wait_all(stores)
 
 
 def pack(ring, where, grad):
@@ -139,7 +147,7 @@
         out_shape=[jax.ShapeDtypeStruct((128, width), BF)] * 4,
         in_specs=[SMEM, ANY],
         out_specs=[ANY] * 4,
-        scratch_shapes=[pltpu.VMEM((4, 128, width), BF), DMA((4, 16)), DMA((4,))]
+        scratch_shapes=[pltpu.VMEM((4, 128, width), BF), DMA((4,)), DMA((4,))]
         + ([pltpu.VMEM((16, 128, 128), BF), DMA((16,))] if ring == "x" else []),
         cost_estimate=estimate(0, 4 * 128 * width * 4),
     )(where, grad)
@@ -152,20 +160,21 @@
     else:
         out, held, in_sem, out_sem = refs[-4:]
     t = place(where, ring)
-    wait_all(
-        start_all(
+    start_all(
+        [
+            pltpu.make_async_copy(blocks[k], held.at[(t + 4 - step) % 4], in_sem.at[(t + 4 - step) % 4])
+            for k, step in enumerate(STEPS)
+        ]
+    )
+    stores = []
+    for at in range(4):
+        wait_for(held.at[at], in_sem.at[at])
+        stores += start_all(
             [
-                pltpu.make_async_copy(blocks[k], held.at[(t + 4 - step) % 4], in_sem.at[k])
-                for k, step in enumerate(STEPS)
+                pltpu.make_async_copy(held.at[at, :, pl.ds(to, count)], out.at[:, pl.ds(source, count)], out_sem.at[at, j])
+                for j, (to, source, count) in enumerate(runs(ring, at))
             ]
         )
-    )
-    stores = [
-        pltpu.make_async_copy(held.at[at, :, pl.ds(to, count)], out.at[:, pl.ds(source, count)], out_sem.at[at, j])
-        for at in range(4)
-        for j, (to, source, count) in enumerate(runs(ring, at))
-    ]
-    start_all(stores)
     if ring == "x":
         left = lax.broadcasted_iota(jnp.int32, (128, 128), 1) < 64
         for xh, core, pair in itertools.product(range(2), range(2), range(2)):
@@ -174,10 +183,8 @@
             block = 2 * pair * 4 + xh * 2 + core
             ends[block] = jnp.where(left, one, turned(two))
             ends[block + 4] = jnp.where(left, turned(one), two)
-        wait_all(
-            start_all(
-                [pltpu.make_async_copy(ends.at[b], out.at[:, pl.ds(b * 1664 + 1536, 128)], end_sem.at[b]) for b in range(16)]
-            )
+        stores += start_all(
+            [pltpu.make_async_copy(ends.at[b], out.at[:, pl.ds(b * 1664 + 1536, 128)], end_sem.at[b]) for b in range(16)]
         )
     wait_all(stores)
 
@@ -214,14 +221,15 @@
     return base.at[pl.ds(pl.multiple_of(first * 128, 128), 128), :]
 
 
-def load_blocks(ring, where, blocks, columns, bases, held, base, in_sem, base_sem):
-    copies = []
+def start_blocks(ring, where, blocks, first, chunk, tile, bases, held, base, in_sem, base_sem):
     for k, step in enumerate(STEPS):
-        rows = pl.ds(k * 128, 128)
-        copies.append(pltpu.make_async_copy(blocks[k].at[:, columns], held.at[rows, :], in_sem.at[k]))
         source = basis_rows(ring, where, 4 - step, bases)
-        copies.append(pltpu.make_async_copy(source, base.at[rows, :], base_sem.at[k]))
-    return copies
+        pltpu.make_async_copy(source, base.at[pl.ds(k * 128, 128), :], base_sem).start()
+    for i in range(chunk // tile):
+        for k in range(4):
+            columns = pl.ds(pl.multiple_of(first + i * tile, 128), tile)
+            target = held.at[pl.ds(k * 128, 128), pl.ds(i * tile, tile)]
+            pltpu.make_async_copy(blocks[k].at[:, columns], target, in_sem.at[i]).start()
 
 
 def project_kernel(group, own, where, *refs):
@@ -231,39 +239,38 @@
         other, outs, (held, base, total, in_sem, base_sem, other_sem, out_sem) = refs[0], refs[1:5], refs[5:]
     else:
         out, held, base, total, in_sem, base_sem, out_sem = refs
-    chunk = GROUPS[group][0]
+    chunk, tile = GROUPS[group][0], TILE[group]
     core = place(where, "core")
-    scratch = (bases, held, base, in_sem, base_sem)
+    scratch = (chunk, tile, bases, held, base, in_sem, base_sem)
+    if group == 0:
+        on_y = core == (0 if own else 1)
+        for ring, mine, chosen in (("y", blocks[:4], on_y), ("z", blocks[4:], jnp.logical_not(on_y))):
+
+            @pl.when(chosen)
+            def _():
+                start_blocks(ring, where, mine, 0, *scratch)
+
+    else:
+        start_blocks("x", where, blocks, (core if own else 1 - core) * chunk, *scratch)
     if own:
         copy = pltpu.make_async_copy(other, total, other_sem)
         copy.start()
-    if group == 0:
-        on_y = core == (0 if own else 1)
-        for ring, mine, chosen in (("y", blocks[:4], on_y), ("z", blocks[4:], jnp.logical_not(on_y))):
-
-            @pl.when(chosen)
-            def _():
-                wait_all(start_all(load_blocks(ring, where, mine, pl.ds(0, chunk), *scratch)))
-
-    else:
-        first = (core if own else 1 - core) * chunk
-        columns = pl.ds(pl.multiple_of(first, 128), chunk)
-        wait_all(start_all(load_blocks("x", where, blocks, columns, *scratch)))
-    if own:
         copy.wait()
-
-    tile = TILE[group]
+    wait_for(base, base_sem)
 
     @pl.loop(0, chunk // tile)
     def _(i):
         some = pl.ds(pl.multiple_of(i * tile, tile), tile)
+        wait_for(held.at[:, some], in_sem.at[i])
         product = lax.dot_general(held[:, some], base[...], (((0,), (0,)), ((), ())), preferred_element_type=F32)
         if own:
             product = product + total[some, :].astype(F32)
         total[some, :] = product.astype(BF)
+        if not own:
+            pltpu.make_async_copy(total.at[some, :], out.at[some, :], out_sem).start()
 
     if not own:
-        wait_all(start_all([pltpu.make_async_copy(total, out, out_sem)]))
+        wait_for(total, out_sem)
         return
     stores = []
     for j in range(4):
@@ -292,7 +299,7 @@
             pltpu.VMEM((512, 512), BF),
             pltpu.VMEM((chunk, 512), BF),
             DMA((4,)),
-            DMA((4,)),
+            DMA,
         ]
         + ([DMA, DMA((4, 8))] if own else [DMA]),
         cost_estimate=estimate(2 * 512 * 512 * chunk, 512 * chunk * 2 + 512 * 1024 + chunk * 1024),
@@ -322,9 +329,71 @@
     )(where, *arrays)
 
 
+def moments_kernel(where, first, second, new, old, out, half, old_held, sem):
+    core = place(where, "core")
+    columns = pl.ds(pl.multiple_of(core * 256, 256), 256)
+    copies = start_all([pltpu.make_async_copy(new.at[:, columns], half, sem.at[0]), pltpu.make_async_copy(old, old_held, sem.at[1])])
+    left = lax.broadcasted_iota(jnp.int32, (64, 128), 1) < 64
+    for q in range(8):
+        for ref, begin in ((first, 0), (second, 128)):
+            one = ref[:, q * 128 : q * 128 + 128]
+            two = ref[:, 1024 + q // 2 * 128 : 1152 + q // 2 * 128]
+            if q % 2:
+                two = pltpu.roll(two, 64, 1)
+            two = jnp.where(left, two, pltpu.roll(ref[:, 1536:1664], (192 - q * 16) % 128, 1))
+            for i, value in enumerate((one, two)):
+                high = value.astype(BF)
+                out[q, begin : begin + 64, i * 128 : i * 128 + 128] = high
+                if begin == 0:
+                    out[q, 64:128, i * 128 : i * 128 + 128] = (value - high.astype(F32)).astype(BF)
+    wait_all(copies)
+    margin = lax.dot_general(half[...], old_held[...], (((0,), (0,)), ((), ())), preferred_element_type=F32)
+    margin = margin.astype(BF)
+    for q in range(8):
+        for i in range(2):
+            out[q, 192 + 32 * i : 224 + 32 * i, :] = margin[q * 32 : q * 32 + 32, i * 256 : i * 256 + 256]
+
+
+def cut_moments(where, first, second, new, old):
+    return pl.pallas_call(
+        moments_kernel,
+        out_shape=jax.ShapeDtypeStruct((8, 256, 256), BF),
+        in_specs=[SMEM, VMEM, VMEM, ANY, ANY],
+        out_specs=VMEM,
+        scratch_shapes=[pltpu.VMEM((2048, 256), BF), pltpu.VMEM((2048, 512), BF), DMA((2,))],
+        cost_estimate=estimate(2 * 2048 * 256 * 512, 6 * 2**20),
+        name="cut_moments",
+    )(where, first, second, new, old)
+
+
+def margin_kernel(moments, out, held, sem):
+    copy = pltpu.make_async_copy(moments.at[:, pl.ds(192, 64), :], held, sem)
+    copy.start()
+    copy.wait()
+    total = held[0].astype(F32)
+    for i in range(1, 8):
+        total = total + held[i].astype(F32)
+    total = total.astype(BF)
+    for i in range(8):
+        out[i, :, 0:256] = total[:32]
+        out[i, :, 256:512] = total[32:]
+
+
+def sum_margin(moments):
+    return pl.pallas_call(
+        margin_kernel,
+        out_shape=jax.ShapeDtypeStruct((8, 32, 512), BF),
+        in_specs=[ANY],
+        out_specs=VMEM,
+        scratch_shapes=[pltpu.VMEM((8, 64, 256), BF), DMA],
+        cost_estimate=estimate(8 * 64 * 256, 2**19),
+        name="sum_margin",
+    )(moments)
+
+
 def step_kernel(where, *refs):
-    sums, (own, other, one, one_low, two), lows = refs[:8], refs[8:13], refs[13:15]
-    first_out, second_out, margin = refs[15:]
+    sums, (own, other, moments), lows = refs[:8], refs[8:11], refs[11:13]
+    first_out, second_out, margin = refs[13:]
     core = place(where, "core")
     margin[rows_at(core * 256, 256), :] = own[...]
     margin[rows_at(256 - core * 256, 256), :] = other[...]
@@ -332,12 +401,13 @@
         [sum(ref[...].astype(F32) for ref in sums[4 * g : 4 * g + 4]) for g in range(2)], axis=0
     )
     contract = (((0,), (1,)), ((), ()))
-    rotated_one = lax.dot_general(one[...], margin[...], contract, preferred_element_type=F32)
-    rotated_one = rotated_one + lax.dot_general(one_low[...], margin[...], contract, preferred_element_type=F32)
+    one, one_low, two = (moments[:, i * 64 : i * 64 + 64, :].reshape(512, 256) for i in range(3))
+    rotated_one = lax.dot_general(one, margin[...], contract, preferred_element_type=F32)
+    rotated_one = rotated_one + lax.dot_general(one_low, margin[...], contract, preferred_element_type=F32)
     wide = margin[...].astype(F32)
-    rotated_two = lax.dot_general(two[...], (wide * wide).astype(BF), contract, preferred_element_type=F32)
-    first_new = 0.9 * rotated_one + 0.1 * projected
-    second_new = 0.999 * rotated_two + 0.001 * projected * projected
+    rotated_two = lax.dot_general(two, (wide * wide).astype(BF), contract, preferred_element_type=F32)
+    first_new = 0.9 * rotated_one[:208] + 0.1 * projected
+    second_new = 0.999 * rotated_two[:208] + 0.001 * projected * projected
     low_step = (
         first_new / (1.0 - 0.9**STEP) / (jnp.sqrt(second_new / (1.0 - 0.999**STEP)) + 1e-08)
     ).astype(BF)
@@ -354,12 +424,58 @@
         step_kernel,
         out_shape=[jax.ShapeDtypeStruct((piece, 512), BF) for _, piece in GROUPS]
         + [jax.ShapeDtypeStruct((208, 512), F32)] * 2,
-        in_specs=[SMEM] + [VMEM] * 13,
+        in_specs=[SMEM] + [VMEM] * 11,
         out_specs=[VMEM] * 4,
         scratch_shapes=[pltpu.VMEM((512, 512), BF)],
         cost_estimate=estimate(6 * 208 * 512 * 512, 4 * 2**20),
         name="step",
     )(where, *sums, *rest)
+
+
+def turn_kernel(first, second, out, wide):
+    wide[208:, :] = jnp.zeros((48, 512), F32)
+    for i, ref in enumerate((first, second)):
+        wide[:208, :] = ref[...]
+        out[:, i * 64 : i * 64 + 64, :] = wide[...].T.astype(BF).reshape(8, 64, 256)
+
+
+def turn_back(first, second):
+    return pl.pallas_call(
+        turn_kernel,
+        out_shape=jax.ShapeDtypeStruct((8, 128, 256), BF),
+        in_specs=[VMEM] * 2,
+        out_specs=VMEM,
+        scratch_shapes=[pltpu.VMEM((256, 512), F32)],
+        cost_estimate=estimate(208 * 1024, 3 * 2**19),
+        name="turn_back",
+    )(first, second)
+
+
+def finish_kernel(new, *outs):
+    lane = lax.broadcasted_iota(jnp.int32, (64, 128), 1)
+    for i, out in enumerate(outs):
+        rest = []
+        for q in range(8):
+            block = new[q, i * 64 : i * 64 + 64, :].astype(F32)
+            out[:, q * 128 : q * 128 + 128] = block[:, :128]
+            rest.append(block[:, 128:])
+        for j in range(4):
+            out[:, 1024 + j * 128 : 1152 + j * 128] = jnp.where(lane < 64, rest[2 * j], pltpu.roll(rest[2 * j + 1], 64, 1))
+        last = pltpu.roll(rest[0], 64, 1)
+        for q in range(1, 8):
+            last = jnp.where(lane // 16 == q, pltpu.roll(rest[q], (64 + q * 16) % 128, 1) if q != 4 else rest[q], last)
+        out[:, 1536:1664] = last
+
+
+def finish(new):
+    return pl.pallas_call(
+        finish_kernel,
+        out_shape=[jax.ShapeDtypeStruct((64, 1664), F32)] * 2,
+        in_specs=[VMEM],
+        out_specs=[VMEM] * 2,
+        cost_estimate=estimate(64 * 1664 * 4, 3 * 2**19),
+        name="finish",
+    )(new)
 
 
 def join_kernel(group, where, *refs):
@@ -389,10 +505,11 @@
     copies = []
     for j in range(4):
         done = 0
-        for i, (first, size) in enumerate(pieces(group, (u + 4 - j) % 4)):
+        at = (u + 4 - j) % 4
+        for first, size in pieces(group, at):
             copies.append(
                 pltpu.make_async_copy(
-                    arrays[j].at[pl.ds(done, size), :], low.at[rows_at(begin + first, size), :], in_sem.at[j, i]
+                    arrays[j].at[pl.ds(done, size), :], low.at[rows_at(begin + first, size), :], in_sem.at[at]
                 )
             )
             done += size
@@ -404,34 +521,39 @@
     low, base, held, in_sem, other_sem, base_sem, out_sem = refs[17:]
     core = place(where, "core")
     width = WIDTH[ring]
-    copies = []
     for k, step in enumerate(STEPS):
         source = basis_rows(ring, where, step, bases)
-        copies.append(pltpu.make_async_copy(source, base.at[pl.ds(k * 128, 128), :], base_sem.at[k]))
-    start_all(copies)
+        pltpu.make_async_copy(source, base.at[pl.ds(k * 128, 128), :], base_sem).start()
     if ring == "x":
-        more = low_copies(1, where, own, core * 1280, low, in_sem, core)
-        more += low_copies(1, where, other, (1 - core) * 1280, low, other_sem, 1 - core)
-        wait_all(start_all(more))
+        start_all(low_copies(1, where, own, core * 1280, low, in_sem, core))
+        start_all(low_copies(1, where, other, (1 - core) * 1280, low, other_sem, 1 - core))
+        for at in range(4):
+            wait_for(low.at[pl.ds(0, 320), :], in_sem.at[at])
+            wait_for(low.at[pl.ds(0, 320), :], other_sem.at[at])
     else:
         part_core = 0 if ring == "y" else 1
         for arrays, chosen in ((own, core == part_core), (other, core != part_core)):
 
             @pl.when(chosen)
             def _():
-                wait_all(start_all(low_copies(0, where, arrays, 0, low, in_sem, jnp.int32(part_core))))
-
-    wait_all(copies)
+                start_all(low_copies(0, where, arrays, 0, low, in_sem, jnp.int32(part_core)))
+
+    wait_for(base, base_sem)
 
     @pl.loop(0, width // 512)
     def _(i):
         columns = pl.ds(pl.multiple_of(i * 512, 512), 512)
+        if ring != "x":
+            wait_for(low.at[columns, :], in_sem.at[i])
         product = lax.dot_general(base[...], low[columns, :], (((1,), (1,)), ((), ())), preferred_element_type=F32)
         held[:, columns] = (8.0 * product).astype(BF)
-
-    wait_all(
-        start_all([pltpu.make_async_copy(held.at[pl.ds(k * 128, 128), :], outs[k], out_sem.at[k]) for k in range(4)])
-    )
+        for k in range(4):
+            pltpu.make_async_copy(
+                held.at[pl.ds(k * 128, 128), columns], outs[k].at[:, columns], out_sem.at[k]
+            ).start()
+
+    for k in range(4):
+        wait_for(held.at[pl.ds(k * 128, 128), :], out_sem.at[k])
 
 
 def update_blocks(ring, where, arrays, bases):
@@ -445,30 +567,22 @@
             pltpu.VMEM((width, 512), BF),
             pltpu.VMEM((512, 512), BF),
             pltpu.VMEM((512, width), BF),
-            DMA((4, 8)),
-            DMA((4, 8)),
             DMA((4,)),
+            DMA((4,)),
+            DMA,
             DMA((4,)),
         ],
         cost_estimate=estimate(2 * 512 * 512 * width, 512 * width * 2 + 512 * 1024 + width * 1024),
     )(where, *arrays, *bases)
 
 
-def spread(moment):
-    own = moment.shape[0]
-    parts = [moment[:, :1024].reshape(own, 8, 128), moment[:, 1024:1536].reshape(own, 8, 64), moment[:, 1536:].reshape(own, 8, 16)]
-    return jnp.concatenate(parts, axis=-1).transpose(1, 0, 2)
-
-
-def gather_back(moment):
-    own = moment.shape[1]
-    moment = moment.transpose(1, 0, 2)
-    parts = [moment[:, :, :128].reshape(own, 1024), moment[:, :, 128:192].reshape(own, 512), moment[:, :, 192:].reshape(own, 128)]
-    return jnp.concatenate(parts, axis=-1)
-
-
 def exchange(blocks, rings):
     return [blocks[0]] + [shift(block, rings, step) for block, step in zip(blocks[1:], STEPS[1:])]
+
+
+def ordered(arrays, rings):
+    out = dict([(0, arrays[0])] + [(j, shift(arrays[j], rings, j)) for j in STEPS[1:]])
+    return [out[j] for j in range(4)]
 
 
 def compute(grad, basis_new, basis_old, moment_first, moment_second):
@@ -489,20 +603,9 @@
     bases = [basis_new] + [shift(by_z, RINGS["z"], 4 - step) for step in range(1, 4)]
     bases.append(lax.ppermute(by_x.reshape(256, 512), "xl", [(0, 1), (1, 0)]))
 
-    half = lax.dynamic_slice_in_dim(basis_new, core * 256, 256, 1)
-    margin = jnp.dot(half.T, basis_old, preferred_element_type=F32).astype(BF).reshape(8, 32, 512)
-    margin = jnp.pad(margin, ((0, 0), (0, 0), (0, 112))).reshape(8, 32, 3, 208).transpose(0, 2, 1, 3)
-    first = spread(moment_first)
-    first_high = first.astype(BF)
-    first_low = (first - first_high.astype(F32)).astype(BF)
-    moments = jnp.concatenate(
-        [first_high, first_low, spread(moment_second).astype(BF), margin.reshape(8, 96, 208)], axis=1
-    )
+    moments = cut_moments(where, moment_first, moment_second, basis_new, basis_old)
     moments = lax.all_to_all(moments, ROW, 0, 0, tiled=True)
-    one, one_low, two = (moments[:, i * 64 : i * 64 + 64].reshape(512, 208) for i in range(3))
-    margin = jnp.sum(moments[:, 192:].astype(F32), axis=0).astype(BF)
-    margin = margin.reshape(3, 32, 208).transpose(1, 0, 2).reshape(32, 624)[:, :512]
-    margin = jnp.broadcast_to(margin, (8, 32, 512))
+    margin = sum_margin(moments)
     margin = lax.all_to_all(margin, ROW, 0, 0, tiled=True).reshape(256, 512)
     margin_other = shift(margin, RINGS["core"], 1)
 
@@ -511,20 +614,18 @@
         other = project(group, where, blocks, bases)
         other = shift(other, RINGS["core"], 1)
         partial = project(group, where, blocks, bases, other)
-        halves = [partial[0]] + [shift(partial[j], U[group], j) for j in (2, 1, 3)]
+        halves = ordered(partial, U[group])
         rest = add_up(group, where, halves)
-        totals[group] = [rest[0]] + [shift(rest[j], V[group], j) for j in (2, 1, 3)]
-
-    *lows, first_new, second_new = take_step(
-        where, totals[0] + totals[1], margin, margin_other, one, one_low, two
-    )
+        totals[group] = ordered(rest, V[group])
+
+    *lows, first_new, second_new = take_step(where, totals[0] + totals[1], margin, margin_other, moments)
 
     sent = {}
     for group, rings in ((1, ("x",)), (0, ("y", "z"))):
         low = lows[group]
-        quarters = [low] + [shift(low, V[group], j) for j in range(1, 4)]
+        quarters = ordered([low] * 4, V[group])
         quarter = join(group, where, quarters)
-        whole = [quarter] + [shift(quarter, U[group], j) for j in range(1, 4)]
+        whole = ordered([quarter] * 4, U[group])
         whole = whole + [shift(array, RINGS["core"], 1) for array in whole]
         for ring in rings:
             blocks = update_blocks(ring, where, whole, bases)
@@ -533,9 +634,10 @@
     for ring in ("x", "y", "z"):
         update = unpack(ring, where, sent[ring], update, grad.shape[1])
 
-    new = jnp.stack([first_new.T.reshape(8, 64, 208), second_new.T.reshape(8, 64, 208)], axis=1).astype(BF)
-    new = lax.all_to_all(new, ROW, 0, 0, tiled=True).astype(F32)
-    return update, gather_back(new[:, 0]), gather_back(new[:, 1])
+    new = turn_back(first_new, second_new)
+    new = lax.all_to_all(new, ROW, 0, 0, tiled=True)
+    first, second = finish(new)
+    return update, first, second
 
 
 def solution(mesh):

time: 291 us -> 293 us (level)
  the two profiles are of different devices: /device:TPU:1 before, /device:TPU:6 now
where the time goes in v1:
time: 293 us; the launch traced here: 292 us
  starting transfers between devices  91.5 us (31%)
  Pallas kernels  83.2 us (28%)
  waiting for transfers between devices  77.5 us (26%)
  blocking collectives  24.1 us (8%)
  local copies, waits for them, and re-layouts  13.7 us (5%)
    ppermute x56, starting transfers between devices, shift(): return lax.ppermute(array, NAMES, pairs)  80.4 us
    ppermute x56, waiting for transfers between devices, shift(): return lax.ppermute(array, NAMES, pairs)  72.9 us
    all_to_all x1, blocking collectives, compute(): new = lax.all_to_all(new, ROW, 0, 0, tiled=True)  24.1 us
    pallas_call x4, Pallas kernels, project(): pl.pallas_call(functools.partial(project_kernel, group, own), out_shape=s...  21.3 us
    pallas_call x3, Pallas kernels, update_blocks(): pl.pallas_call(functools.partial(update_kernel, ring), out_shape=[jax.Sha...  16.2 us
    pallas_call x3, Pallas kernels, unpack(): pl.pallas_call(functools.partial(unpack_kernel, ring), out_shape=jax.Shap...  11.9 us
    unnamed x98, local copies, waits for them, and re-layouts  11.8 us
    pallas_call x3, Pallas kernels, pack(): pl.pallas_call(functools.partial(pack_kernel, ring), out_shape=[jax.Shape...  10.8 us
  transfers between devices with their start and end apart: 59, of which 16 were waited for; matrix products, arithmetic and copies ran while one was open for 1% of the time, Pallas kernels for 24%

profile of v1, /device:TPU:6, one launch (start us, length us, event | category | flops | bytes accessed | tf_op | source)
XLA Modules:
  0.0 292.0 jit_solution(4357569990502182457)
XLA Ops:
  1.2 3.3 %shard_map.76 = (bf16[128,2048]{1,0:T(8,128)(2,1)}, bf16[128,2048]{1,0:T(8,128)(2,1)}, bf16[128,2048]{1,0:T(8,128)(2,1)}, bf16[128,2048]{1,0:T(8,128)(2,1)}) custom-call(s32[8]{0:T(128)} %compare_select_fusion.6.where, bf16[128,26624]{1,0:T(8,128)(2,1)} %grad.5), custom_call_target="tpu_custom_call" | custom-call | bytes 4194304 | tf_op jit(solution)/shard_map/pallas_call | solution.py:145
  4.5 1.7 collective-permute-start
  9.0 2.0 collective-permute-start.8
  10.9 3.6 %collective-permute-start.7 = (bf16[128,512]{1,0:T(8,128)(2,1)S(1)}, bf16[128,512]{1,0:T(8,128)(2,1)S(1)}, u32[]{:S(2)}, u32[]{:S(2)}) collective-permute-start(bf16[128,512]{1,0:T(8,128)(2,1)S(1)} %dynamic-slice_bitcast_fusion), channel_id=1, source_target_pairs={{0,32},{1,33},{2,34},{3,35},{4,36},{5,37},{6,38},{7,39},{8,40},{9,... | collective-permute-start | bytes 393224 | tf_op jit(solution)/shard_map/ppermute | solution.py:50
  15.5 3.2 %shard_map.77 = (bf16[128,2048]{1,0:T(8,128)(2,1)}, bf16[128,2048]{1,0:T(8,128)(2,1)}, bf16[128,2048]{1,0:T(8,128)(2,1)}, bf16[128,2048]{1,0:T(8,128)(2,1)}) custom-call(s32[8]{0:T(128)} %compare_select_fusion.6.where, bf16[128,26624]{1,0:T(8,128)(2,1)} %grad.5), custom_call_target="tpu_custom_call" | custom-call | bytes 4194304 | tf_op jit(solution)/shard_map/pallas_call | solution.py:145
  18.8 1.9 collective-permute-start.1
  20.7 2.5 collective-permute-start.2
  23.7 2.7 collective-permute-start.4
  26.5 4.3 %shard_map.81 = (bf16[128,2560]{1,0:T(8,128)(2,1)}, bf16[128,2560]{1,0:T(8,128)(2,1)}, bf16[128,2560]{1,0:T(8,128)(2,1)}, bf16[128,2560]{1,0:T(8,128)(2,1)}) custom-call(s32[8]{0:T(128)} %compare_select_fusion.6.where, bf16[128,26624]{1,0:T(8,128)(2,1)} %grad.5), custom_call_target="tpu_custom_call" | custom-call | bytes 5242880 | tf_op jit(solution)/shard_map/pallas_call | solution.py:145
  30.9 11.5 %collective-permute-done.1.refs_2_ = bf16[128,2048]{1,0:T(8,128)(2,1)S(1)} collective-permute-done((bf16[128,2048]{1,0:T(8,128)(2,1)}, bf16[128,2048]{1,0:T(8,128)(2,1)S(1)}, u32[]{:S(2)}, u32[]{:S(2)}) %collective-permute-start.1) | collective-permute-done | bytes 524320 | tf_op jit(solution)/shard_map/ppermute | solution.py:50
  44.3 3.2 %collective-permute-done.3.refs_5_ = bf16[128,2048]{1,0:T(8,128)(2,1)S(1)} collective-permute-done((bf16[128,2048]{1,0:T(8,128)(2,1)}, bf16[128,2048]{1,0:T(8,128)(2,1)S(1)}, u32[]{:S(2)}, u32[]{:S(2)}) %collective-permute-start.3) | collective-permute-done | bytes 524320 | tf_op jit(solution)/shard_map/ppermute | solution.py:50
  49.5 5.2 %shard_map.78 = bf16[2048,512]{1,0:T(8,128)(2,1)} custom-call(s32[8]{0:T(128)} %compare_select_fusion.6.where, bf16[128,2048]{1,0:T(8,128)(2,1)} %get-tuple-element.49.refs_0_, bf16[128,2048]{1,0:T(8,128)(2,1)} %copy-done.8, bf16[128,2048]{1,0:T(8,128)(2,1)} %copy-done.9, bf16[128,2048]{1,0:T(8,128)(2,1)} %copy-done.10, ...), custom_call_target="tpu_custom_call" | custom-call | flops 1073741824 | bytes 4718592 | tf_op jit(solution)/shard_map/pallas_call | solution.py:292
  54.8 9.5 %collective-permute-done.18.refs_2_ = bf16[128,2560]{1,0:T(8,128)(2,1)S(1)} collective-permute-done((bf16[128,2560]{1,0:T(8,128)(2,1)}, bf16[128,2560]{1,0:T(8,128)(2,1)S(1)}, u32[]{:S(2)}, u32[]{:S(2)}) %collective-permute-start.18) | collective-permute-done | bytes 655392 | tf_op jit(solution)/shard_map/ppermute | solution.py:50
  65.5 4.2 %shard_map.82 = bf16[1280,512]{1,0:T(8,128)(2,1)} custom-call(s32[8]{0:T(128)} %compare_select_fusion.6.where, bf16[128,2560]{1,0:T(8,128)(2,1)} %get-tuple-element.65.refs_0_, bf16[128,2560]{1,0:T(8,128)(2,1)} %copy-done.5, bf16[128,2560]{1,0:T(8,128)(2,1)} %copy-done.6, bf16[128,2560]{1,0:T(8,128)(2,1)} %copy-done.7, bf16[2048,512]{1,0:T(8,128)(2,1)} %refs_8_.9, ...), custom_call_target="tpu_custom_call" | custom-call | flops 671088640 | bytes 3145728 | tf_op jit(solution)/shard_map/pallas_call | solution.py:292
  69.8 4.8 %cut_moments.1 = bf16[8,256,256]{2,1,0:T(8,128)(2,1)} custom-call(s32[8]{0:T(128)} %compare_select_fusion.6.where, f32[64,1664]{1,0:T(8,128)} %first.1, f32[64,1664]{1,0:T(8,128)} %second.1, bf16[2048,512]{1,0:T(8,128)(2,1)} %refs_8_.9, bf16[2048,512]{1,0:T(8,128)(2,1)} %old.1), custom_call_target="tpu_custom_call" | custom-call | flops 536870912 | bytes 6291456 | tf_op jit(solution)/shard_map/cut_moments/pallas_call | solution.py:358
  74.6 5.9 %all-to-all-start = ((bf16[8,256,256]{2,1,0:T(8,128)(2,1)}), bf16[8,256,256]{2,1,0:T(8,128)(2,1)S(1)}, u32[]{:S(2)}, u32[]{:S(2)}) async-start(bf16[8,256,256]{2,1,0:T(8,128)(2,1)} %cut_moments.1), calls=%async_computation | async-start | bytes 2097152 | tf_op jit(solution)/shard_map/all_to_all | solution.py:607
  81.6 5.1 %shard_map.83 = (bf16[320,512]{1,0:T(8,128)(2,1)}, bf16[320,512]{1,0:T(8,128)(2,1)}, bf16[320,512]{1,0:T(8,128)(2,1)}, bf16[320,512]{1,0:T(8,128)(2,1)}) custom-call(s32[8]{0:T(128)} %compare_select_fusion.6.where, bf16[128,2560]{1,0:T(8,128)(2,1)} %get-tuple-element.65.refs_0_, bf16[128,2560]{1,0:T(8,128)(2,1)} %copy-done.5, bf16[128,2560]{1,0:T(8,128)(2,1)} %copy-done.6, ...), custom_call_target="tpu_custom_call" | custom-call | flops 671088640 | bytes 3145728 | tf_op jit(solution)/shard_map/pallas_call | solution.py:292
  86.7 1.5 collective-permute-start.21
  88.2 2.7 collective-permute-start.22
  90.9 6.8 %shard_map.79 = (bf16[512,512]{1,0:T(8,128)(2,1)}, bf16[512,512]{1,0:T(8,128)(2,1)}, bf16[512,512]{1,0:T(8,128)(2,1)}, bf16[512,512]{1,0:T(8,128)(2,1)}) custom-call(s32[8]{0:T(128)} %compare_select_fusion.6.where, bf16[128,2048]{1,0:T(8,128)(2,1)} %get-tuple-element.49.refs_0_, bf16[128,2048]{1,0:T(8,128)(2,1)} %copy-done.8, bf16[128,2048]{1,0:T(8,128)(2,1)} %copy-done.9, ...), custom_call_target="tpu_custom_call" | custom-call | flops 1073741824 | bytes 4718592 | tf_op jit(solution)/shard_map/pallas_call | solution.py:292
  97.8 2.6 collective-permute-start.12
  101.4 1.7 sum_margin.1
  103.1 4.3 %all-to-all-start.1 = ((bf16[8,32,512]{2,1,0:T(8,128)(2,1)}), bf16[8,32,512]{2,1,0:T(8,128)(2,1)S(1)}, u32[]{:S(2)}, u32[]{:S(2)}) async-start(bf16[8,32,512]{2,1,0:T(8,128)(2,1)} %sum_margin.1), calls=%async_computation.1 | async-start | bytes 524288 | tf_op jit(solution)/shard_map/all_to_all | solution.py:609
  107.4 2.8 collective-permute-start.23
  110.1 4.6 %all-to-all-done.1 = bf16[8,32,512]{2,1,0:T(8,128)(2,1)S(1)} async-done(((bf16[8,32,512]{2,1,0:T(8,128)(2,1)}), bf16[8,32,512]{2,1,0:T(8,128)(2,1)S(1)}, u32[]{:S(2)}, u32[]{:S(2)}) %all-to-all-start.1) | async-done | bytes 262176 | tf_op jit(solution)/shard_map/all_to_all | solution.py:609
  114.7 4.7 %collective-permute-start.27 = (bf16[256,512]{1,0:T(8,128)(2,1)S(1)}, bf16[256,512]{1,0:T(8,128)(2,1)S(1)}, u32[]{:S(2)}, u32[]{:S(2)}) collective-permute-start(bf16[256,512]{1,0:T(8,128)(2,1)S(1)} %bitcast.9), channel_id=1, source_target_pairs={{0,1},{1,0},{2,3},{3,2},{4,5},{5,4},{6,7},{7,6},{8,9},{9,8},{10,11... | collective-permute-start | bytes 786440 | tf_op jit(solution)/shard_map/ppermute | solution.py:50
  120.2 2.3 shard_map.84
  122.5 8.0 %collective-permute-start.24 = (bf16[80,512]{1,0:T(8,128)(2,1)}, bf16[80,512]{1,0:T(8,128)(2,1)S(1)}, u32[]{:S(2)}, u32[]{:S(2)}) collective-permute-start(bf16[80,512]{1,0:T(8,128)(2,1)} %get-tuple-element.74), channel_id=1, source_target_pairs={{0,4},{1,5},{2,6},{3,7},{4,8},{5,9},{6,10},{7,11},{8,12},{9,13},{1... | collective-permute-start | bytes 245768 | tf_op jit(solution)/shard_map/ppermute | solution.py:50
  131.7 2.8 shard_map.80
  134.5 1.5 collective-permute-start.14
  136.0 2.7 collective-permute-start.15
  138.6 1.2 collective-permute-start.16
  139.8 2.1 collective-permute-start.25
  142.7 3.2 %collective-permute-done.25.refs_6_ = bf16[80,512]{1,0:T(8,128)(2,1)S(1)} collective-permute-done((bf16[80,512]{1,0:T(8,128)(2,1)S(1)}, bf16[80,512]{1,0:T(8,128)(2,1)S(1)}, u32[]{:S(2)}, u32[]{:S(2)}) %collective-permute-start.25) | collective-permute-done | bytes 81952 | tf_op jit(solution)/shard_map/ppermute | solution.py:50
  147.3 3.5 %step.1 = (bf16[128,512]{1,0:T(8,128)(2,1)}, bf16[80,512]{1,0:T(8,128)(2,1)}, f32[208,512]{1,0:T(8,128)}, f32[208,512]{1,0:T(8,128)}) custom-call(s32[8]{0:T(128)} %compare_select_fusion.6.where, bf16[128,512]{1,0:T(8,128)(2,1)} %get-tuple-element.61.refs_0_, bf16[128,512]{1,0:T(8,128)(2,1)} %copy-done.38, bf16[128,512]{1,0:T(8,128)(2,1)} %copy-done.39, ...), custom_call_target="tpu_custom_call" | custom-call | flops 327155712 | bytes 4194304 | tf_op jit(solution)/shard_map/step/pallas_call | solution.py:423
  150.8 1.8 collective-permute-start.46
  153.7 2.1 collective-permute-done.46.refs_3_
  155.8 3.0 %collective-permute-done.45.refs_2_ = bf16[80,512]{1,0:T(8,128)(2,1)S(1)} collective-permute-done((bf16[80,512]{1,0:T(8,128)(2,1)}, bf16[80,512]{1,0:T(8,128)(2,1)S(1)}, u32[]{:S(2)}, u32[]{:S(2)}) %collective-permute-start.45) | collective-permute-done | bytes 81952 | tf_op jit(solution)/shard_map/ppermute | solution.py:50
  160.3 1.8 shard_map.88.refs_0_
  163.5 2.7 collective-permute-start.29
  166.4 8.8 %collective-permute-done.30.refs_3_ = bf16[128,512]{1,0:T(8,128)(2,1)S(1)} collective-permute-done((bf16[128,512]{1,0:T(8,128)(2,1)}, bf16[128,512]{1,0:T(8,128)(2,1)S(1)}, u32[]{:S(2)}, u32[]{:S(2)}) %collective-permute-start.30) | collective-permute-done | bytes 131104 | tf_op jit(solution)/shard_map/ppermute | solution.py:50
  175.2 4.1 %collective-permute-start.48 = (bf16[320,512]{1,0:T(8,128)(2,1)}, bf16[320,512]{1,0:T(8,128)(2,1)}, u32[]{:S(2)}, u32[]{:S(2)}) collective-permute-start(bf16[320,512]{1,0:T(8,128)(2,1)} %shard_map.88.refs_0_), channel_id=1, source_target_pairs={{0,32},{1,33},{2,34},{3,35},{4,36},{5,37},{6,38},{7,39},{8,40},{9,... | collective-permute-start | bytes 983048 | tf_op jit(solution)/shard_map/ppermute | solution.py:50
  180.6 1.9 shard_map.85.refs_0_
  183.2 1.8 collective-permute-start.32
  185.0 1.5 collective-permute-start.31
  186.5 1.5 collective-permute-done.47.refs_1_
  188.8 10.0 %collective-permute-done.33.refs_3_ = bf16[512,512]{1,0:T(8,128)(2,1)S(1)} collective-permute-done((bf16[512,512]{1,0:T(8,128)(2,1)}, bf16[512,512]{1,0:T(8,128)(2,1)S(1)}, u32[]{:S(2)}, u32[]{:S(2)}) %collective-permute-start.33) | collective-permute-done | bytes 524320 | tf_op jit(solution)/shard_map/ppermute | solution.py:50
  200.3 3.5 %collective-permute-done.51.refs_5_ = bf16[320,512]{1,0:T(8,128)(2,1)} collective-permute-done((bf16[320,512]{1,0:T(8,128)(2,1)}, bf16[320,512]{1,0:T(8,128)(2,1)}, u32[]{:S(2)}, u32[]{:S(2)}) %collective-permute-start.51) | collective-permute-done | bytes 327712 | tf_op jit(solution)/shard_map/ppermute | solution.py:50
  203.7 5.9 %shard_map.89 = (bf16[128,2560]{1,0:T(8,128)(2,1)}, bf16[128,2560]{1,0:T(8,128)(2,1)}, bf16[128,2560]{1,0:T(8,128)(2,1)}, bf16[128,2560]{1,0:T(8,128)(2,1)}) custom-call(s32[8]{0:T(128)} %compare_select_fusion.6.where, bf16[320,512]{1,0:T(8,128)(2,1)} %shard_map.88.refs_0_, bf16[320,512]{1,0:T(8,128)(2,1)} %copy-done.30, ...), custom_call_target="tpu_custom_call" | custom-call | flops 1342177280 | bytes 5767168 | tf_op jit(solution)/shard_map/pallas_call | solution.py:561
  209.7 1.9 collective-permute-start.54
  211.8 1.4 collective-permute-start.56
  214.0 5.2 %shard_map.87 = (bf16[128,2048]{1,0:T(8,128)(2,1)}, bf16[128,2048]{1,0:T(8,128)(2,1)}, bf16[128,2048]{1,0:T(8,128)(2,1)}, bf16[128,2048]{1,0:T(8,128)(2,1)}) custom-call(s32[8]{0:T(128)} %compare_select_fusion.6.where, bf16[512,512]{1,0:T(8,128)(2,1)} %shard_map.85.refs_0_, bf16[512,512]{1,0:T(8,128)(2,1)} %copy-done.14, bf16[512,512]{1,0:T(8,128)(2,1)} %copy-done.13, ...), custom_call_target="tpu_custom_call" | custom-call | flops 1073741824 | bytes 4718592 | tf_op jit(solution)/shard_map/pallas_call | solution.py:561
  219.5 3.2 %collective-permute-start.42 = (bf16[128,2048]{1,0:T(8,128)(2,1)}, bf16[128,2048]{1,0:T(8,128)(2,1)S(1)}, u32[]{:S(2)}, u32[]{:S(2)}) collective-permute-start(bf16[128,2048]{1,0:T(8,128)(2,1)} %get-tuple-element.84), channel_id=1, source_target_pairs={{0,12},{1,13},{2,14},{3,15},{4,0},{5,1},{6,2},{7,3},{8,4},{9,5},{1... | collective-permute-start | bytes 1572872 | tf_op jit(solution)/shard_map/ppermute | solution.py:50
  222.7 5.1 %shard_map.86 = (bf16[128,2048]{1,0:T(8,128)(2,1)}, bf16[128,2048]{1,0:T(8,128)(2,1)}, bf16[128,2048]{1,0:T(8,128)(2,1)}, bf16[128,2048]{1,0:T(8,128)(2,1)}) custom-call(s32[8]{0:T(128)} %compare_select_fusion.6.where, bf16[512,512]{1,0:T(8,128)(2,1)} %shard_map.85.refs_0_, bf16[512,512]{1,0:T(8,128)(2,1)} %copy-done.14, bf16[512,512]{1,0:T(8,128)(2,1)} %copy-done.13, ...), custom_call_target="tpu_custom_call" | custom-call | flops 1073741824 | bytes 4718592 | tf_op jit(solution)/shard_map/pallas_call | solution.py:561
  227.8 12.5 %collective-permute-done.54.refs_1_ = bf16[128,2560]{1,0:T(8,128)(2,1)} collective-permute-done((bf16[128,2560]{1,0:T(8,128)(2,1)}, bf16[128,2560]{1,0:T(8,128)(2,1)}, u32[]{:S(2)}, u32[]{:S(2)}) %collective-permute-start.54) | collective-permute-done | bytes 655392 | tf_op jit(solution)/shard_map/ppermute | solution.py:50
  241.4 2.2 collective-permute-done.55.refs_2_
  244.0 2.9 %collective-permute-start.39 = (bf16[128,2048]{1,0:T(8,128)(2,1)}, bf16[128,2048]{1,0:T(8,128)(2,1)S(1)}, u32[]{:S(2)}, u32[]{:S(2)}) collective-permute-start(bf16[128,2048]{1,0:T(8,128)(2,1)} %get-tuple-element.80), channel_id=1, source_target_pairs={{0,48},{1,49},{2,50},{3,51},{4,52},{5,53},{6,54},{7,55},{8,56},{9,... | collective-permute-start | bytes 1572872 | tf_op jit(solution)/shard_map/ppermute | solution.py:50
  246.9 2.6 collective-permute-start.40
  249.5 2.1 turn_back.1
  251.6 24.1 %all_to_all.15.new = bf16[8,128,256]{2,1,0:T(8,128)(2,1)} all-to-all(bf16[8,128,256]{2,1,0:T(8,128)(2,1)} %turn_back.1), channel_id=1, replica_groups=mesh['xl'=2,'z'=4,'y'=4,'xh'=2,'core'=2] {'xl','z'}, dimensions={0} | all-to-all | bytes 1048576 | tf_op jit(solution)/shard_map/all_to_all | solution.py:638
  275.7 2.1 finish.1
  277.7 4.4 %shard_map.90.refs_4_ = bf16[128,26624]{1,0:T(8,128)(2,1)} custom-call(s32[8]{0:T(128)} %compare_select_fusion.6.where, bf16[128,2560]{1,0:T(8,128)(2,1)} %get-tuple-element.87.refs_0_, bf16[128,2560]{1,0:T(8,128)(2,1)} %collective-permute-done.54.refs_1_, bf16[128,2560]{1,0:T(8,128)(2,1)} %collective-permute-done.55.refs_2_, ...), custom_call_target="tpu_custom_call" | custom-call | bytes 5242880 | tf_op jit(solution)/shard_map/pallas_call | solution.py:195
  283.2 3.8 %shard_map.91.refs_4_ = bf16[128,26624]{1,0:T(8,128)(2,1)} custom-call(s32[8]{0:T(128)} %compare_select_fusion.6.where, bf16[128,2048]{1,0:T(8,128)(2,1)} %get-tuple-element.82.refs_0_, bf16[128,2048]{1,0:T(8,128)(2,1)} %copy-done.20, bf16[128,2048]{1,0:T(8,128)(2,1)} %copy-done.22, bf16[128,2048]{1,0:T(8,128)(2,1)} %copy-done.27, ...), custom_call_target="tpu_custom_call", output_to_operand_aliasing={{}: (5, {})} | custom-call | bytes 4194304 | tf_op jit(solution)/shard_map/pallas_call | solution.py:195
  288.1 3.7 %shard_map.92 = bf16[128,26624]{1,0:T(8,128)(2,1)} custom-call(s32[8]{0:T(128)} %compare_select_fusion.6.where, bf16[128,2048]{1,0:T(8,128)(2,1)} %get-tuple-element.78.refs_0_, bf16[128,2048]{1,0:T(8,128)(2,1)} %copy-done.25, bf16[128,2048]{1,0:T(8,128)(2,1)} %copy-done.26, bf16[128,2048]{1,0:T(8,128)(2,1)} %copy-done.28, ...), custom_call_target="tpu_custom_call", output_to_operand_aliasing={{}: (5, {})} | custom-call | bytes 4194304 | tf_op jit(solution)/shard_map/pallas_call | solution.py:195
  (178 shorter events, 29.6 us)
Async XLA Ops:
  4.5 22.0 %collective-permute-start = (bf16[128,2048]{1,0:T(8,128)(2,1)}, bf16[128,2048]{1,0:T(8,128)(2,1)S(1)}, u32[]{:S(2)}, u32[]{:S(2)}) collective-permute-start(bf16[128,2048]{1,0:T(8,128)(2,1)} %get-tuple-element.50), channel_id=1, source_target_pairs={{0,4},{1,5},{2,6},{3,7},{4,8},{5,9},{6,10},{7,11},{8,12},{9,13},{1... | collective-permute-start | bytes 1572872 | tf_op jit(solution)/shard_map/ppermute | solution.py:50
  7.1 16.6 %collective-permute-start.9 = (bf16[256,512]{1,0:T(8,128)(2,1)S(1)}, bf16[256,512]{1,0:T(8,128)(2,1)S(1)}, u32[]{:S(2)}, u32[]{:S(2)}) collective-permute-start(bf16[256,512]{1,0:T(8,128)(2,1)S(1)} %bitcast.11), channel_id=1, source_target_pairs={{0,64},{64,0},{1,65},{65,1},{2,66},{66,2},{3,67},{67,3},{4,68},{68... | collective-permute-start | bytes 786440 | tf_op jit(solution)/shard_map/ppermute | solution.py:604
  9.0 9.8 %collective-permute-start.8 = (bf16[128,512]{1,0:T(8,128)(2,1)S(1)}, bf16[128,512]{1,0:T(8,128)(2,1)S(1)}, u32[]{:S(2)}, u32[]{:S(2)}) collective-permute-start(bf16[128,512]{1,0:T(8,128)(2,1)S(1)} %dynamic-slice_bitcast_fusion), channel_id=1, source_target_pairs={{0,16},{1,17},{2,18},{3,19},{4,20},{5,21},{6,22},{7,23},{8,24},{9,... | collective-permute-start | bytes 393224 | tf_op jit(solution)/shard_map/ppermute | solution.py:50
  10.9 9.7 %collective-permute-start.7 = (bf16[128,512]{1,0:T(8,128)(2,1)S(1)}, bf16[128,512]{1,0:T(8,128)(2,1)S(1)}, u32[]{:S(2)}, u32[]{:S(2)}) collective-permute-start(bf16[128,512]{1,0:T(8,128)(2,1)S(1)} %dynamic-slice_bitcast_fusion), channel_id=1, source_target_pairs={{0,32},{1,33},{2,34},{3,35},{4,36},{5,37},{6,38},{7,39},{8,40},{9,... | collective-permute-start | bytes 393224 | tf_op jit(solution)/shard_map/ppermute | solution.py:50
  14.5 8.7 %collective-permute-start.6 = (bf16[128,512]{1,0:T(8,128)(2,1)S(1)}, bf16[128,512]{1,0:T(8,128)(2,1)S(1)}, u32[]{:S(2)}, u32[]{:S(2)}) collective-permute-start(bf16[128,512]{1,0:T(8,128)(2,1)S(1)} %dynamic-slice_bitcast_fusion), channel_id=1, source_target_pairs={{0,48},{1,49},{2,50},{3,51},{4,52},{5,53},{6,54},{7,55},{8,56},{9,... | collective-permute-start | bytes 393224 | tf_op jit(solution)/shard_map/ppermute | solution.py:50
  18.8 23.5 %collective-permute-start.1 = (bf16[128,2048]{1,0:T(8,128)(2,1)}, bf16[128,2048]{1,0:T(8,128)(2,1)S(1)}, u32[]{:S(2)}, u32[]{:S(2)}) collective-permute-start(bf16[128,2048]{1,0:T(8,128)(2,1)} %get-tuple-element.51), channel_id=1, source_target_pairs={{0,12},{1,13},{2,14},{3,15},{4,0},{5,1},{6,2},{7,3},{8,4},{9,5},{1... | collective-permute-start | bytes 1572872 | tf_op jit(solution)/shard_map/ppermute | solution.py:50
  20.7 22.8 %collective-permute-start.2 = (bf16[128,2048]{1,0:T(8,128)(2,1)}, bf16[128,2048]{1,0:T(8,128)(2,1)S(1)}, u32[]{:S(2)}, u32[]{:S(2)}) collective-permute-start(bf16[128,2048]{1,0:T(8,128)(2,1)} %get-tuple-element.52), channel_id=1, source_target_pairs={{0,8},{1,9},{2,10},{3,11},{4,12},{5,13},{6,14},{7,15},{8,0},{9,1},... | collective-permute-start | bytes 1572872 | tf_op jit(solution)/shard_map/ppermute | solution.py:50
  23.2 24.3 %collective-permute-start.3 = (bf16[128,2048]{1,0:T(8,128)(2,1)}, bf16[128,2048]{1,0:T(8,128)(2,1)S(1)}, u32[]{:S(2)}, u32[]{:S(2)}) collective-permute-start(bf16[128,2048]{1,0:T(8,128)(2,1)} %get-tuple-element.54), channel_id=1, source_target_pairs={{0,16},{1,17},{2,18},{3,19},{4,20},{5,21},{6,22},{7,23},{8,24},{9,... | collective-permute-start | bytes 1572872 | tf_op jit(solution)/shard_map/ppermute | solution.py:50
  23.7 25.8 %collective-permute-start.4 = (bf16[128,2048]{1,0:T(8,128)(2,1)}, bf16[128,2048]{1,0:T(8,128)(2,1)}, u32[]{:S(2)}, u32[]{:S(2)}) collective-permute-start(bf16[128,2048]{1,0:T(8,128)(2,1)} %get-tuple-element.55), channel_id=1, source_target_pairs={{0,48},{1,49},{2,50},{3,51},{4,52},{5,53},{6,54},{7,55},{8,56},{9,... | collective-permute-start | bytes 1572872 | tf_op jit(solution)/shard_map/ppermute | solution.py:50
  26.5 23.0 %collective-permute-start.5 = (bf16[128,2048]{1,0:T(8,128)(2,1)}, bf16[128,2048]{1,0:T(8,128)(2,1)}, u32[]{:S(2)}, u32[]{:S(2)}) collective-permute-start(bf16[128,2048]{1,0:T(8,128)(2,1)} %get-tuple-element.56), channel_id=1, source_target_pairs={{0,32},{1,33},{2,34},{3,35},{4,36},{5,37},{6,38},{7,39},{8,40},{9,... | collective-permute-start | bytes 1572872 | tf_op jit(solution)/shard_map/ppermute | solution.py:50
  42.3 12.5 %collective-permute-start.17 = (bf16[128,2560]{1,0:T(8,128)(2,1)}, bf16[128,2560]{1,0:T(8,128)(2,1)S(1)}, u32[]{:S(2)}, u32[]{:S(2)}) collective-permute-start(bf16[128,2560]{1,0:T(8,128)(2,1)} %get-tuple-element.66), channel_id=1, source_target_pairs={{0,64},{1,65},{2,66},{3,67},{4,68},{5,69},{6,70},{7,71},{8,72},{9,... | collective-permute-start | bytes 1966088 | tf_op jit(solution)/shard_map/ppermute | solution.py:50
  43.5 20.9 %collective-permute-start.18 = (bf16[128,2560]{1,0:T(8,128)(2,1)}, bf16[128,2560]{1,0:T(8,128)(2,1)S(1)}, u32[]{:S(2)}, u32[]{:S(2)}) collective-permute-start(bf16[128,2560]{1,0:T(8,128)(2,1)} %get-tuple-element.67), channel_id=1, source_target_pairs={{0,66},{1,67},{2,64},{3,65},{4,70},{5,71},{6,68},{7,69},{8,74},{9,... | collective-permute-start | bytes 1966088 | tf_op jit(solution)/shard_map/ppermute | solution.py:50
  48.4 16.0 %collective-permute-start.19 = (bf16[128,2560]{1,0:T(8,128)(2,1)}, bf16[128,2560]{1,0:T(8,128)(2,1)S(1)}, u32[]{:S(2)}, u32[]{:S(2)}) collective-permute-start(bf16[128,2560]{1,0:T(8,128)(2,1)} %get-tuple-element.68), channel_id=1, source_target_pairs={{0,2},{1,3},{2,0},{3,1},{4,6},{5,7},{6,4},{7,5},{8,10},{9,11},{10,... | collective-permute-start | bytes 1966088 | tf_op jit(solution)/shard_map/ppermute | solution.py:50
  54.7 36.2 %collective-permute-start.10 = (bf16[2048,512]{1,0:T(8,128)(2,1)}, bf16[2048,512]{1,0:T(8,128)(2,1)}, u32[]{:S(2)}, u32[]{:S(2)}) collective-permute-start(bf16[2048,512]{1,0:T(8,128)(2,1)} %shard_map.78), channel_id=1, source_target_pairs={{0,1},{1,0},{2,3},{3,2},{4,5},{5,4},{6,7},{7,6},{8,9},{9,8},{10,11... | collective-permute-start | bytes 6291464 | tf_op jit(solution)/shard_map/ppermute | solution.py:50
  69.7 10.8 %collective-permute-start.20 = (bf16[1280,512]{1,0:T(8,128)(2,1)}, bf16[1280,512]{1,0:T(8,128)(2,1)S(1)}, u32[]{:S(2)}, u32[]{:S(2)}) collective-permute-start(bf16[1280,512]{1,0:T(8,128)(2,1)} %shard_map.82), channel_id=1, source_target_pairs={{0,1},{1,0},{2,3},{3,2},{4,5},{5,4},{6,7},{7,6},{8,9},{9,8},{10,11... | collective-permute-start | bytes 3932168 | tf_op jit(solution)/shard_map/ppermute | solution.py:50
  74.6 25.8 %all-to-all-start = ((bf16[8,256,256]{2,1,0:T(8,128)(2,1)}), bf16[8,256,256]{2,1,0:T(8,128)(2,1)S(1)}, u32[]{:S(2)}, u32[]{:S(2)}) async-start(bf16[8,256,256]{2,1,0:T(8,128)(2,1)} %cut_moments.1), calls=%async_computation | async-start | bytes 2097152 | tf_op jit(solution)/shard_map/all_to_all | solution.py:607
  86.7 20.7 %collective-permute-start.21 = (bf16[320,512]{1,0:T(8,128)(2,1)}, bf16[320,512]{1,0:T(8,128)(2,1)S(1)}, u32[]{:S(2)}, u32[]{:S(2)}) collective-permute-start(bf16[320,512]{1,0:T(8,128)(2,1)} %get-tuple-element.70), channel_id=1, source_target_pairs={{0,16},{1,17},{2,18},{3,19},{4,20},{5,21},{6,22},{7,23},{8,24},{9,... | collective-permute-start | bytes 983048 | tf_op jit(solution)/shard_map/ppermute | solution.py:50
  88.2 26.5 %collective-permute-start.22 = (bf16[320,512]{1,0:T(8,128)(2,1)}, bf16[320,512]{1,0:T(8,128)(2,1)S(1)}, u32[]{:S(2)}, u32[]{:S(2)}) collective-permute-start(bf16[320,512]{1,0:T(8,128)(2,1)} %get-tuple-element.71), channel_id=1, source_target_pairs={{0,32},{1,33},{2,34},{3,35},{4,36},{5,37},{6,38},{7,39},{8,40},{9,... | collective-permute-start | bytes 983048 | tf_op jit(solution)/shard_map/ppermute | solution.py:50
  97.7 32.8 %collective-permute-start.11 = (bf16[512,512]{1,0:T(8,128)(2,1)}, bf16[512,512]{1,0:T(8,128)(2,1)S(1)}, u32[]{:S(2)}, u32[]{:S(2)}) collective-permute-start(bf16[512,512]{1,0:T(8,128)(2,1)} %get-tuple-element.58), channel_id=1, source_target_pairs={{0,64},{1,5},{2,66},{3,7},{4,68},{5,9},{6,70},{7,11},{8,72},{9,13}... | collective-permute-start | bytes 1572872 | tf_op jit(solution)/shard_map/ppermute | solution.py:50
  97.8 32.8 %collective-permute-start.12 = (bf16[512,512]{1,0:T(8,128)(2,1)}, bf16[512,512]{1,0:T(8,128)(2,1)S(1)}, u32[]{:S(2)}, u32[]{:S(2)}) collective-permute-start(bf16[512,512]{1,0:T(8,128)(2,1)} %get-tuple-element.59), channel_id=1, source_target_pairs={{0,2},{1,9},{2,0},{3,11},{4,6},{5,13},{6,4},{7,15},{8,10},{9,1},{1... | collective-permute-start | bytes 1572872 | tf_op jit(solution)/shard_map/ppermute | solution.py:50
  100.4 30.1 %collective-permute-start.13 = (bf16[512,512]{1,0:T(8,128)(2,1)}, bf16[512,512]{1,0:T(8,128)(2,1)S(1)}, u32[]{:S(2)}, u32[]{:S(2)}) collective-permute-start(bf16[512,512]{1,0:T(8,128)(2,1)} %get-tuple-element.60), channel_id=1, source_target_pairs={{0,66},{1,13},{2,64},{3,15},{4,70},{5,1},{6,68},{7,3},{8,74},{9,5}... | collective-permute-start | bytes 1572872 | tf_op jit(solution)/shard_map/ppermute | solution.py:50
  103.1 11.7 %all-to-all-start.1 = ((bf16[8,32,512]{2,1,0:T(8,128)(2,1)}), bf16[8,32,512]{2,1,0:T(8,128)(2,1)S(1)}, u32[]{:S(2)}, u32[]{:S(2)}) async-start(bf16[8,32,512]{2,1,0:T(8,128)(2,1)} %sum_margin.1), calls=%async_computation.1 | async-start | bytes 524288 | tf_op jit(solution)/shard_map/all_to_all | solution.py:609
  107.4 12.1 %collective-permute-start.23 = (bf16[320,512]{1,0:T(8,128)(2,1)}, bf16[320,512]{1,0:T(8,128)(2,1)S(1)}, u32[]{:S(2)}, u32[]{:S(2)}) collective-permute-start(bf16[320,512]{1,0:T(8,128)(2,1)} %get-tuple-element.72), channel_id=1, source_target_pairs={{0,48},{1,49},{2,50},{3,51},{4,52},{5,53},{6,54},{7,55},{8,56},{9,... | collective-permute-start | bytes 983048 | tf_op jit(solution)/shard_map/ppermute | solution.py:50
  114.7 31.8 %copy-start.19 = (bf16[8,32,512]{2,1,0:T(8,128)(2,1)}, bf16[8,32,512]{2,1,0:T(8,128)(2,1)S(1)}, u32[]{:S(2)}) copy-start(bf16[8,32,512]{2,1,0:T(8,128)(2,1)S(1)} %all-to-all-done.1) | copy-start | bytes 786436
  114.7 25.1 %collective-permute-start.27 = (bf16[256,512]{1,0:T(8,128)(2,1)S(1)}, bf16[256,512]{1,0:T(8,128)(2,1)S(1)}, u32[]{:S(2)}, u32[]{:S(2)}) collective-permute-start(bf16[256,512]{1,0:T(8,128)(2,1)S(1)} %bitcast.9), channel_id=1, source_target_pairs={{0,1},{1,0},{2,3},{3,2},{4,5},{5,4},{6,7},{7,6},{8,9},{9,8},{10,11... | collective-permute-start | bytes 786440 | tf_op jit(solution)/shard_map/ppermute | solution.py:50
  122.5 17.3 %copy-start.48 = (bf16[80,512]{1,0:T(8,128)(2,1)S(1)}, bf16[80,512]{1,0:T(8,128)(2,1)}, u32[]{:S(2)}) copy-start(bf16[80,512]{1,0:T(8,128)(2,1)} %get-tuple-element.75) | copy-start | bytes 245764
  122.5 19.4 %copy-start.47 = (bf16[80,512]{1,0:T(8,128)(2,1)S(1)}, bf16[80,512]{1,0:T(8,128)(2,1)}, u32[]{:S(2)}) copy-start(bf16[80,512]{1,0:T(8,128)(2,1)} %get-tuple-element.76) | copy-start | bytes 245764
  122.5 19.4 %collective-permute-start.24 = (bf16[80,512]{1,0:T(8,128)(2,1)}, bf16[80,512]{1,0:T(8,128)(2,1)S(1)}, u32[]{:S(2)}, u32[]{:S(2)}) collective-permute-start(bf16[80,512]{1,0:T(8,128)(2,1)} %get-tuple-element.74), channel_id=1, source_target_pairs={{0,4},{1,5},{2,6},{3,7},{4,8},{5,9},{6,10},{7,11},{8,12},{9,13},{1... | collective-permute-start | bytes 245768 | tf_op jit(solution)/shard_map/ppermute | solution.py:50
  134.5 12.0 %collective-permute-start.14 = (bf16[128,512]{1,0:T(8,128)(2,1)}, bf16[128,512]{1,0:T(8,128)(2,1)S(1)}, u32[]{:S(2)}, u32[]{:S(2)}) collective-permute-start(bf16[128,512]{1,0:T(8,128)(2,1)} %get-tuple-element.62), channel_id=1, source_target_pairs={{0,16},{1,65},{2,18},{3,67},{4,20},{5,69},{6,22},{7,71},{8,24},{9,... | collective-permute-start | bytes 393224 | tf_op jit(solution)/shard_map/ppermute | solution.py:50
  136.0 10.5 %collective-permute-start.15 = (bf16[128,512]{1,0:T(8,128)(2,1)}, bf16[128,512]{1,0:T(8,128)(2,1)S(1)}, u32[]{:S(2)}, u32[]{:S(2)}) collective-permute-start(bf16[128,512]{1,0:T(8,128)(2,1)} %get-tuple-element.63), channel_id=1, source_target_pairs={{0,32},{1,3},{2,34},{3,1},{4,36},{5,7},{6,38},{7,5},{8,40},{9,11},... | collective-permute-start | bytes 393224 | tf_op jit(solution)/shard_map/ppermute | solution.py:50
  138.6 7.9 %collective-permute-start.16 = (bf16[128,512]{1,0:T(8,128)(2,1)}, bf16[128,512]{1,0:T(8,128)(2,1)S(1)}, u32[]{:S(2)}, u32[]{:S(2)}) collective-permute-start(bf16[128,512]{1,0:T(8,128)(2,1)} %get-tuple-element.64), channel_id=1, source_target_pairs={{0,48},{1,67},{2,50},{3,65},{4,52},{5,71},{6,54},{7,69},{8,56},{9,... | collective-permute-start | bytes 393224 | tf_op jit(solution)/shard_map/ppermute | solution.py:50
  139.8 6.0 %collective-permute-start.25 = (bf16[80,512]{1,0:T(8,128)(2,1)S(1)}, bf16[80,512]{1,0:T(8,128)(2,1)S(1)}, u32[]{:S(2)}, u32[]{:S(2)}) collective-permute-start(bf16[80,512]{1,0:T(8,128)(2,1)S(1)} %copy-done.48), channel_id=1, source_target_pairs={{0,8},{1,9},{2,10},{3,11},{4,12},{5,13},{6,14},{7,15},{8,0},{9,1},... | collective-permute-start | bytes 245768 | tf_op jit(solution)/shard_map/ppermute | solution.py:50
  142.0 4.5 %collective-permute-start.26 = (bf16[80,512]{1,0:T(8,128)(2,1)S(1)}, bf16[80,512]{1,0:T(8,128)(2,1)S(1)}, u32[]{:S(2)}, u32[]{:S(2)}) collective-permute-start(bf16[80,512]{1,0:T(8,128)(2,1)S(1)} %copy-done.47), channel_id=1, source_target_pairs={{0,12},{1,13},{2,14},{3,15},{4,0},{5,1},{6,2},{7,3},{8,4},{9,5},{1... | collective-permute-start | bytes 245768 | tf_op jit(solution)/shard_map/ppermute | solution.py:50
  150.8 5.0 %collective-permute-start.46 = (bf16[80,512]{1,0:T(8,128)(2,1)}, bf16[80,512]{1,0:T(8,128)(2,1)S(1)}, u32[]{:S(2)}, u32[]{:S(2)}) collective-permute-start(bf16[80,512]{1,0:T(8,128)(2,1)} %get-tuple-element.86.refs_0_), channel_id=1, source_target_pairs={{0,12},{1,13},{2,14},{3,15},{4,0},{5,1},{6,2},{7,3},{8,4},{9,5},{1... | collective-permute-start | bytes 245768 | tf_op jit(solution)/shard_map/ppermute | solution.py:50
  152.6 6.2 %collective-permute-start.45 = (bf16[80,512]{1,0:T(8,128)(2,1)}, bf16[80,512]{1,0:T(8,128)(2,1)S(1)}, u32[]{:S(2)}, u32[]{:S(2)}) collective-permute-start(bf16[80,512]{1,0:T(8,128)(2,1)} %get-tuple-element.86.refs_0_), channel_id=1, source_target_pairs={{0,8},{1,9},{2,10},{3,11},{4,12},{5,13},{6,14},{7,15},{8,0},{9,1},... | collective-permute-start | bytes 245768 | tf_op jit(solution)/shard_map/ppermute | solution.py:50
  153.1 6.5 %collective-permute-start.44 = (bf16[80,512]{1,0:T(8,128)(2,1)}, bf16[80,512]{1,0:T(8,128)(2,1)S(1)}, u32[]{:S(2)}, u32[]{:S(2)}) collective-permute-start(bf16[80,512]{1,0:T(8,128)(2,1)} %get-tuple-element.86.refs_0_), channel_id=1, source_target_pairs={{0,4},{1,5},{2,6},{3,7},{4,8},{5,9},{6,10},{7,11},{8,12},{9,13},{1... | collective-permute-start | bytes 245768 | tf_op jit(solution)/shard_map/ppermute | solution.py:50
  162.0 21.2 %collective-permute-start.50 = (bf16[320,512]{1,0:T(8,128)(2,1)}, bf16[320,512]{1,0:T(8,128)(2,1)S(1)}, u32[]{:S(2)}, u32[]{:S(2)}) collective-permute-start(bf16[320,512]{1,0:T(8,128)(2,1)} %shard_map.88.refs_0_), channel_id=1, source_target_pairs={{0,1},{1,0},{2,3},{3,2},{4,5},{5,4},{6,7},{7,6},{8,9},{9,8},{10,11... | collective-permute-start | bytes 983048 | tf_op jit(solution)/shard_map/ppermute | solution.py:50
  162.1 22.9 %collective-permute-start.49 = (bf16[320,512]{1,0:T(8,128)(2,1)}, bf16[320,512]{1,0:T(8,128)(2,1)}, u32[]{:S(2)}, u32[]{:S(2)}) collective-permute-start(bf16[320,512]{1,0:T(8,128)(2,1)} %shard_map.88.refs_0_), channel_id=1, source_target_pairs={{0,48},{1,49},{2,50},{3,51},{4,52},{5,53},{6,54},{7,55},{8,56},{9,... | collective-permute-start | bytes 983048 | tf_op jit(solution)/shard_map/ppermute | solution.py:50
  162.3 12.9 %collective-permute-start.30 = (bf16[128,512]{1,0:T(8,128)(2,1)}, bf16[128,512]{1,0:T(8,128)(2,1)S(1)}, u32[]{:S(2)}, u32[]{:S(2)}) collective-permute-start(bf16[128,512]{1,0:T(8,128)(2,1)} %get-tuple-element.77.refs_0_), channel_id=1, source_target_pairs={{0,48},{1,67},{2,50},{3,65},{4,52},{5,71},{6,54},{7,69},{8,56},{9,... | collective-permute-start | bytes 393224 | tf_op jit(solution)/shard_map/ppermute | solution.py:50
  163.5 15.8 %collective-permute-start.29 = (bf16[128,512]{1,0:T(8,128)(2,1)}, bf16[128,512]{1,0:T(8,128)(2,1)S(1)}, u32[]{:S(2)}, u32[]{:S(2)}) collective-permute-start(bf16[128,512]{1,0:T(8,128)(2,1)} %get-tuple-element.77.refs_0_), channel_id=1, source_target_pairs={{0,32},{1,3},{2,34},{3,1},{4,36},{5,7},{6,38},{7,5},{8,40},{9,11},... | collective-permute-start | bytes 393224 | tf_op jit(solution)/shard_map/ppermute | solution.py:50
  166.1 13.5 %collective-permute-start.28 = (bf16[128,512]{1,0:T(8,128)(2,1)}, bf16[128,512]{1,0:T(8,128)(2,1)S(1)}, u32[]{:S(2)}, u32[]{:S(2)}) collective-permute-start(bf16[128,512]{1,0:T(8,128)(2,1)} %get-tuple-element.77.refs_0_), channel_id=1, source_target_pairs={{0,16},{1,65},{2,18},{3,67},{4,20},{5,69},{6,22},{7,71},{8,24},{9,... | collective-permute-start | bytes 393224 | tf_op jit(solution)/shard_map/ppermute | solution.py:50
  175.2 11.3 %collective-permute-start.48 = (bf16[320,512]{1,0:T(8,128)(2,1)}, bf16[320,512]{1,0:T(8,128)(2,1)}, u32[]{:S(2)}, u32[]{:S(2)}) collective-permute-start(bf16[320,512]{1,0:T(8,128)(2,1)} %shard_map.88.refs_0_), channel_id=1, source_target_pairs={{0,32},{1,33},{2,34},{3,35},{4,36},{5,37},{6,38},{7,39},{8,40},{9,... | collective-permute-start | bytes 983048 | tf_op jit(solution)/shard_map/ppermute | solution.py:50
  179.3 8.8 %collective-permute-start.47 = (bf16[320,512]{1,0:T(8,128)(2,1)}, bf16[320,512]{1,0:T(8,128)(2,1)S(1)}, u32[]{:S(2)}, u32[]{:S(2)}) collective-permute-start(bf16[320,512]{1,0:T(8,128)(2,1)} %shard_map.88.refs_0_), channel_id=1, source_target_pairs={{0,16},{1,17},{2,18},{3,19},{4,20},{5,21},{6,22},{7,23},{8,24},{9,... | collective-permute-start | bytes 983048 | tf_op jit(solution)/shard_map/ppermute | solution.py:50
  182.5 16.2 %collective-permute-start.33 = (bf16[512,512]{1,0:T(8,128)(2,1)}, bf16[512,512]{1,0:T(8,128)(2,1)S(1)}, u32[]{:S(2)}, u32[]{:S(2)}) collective-permute-start(bf16[512,512]{1,0:T(8,128)(2,1)} %shard_map.85.refs_0_), channel_id=1, source_target_pairs={{0,66},{1,13},{2,64},{3,15},{4,70},{5,1},{6,68},{7,3},{8,74},{9,5}... | collective-permute-start | bytes 1572872 | tf_op jit(solution)/shard_map/ppermute | solution.py:50
  183.2 20.5 %copy-start.29 = (bf16[320,512]{1,0:T(8,128)(2,1)}, bf16[320,512]{1,0:T(8,128)(2,1)S(1)}, u32[]{:S(2)}) copy-start(bf16[320,512]{1,0:T(8,128)(2,1)S(1)} %collective-permute-done.50.refs_4_) | copy-start | bytes 983044
  183.2 15.5 %collective-permute-start.32 = (bf16[512,512]{1,0:T(8,128)(2,1)}, bf16[512,512]{1,0:T(8,128)(2,1)S(1)}, u32[]{:S(2)}, u32[]{:S(2)}) collective-permute-start(bf16[512,512]{1,0:T(8,128)(2,1)} %shard_map.85.refs_0_), channel_id=1, source_target_pairs={{0,2},{1,9},{2,0},{3,11},{4,6},{5,13},{6,4},{7,15},{8,10},{9,1},{1... | collective-permute-start | bytes 1572872 | tf_op jit(solution)/shard_map/ppermute | solution.py:50
  185.0 14.7 %collective-permute-start.31 = (bf16[512,512]{1,0:T(8,128)(2,1)}, bf16[512,512]{1,0:T(8,128)(2,1)S(1)}, u32[]{:S(2)}, u32[]{:S(2)}) collective-permute-start(bf16[512,512]{1,0:T(8,128)(2,1)} %shard_map.85.refs_0_), channel_id=1, source_target_pairs={{0,64},{1,5},{2,66},{3,7},{4,68},{5,9},{6,70},{7,11},{8,72},{9,13}... | collective-permute-start | bytes 1572872 | tf_op jit(solution)/shard_map/ppermute | solution.py:50
  186.5 13.1 %collective-permute-start.53 = (bf16[320,512]{1,0:T(8,128)(2,1)}, bf16[320,512]{1,0:T(8,128)(2,1)}, u32[]{:S(2)}, u32[]{:S(2)}) collective-permute-start(bf16[320,512]{1,0:T(8,128)(2,1)} %collective-permute-done.49.refs_3_), channel_id=1, source_target_pairs={{0,1},{1,0},{2,3},{3,2},{4,5},{5,4},{6,7},{7,6},{8,9},{9,8},{10,11... | collective-permute-start | bytes 983048 | tf_op jit(solution)/shard_map/ppermute | solution.py:50
  188.1 12.1 %collective-permute-start.52 = (bf16[320,512]{1,0:T(8,128)(2,1)}, bf16[320,512]{1,0:T(8,128)(2,1)}, u32[]{:S(2)}, u32[]{:S(2)}) collective-permute-start(bf16[320,512]{1,0:T(8,128)(2,1)} %collective-permute-done.48.refs_2_), channel_id=1, source_target_pairs={{0,1},{1,0},{2,3},{3,2},{4,5},{5,4},{6,7},{7,6},{8,9},{9,8},{10,11... | collective-permute-start | bytes 983048 | tf_op jit(solution)/shard_map/ppermute | solution.py:50
  198.8 12.8 %collective-permute-start.34 = (bf16[512,512]{1,0:T(8,128)(2,1)}, bf16[512,512]{1,0:T(8,128)(2,1)S(1)}, u32[]{:S(2)}, u32[]{:S(2)}) collective-permute-start(bf16[512,512]{1,0:T(8,128)(2,1)} %shard_map.85.refs_0_), channel_id=1, source_target_pairs={{0,1},{1,0},{2,3},{3,2},{4,5},{5,4},{6,7},{7,6},{8,9},{9,8},{10,11... | collective-permute-start | bytes 1572872 | tf_op jit(solution)/shard_map/ppermute | solution.py:50
  198.8 13.0 %collective-permute-start.37 = (bf16[512,512]{1,0:T(8,128)(2,1)S(1)}, bf16[512,512]{1,0:T(8,128)(2,1)S(1)}, u32[]{:S(2)}, u32[]{:S(2)}) collective-permute-start(bf16[512,512]{1,0:T(8,128)(2,1)S(1)} %collective-permute-done.33.refs_3_), channel_id=1, source_target_pairs={{0,1},{1,0},{2,3},{3,2},{4,5},{5,4},{6,7},{7,6},{8,9},{9,8},{10,11... | collective-permute-start | bytes 1572872 | tf_op jit(solution)/shard_map/ppermute | solution.py:50
  199.7 13.5 %collective-permute-start.36 = (bf16[512,512]{1,0:T(8,128)(2,1)S(1)}, bf16[512,512]{1,0:T(8,128)(2,1)S(1)}, u32[]{:S(2)}, u32[]{:S(2)}) collective-permute-start(bf16[512,512]{1,0:T(8,128)(2,1)S(1)} %collective-permute-done.32.refs_2_), channel_id=1, source_target_pairs={{0,1},{1,0},{2,3},{3,2},{4,5},{5,4},{6,7},{7,6},{8,9},{9,8},{10,11... | collective-permute-start | bytes 1572872 | tf_op jit(solution)/shard_map/ppermute | solution.py:50
  199.7 13.5 %collective-permute-start.35 = (bf16[512,512]{1,0:T(8,128)(2,1)S(1)}, bf16[512,512]{1,0:T(8,128)(2,1)}, u32[]{:S(2)}, u32[]{:S(2)}) collective-permute-start(bf16[512,512]{1,0:T(8,128)(2,1)S(1)} %collective-permute-done.31.refs_1_), channel_id=1, source_target_pairs={{0,1},{1,0},{2,3},{3,2},{4,5},{5,4},{6,7},{7,6},{8,9},{9,8},{10,11... | collective-permute-start | bytes 1572872 | tf_op jit(solution)/shard_map/ppermute | solution.py:50
  200.2 3.5 %collective-permute-start.51 = (bf16[320,512]{1,0:T(8,128)(2,1)}, bf16[320,512]{1,0:T(8,128)(2,1)}, u32[]{:S(2)}, u32[]{:S(2)}) collective-permute-start(bf16[320,512]{1,0:T(8,128)(2,1)} %copy-done.30), channel_id=1, source_target_pairs={{0,1},{1,0},{2,3},{3,2},{4,5},{5,4},{6,7},{7,6},{8,9},{9,8},{10,11... | collective-permute-start | bytes 983048 | tf_op jit(solution)/shard_map/ppermute | solution.py:50
  209.7 30.6 %collective-permute-start.54 = (bf16[128,2560]{1,0:T(8,128)(2,1)}, bf16[128,2560]{1,0:T(8,128)(2,1)}, u32[]{:S(2)}, u32[]{:S(2)}) collective-permute-start(bf16[128,2560]{1,0:T(8,128)(2,1)} %get-tuple-element.88), channel_id=1, source_target_pairs={{0,64},{1,65},{2,66},{3,67},{4,68},{5,69},{6,70},{7,71},{8,72},{9,... | collective-permute-start | bytes 1966088 | tf_op jit(solution)/shard_map/ppermute | solution.py:50
  211.6 32.1 %collective-permute-start.55 = (bf16[128,2560]{1,0:T(8,128)(2,1)}, bf16[128,2560]{1,0:T(8,128)(2,1)}, u32[]{:S(2)}, u32[]{:S(2)}) collective-permute-start(bf16[128,2560]{1,0:T(8,128)(2,1)} %get-tuple-element.89), channel_id=1, source_target_pairs={{0,66},{1,67},{2,64},{3,65},{4,70},{5,71},{6,68},{7,69},{8,74},{9,... | collective-permute-start | bytes 1966088 | tf_op jit(solution)/shard_map/ppermute | solution.py:50
  211.8 32.2 %collective-permute-start.56 = (bf16[128,2560]{1,0:T(8,128)(2,1)}, bf16[128,2560]{1,0:T(8,128)(2,1)}, u32[]{:S(2)}, u32[]{:S(2)}) collective-permute-start(bf16[128,2560]{1,0:T(8,128)(2,1)} %get-tuple-element.90), channel_id=1, source_target_pairs={{0,2},{1,3},{2,0},{3,1},{4,6},{5,7},{6,4},{7,5},{8,10},{9,11},{10,... | collective-permute-start | bytes 1966088 | tf_op jit(solution)/shard_map/ppermute | solution.py:50
  219.2 27.7 %collective-permute-start.41 = (bf16[128,2048]{1,0:T(8,128)(2,1)}, bf16[128,2048]{1,0:T(8,128)(2,1)S(1)}, u32[]{:S(2)}, u32[]{:S(2)}) collective-permute-start(bf16[128,2048]{1,0:T(8,128)(2,1)} %get-tuple-element.83), channel_id=1, source_target_pairs={{0,4},{1,5},{2,6},{3,7},{4,8},{5,9},{6,10},{7,11},{8,12},{9,13},{1... | collective-permute-start | bytes 1572872 | tf_op jit(solution)/shard_map/ppermute | solution.py:50
  219.5 62.7 %collective-permute-start.42 = (bf16[128,2048]{1,0:T(8,128)(2,1)}, bf16[128,2048]{1,0:T(8,128)(2,1)S(1)}, u32[]{:S(2)}, u32[]{:S(2)}) collective-permute-start(bf16[128,2048]{1,0:T(8,128)(2,1)} %get-tuple-element.84), channel_id=1, source_target_pairs={{0,12},{1,13},{2,14},{3,15},{4,0},{5,1},{6,2},{7,3},{8,4},{9,5},{1... | collective-permute-start | bytes 1572872 | tf_op jit(solution)/shard_map/ppermute | solution.py:50
  240.3 41.9 %collective-permute-start.43 = (bf16[128,2048]{1,0:T(8,128)(2,1)}, bf16[128,2048]{1,0:T(8,128)(2,1)S(1)}, u32[]{:S(2)}, u32[]{:S(2)}) collective-permute-start(bf16[128,2048]{1,0:T(8,128)(2,1)} %get-tuple-element.85), channel_id=1, source_target_pairs={{0,8},{1,9},{2,10},{3,11},{4,12},{5,13},{6,14},{7,15},{8,0},{9,1},... | collective-permute-start | bytes 1572872 | tf_op jit(solution)/shard_map/ppermute | solution.py:50
  243.7 43.3 %collective-permute-start.38 = (bf16[128,2048]{1,0:T(8,128)(2,1)}, bf16[128,2048]{1,0:T(8,128)(2,1)S(1)}, u32[]{:S(2)}, u32[]{:S(2)}) collective-permute-start(bf16[128,2048]{1,0:T(8,128)(2,1)} %get-tuple-element.79), channel_id=1, source_target_pairs={{0,16},{1,17},{2,18},{3,19},{4,20},{5,21},{6,22},{7,23},{8,24},{9,... | collective-permute-start | bytes 1572872 | tf_op jit(solution)/shard_map/ppermute | solution.py:50
  244.0 43.0 %collective-permute-start.39 = (bf16[128,2048]{1,0:T(8,128)(2,1)}, bf16[128,2048]{1,0:T(8,128)(2,1)S(1)}, u32[]{:S(2)}, u32[]{:S(2)}) collective-permute-start(bf16[128,2048]{1,0:T(8,128)(2,1)} %get-tuple-element.80), channel_id=1, source_target_pairs={{0,48},{1,49},{2,50},{3,51},{4,52},{5,53},{6,54},{7,55},{8,56},{9,... | collective-permute-start | bytes 1572872 | tf_op jit(solution)/shard_map/ppermute | solution.py:50
  246.9 35.2 %copy-start.20 = (bf16[128,2048]{1,0:T(8,128)(2,1)}, bf16[128,2048]{1,0:T(8,128)(2,1)S(1)}, u32[]{:S(2)}) copy-start(bf16[128,2048]{1,0:T(8,128)(2,1)S(1)} %collective-permute-done.41.refs_1_) | copy-start | bytes 1572868
  246.9 40.1 %collective-permute-start.40 = (bf16[128,2048]{1,0:T(8,128)(2,1)}, bf16[128,2048]{1,0:T(8,128)(2,1)S(1)}, u32[]{:S(2)}, u32[]{:S(2)}) collective-permute-start(bf16[128,2048]{1,0:T(8,128)(2,1)} %get-tuple-element.81), channel_id=1, source_target_pairs={{0,32},{1,33},{2,34},{3,35},{4,36},{5,37},{6,38},{7,39},{8,40},{9,... | collective-permute-start | bytes 1572872 | tf_op jit(solution)/shard_map/ppermute | solution.py:50
  (44 other events, 156.2 us)

commit v2 on v1

--- a/solution.py
+++ b/solution.py
@@ -17,9 +17,12 @@
 ANY = pl.BlockSpec(memory_space=pl.ANY)
 SMEM = pl.BlockSpec(memory_space=pltpu.SMEM)
 VMEM = pl.BlockSpec(memory_space=pltpu.VMEM)
+HBM = pl.BlockSpec(memory_space=pltpu.HBM)
 DMA = pltpu.SemaphoreType.DMA
+LIMIT = pltpu.CompilerParams(vmem_limit_bytes=16 * 2**20)
 STEPS = (0, 1, 3, 2)
 WIDTH = {"y": 2048, "z": 2048, "x": 2560}
+EXTRA = {"y": 0, "z": 512, "x": 512}
 GROUPS = ((2048, 128), (1280, 80))
 TILE = (512, 640)
 SLOT = {"x": 0, "y": 1, "z": 2, "core": 3, "xh": 4, "u0": 5, "v0": 6, "u1": 2, "v1": 1}
@@ -105,7 +108,7 @@
     return pltpu.roll(tile.astype(F32), 64, 1).astype(BF)
 
 
-def pack_kernel(ring, where, grad, *refs):
+def pack_kernel(ring, where, grad, basis, *refs):
     outs, (held, in_sem, out_sem), more = refs[:4], refs[4:7], refs[7:]
     if ring == "x":
         ends, end_sem = more
@@ -119,6 +122,9 @@
                 for to, source, count in runs(ring, at)
             ]
         )
+        if EXTRA[ring]:
+            rows = basis_rows("x", where, 0, basis)
+            pltpu.make_async_copy(rows, held.at[at, :, pl.ds(WIDTH[ring], 512)], in_sem.at[at]).start()
     whole = held
     if ring == "x":
         wait_all(end_copies)
@@ -128,7 +134,7 @@
             columns = pl.ds(core * 1280 + 1024 + pair * 128, 128)
             held[xh * 2, :, columns] = jnp.where(left, one, turned(two))
             held[xh * 2 + 1, :, columns] = jnp.where(left, turned(one), two)
-        whole = held.at[:, :, pl.ds(0, 2048)]
+        whole = held.at[:, :, pl.ds(0, 2560)]
     t = place(where, ring)
     stores = []
     for k, step in enumerate(STEPS):
@@ -140,17 +146,18 @@
     wait_all(stores)
 
 
-def pack(ring, where, grad):
-    width = WIDTH[ring]
+def pack(ring, where, grad, basis):
+    width = WIDTH[ring] + EXTRA[ring]
     return pl.pallas_call(
         functools.partial(pack_kernel, ring),
         out_shape=[jax.ShapeDtypeStruct((128, width), BF)] * 4,
-        in_specs=[SMEM, ANY],
+        in_specs=[SMEM, HBM, ANY],
         out_specs=[ANY] * 4,
         scratch_shapes=[pltpu.VMEM((4, 128, width), BF), DMA((4,)), DMA((4,))]
         + ([pltpu.VMEM((16, 128, 128), BF), DMA((16,))] if ring == "x" else []),
+        compiler_params=LIMIT,
         cost_estimate=estimate(0, 4 * 128 * width * 4),
-    )(where, grad)
+    )(where, grad, basis)
 
 
 def unpack_kernel(ring, where, *refs):
@@ -200,30 +207,24 @@
         scratch_shapes=[pltpu.VMEM((4, 128, width), BF), DMA((4,)), DMA((4, 16))]
         + ([pltpu.VMEM((16, 128, 128), BF), DMA((16,))] if ring == "x" else []),
         input_output_aliases={5: 0} if more else {},
+        compiler_params=LIMIT,
         cost_estimate=estimate(0, 4 * 128 * width * 4),
     )(where, *blocks, *more)
 
 
-def basis_rows(ring, where, step, bases):
+def basis_rows(ring, where, step, base):
     y, xh, core = place(where, "y"), place(where, "xh"), place(where, "core")
-    base = bases[0]
     if ring == "y":
-        first = ((y + step) % 4) * 4 + xh * 2 + core
-    elif ring == "z":
-        first = y * 4 + xh * 2 + core
-        if step % 4:
-            base, first = bases[step % 4], 0
-    else:
-        at = (place(where, "x") + step) % 4
-        first = y * 4 + (at // 2) * 2 + core
-        if step % 2:
-            base, first = bases[4], at // 2
-    return base.at[pl.ds(pl.multiple_of(first * 128, 128), 128), :]
-
-
-def start_blocks(ring, where, blocks, first, chunk, tile, bases, held, base, in_sem, base_sem):
+        y = (y + step) % 4
+    return base.at[pl.ds(pl.multiple_of((y * 4 + xh * 2 + core) * 128, 128), 128), :]
+
+
+def start_blocks(ring, where, blocks, first, chunk, tile, basis, held, base, in_sem, base_sem):
     for k, step in enumerate(STEPS):
-        source = basis_rows(ring, where, 4 - step, bases)
+        if EXTRA[ring]:
+            source = blocks[k].at[:, pl.ds(WIDTH[ring], 512)]
+        else:
+            source = basis_rows(ring, where, 4 - step, basis)
         pltpu.make_async_copy(source, base.at[pl.ds(k * 128, 128), :], base_sem).start()
     for i in range(chunk // tile):
         for k in range(4):
@@ -234,14 +235,14 @@
 
 def project_kernel(group, own, where, *refs):
     count = 8 if group == 0 else 4
-    blocks, bases, refs = refs[:count], refs[count : count + 5], refs[count + 5 :]
+    blocks, basis, refs = refs[:count], refs[count], refs[count + 1 :]
     if own:
         other, outs, (held, base, total, in_sem, base_sem, other_sem, out_sem) = refs[0], refs[1:5], refs[5:]
     else:
         out, held, base, total, in_sem, base_sem, out_sem = refs
     chunk, tile = GROUPS[group][0], TILE[group]
     core = place(where, "core")
-    scratch = (chunk, tile, bases, held, base, in_sem, base_sem)
+    scratch = (chunk, tile, basis, held, base, in_sem, base_sem)
     if group == 0:
         on_y = core == (0 if own else 1)
         for ring, mine, chosen in (("y", blocks[:4], on_y), ("z", blocks[4:], jnp.logical_not(on_y))):
@@ -285,14 +286,14 @@
     wait_all(start_all(stores))
 
 
-def project(group, where, blocks, bases, other=None):
+def project(group, where, blocks, basis, other=None):
     chunk = GROUPS[group][0]
     own = other is not None
     shapes = [jax.ShapeDtypeStruct((chunk // 4, 512), BF)] * 4 if own else jax.ShapeDtypeStruct((chunk, 512), BF)
     return pl.pallas_call(
         functools.partial(project_kernel, group, own),
         out_shape=shapes,
-        in_specs=[SMEM] + [ANY] * (len(blocks) + len(bases) + own),
+        in_specs=[SMEM] + [ANY] * (len(blocks) + 1 + own),
         out_specs=[ANY] * 4 if own else ANY,
         scratch_shapes=[
             pltpu.VMEM((512, chunk), BF),
@@ -302,8 +303,9 @@
             DMA,
         ]
         + ([DMA, DMA((4, 8))] if own else [DMA]),
+        compiler_params=LIMIT,
         cost_estimate=estimate(2 * 512 * 512 * chunk, 512 * chunk * 2 + 512 * 1024 + chunk * 1024),
-    )(where, *blocks, *bases, *([other] if own else []))
+    )(where, *blocks, basis, *([other] if own else []))
 
 
 def add_kernel(group, where, a, b, c, d, *refs):
@@ -325,6 +327,7 @@
         in_specs=[SMEM] + [VMEM] * 4,
         out_specs=[VMEM] * 4,
         scratch_shapes=[pltpu.VMEM((chunk // 4, 512), BF)],
+        compiler_params=LIMIT,
         cost_estimate=estimate(3 * chunk * 128, 5 * chunk * 256),
     )(where, *arrays)
 
@@ -361,6 +364,7 @@
         in_specs=[SMEM, VMEM, VMEM, ANY, ANY],
         out_specs=VMEM,
         scratch_shapes=[pltpu.VMEM((2048, 256), BF), pltpu.VMEM((2048, 512), BF), DMA((2,))],
+        compiler_params=LIMIT,
         cost_estimate=estimate(2 * 2048 * 256 * 512, 6 * 2**20),
         name="cut_moments",
     )(where, first, second, new, old)
@@ -386,6 +390,7 @@
         in_specs=[ANY],
         out_specs=VMEM,
         scratch_shapes=[pltpu.VMEM((8, 64, 256), BF), DMA],
+        compiler_params=LIMIT,
         cost_estimate=estimate(8 * 64 * 256, 2**19),
         name="sum_margin",
     )(moments)
@@ -427,6 +432,7 @@
         in_specs=[SMEM] + [VMEM] * 11,
         out_specs=[VMEM] * 4,
         scratch_shapes=[pltpu.VMEM((512, 512), BF)],
+        compiler_params=LIMIT,
         cost_estimate=estimate(6 * 208 * 512 * 512, 4 * 2**20),
         name="step",
     )(where, *sums, *rest)
@@ -446,6 +452,7 @@
         in_specs=[VMEM] * 2,
         out_specs=VMEM,
         scratch_shapes=[pltpu.VMEM((256, 512), F32)],
+        compiler_params=LIMIT,
         cost_estimate=estimate(208 * 1024, 3 * 2**19),
         name="turn_back",
     )(first, second)
@@ -473,6 +480,7 @@
         out_shape=[jax.ShapeDtypeStruct((64, 1664), F32)] * 2,
         in_specs=[VMEM],
         out_specs=[VMEM] * 2,
+        compiler_params=LIMIT,
         cost_estimate=estimate(64 * 1664 * 4, 3 * 2**19),
         name="finish",
     )(new)
@@ -493,6 +501,7 @@
         out_shape=jax.ShapeDtypeStruct((chunk // 4, 512), BF),
         in_specs=[SMEM] + [VMEM] * 4,
         out_specs=VMEM,
+        compiler_params=LIMIT,
         cost_estimate=estimate(0, chunk * 512),
     )(where, *arrays)
 
@@ -517,12 +526,16 @@
 
 
 def update_kernel(ring, where, *refs):
-    own, other, bases, outs = refs[:4], refs[4:8], refs[8:13], refs[13:17]
-    low, base, held, in_sem, other_sem, base_sem, out_sem = refs[17:]
+    count = 4 if EXTRA[ring] else 1
+    own, other, bases, outs = refs[:4], refs[4:8], refs[8 : 8 + count], refs[8 + count : 12 + count]
+    low, base, held, in_sem, other_sem, base_sem, out_sem = refs[12 + count :]
     core = place(where, "core")
     width = WIDTH[ring]
     for k, step in enumerate(STEPS):
-        source = basis_rows(ring, where, step, bases)
+        if EXTRA[ring]:
+            source = bases[STEPS.index((4 - step) % 4)].at[:, pl.ds(width, 512)]
+        else:
+            source = basis_rows(ring, where, step, bases[0])
         pltpu.make_async_copy(source, base.at[pl.ds(k * 128, 128), :], base_sem).start()
     if ring == "x":
         start_all(low_copies(1, where, own, core * 1280, low, in_sem, core))
@@ -572,6 +585,7 @@
             DMA,
             DMA((4,)),
         ],
+        compiler_params=LIMIT,
         cost_estimate=estimate(2 * 512 * 512 * width, 512 * width * 2 + 512 * 1024 + width * 1024),
     )(where, *arrays, *bases)
 
@@ -594,14 +608,9 @@
         where = jnp.where(spot == i, value, where)
 
     arrived = {}
-    for ring in ("x", "y", "z"):
-        blocks = pack(ring, where, grad)
+    for ring in ("x", "z", "y"):
+        blocks = pack(ring, where, grad, basis_new)
         arrived[ring] = exchange(blocks, RINGS[ring])
-    by_core = basis_new.reshape(4, 2, 2, 128, 512)
-    by_x = lax.dynamic_index_in_dim(lax.dynamic_index_in_dim(by_core, core, 2, False), y, 0, False)
-    by_z = lax.dynamic_index_in_dim(by_x, xh, 0, False)
-    bases = [basis_new] + [shift(by_z, RINGS["z"], 4 - step) for step in range(1, 4)]
-    bases.append(lax.ppermute(by_x.reshape(256, 512), "xl", [(0, 1), (1, 0)]))
 
     moments = cut_moments(where, moment_first, moment_second, basis_new, basis_old)
     moments = lax.all_to_all(moments, ROW, 0, 0, tiled=True)
@@ -611,9 +620,9 @@
 
     totals = {}
     for group, blocks in ((1, arrived["x"]), (0, arrived["y"] + arrived["z"])):
-        other = project(group, where, blocks, bases)
+        other = project(group, where, blocks, basis_new)
         other = shift(other, RINGS["core"], 1)
-        partial = project(group, where, blocks, bases, other)
+        partial = project(group, where, blocks, basis_new, other)
         halves = ordered(partial, U[group])
         rest = add_up(group, where, halves)
         totals[group] = ordered(rest, V[group])
@@ -628,7 +637,7 @@
         whole = ordered([quarter] * 4, U[group])
         whole = whole + [shift(array, RINGS["core"], 1) for array in whole]
         for ring in rings:
-            blocks = update_blocks(ring, where, whole, bases)
+            blocks = update_blocks(ring, where, whole, arrived[ring] if EXTRA[ring] else [basis_new])
             sent[ring] = exchange(blocks, RINGS[ring])
     update = None
     for ring in ("x", "y", "z"):

time: 293 us -> 281 us (0.959)
  the two profiles are of different devices: /device:TPU:6 before, /device:TPU:38 now
where the time goes in v2:
time: 281 us; the launch traced here: 280 us
  waiting for transfers between devices  107 us (38%)
  starting transfers between devices  74.3 us (26%)
  Pallas kernels  56.6 us (20%)
  blocking collectives  27.1 us (10%)
  local copies, waits for them, and re-layouts  13.8 us (5%)
    ppermute x53, waiting for transfers between devices, shift(): return lax.ppermute(array, NAMES, pairs)  97.6 us
    ppermute x53, starting transfers between devices, shift(): return lax.ppermute(array, NAMES, pairs)  61.9 us
    all_to_all x1, blocking collectives, compute(): new = lax.all_to_all(new, ROW, 0, 0, tiled=True)  27.1 us
    pallas_call x4, Pallas kernels, project(): pl.pallas_call(functools.partial(project_kernel, group, own), out_shape=s...  18.6 us
    pallas_call x3, Pallas kernels, update_blocks(): pl.pallas_call(functools.partial(update_kernel, ring), out_shape=[jax.Sha...  14.7 us
    unnamed x88, local copies, waits for them, and re-layouts  13.8 us
    all_to_all x1, waiting for transfers between devices, compute(): margin = lax.all_to_all(margin, ROW, 0, 0, tiled=True).reshape(256, 512)  9.22 us
    pallas_call x3, Pallas kernels, unpack(): pl.pallas_call(functools.partial(unpack_kernel, ring), out_shape=jax.Shap...  8.79 us
  transfers between devices with their start and end apart: 55, of which 21 were waited for; matrix products, arithmetic and copies ran while one was open for 0% of the time, Pallas kernels for 18%

profile of v2, /device:TPU:38, one launch (start us, length us, event | category | flops | bytes accessed | tf_op | source)
XLA Modules:
  0.0 280.1 jit_solution(12587996668888338191)
XLA Ops:
  0.7 1.6 copy-done
  2.3 2.9 %copy-done.2 = bf16[128,26624]{1,0:T(8,128)(2,1)S(1)} copy-done((bf16[128,26624]{1,0:T(8,128)(2,1)S(1)}, bf16[128,26624]{1,0:T(8,128)(2,1)}, u32[]{:S(2)}) %copy-start.2) | copy-done | bytes 6815768
  6.2 1.6 collective-permute-start
  7.8 2.1 shard_map.77
  9.9 2.0 collective-permute-start.3
  12.0 3.0 %collective-permute-start.5 = (bf16[128,2560]{1,0:T(8,128)(2,1)S(1)}, bf16[128,2560]{1,0:T(8,128)(2,1)S(1)}, u32[]{:S(2)}, u32[]{:S(2)}) collective-permute-start(bf16[128,2560]{1,0:T(8,128)(2,1)S(1)} %get-tuple-element.56), channel_id=1, source_target_pairs={{0,32},{1,33},{2,34},{3,35},{4,36},{5,37},{6,38},{7,39},{8,40},{9,... | collective-permute-start | bytes 1966088 | tf_op jit(solution)/shard_map/ppermute | solution.py:53
  15.0 1.7 collective-permute-start.1
  16.7 4.5 %collective-permute-done.refs_1_ = bf16[128,2048]{1,0:T(8,128)(2,1)S(1)} collective-permute-done((bf16[128,2048]{1,0:T(8,128)(2,1)S(1)}, bf16[128,2048]{1,0:T(8,128)(2,1)S(1)}, u32[]{:S(2)}, u32[]{:S(2)}) %collective-permute-start) | collective-permute-done | bytes 524320 | tf_op jit(solution)/shard_map/ppermute | solution.py:53
  21.2 1.9 collective-permute-start.2
  23.1 1.8 shard_map.81
  24.9 4.9 %collective-permute-done.1.refs_2_ = bf16[128,2048]{1,0:T(8,128)(2,1)S(1)} collective-permute-done((bf16[128,2048]{1,0:T(8,128)(2,1)S(1)}, bf16[128,2048]{1,0:T(8,128)(2,1)S(1)}, u32[]{:S(2)}, u32[]{:S(2)}) %collective-permute-start.1) | collective-permute-done | bytes 524320 | tf_op jit(solution)/shard_map/ppermute | solution.py:53
  30.3 5.3 %collective-permute-done.2.refs_3_ = bf16[128,2048]{1,0:T(8,128)(2,1)S(1)} collective-permute-done((bf16[128,2048]{1,0:T(8,128)(2,1)S(1)}, bf16[128,2048]{1,0:T(8,128)(2,1)S(1)}, u32[]{:S(2)}, u32[]{:S(2)}) %collective-permute-start.2) | collective-permute-done | bytes 524320 | tf_op jit(solution)/shard_map/ppermute | solution.py:53
  36.4 3.3 %collective-permute-done.3.refs_5_.refs_9_ = bf16[128,2560]{1,0:T(8,128)(2,1)S(1)} collective-permute-done((bf16[128,2560]{1,0:T(8,128)(2,1)S(1)}, bf16[128,2560]{1,0:T(8,128)(2,1)S(1)}, u32[]{:S(2)}, u32[]{:S(2)}) %collective-permute-start.3) | collective-permute-done | bytes 655392 | tf_op jit(solution)/shard_map/ppermute | solution.py:53
  39.7 1.4 collective-permute-start.15
  41.1 1.8 collective-permute-done.5.refs_7_.refs_11_
  43.0 3.7 %shard_map.78 = bf16[2048,512]{1,0:T(8,128)(2,1)} custom-call(s32[8]{0:T(128)S(1)} %compare_select_fusion.6.where, bf16[128,2048]{1,0:T(8,128)(2,1)S(1)} %get-tuple-element.49.refs_0_, bf16[128,2048]{1,0:T(8,128)(2,1)S(1)} %collective-permute-done.refs_1_, bf16[128,2048]{1,0:T(8,128)(2,1)S(1)} %collective-permute-done.1.refs_2_, ...), custom_call_target="tpu_custom_call" | custom-call | flops 1073741824 | bytes 4718592 | tf_op jit(solution)/shard_map/pallas_call | solution.py:293
  46.8 3.4 %collective-permute-done.13.refs_1_.refs_9_ = bf16[128,3072]{1,0:T(8,128)(2,1)S(1)} collective-permute-done((bf16[128,3072]{1,0:T(8,128)(2,1)S(1)}, bf16[128,3072]{1,0:T(8,128)(2,1)S(1)}, u32[]{:S(2)}, u32[]{:S(2)}) %collective-permute-start.13) | collective-permute-done | bytes 786464 | tf_op jit(solution)/shard_map/ppermute | solution.py:53
  50.2 21.0 %collective-permute-done.14.refs_2_.refs_10_ = bf16[128,3072]{1,0:T(8,128)(2,1)S(1)} collective-permute-done((bf16[128,3072]{1,0:T(8,128)(2,1)S(1)}, bf16[128,3072]{1,0:T(8,128)(2,1)S(1)}, u32[]{:S(2)}, u32[]{:S(2)}) %collective-permute-start.14) | collective-permute-done | bytes 786464 | tf_op jit(solution)/shard_map/ppermute | solution.py:53
  71.3 2.8 %shard_map.82 = bf16[1280,512]{1,0:T(8,128)(2,1)} custom-call(s32[8]{0:T(128)S(1)} %compare_select_fusion.6.where, bf16[128,3072]{1,0:T(8,128)(2,1)S(1)} %get-tuple-element.65.refs_0_.refs_8_, bf16[128,3072]{1,0:T(8,128)(2,1)S(1)} %collective-permute-done.13.refs_1_.refs_9_, bf16[128,3072]{1,0:T(8,128)(2,1)S(1)} %collective-permute-done.14.refs_2_.refs_10_, ...), custom_call_target="tpu_custom_call" | custom-call | flops 671088640 | bytes 3145728 | tf_op jit(solution)/shard_map/pallas_call | solution.py:293
  74.3 1.7 cut_moments.1
  77.1 6.3 %all-to-all-start = ((bf16[8,256,256]{2,1,0:T(8,128)(2,1)}), bf16[8,256,256]{2,1,0:T(8,128)(2,1)S(1)}, u32[]{:S(2)}, u32[]{:S(2)}) async-start(bf16[8,256,256]{2,1,0:T(8,128)(2,1)} %copy-done.27), calls=%async_computation | async-start | bytes 2097152 | tf_op jit(solution)/shard_map/all_to_all | solution.py:616
  88.0 5.2 %shard_map.83 = (bf16[320,512]{1,0:T(8,128)(2,1)S(1)}, bf16[320,512]{1,0:T(8,128)(2,1)}, bf16[320,512]{1,0:T(8,128)(2,1)}, bf16[320,512]{1,0:T(8,128)(2,1)S(1)}) custom-call(s32[8]{0:T(128)S(1)} %compare_select_fusion.6.where, bf16[128,3072]{1,0:T(8,128)(2,1)S(1)} %copy-done.4, bf16[128,3072]{1,0:T(8,128)(2,1)S(1)} %copy-done.7, ...), custom_call_target="tpu_custom_call" | custom-call | flops 671088640 | bytes 3145728 | tf_op jit(solution)/shard_map/pallas_call | solution.py:293
  94.0 1.5 collective-permute-start.17
  95.4 1.2 collective-permute-start.18
  96.7 6.9 %shard_map.79 = (bf16[512,512]{1,0:T(8,128)(2,1)S(1)}, bf16[512,512]{1,0:T(8,128)(2,1)}, bf16[512,512]{1,0:T(8,128)(2,1)}, bf16[512,512]{1,0:T(8,128)(2,1)}) custom-call(s32[8]{0:T(128)S(1)} %compare_select_fusion.6.where, bf16[128,2048]{1,0:T(8,128)(2,1)S(1)} %copy-done.30, bf16[128,2048]{1,0:T(8,128)(2,1)S(1)} %copy-done.32, ...), custom_call_target="tpu_custom_call" | custom-call | flops 1073741824 | bytes 4718592 | tf_op jit(solution)/shard_map/pallas_call | solution.py:293
  104.4 2.1 collective-permute-start.8
  107.7 6.0 %all-to-all-start.1 = ((bf16[8,32,512]{2,1,0:T(8,128)(2,1)}), bf16[8,32,512]{2,1,0:T(8,128)(2,1)S(1)}, u32[]{:S(2)}, u32[]{:S(2)}) async-start(bf16[8,32,512]{2,1,0:T(8,128)(2,1)} %sum_margin.1), calls=%async_computation.1 | async-start | bytes 524288 | tf_op jit(solution)/shard_map/all_to_all | solution.py:618
  114.3 9.2 %all-to-all-done.1 = bf16[8,32,512]{2,1,0:T(8,128)(2,1)S(1)} async-done(((bf16[8,32,512]{2,1,0:T(8,128)(2,1)}), bf16[8,32,512]{2,1,0:T(8,128)(2,1)S(1)}, u32[]{:S(2)}, u32[]{:S(2)}) %all-to-all-start.1) | async-done | bytes 262176 | tf_op jit(solution)/shard_map/all_to_all | solution.py:618
  123.5 2.8 %collective-permute-done.19.d = bf16[320,512]{1,0:T(8,128)(2,1)} collective-permute-done((bf16[320,512]{1,0:T(8,128)(2,1)}, bf16[320,512]{1,0:T(8,128)(2,1)}, u32[]{:S(2)}, u32[]{:S(2)}) %collective-permute-start.19) | collective-permute-done | bytes 327712 | tf_op jit(solution)/shard_map/ppermute | solution.py:53
  127.3 1.5 shard_map.84
  128.8 2.5 collective-permute-start.20
  132.3 1.9 shard_map.80
  134.3 1.2 collective-permute-start.10
  135.5 1.5 collective-permute-start.11
  137.0 2.2 collective-permute-start.12
  139.2 1.6 collective-permute-start.21
  141.9 3.2 %collective-permute-done.21.refs_6_ = bf16[80,512]{1,0:T(8,128)(2,1)S(1)} collective-permute-done((bf16[80,512]{1,0:T(8,128)(2,1)S(1)}, bf16[80,512]{1,0:T(8,128)(2,1)S(1)}, u32[]{:S(2)}, u32[]{:S(2)}) %collective-permute-start.21) | collective-permute-done | bytes 81952 | tf_op jit(solution)/shard_map/ppermute | solution.py:53
  145.3 1.4 step.1
  146.7 2.3 collective-permute-start.42
  150.1 1.8 collective-permute-done.42.refs_3_
  151.9 3.1 %collective-permute-done.41.refs_2_ = bf16[80,512]{1,0:T(8,128)(2,1)S(1)} collective-permute-done((bf16[80,512]{1,0:T(8,128)(2,1)S(1)}, bf16[80,512]{1,0:T(8,128)(2,1)S(1)}, u32[]{:S(2)}, u32[]{:S(2)}) %collective-permute-start.41) | collective-permute-done | bytes 81952 | tf_op jit(solution)/shard_map/ppermute | solution.py:53
  156.5 1.1 collective-permute-start.45
  158.1 2.0 collective-permute-start.25
  160.7 12.2 %collective-permute-done.26.refs_3_ = bf16[128,512]{1,0:T(8,128)(2,1)S(1)} collective-permute-done((bf16[128,512]{1,0:T(8,128)(2,1)S(1)}, bf16[128,512]{1,0:T(8,128)(2,1)S(1)}, u32[]{:S(2)}, u32[]{:S(2)}) %collective-permute-start.26) | collective-permute-done | bytes 131104 | tf_op jit(solution)/shard_map/ppermute | solution.py:53
  173.6 1.7 collective-permute-start.29
  175.3 3.2 %collective-permute-start.28 = (bf16[512,512]{1,0:T(8,128)(2,1)S(1)}, bf16[512,512]{1,0:T(8,128)(2,1)S(1)}, u32[]{:S(2)}, u32[]{:S(2)}) collective-permute-start(bf16[512,512]{1,0:T(8,128)(2,1)S(1)} %shard_map.85.refs_0_), channel_id=1, source_target_pairs={{0,2},{1,9},{2,0},{3,11},{4,6},{5,13},{6,4},{7,15},{8,10},{9,1},{1... | collective-permute-start | bytes 1572872 | tf_op jit(solution)/shard_map/ppermute | solution.py:53
  178.6 2.5 collective-permute-start.27
  181.5 1.7 collective-permute-done.43.refs_1_
  184.0 7.2 %collective-permute-done.28.refs_2_ = bf16[512,512]{1,0:T(8,128)(2,1)S(1)} collective-permute-done((bf16[512,512]{1,0:T(8,128)(2,1)S(1)}, bf16[512,512]{1,0:T(8,128)(2,1)S(1)}, u32[]{:S(2)}, u32[]{:S(2)}) %collective-permute-start.28) | collective-permute-done | bytes 524320 | tf_op jit(solution)/shard_map/ppermute | solution.py:53
  192.3 2.8 %collective-permute-done.47.refs_5_ = bf16[320,512]{1,0:T(8,128)(2,1)S(1)} collective-permute-done((bf16[320,512]{1,0:T(8,128)(2,1)S(1)}, bf16[320,512]{1,0:T(8,128)(2,1)S(1)}, u32[]{:S(2)}, u32[]{:S(2)}) %collective-permute-start.47) | collective-permute-done | bytes 327712 | tf_op jit(solution)/shard_map/ppermute | solution.py:53
  195.1 7.7 %shard_map.89 = (bf16[128,2560]{1,0:T(8,128)(2,1)S(1)}, bf16[128,2560]{1,0:T(8,128)(2,1)S(1)}, bf16[128,2560]{1,0:T(8,128)(2,1)S(1)}, bf16[128,2560]{1,0:T(8,128)(2,1)S(1)}) custom-call(s32[8]{0:T(128)S(1)} %compare_select_fusion.6.where, bf16[320,512]{1,0:T(8,128)(2,1)S(1)} %shard_map.88.refs_0_, bf16[320,512]{1,0:T(8,128)(2,1)S(1)} %collective-permute-done.43.refs_1_, ...), custom_call_target="tpu_custom_call" | custom-call | flops 1342177280 | bytes 5767168 | tf_op jit(solution)/shard_map/pallas_call | solution.py:574
  202.8 2.2 collective-permute-start.50
  205.1 3.5 %collective-permute-start.52 = (bf16[128,2560]{1,0:T(8,128)(2,1)S(1)}, bf16[128,2560]{1,0:T(8,128)(2,1)S(1)}, u32[]{:S(2)}, u32[]{:S(2)}) collective-permute-start(bf16[128,2560]{1,0:T(8,128)(2,1)S(1)} %get-tuple-element.90), channel_id=1, source_target_pairs={{0,2},{1,3},{2,0},{3,1},{4,6},{5,7},{6,4},{7,5},{8,10},{9,11},{10,... | collective-permute-start | bytes 1966088 | tf_op jit(solution)/shard_map/ppermute | solution.py:53
  208.6 3.8 %shard_map.87 = (bf16[128,2048]{1,0:T(8,128)(2,1)S(1)}, bf16[128,2048]{1,0:T(8,128)(2,1)S(1)}, bf16[128,2048]{1,0:T(8,128)(2,1)S(1)}, bf16[128,2048]{1,0:T(8,128)(2,1)S(1)}) custom-call(s32[8]{0:T(128)S(1)} %compare_select_fusion.6.where, bf16[512,512]{1,0:T(8,128)(2,1)S(1)} %shard_map.85.refs_0_, bf16[512,512]{1,0:T(8,128)(2,1)S(1)} %collective-permute-done.27.refs_1_, ...), custom_call_target="tpu_custom_call" | custom-call | flops 1073741824 | bytes 4718592 | tf_op jit(solution)/shard_map/pallas_call | solution.py:574
  212.6 3.2 %shard_map.86 = (bf16[128,2048]{1,0:T(8,128)(2,1)S(1)}, bf16[128,2048]{1,0:T(8,128)(2,1)S(1)}, bf16[128,2048]{1,0:T(8,128)(2,1)S(1)}, bf16[128,2048]{1,0:T(8,128)(2,1)S(1)}) custom-call(s32[8]{0:T(128)S(1)} %compare_select_fusion.6.where, bf16[512,512]{1,0:T(8,128)(2,1)S(1)} %shard_map.85.refs_0_, bf16[512,512]{1,0:T(8,128)(2,1)S(1)} %collective-permute-done.27.refs_1_, ...), custom_call_target="tpu_custom_call" | custom-call | flops 1073741824 | bytes 4718592 | tf_op jit(solution)/shard_map/pallas_call | solution.py:574
  215.8 1.5 collective-permute-start.34
  217.3 16.1 %collective-permute-done.50.refs_1_ = bf16[128,2560]{1,0:T(8,128)(2,1)S(1)} collective-permute-done((bf16[128,2560]{1,0:T(8,128)(2,1)S(1)}, bf16[128,2560]{1,0:T(8,128)(2,1)S(1)}, u32[]{:S(2)}, u32[]{:S(2)}) %collective-permute-start.50) | collective-permute-done | bytes 655392 | tf_op jit(solution)/shard_map/ppermute | solution.py:53
  233.9 3.3 %collective-permute-start.39 = (bf16[128,2048]{1,0:T(8,128)(2,1)S(1)}, bf16[128,2048]{1,0:T(8,128)(2,1)S(1)}, u32[]{:S(2)}, u32[]{:S(2)}) collective-permute-start(bf16[128,2048]{1,0:T(8,128)(2,1)S(1)} %get-tuple-element.85), channel_id=1, source_target_pairs={{0,8},{1,9},{2,10},{3,11},{4,12},{5,13},{6,14},{7,15},{8,0},{9,1},... | collective-permute-start | bytes 1572872 | tf_op jit(solution)/shard_map/ppermute | solution.py:53
  237.2 2.0 collective-permute-start.35
  239.2 3.5 %collective-permute-start.36 = (bf16[128,2048]{1,0:T(8,128)(2,1)S(1)}, bf16[128,2048]{1,0:T(8,128)(2,1)S(1)}, u32[]{:S(2)}, u32[]{:S(2)}) collective-permute-start(bf16[128,2048]{1,0:T(8,128)(2,1)S(1)} %get-tuple-element.81), channel_id=1, source_target_pairs={{0,32},{1,33},{2,34},{3,35},{4,36},{5,37},{6,38},{7,39},{8,40},{9,... | collective-permute-start | bytes 1572872 | tf_op jit(solution)/shard_map/ppermute | solution.py:53
  242.9 27.1 %all_to_all.15.new = bf16[8,128,256]{2,1,0:T(8,128)(2,1)S(1)} all-to-all(bf16[8,128,256]{2,1,0:T(8,128)(2,1)S(1)} %turn_back.1), channel_id=1, replica_groups=mesh['xl'=2,'z'=4,'y'=4,'xh'=2,'core'=2] {'xl','z'}, dimensions={0} | all-to-all | bytes 1048576 | tf_op jit(solution)/shard_map/all_to_all | solution.py:647
  271.1 3.6 %shard_map.90.refs_4_ = bf16[128,26624]{1,0:T(8,128)(2,1)} custom-call(s32[8]{0:T(128)S(1)} %compare_select_fusion.6.where, bf16[128,2560]{1,0:T(8,128)(2,1)S(1)} %get-tuple-element.87.refs_0_, bf16[128,2560]{1,0:T(8,128)(2,1)S(1)} %collective-permute-done.50.refs_1_, bf16[128,2560]{1,0:T(8,128)(2,1)S(1)} %collective-permute-done.51.refs_2_, ...), custom_call_target="tpu_custom_call" | custom-call | bytes 5242880 | tf_op jit(solution)/shard_map/pallas_call | solution.py:202
  274.7 2.6 shard_map.91.refs_4_
  277.4 2.6 shard_map.92
  (158 shorter events, 23.3 us)
Async XLA Ops:
  6.1 36.8 %copy-start.29 = (bf16[128,2048]{1,0:T(8,128)(2,1)}, bf16[128,2048]{1,0:T(8,128)(2,1)S(1)}, u32[]{:S(2)}) copy-start(bf16[128,2048]{1,0:T(8,128)(2,1)S(1)} %get-tuple-element.49.refs_0_) | copy-start | bytes 1572868
  6.2 15.0 %collective-permute-start = (bf16[128,2048]{1,0:T(8,128)(2,1)S(1)}, bf16[128,2048]{1,0:T(8,128)(2,1)S(1)}, u32[]{:S(2)}, u32[]{:S(2)}) collective-permute-start(bf16[128,2048]{1,0:T(8,128)(2,1)S(1)} %get-tuple-element.50), channel_id=1, source_target_pairs={{0,4},{1,5},{2,6},{3,7},{4,8},{5,9},{6,10},{7,11},{8,12},{9,13},{1... | collective-permute-start | bytes 1572872 | tf_op jit(solution)/shard_map/ppermute | solution.py:53
  9.9 33.0 %copy-start.15 = (bf16[128,2560]{1,0:T(8,128)(2,1)}, bf16[128,2560]{1,0:T(8,128)(2,1)S(1)}, u32[]{:S(2)}) copy-start(bf16[128,2560]{1,0:T(8,128)(2,1)S(1)} %get-tuple-element.53.refs_4_.refs_8_) | copy-start | bytes 1966084
  9.9 29.8 %collective-permute-start.3 = (bf16[128,2560]{1,0:T(8,128)(2,1)S(1)}, bf16[128,2560]{1,0:T(8,128)(2,1)S(1)}, u32[]{:S(2)}, u32[]{:S(2)}) collective-permute-start(bf16[128,2560]{1,0:T(8,128)(2,1)S(1)} %get-tuple-element.54), channel_id=1, source_target_pairs={{0,16},{1,17},{2,18},{3,19},{4,20},{5,21},{6,22},{7,23},{8,24},{9,... | collective-permute-start | bytes 1966088 | tf_op jit(solution)/shard_map/ppermute | solution.py:53
  11.9 29.2 %collective-permute-start.4 = (bf16[128,2560]{1,0:T(8,128)(2,1)S(1)}, bf16[128,2560]{1,0:T(8,128)(2,1)S(1)}, u32[]{:S(2)}, u32[]{:S(2)}) collective-permute-start(bf16[128,2560]{1,0:T(8,128)(2,1)S(1)} %get-tuple-element.55), channel_id=1, source_target_pairs={{0,48},{1,49},{2,50},{3,51},{4,52},{5,53},{6,54},{7,55},{8,56},{9,... | collective-permute-start | bytes 1966088 | tf_op jit(solution)/shard_map/ppermute | solution.py:53
  12.0 30.9 %collective-permute-start.5 = (bf16[128,2560]{1,0:T(8,128)(2,1)S(1)}, bf16[128,2560]{1,0:T(8,128)(2,1)S(1)}, u32[]{:S(2)}, u32[]{:S(2)}) collective-permute-start(bf16[128,2560]{1,0:T(8,128)(2,1)S(1)} %get-tuple-element.56), channel_id=1, source_target_pairs={{0,32},{1,33},{2,34},{3,35},{4,36},{5,37},{6,38},{7,39},{8,40},{9,... | collective-permute-start | bytes 1966088 | tf_op jit(solution)/shard_map/ppermute | solution.py:53
  15.0 14.8 %collective-permute-start.1 = (bf16[128,2048]{1,0:T(8,128)(2,1)S(1)}, bf16[128,2048]{1,0:T(8,128)(2,1)S(1)}, u32[]{:S(2)}, u32[]{:S(2)}) collective-permute-start(bf16[128,2048]{1,0:T(8,128)(2,1)S(1)} %get-tuple-element.51), channel_id=1, source_target_pairs={{0,12},{1,13},{2,14},{3,15},{4,0},{5,1},{6,2},{7,3},{8,4},{9,5},{1... | collective-permute-start | bytes 1572872 | tf_op jit(solution)/shard_map/ppermute | solution.py:53
  21.2 21.8 %copy-start.1 = (bf16[2048,512]{1,0:T(8,128)(2,1)S(1)}, bf16[2048,512]{1,0:T(8,128)(2,1)}, u32[]{:S(2)}) copy-start(bf16[2048,512]{1,0:T(8,128)(2,1)} %refs_8_.5) | copy-start | bytes 6291460
  21.2 14.4 %collective-permute-start.2 = (bf16[128,2048]{1,0:T(8,128)(2,1)S(1)}, bf16[128,2048]{1,0:T(8,128)(2,1)S(1)}, u32[]{:S(2)}, u32[]{:S(2)}) collective-permute-start(bf16[128,2048]{1,0:T(8,128)(2,1)S(1)} %get-tuple-element.52), channel_id=1, source_target_pairs={{0,8},{1,9},{2,10},{3,11},{4,12},{5,13},{6,14},{7,15},{8,0},{9,1},... | collective-permute-start | bytes 1572872 | tf_op jit(solution)/shard_map/ppermute | solution.py:53
  24.9 46.4 %copy-start.3 = (bf16[128,3072]{1,0:T(8,128)(2,1)}, bf16[128,3072]{1,0:T(8,128)(2,1)S(1)}, u32[]{:S(2)}) copy-start(bf16[128,3072]{1,0:T(8,128)(2,1)S(1)} %get-tuple-element.65.refs_0_.refs_8_) | copy-start | bytes 2359300
  29.8 20.4 %collective-permute-start.13 = (bf16[128,3072]{1,0:T(8,128)(2,1)S(1)}, bf16[128,3072]{1,0:T(8,128)(2,1)S(1)}, u32[]{:S(2)}, u32[]{:S(2)}) collective-permute-start(bf16[128,3072]{1,0:T(8,128)(2,1)S(1)} %get-tuple-element.66), channel_id=1, source_target_pairs={{0,64},{1,65},{2,66},{3,67},{4,68},{5,69},{6,70},{7,71},{8,72},{9,... | collective-permute-start | bytes 2359304 | tf_op jit(solution)/shard_map/ppermute | solution.py:53
  35.5 35.7 %collective-permute-start.14 = (bf16[128,3072]{1,0:T(8,128)(2,1)S(1)}, bf16[128,3072]{1,0:T(8,128)(2,1)S(1)}, u32[]{:S(2)}, u32[]{:S(2)}) collective-permute-start(bf16[128,3072]{1,0:T(8,128)(2,1)S(1)} %get-tuple-element.67), channel_id=1, source_target_pairs={{0,66},{1,67},{2,64},{3,65},{4,70},{5,71},{6,68},{7,69},{8,74},{9,... | collective-permute-start | bytes 2359304 | tf_op jit(solution)/shard_map/ppermute | solution.py:53
  39.7 31.5 %collective-permute-start.15 = (bf16[128,3072]{1,0:T(8,128)(2,1)S(1)}, bf16[128,3072]{1,0:T(8,128)(2,1)S(1)}, u32[]{:S(2)}, u32[]{:S(2)}) collective-permute-start(bf16[128,3072]{1,0:T(8,128)(2,1)S(1)} %get-tuple-element.68), channel_id=1, source_target_pairs={{0,2},{1,3},{2,0},{3,1},{4,6},{5,7},{6,4},{7,5},{8,10},{9,11},{10,... | collective-permute-start | bytes 2359304 | tf_op jit(solution)/shard_map/ppermute | solution.py:53
  46.7 49.9 %collective-permute-start.6 = (bf16[2048,512]{1,0:T(8,128)(2,1)}, bf16[2048,512]{1,0:T(8,128)(2,1)}, u32[]{:S(2)}, u32[]{:S(2)}) collective-permute-start(bf16[2048,512]{1,0:T(8,128)(2,1)} %shard_map.78), channel_id=1, source_target_pairs={{0,1},{1,0},{2,3},{3,2},{4,5},{5,4},{6,7},{7,6},{8,9},{9,8},{10,11... | collective-permute-start | bytes 6291464 | tf_op jit(solution)/shard_map/ppermute | solution.py:53
  50.2 23.9 %copy-start.6 = (bf16[128,3072]{1,0:T(8,128)(2,1)}, bf16[128,3072]{1,0:T(8,128)(2,1)S(1)}, u32[]{:S(2)}) copy-start(bf16[128,3072]{1,0:T(8,128)(2,1)S(1)} %collective-permute-done.13.refs_1_.refs_9_) | copy-start | bytes 2359300
  74.1 9.3 %collective-permute-start.16 = (bf16[1280,512]{1,0:T(8,128)(2,1)}, bf16[1280,512]{1,0:T(8,128)(2,1)}, u32[]{:S(2)}, u32[]{:S(2)}) collective-permute-start(bf16[1280,512]{1,0:T(8,128)(2,1)} %shard_map.82), channel_id=1, source_target_pairs={{0,1},{1,0},{2,3},{3,2},{4,5},{5,4},{6,7},{7,6},{8,9},{9,8},{10,11... | collective-permute-start | bytes 3932168 | tf_op jit(solution)/shard_map/ppermute | solution.py:53
  77.1 29.8 %all-to-all-start = ((bf16[8,256,256]{2,1,0:T(8,128)(2,1)}), bf16[8,256,256]{2,1,0:T(8,128)(2,1)S(1)}, u32[]{:S(2)}, u32[]{:S(2)}) async-start(bf16[8,256,256]{2,1,0:T(8,128)(2,1)} %copy-done.27), calls=%async_computation | async-start | bytes 2097152 | tf_op jit(solution)/shard_map/all_to_all | solution.py:616
  94.0 19.7 %collective-permute-start.17 = (bf16[320,512]{1,0:T(8,128)(2,1)}, bf16[320,512]{1,0:T(8,128)(2,1)}, u32[]{:S(2)}, u32[]{:S(2)}) collective-permute-start(bf16[320,512]{1,0:T(8,128)(2,1)} %get-tuple-element.70), channel_id=1, source_target_pairs={{0,16},{1,17},{2,18},{3,19},{4,20},{5,21},{6,22},{7,23},{8,24},{9,... | collective-permute-start | bytes 983048 | tf_op jit(solution)/shard_map/ppermute | solution.py:53
  95.4 28.1 %collective-permute-start.18 = (bf16[320,512]{1,0:T(8,128)(2,1)}, bf16[320,512]{1,0:T(8,128)(2,1)}, u32[]{:S(2)}, u32[]{:S(2)}) collective-permute-start(bf16[320,512]{1,0:T(8,128)(2,1)} %get-tuple-element.71), channel_id=1, source_target_pairs={{0,32},{1,33},{2,34},{3,35},{4,36},{5,37},{6,38},{7,39},{8,40},{9,... | collective-permute-start | bytes 983048 | tf_op jit(solution)/shard_map/ppermute | solution.py:53
  104.4 26.9 %collective-permute-start.7 = (bf16[512,512]{1,0:T(8,128)(2,1)}, bf16[512,512]{1,0:T(8,128)(2,1)}, u32[]{:S(2)}, u32[]{:S(2)}) collective-permute-start(bf16[512,512]{1,0:T(8,128)(2,1)} %get-tuple-element.58), channel_id=1, source_target_pairs={{0,64},{1,5},{2,66},{3,7},{4,68},{5,9},{6,70},{7,11},{8,72},{9,13}... | collective-permute-start | bytes 1572872 | tf_op jit(solution)/shard_map/ppermute | solution.py:53
  104.4 26.9 %collective-permute-start.8 = (bf16[512,512]{1,0:T(8,128)(2,1)}, bf16[512,512]{1,0:T(8,128)(2,1)}, u32[]{:S(2)}, u32[]{:S(2)}) collective-permute-start(bf16[512,512]{1,0:T(8,128)(2,1)} %get-tuple-element.59), channel_id=1, source_target_pairs={{0,2},{1,9},{2,0},{3,11},{4,6},{5,13},{6,4},{7,15},{8,10},{9,1},{1... | collective-permute-start | bytes 1572872 | tf_op jit(solution)/shard_map/ppermute | solution.py:53
  106.4 24.9 %collective-permute-start.9 = (bf16[512,512]{1,0:T(8,128)(2,1)}, bf16[512,512]{1,0:T(8,128)(2,1)}, u32[]{:S(2)}, u32[]{:S(2)}) collective-permute-start(bf16[512,512]{1,0:T(8,128)(2,1)} %get-tuple-element.60), channel_id=1, source_target_pairs={{0,66},{1,13},{2,64},{3,15},{4,70},{5,1},{6,68},{7,3},{8,74},{9,5}... | collective-permute-start | bytes 1572872 | tf_op jit(solution)/shard_map/ppermute | solution.py:53
  107.7 15.8 %all-to-all-start.1 = ((bf16[8,32,512]{2,1,0:T(8,128)(2,1)}), bf16[8,32,512]{2,1,0:T(8,128)(2,1)S(1)}, u32[]{:S(2)}, u32[]{:S(2)}) async-start(bf16[8,32,512]{2,1,0:T(8,128)(2,1)} %sum_margin.1), calls=%async_computation.1 | async-start | bytes 524288 | tf_op jit(solution)/shard_map/all_to_all | solution.py:618
  113.7 12.6 %collective-permute-start.19 = (bf16[320,512]{1,0:T(8,128)(2,1)}, bf16[320,512]{1,0:T(8,128)(2,1)}, u32[]{:S(2)}, u32[]{:S(2)}) collective-permute-start(bf16[320,512]{1,0:T(8,128)(2,1)} %copy-done.43), channel_id=1, source_target_pairs={{0,48},{1,49},{2,50},{3,51},{4,52},{5,53},{6,54},{7,55},{8,56},{9,... | collective-permute-start | bytes 983048 | tf_op jit(solution)/shard_map/ppermute | solution.py:53
  123.5 15.7 %collective-permute-start.23 = (bf16[256,512]{1,0:T(8,128)(2,1)S(1)}, bf16[256,512]{1,0:T(8,128)(2,1)S(1)}, u32[]{:S(2)}, u32[]{:S(2)}) collective-permute-start(bf16[256,512]{1,0:T(8,128)(2,1)S(1)} %bitcast.1), channel_id=1, source_target_pairs={{0,1},{1,0},{2,3},{3,2},{4,5},{5,4},{6,7},{7,6},{8,9},{9,8},{10,11... | collective-permute-start | bytes 786440 | tf_op jit(solution)/shard_map/ppermute | solution.py:53
  128.8 12.0 %collective-permute-start.20 = (bf16[80,512]{1,0:T(8,128)(2,1)S(1)}, bf16[80,512]{1,0:T(8,128)(2,1)S(1)}, u32[]{:S(2)}, u32[]{:S(2)}) collective-permute-start(bf16[80,512]{1,0:T(8,128)(2,1)S(1)} %get-tuple-element.74), channel_id=1, source_target_pairs={{0,4},{1,5},{2,6},{3,7},{4,8},{5,9},{6,10},{7,11},{8,12},{9,13},{1... | collective-permute-start | bytes 245768 | tf_op jit(solution)/shard_map/ppermute | solution.py:53
  134.3 60.9 %copy-start.5 = (bf16[128,3072]{1,0:T(8,128)(2,1)S(1)}, bf16[128,3072]{1,0:T(8,128)(2,1)}, u32[]{:S(2)}) copy-start(bf16[128,3072]{1,0:T(8,128)(2,1)} %copy-done.3) | copy-start | bytes 2359300
  134.3 60.8 %copy-start.8 = (bf16[128,3072]{1,0:T(8,128)(2,1)S(1)}, bf16[128,3072]{1,0:T(8,128)(2,1)}, u32[]{:S(2)}) copy-start(bf16[128,3072]{1,0:T(8,128)(2,1)} %copy-done.6) | copy-start | bytes 2359300
  134.3 60.8 %copy-start.11 = (bf16[128,3072]{1,0:T(8,128)(2,1)S(1)}, bf16[128,3072]{1,0:T(8,128)(2,1)}, u32[]{:S(2)}) copy-start(bf16[128,3072]{1,0:T(8,128)(2,1)} %copy-done.9) | copy-start | bytes 2359300
  134.3 60.8 %copy-start.14 = (bf16[128,3072]{1,0:T(8,128)(2,1)S(1)}, bf16[128,3072]{1,0:T(8,128)(2,1)}, u32[]{:S(2)}) copy-start(bf16[128,3072]{1,0:T(8,128)(2,1)} %copy-done.12) | copy-start | bytes 2359300
  134.3 11.0 %collective-permute-start.10 = (bf16[128,512]{1,0:T(8,128)(2,1)S(1)}, bf16[128,512]{1,0:T(8,128)(2,1)S(1)}, u32[]{:S(2)}, u32[]{:S(2)}) collective-permute-start(bf16[128,512]{1,0:T(8,128)(2,1)S(1)} %get-tuple-element.62), channel_id=1, source_target_pairs={{0,16},{1,65},{2,18},{3,67},{4,20},{5,69},{6,22},{7,71},{8,24},{9,... | collective-permute-start | bytes 393224 | tf_op jit(solution)/shard_map/ppermute | solution.py:53
  135.5 9.7 %collective-permute-start.11 = (bf16[128,512]{1,0:T(8,128)(2,1)S(1)}, bf16[128,512]{1,0:T(8,128)(2,1)S(1)}, u32[]{:S(2)}, u32[]{:S(2)}) collective-permute-start(bf16[128,512]{1,0:T(8,128)(2,1)S(1)} %get-tuple-element.63), channel_id=1, source_target_pairs={{0,32},{1,3},{2,34},{3,1},{4,36},{5,7},{6,38},{7,5},{8,40},{9,11},... | collective-permute-start | bytes 393224 | tf_op jit(solution)/shard_map/ppermute | solution.py:53
  137.0 8.3 %collective-permute-start.12 = (bf16[128,512]{1,0:T(8,128)(2,1)S(1)}, bf16[128,512]{1,0:T(8,128)(2,1)S(1)}, u32[]{:S(2)}, u32[]{:S(2)}) collective-permute-start(bf16[128,512]{1,0:T(8,128)(2,1)S(1)} %get-tuple-element.64), channel_id=1, source_target_pairs={{0,48},{1,67},{2,50},{3,65},{4,52},{5,71},{6,54},{7,69},{8,56},{9,... | collective-permute-start | bytes 393224 | tf_op jit(solution)/shard_map/ppermute | solution.py:53
  139.2 5.9 %collective-permute-start.21 = (bf16[80,512]{1,0:T(8,128)(2,1)S(1)}, bf16[80,512]{1,0:T(8,128)(2,1)S(1)}, u32[]{:S(2)}, u32[]{:S(2)}) collective-permute-start(bf16[80,512]{1,0:T(8,128)(2,1)S(1)} %get-tuple-element.75), channel_id=1, source_target_pairs={{0,8},{1,9},{2,10},{3,11},{4,12},{5,13},{6,14},{7,15},{8,0},{9,1},... | collective-permute-start | bytes 245768 | tf_op jit(solution)/shard_map/ppermute | solution.py:53
  140.8 4.4 %collective-permute-start.22 = (bf16[80,512]{1,0:T(8,128)(2,1)S(1)}, bf16[80,512]{1,0:T(8,128)(2,1)S(1)}, u32[]{:S(2)}, u32[]{:S(2)}) collective-permute-start(bf16[80,512]{1,0:T(8,128)(2,1)S(1)} %get-tuple-element.76), channel_id=1, source_target_pairs={{0,12},{1,13},{2,14},{3,15},{4,0},{5,1},{6,2},{7,3},{8,4},{9,5},{1... | collective-permute-start | bytes 245768 | tf_op jit(solution)/shard_map/ppermute | solution.py:53
  146.7 5.2 %collective-permute-start.42 = (bf16[80,512]{1,0:T(8,128)(2,1)S(1)}, bf16[80,512]{1,0:T(8,128)(2,1)S(1)}, u32[]{:S(2)}, u32[]{:S(2)}) collective-permute-start(bf16[80,512]{1,0:T(8,128)(2,1)S(1)} %get-tuple-element.86.refs_0_), channel_id=1, source_target_pairs={{0,12},{1,13},{2,14},{3,15},{4,0},{5,1},{6,2},{7,3},{8,4},{9,5},{1... | collective-permute-start | bytes 245768 | tf_op jit(solution)/shard_map/ppermute | solution.py:53
  149.0 6.0 %collective-permute-start.41 = (bf16[80,512]{1,0:T(8,128)(2,1)S(1)}, bf16[80,512]{1,0:T(8,128)(2,1)S(1)}, u32[]{:S(2)}, u32[]{:S(2)}) collective-permute-start(bf16[80,512]{1,0:T(8,128)(2,1)S(1)} %get-tuple-element.86.refs_0_), channel_id=1, source_target_pairs={{0,8},{1,9},{2,10},{3,11},{4,12},{5,13},{6,14},{7,15},{8,0},{9,1},... | collective-permute-start | bytes 245768 | tf_op jit(solution)/shard_map/ppermute | solution.py:53
  149.6 6.3 %collective-permute-start.40 = (bf16[80,512]{1,0:T(8,128)(2,1)S(1)}, bf16[80,512]{1,0:T(8,128)(2,1)S(1)}, u32[]{:S(2)}, u32[]{:S(2)}) collective-permute-start(bf16[80,512]{1,0:T(8,128)(2,1)S(1)} %get-tuple-element.86.refs_0_), channel_id=1, source_target_pairs={{0,4},{1,5},{2,6},{3,7},{4,8},{5,9},{6,10},{7,11},{8,12},{9,13},{1... | collective-permute-start | bytes 245768 | tf_op jit(solution)/shard_map/ppermute | solution.py:53
  156.4 18.9 %collective-permute-start.46 = (bf16[320,512]{1,0:T(8,128)(2,1)S(1)}, bf16[320,512]{1,0:T(8,128)(2,1)S(1)}, u32[]{:S(2)}, u32[]{:S(2)}) collective-permute-start(bf16[320,512]{1,0:T(8,128)(2,1)S(1)} %shard_map.88.refs_0_), channel_id=1, source_target_pairs={{0,1},{1,0},{2,3},{3,2},{4,5},{5,4},{6,7},{7,6},{8,9},{9,8},{10,11... | collective-permute-start | bytes 983048 | tf_op jit(solution)/shard_map/ppermute | solution.py:53
  156.5 22.0 %collective-permute-start.45 = (bf16[320,512]{1,0:T(8,128)(2,1)S(1)}, bf16[320,512]{1,0:T(8,128)(2,1)S(1)}, u32[]{:S(2)}, u32[]{:S(2)}) collective-permute-start(bf16[320,512]{1,0:T(8,128)(2,1)S(1)} %shard_map.88.refs_0_), channel_id=1, source_target_pairs={{0,48},{1,49},{2,50},{3,51},{4,52},{5,53},{6,54},{7,55},{8,56},{9,... | collective-permute-start | bytes 983048 | tf_op jit(solution)/shard_map/ppermute | solution.py:53
  157.7 15.3 %collective-permute-start.26 = (bf16[128,512]{1,0:T(8,128)(2,1)S(1)}, bf16[128,512]{1,0:T(8,128)(2,1)S(1)}, u32[]{:S(2)}, u32[]{:S(2)}) collective-permute-start(bf16[128,512]{1,0:T(8,128)(2,1)S(1)} %get-tuple-element.77.refs_0_), channel_id=1, source_target_pairs={{0,48},{1,67},{2,50},{3,65},{4,52},{5,71},{6,54},{7,69},{8,56},{9,... | collective-permute-start | bytes 393224 | tf_op jit(solution)/shard_map/ppermute | solution.py:53
  158.1 14.9 %collective-permute-start.25 = (bf16[128,512]{1,0:T(8,128)(2,1)S(1)}, bf16[128,512]{1,0:T(8,128)(2,1)S(1)}, u32[]{:S(2)}, u32[]{:S(2)}) collective-permute-start(bf16[128,512]{1,0:T(8,128)(2,1)S(1)} %get-tuple-element.77.refs_0_), channel_id=1, source_target_pairs={{0,32},{1,3},{2,34},{3,1},{4,36},{5,7},{6,38},{7,5},{8,40},{9,11},... | collective-permute-start | bytes 393224 | tf_op jit(solution)/shard_map/ppermute | solution.py:53
  160.1 12.9 %collective-permute-start.24 = (bf16[128,512]{1,0:T(8,128)(2,1)S(1)}, bf16[128,512]{1,0:T(8,128)(2,1)S(1)}, u32[]{:S(2)}, u32[]{:S(2)}) collective-permute-start(bf16[128,512]{1,0:T(8,128)(2,1)S(1)} %get-tuple-element.77.refs_0_), channel_id=1, source_target_pairs={{0,16},{1,65},{2,18},{3,67},{4,20},{5,69},{6,22},{7,71},{8,24},{9,... | collective-permute-start | bytes 393224 | tf_op jit(solution)/shard_map/ppermute | solution.py:53
  173.0 8.6 %collective-permute-start.44 = (bf16[320,512]{1,0:T(8,128)(2,1)S(1)}, bf16[320,512]{1,0:T(8,128)(2,1)S(1)}, u32[]{:S(2)}, u32[]{:S(2)}) collective-permute-start(bf16[320,512]{1,0:T(8,128)(2,1)S(1)} %shard_map.88.refs_0_), channel_id=1, source_target_pairs={{0,32},{1,33},{2,34},{3,35},{4,36},{5,37},{6,38},{7,39},{8,40},{9,... | collective-permute-start | bytes 983048 | tf_op jit(solution)/shard_map/ppermute | solution.py:53
  173.0 10.2 %collective-permute-start.43 = (bf16[320,512]{1,0:T(8,128)(2,1)S(1)}, bf16[320,512]{1,0:T(8,128)(2,1)S(1)}, u32[]{:S(2)}, u32[]{:S(2)}) collective-permute-start(bf16[320,512]{1,0:T(8,128)(2,1)S(1)} %shard_map.88.refs_0_), channel_id=1, source_target_pairs={{0,16},{1,17},{2,18},{3,19},{4,20},{5,21},{6,22},{7,23},{8,24},{9,... | collective-permute-start | bytes 983048 | tf_op jit(solution)/shard_map/ppermute | solution.py:53
  173.6 10.5 %collective-permute-start.29 = (bf16[512,512]{1,0:T(8,128)(2,1)S(1)}, bf16[512,512]{1,0:T(8,128)(2,1)S(1)}, u32[]{:S(2)}, u32[]{:S(2)}) collective-permute-start(bf16[512,512]{1,0:T(8,128)(2,1)S(1)} %shard_map.85.refs_0_), channel_id=1, source_target_pairs={{0,66},{1,13},{2,64},{3,15},{4,70},{5,1},{6,68},{7,3},{8,74},{9,5}... | collective-permute-start | bytes 1572872 | tf_op jit(solution)/shard_map/ppermute | solution.py:53
  175.3 15.9 %collective-permute-start.28 = (bf16[512,512]{1,0:T(8,128)(2,1)S(1)}, bf16[512,512]{1,0:T(8,128)(2,1)S(1)}, u32[]{:S(2)}, u32[]{:S(2)}) collective-permute-start(bf16[512,512]{1,0:T(8,128)(2,1)S(1)} %shard_map.85.refs_0_), channel_id=1, source_target_pairs={{0,2},{1,9},{2,0},{3,11},{4,6},{5,13},{6,4},{7,15},{8,10},{9,1},{1... | collective-permute-start | bytes 1572872 | tf_op jit(solution)/shard_map/ppermute | solution.py:53
  178.6 12.7 %collective-permute-start.27 = (bf16[512,512]{1,0:T(8,128)(2,1)S(1)}, bf16[512,512]{1,0:T(8,128)(2,1)S(1)}, u32[]{:S(2)}, u32[]{:S(2)}) collective-permute-start(bf16[512,512]{1,0:T(8,128)(2,1)S(1)} %shard_map.85.refs_0_), channel_id=1, source_target_pairs={{0,64},{1,5},{2,66},{3,7},{4,68},{5,9},{6,70},{7,11},{8,72},{9,13}... | collective-permute-start | bytes 1572872 | tf_op jit(solution)/shard_map/ppermute | solution.py:53
  181.5 10.2 %collective-permute-start.49 = (bf16[320,512]{1,0:T(8,128)(2,1)S(1)}, bf16[320,512]{1,0:T(8,128)(2,1)S(1)}, u32[]{:S(2)}, u32[]{:S(2)}) collective-permute-start(bf16[320,512]{1,0:T(8,128)(2,1)S(1)} %collective-permute-done.45.refs_3_), channel_id=1, source_target_pairs={{0,1},{1,0},{2,3},{3,2},{4,5},{5,4},{6,7},{7,6},{8,9},{9,8},{10,11... | collective-permute-start | bytes 983048 | tf_op jit(solution)/shard_map/ppermute | solution.py:53
  183.2 8.6 %collective-permute-start.48 = (bf16[320,512]{1,0:T(8,128)(2,1)S(1)}, bf16[320,512]{1,0:T(8,128)(2,1)S(1)}, u32[]{:S(2)}, u32[]{:S(2)}) collective-permute-start(bf16[320,512]{1,0:T(8,128)(2,1)S(1)} %collective-permute-done.44.refs_2_), channel_id=1, source_target_pairs={{0,1},{1,0},{2,3},{3,2},{4,5},{5,4},{6,7},{7,6},{8,9},{9,8},{10,11... | collective-permute-start | bytes 983048 | tf_op jit(solution)/shard_map/ppermute | solution.py:53
  184.0 21.0 %collective-permute-start.30 = (bf16[512,512]{1,0:T(8,128)(2,1)S(1)}, bf16[512,512]{1,0:T(8,128)(2,1)S(1)}, u32[]{:S(2)}, u32[]{:S(2)}) collective-permute-start(bf16[512,512]{1,0:T(8,128)(2,1)S(1)} %shard_map.85.refs_0_), channel_id=1, source_target_pairs={{0,1},{1,0},{2,3},{3,2},{4,5},{5,4},{6,7},{7,6},{8,9},{9,8},{10,11... | collective-permute-start | bytes 1572872 | tf_op jit(solution)/shard_map/ppermute | solution.py:53
  191.2 13.9 %collective-permute-start.33 = (bf16[512,512]{1,0:T(8,128)(2,1)S(1)}, bf16[512,512]{1,0:T(8,128)(2,1)S(1)}, u32[]{:S(2)}, u32[]{:S(2)}) collective-permute-start(bf16[512,512]{1,0:T(8,128)(2,1)S(1)} %collective-permute-done.29.refs_3_), channel_id=1, source_target_pairs={{0,1},{1,0},{2,3},{3,2},{4,5},{5,4},{6,7},{7,6},{8,9},{9,8},{10,11... | collective-permute-start | bytes 1572872 | tf_op jit(solution)/shard_map/ppermute | solution.py:53
  191.2 17.4 %collective-permute-start.32 = (bf16[512,512]{1,0:T(8,128)(2,1)S(1)}, bf16[512,512]{1,0:T(8,128)(2,1)S(1)}, u32[]{:S(2)}, u32[]{:S(2)}) collective-permute-start(bf16[512,512]{1,0:T(8,128)(2,1)S(1)} %collective-permute-done.28.refs_2_), channel_id=1, source_target_pairs={{0,1},{1,0},{2,3},{3,2},{4,5},{5,4},{6,7},{7,6},{8,9},{9,8},{10,11... | collective-permute-start | bytes 1572872 | tf_op jit(solution)/shard_map/ppermute | solution.py:53
  191.7 16.9 %collective-permute-start.31 = (bf16[512,512]{1,0:T(8,128)(2,1)S(1)}, bf16[512,512]{1,0:T(8,128)(2,1)S(1)}, u32[]{:S(2)}, u32[]{:S(2)}) collective-permute-start(bf16[512,512]{1,0:T(8,128)(2,1)S(1)} %collective-permute-done.27.refs_1_), channel_id=1, source_target_pairs={{0,1},{1,0},{2,3},{3,2},{4,5},{5,4},{6,7},{7,6},{8,9},{9,8},{10,11... | collective-permute-start | bytes 1572872 | tf_op jit(solution)/shard_map/ppermute | solution.py:53
  191.8 3.3 %collective-permute-start.47 = (bf16[320,512]{1,0:T(8,128)(2,1)S(1)}, bf16[320,512]{1,0:T(8,128)(2,1)S(1)}, u32[]{:S(2)}, u32[]{:S(2)}) collective-permute-start(bf16[320,512]{1,0:T(8,128)(2,1)S(1)} %collective-permute-done.43.refs_1_), channel_id=1, source_target_pairs={{0,1},{1,0},{2,3},{3,2},{4,5},{5,4},{6,7},{7,6},{8,9},{9,8},{10,11... | collective-permute-start | bytes 983048 | tf_op jit(solution)/shard_map/ppermute | solution.py:53
  202.8 30.5 %collective-permute-start.50 = (bf16[128,2560]{1,0:T(8,128)(2,1)S(1)}, bf16[128,2560]{1,0:T(8,128)(2,1)S(1)}, u32[]{:S(2)}, u32[]{:S(2)}) collective-permute-start(bf16[128,2560]{1,0:T(8,128)(2,1)S(1)} %get-tuple-element.88), channel_id=1, source_target_pairs={{0,64},{1,65},{2,66},{3,67},{4,68},{5,69},{6,70},{7,71},{8,72},{9,... | collective-permute-start | bytes 1966088 | tf_op jit(solution)/shard_map/ppermute | solution.py:53
  205.0 28.9 %collective-permute-start.51 = (bf16[128,2560]{1,0:T(8,128)(2,1)S(1)}, bf16[128,2560]{1,0:T(8,128)(2,1)S(1)}, u32[]{:S(2)}, u32[]{:S(2)}) collective-permute-start(bf16[128,2560]{1,0:T(8,128)(2,1)S(1)} %get-tuple-element.89), channel_id=1, source_target_pairs={{0,66},{1,67},{2,64},{3,65},{4,70},{5,71},{6,68},{7,69},{8,74},{9,... | collective-permute-start | bytes 1966088 | tf_op jit(solution)/shard_map/ppermute | solution.py:53
  205.1 32.1 %collective-permute-start.52 = (bf16[128,2560]{1,0:T(8,128)(2,1)S(1)}, bf16[128,2560]{1,0:T(8,128)(2,1)S(1)}, u32[]{:S(2)}, u32[]{:S(2)}) collective-permute-start(bf16[128,2560]{1,0:T(8,128)(2,1)S(1)} %get-tuple-element.90), channel_id=1, source_target_pairs={{0,2},{1,3},{2,0},{3,1},{4,6},{5,7},{6,4},{7,5},{8,10},{9,11},{10,... | collective-permute-start | bytes 1966088 | tf_op jit(solution)/shard_map/ppermute | solution.py:53
  212.5 26.7 %collective-permute-start.37 = (bf16[128,2048]{1,0:T(8,128)(2,1)S(1)}, bf16[128,2048]{1,0:T(8,128)(2,1)S(1)}, u32[]{:S(2)}, u32[]{:S(2)}) collective-permute-start(bf16[128,2048]{1,0:T(8,128)(2,1)S(1)} %get-tuple-element.83), channel_id=1, source_target_pairs={{0,4},{1,5},{2,6},{3,7},{4,8},{5,9},{6,10},{7,11},{8,12},{9,13},{1... | collective-permute-start | bytes 1572872 | tf_op jit(solution)/shard_map/ppermute | solution.py:53
  215.8 61.5 %collective-permute-start.34 = (bf16[128,2048]{1,0:T(8,128)(2,1)S(1)}, bf16[128,2048]{1,0:T(8,128)(2,1)S(1)}, u32[]{:S(2)}, u32[]{:S(2)}) collective-permute-start(bf16[128,2048]{1,0:T(8,128)(2,1)S(1)} %get-tuple-element.79), channel_id=1, source_target_pairs={{0,16},{1,17},{2,18},{3,19},{4,20},{5,21},{6,22},{7,23},{8,24},{9,... | collective-permute-start | bytes 1572872 | tf_op jit(solution)/shard_map/ppermute | solution.py:53
  233.3 41.3 %collective-permute-start.38 = (bf16[128,2048]{1,0:T(8,128)(2,1)S(1)}, bf16[128,2048]{1,0:T(8,128)(2,1)S(1)}, u32[]{:S(2)}, u32[]{:S(2)}) collective-permute-start(bf16[128,2048]{1,0:T(8,128)(2,1)S(1)} %get-tuple-element.84), channel_id=1, source_target_pairs={{0,12},{1,13},{2,14},{3,15},{4,0},{5,1},{6,2},{7,3},{8,4},{9,5},{1... | collective-permute-start | bytes 1572872 | tf_op jit(solution)/shard_map/ppermute | solution.py:53
  233.9 40.8 %collective-permute-start.39 = (bf16[128,2048]{1,0:T(8,128)(2,1)S(1)}, bf16[128,2048]{1,0:T(8,128)(2,1)S(1)}, u32[]{:S(2)}, u32[]{:S(2)}) collective-permute-start(bf16[128,2048]{1,0:T(8,128)(2,1)S(1)} %get-tuple-element.85), channel_id=1, source_target_pairs={{0,8},{1,9},{2,10},{3,11},{4,12},{5,13},{6,14},{7,15},{8,0},{9,1},... | collective-permute-start | bytes 1572872 | tf_op jit(solution)/shard_map/ppermute | solution.py:53
  237.2 40.1 %collective-permute-start.35 = (bf16[128,2048]{1,0:T(8,128)(2,1)S(1)}, bf16[128,2048]{1,0:T(8,128)(2,1)S(1)}, u32[]{:S(2)}, u32[]{:S(2)}) collective-permute-start(bf16[128,2048]{1,0:T(8,128)(2,1)S(1)} %get-tuple-element.80), channel_id=1, source_target_pairs={{0,48},{1,49},{2,50},{3,51},{4,52},{5,53},{6,54},{7,55},{8,56},{9,... | collective-permute-start | bytes 1572872 | tf_op jit(solution)/shard_map/ppermute | solution.py:53
  239.2 38.1 %collective-permute-start.36 = (bf16[128,2048]{1,0:T(8,128)(2,1)S(1)}, bf16[128,2048]{1,0:T(8,128)(2,1)S(1)}, u32[]{:S(2)}, u32[]{:S(2)}) collective-permute-start(bf16[128,2048]{1,0:T(8,128)(2,1)S(1)} %get-tuple-element.81), channel_id=1, source_target_pairs={{0,32},{1,33},{2,34},{3,35},{4,36},{5,37},{6,38},{7,39},{8,40},{9,... | collective-permute-start | bytes 1572872 | tf_op jit(solution)/shard_map/ppermute | solution.py:53
  (35 other events, 203.4 us)

commit v3 on v2

--- a/solution.py
+++ b/solution.py
@@ -20,9 +20,22 @@
 HBM = pl.BlockSpec(memory_space=pltpu.HBM)
 DMA = pltpu.SemaphoreType.DMA
 LIMIT = pltpu.CompilerParams(vmem_limit_bytes=16 * 2**20)
+ALL_OF_IT = pltpu.CompilerParams(vmem_limit_bytes=60 * 1024 * 1024)
+
+
+def blocks_of(count, shape):
+    return [pltpu.HBM(shape, BF)] + [jax.ShapeDtypeStruct(shape, BF)] * (count - 1)
+
+
 STEPS = (0, 1, 3, 2)
 WIDTH = {"y": 2048, "z": 2048, "x": 2560}
 EXTRA = {"y": 0, "z": 512, "x": 512}
+
+
+def with_basis(ring, step):
+    return ring == "z" or (ring == "x" and step % 2 == 1)
+
+
 GROUPS = ((2048, 128), (1280, 80))
 TILE = (512, 640)
 SLOT = {"x": 0, "y": 1, "z": 2, "core": 3, "xh": 4, "u0": 5, "v0": 6, "u1": 2, "v1": 1}
@@ -140,7 +153,8 @@
     for k, step in enumerate(STEPS):
         at = (t + step) % 4
         wait_for(whole.at[at], in_sem.at[at])
-        copy = pltpu.make_async_copy(held.at[at], outs[k], out_sem.at[k])
+        source = held.at[at] if with_basis(ring, step) else held.at[at, :, pl.ds(0, WIDTH[ring])]
+        copy = pltpu.make_async_copy(source, outs[k], out_sem.at[k])
         copy.start()
         stores.append(copy)
     wait_all(stores)
@@ -150,12 +164,15 @@
     width = WIDTH[ring] + EXTRA[ring]
     return pl.pallas_call(
         functools.partial(pack_kernel, ring),
-        out_shape=[jax.ShapeDtypeStruct((128, width), BF)] * 4,
-        in_specs=[SMEM, HBM, ANY],
+        out_shape=[
+            (jax.ShapeDtypeStruct if step else pltpu.HBM)((128, WIDTH[ring] + 512 * with_basis(ring, step)), BF)
+            for step in STEPS
+        ],
+        in_specs=[SMEM, ANY, ANY],
         out_specs=[ANY] * 4,
         scratch_shapes=[pltpu.VMEM((4, 128, width), BF), DMA((4,)), DMA((4,))]
         + ([pltpu.VMEM((16, 128, 128), BF), DMA((16,))] if ring == "x" else []),
-        compiler_params=LIMIT,
+        compiler_params=ALL_OF_IT if ring == "x" else LIMIT,
         cost_estimate=estimate(0, 4 * 128 * width * 4),
     )(where, grad, basis)
 
@@ -167,6 +184,14 @@
     else:
         out, held, in_sem, out_sem = refs[-4:]
     t = place(where, ring)
+    if ring != "x":
+        stores = []
+        for k, step in enumerate(STEPS):
+            for j, (to, source, count) in enumerate(runs(ring, (t + 4 - step) % 4)):
+                columns = pl.ds(pl.multiple_of(source, 128), count)
+                stores.append(pltpu.make_async_copy(blocks[k].at[:, pl.ds(to, count)], out.at[:, columns], out_sem.at[k, j]))
+        wait_all(start_all(stores))
+        return
     start_all(
         [
             pltpu.make_async_copy(blocks[k], held.at[(t + 4 - step) % 4], in_sem.at[(t + 4 - step) % 4])
@@ -202,9 +227,9 @@
     return pl.pallas_call(
         functools.partial(unpack_kernel, ring),
         out_shape=jax.ShapeDtypeStruct((128, columns), BF),
-        in_specs=[SMEM] + [ANY] * (4 + len(more)),
+        in_specs=[SMEM] + [ANY if ring == "x" else VMEM] * 4 + [ANY] * len(more),
         out_specs=ANY,
-        scratch_shapes=[pltpu.VMEM((4, 128, width), BF), DMA((4,)), DMA((4, 16))]
+        scratch_shapes=[pltpu.VMEM((4, 128, width if ring == "x" else 128), BF), DMA((4,)), DMA((4, 16))]
         + ([pltpu.VMEM((16, 128, 128), BF), DMA((16,))] if ring == "x" else []),
         input_output_aliases={5: 0} if more else {},
         compiler_params=LIMIT,
@@ -216,12 +241,14 @@
     y, xh, core = place(where, "y"), place(where, "xh"), place(where, "core")
     if ring == "y":
         y = (y + step) % 4
+    elif step % 4 == 2:
+        xh = 1 - xh
     return base.at[pl.ds(pl.multiple_of((y * 4 + xh * 2 + core) * 128, 128), 128), :]
 
 
 def start_blocks(ring, where, blocks, first, chunk, tile, basis, held, base, in_sem, base_sem):
     for k, step in enumerate(STEPS):
-        if EXTRA[ring]:
+        if with_basis(ring, step):
             source = blocks[k].at[:, pl.ds(WIDTH[ring], 512)]
         else:
             source = basis_rows(ring, where, 4 - step, basis)
@@ -289,7 +316,7 @@
 def project(group, where, blocks, basis, other=None):
     chunk = GROUPS[group][0]
     own = other is not None
-    shapes = [jax.ShapeDtypeStruct((chunk // 4, 512), BF)] * 4 if own else jax.ShapeDtypeStruct((chunk, 512), BF)
+    shapes = blocks_of(4, (chunk // 4, 512)) if own else jax.ShapeDtypeStruct((chunk, 512), BF)
     return pl.pallas_call(
         functools.partial(project_kernel, group, own),
         out_shape=shapes,
@@ -309,30 +336,32 @@
 
 
 def add_kernel(group, where, a, b, c, d, *refs):
-    outs, total = refs[:4], refs[4]
+    outs, total, sem = refs[:4], refs[4], refs[5]
     piece = GROUPS[group][1]
     total[...] = (
         (a[...].astype(F32) + b[...].astype(F32)) + (c[...].astype(F32) + d[...].astype(F32))
     ).astype(BF)
+    copies = []
     for j in range(4):
         at = (place(where, "v%d" % group) + j) % 4
-        outs[j][...] = total[rows_at(at * piece, piece), :]
+        copies.append(pltpu.make_async_copy(total.at[rows_at(at * piece, piece), :], outs[j], sem.at[j]))
+    wait_all(start_all(copies))
 
 
 def add_up(group, where, arrays):
     chunk, piece = GROUPS[group]
     return pl.pallas_call(
         functools.partial(add_kernel, group),
-        out_shape=[jax.ShapeDtypeStruct((piece, 512), BF)] * 4,
+        out_shape=[pltpu.HBM((piece, 512), BF)] * 4,
         in_specs=[SMEM] + [VMEM] * 4,
-        out_specs=[VMEM] * 4,
-        scratch_shapes=[pltpu.VMEM((chunk // 4, 512), BF)],
+        out_specs=[ANY] * 4,
+        scratch_shapes=[pltpu.VMEM((chunk // 4, 512), BF), DMA((4,))],
         compiler_params=LIMIT,
         cost_estimate=estimate(3 * chunk * 128, 5 * chunk * 256),
     )(where, *arrays)
 
 
-def moments_kernel(where, first, second, new, old, out, half, old_held, sem):
+def moments_kernel(where, first, second, new, old, result, half, old_held, out, sem):
     core = place(where, "core")
     columns = pl.ds(pl.multiple_of(core * 256, 256), 256)
     copies = start_all([pltpu.make_async_copy(new.at[:, columns], half, sem.at[0]), pltpu.make_async_copy(old, old_held, sem.at[1])])
@@ -355,15 +384,21 @@
     for q in range(8):
         for i in range(2):
             out[q, 192 + 32 * i : 224 + 32 * i, :] = margin[q * 32 : q * 32 + 32, i * 256 : i * 256 + 256]
+    wait_all(start_all([pltpu.make_async_copy(out, result, sem.at[2])]))
 
 
 def cut_moments(where, first, second, new, old):
     return pl.pallas_call(
         moments_kernel,
-        out_shape=jax.ShapeDtypeStruct((8, 256, 256), BF),
+        out_shape=pltpu.HBM((8, 256, 256), BF),
         in_specs=[SMEM, VMEM, VMEM, ANY, ANY],
-        out_specs=VMEM,
-        scratch_shapes=[pltpu.VMEM((2048, 256), BF), pltpu.VMEM((2048, 512), BF), DMA((2,))],
+        out_specs=ANY,
+        scratch_shapes=[
+            pltpu.VMEM((2048, 256), BF),
+            pltpu.VMEM((2048, 512), BF),
+            pltpu.VMEM((8, 256, 256), BF),
+            DMA((3,)),
+        ],
         compiler_params=LIMIT,
         cost_estimate=estimate(2 * 2048 * 256 * 512, 6 * 2**20),
         name="cut_moments",
@@ -438,20 +473,21 @@
     )(where, *sums, *rest)
 
 
-def turn_kernel(first, second, out, wide):
+def turn_kernel(first, second, result, wide, out, sem):
     wide[208:, :] = jnp.zeros((48, 512), F32)
     for i, ref in enumerate((first, second)):
         wide[:208, :] = ref[...]
         out[:, i * 64 : i * 64 + 64, :] = wide[...].T.astype(BF).reshape(8, 64, 256)
+    wait_all(start_all([pltpu.make_async_copy(out, result, sem)]))
 
 
 def turn_back(first, second):
     return pl.pallas_call(
         turn_kernel,
-        out_shape=jax.ShapeDtypeStruct((8, 128, 256), BF),
+        out_shape=pltpu.HBM((8, 128, 256), BF),
         in_specs=[VMEM] * 2,
-        out_specs=VMEM,
-        scratch_shapes=[pltpu.VMEM((256, 512), F32)],
+        out_specs=ANY,
+        scratch_shapes=[pltpu.VMEM((256, 512), F32), pltpu.VMEM((8, 128, 256), BF), DMA],
         compiler_params=LIMIT,
         cost_estimate=estimate(208 * 1024, 3 * 2**19),
         name="turn_back",
@@ -526,16 +562,16 @@
 
 
 def update_kernel(ring, where, *refs):
-    count = 4 if EXTRA[ring] else 1
+    count = 5
     own, other, bases, outs = refs[:4], refs[4:8], refs[8 : 8 + count], refs[8 + count : 12 + count]
     low, base, held, in_sem, other_sem, base_sem, out_sem = refs[12 + count :]
     core = place(where, "core")
     width = WIDTH[ring]
     for k, step in enumerate(STEPS):
-        if EXTRA[ring]:
+        if with_basis(ring, step):
             source = bases[STEPS.index((4 - step) % 4)].at[:, pl.ds(width, 512)]
         else:
-            source = basis_rows(ring, where, step, bases[0])
+            source = basis_rows(ring, where, step, bases[4])
         pltpu.make_async_copy(source, base.at[pl.ds(k * 128, 128), :], base_sem).start()
     if ring == "x":
         start_all(low_copies(1, where, own, core * 1280, low, in_sem, core))
@@ -573,7 +609,7 @@
     width = WIDTH[ring]
     return pl.pallas_call(
         functools.partial(update_kernel, ring),
-        out_shape=[jax.ShapeDtypeStruct((128, width), BF)] * 4,
+        out_shape=blocks_of(4, (128, width)),
         in_specs=[SMEM] + [ANY] * (8 + len(bases)),
         out_specs=[ANY] * 4,
         scratch_shapes=[
@@ -637,7 +673,7 @@
         whole = ordered([quarter] * 4, U[group])
         whole = whole + [shift(array, RINGS["core"], 1) for array in whole]
         for ring in rings:
-            blocks = update_blocks(ring, where, whole, arrived[ring] if EXTRA[ring] else [basis_new])
+            blocks = update_blocks(ring, where, whole, arrived[ring] + [basis_new])
             sent[ring] = exchange(blocks, RINGS[ring])
     update = None
     for ring in ("x", "y", "z"):

time: 281 us -> 282 us (level)
  the two profiles are of different devices: /device:TPU:38 before, /device:TPU:1 now
where the time goes in v3:
time: 282 us; the launch traced here: 278 us
  starting transfers between devices  120 us (43%)
  Pallas kernels  67.5 us (24%)
  waiting for transfers between devices  49 us (17%)
  blocking collectives  24.6 us (9%)
  local copies, waits for them, and re-layouts  14.6 us (5%)
    ppermute x53, starting transfers between devices, shift(): return lax.ppermute(array, NAMES, pairs)  110 us
    ppermute x53, waiting for transfers between devices, shift(): return lax.ppermute(array, NAMES, pairs)  44.4 us
    all_to_all x1, blocking collectives, compute(): new = lax.all_to_all(new, ROW, 0, 0, tiled=True)  24.6 us
    pallas_call x4, Pallas kernels, project(): pl.pallas_call(functools.partial(project_kernel, group, own), out_shape=s...  19.4 us
    pallas_call x3, Pallas kernels, update_blocks(): pl.pallas_call(functools.partial(update_kernel, ring), out_shape=blocks_o...  17.6 us
    unnamed x86, local copies, waits for them, and re-layouts  14.6 us
    pallas_call x3, Pallas kernels, pack(): pl.pallas_call(functools.partial(pack_kernel, ring), out_shape=[(jax.Shap...  9.21 us
    pallas_call x3, Pallas kernels, unpack(): pl.pallas_call(functools.partial(unpack_kernel, ring), out_shape=jax.Shap...  8.48 us
  transfers between devices with their start and end apart: 55, of which 14 were waited for; matrix products, arithmetic and copies ran while one was open for 0% of the time, Pallas kernels for 22%

profile of v3, /device:TPU:1, one launch (start us, length us, event | category | flops | bytes accessed | tf_op | source)
XLA Modules:
  0.0 277.5 jit_solution(1999254294613606202)
XLA Ops:
  0.7 1.6 copy-done
  2.3 2.9 %copy-done.2 = bf16[128,26624]{1,0:T(8,128)(2,1)S(1)} copy-done((bf16[128,26624]{1,0:T(8,128)(2,1)S(1)}, bf16[128,26624]{1,0:T(8,128)(2,1)}, u32[]{:S(2)}) %copy-start.2) | copy-done | bytes 6815768
  5.2 1.9 shard_map.76
  7.1 2.2 collective-permute-start
  9.3 2.8 %shard_map.77 = (bf16[128,2560]{1,0:T(8,128)(2,1)}, bf16[128,2560]{1,0:T(8,128)(2,1)}, bf16[128,2560]{1,0:T(8,128)(2,1)}, bf16[128,2560]{1,0:T(8,128)(2,1)}) custom-call(s32[8]{0:T(128)S(1)} %compare_select_fusion.6.where, bf16[128,26624]{1,0:T(8,128)(2,1)S(1)} %copy-done.2, bf16[2048,512]{1,0:T(8,128)(2,1)S(1)} %copy-done), custom_call_target="tpu_custom_call" | custom-call | bytes 5242880 | tf_op jit(solution)/shard_map/pallas_call | solution.py:165
  12.1 1.7 collective-permute-start.3
  13.8 2.2 collective-permute-start.4
  17.2 1.5 collective-permute-start.1
  18.7 3.6 %collective-permute-done.refs_1_.refs_9_ = bf16[128,2048]{1,0:T(8,128)(2,1)S(1)} collective-permute-done((bf16[128,2048]{1,0:T(8,128)(2,1)S(1)}, bf16[128,2048]{1,0:T(8,128)(2,1)S(1)}, u32[]{:S(2)}, u32[]{:S(2)}) %collective-permute-start) | collective-permute-done | bytes 524320 | tf_op jit(solution)/shard_map/ppermute | solution.py:66
  23.1 1.6 collective-permute-start.2
  24.7 4.5 %shard_map.81 = (bf16[128,2560]{1,0:T(8,128)(2,1)}, bf16[128,3072]{1,0:T(8,128)(2,1)}, bf16[128,3072]{1,0:T(8,128)(2,1)}, bf16[128,2560]{1,0:T(8,128)(2,1)}) custom-call(s32[8]{0:T(128)} %copy-done.36, bf16[128,26624]{1,0:T(8,128)(2,1)} %grad.5, bf16[2048,512]{1,0:T(8,128)(2,1)} %refs_12_.5), custom_call_target="tpu_custom_call" | custom-call | bytes 6291456 | tf_op jit(solution)/shard_map/pallas_call | solution.py:165
  29.3 1.3 collective-permute-start.13
  30.5 6.6 %collective-permute-done.2.refs_3_.refs_11_ = bf16[128,2048]{1,0:T(8,128)(2,1)} collective-permute-done((bf16[128,2048]{1,0:T(8,128)(2,1)}, bf16[128,2048]{1,0:T(8,128)(2,1)}, u32[]{:S(2)}, u32[]{:S(2)}) %collective-permute-start.2) | collective-permute-done | bytes 524320 | tf_op jit(solution)/shard_map/ppermute | solution.py:66
  37.1 2.2 collective-permute-start.14
  39.9 5.5 %collective-permute-done.5.refs_7_.refs_11_ = bf16[128,2560]{1,0:T(8,128)(2,1)} collective-permute-done((bf16[128,2560]{1,0:T(8,128)(2,1)}, bf16[128,2560]{1,0:T(8,128)(2,1)}, u32[]{:S(2)}, u32[]{:S(2)}) %collective-permute-start.5) | collective-permute-done | bytes 655392 | tf_op jit(solution)/shard_map/ppermute | solution.py:66
  46.4 5.1 %shard_map.78 = bf16[2048,512]{1,0:T(8,128)(2,1)} custom-call(s32[8]{0:T(128)S(1)} %copy-done.37, bf16[128,2048]{1,0:T(8,128)(2,1)S(1)} %copy-done.21, bf16[128,2048]{1,0:T(8,128)(2,1)S(1)} %copy-done.25, bf16[128,2048]{1,0:T(8,128)(2,1)} %collective-permute-done.1.refs_2_.refs_10_, bf16[128,2048]{1,0:T(8,128)(2,1)} %collective-permute-done.2.refs_3_.refs_11_, ...), custom_call_target="tpu_custom_call" | custom-call | flops 1073741824 | bytes 4718592 | tf_op jit(solution)/shard_map/pallas_call | solution.py:320
  51.6 1.3 collective-permute-start.6
  52.9 7.1 %collective-permute-done.15.refs_3_.refs_11_ = bf16[128,2560]{1,0:T(8,128)(2,1)S(1)} collective-permute-done((bf16[128,2560]{1,0:T(8,128)(2,1)}, bf16[128,2560]{1,0:T(8,128)(2,1)S(1)}, u32[]{:S(2)}, u32[]{:S(2)}) %collective-permute-start.15) | collective-permute-done | bytes 655392 | tf_op jit(solution)/shard_map/ppermute | solution.py:66
  60.0 3.1 %shard_map.82 = bf16[1280,512]{1,0:T(8,128)(2,1)} custom-call(s32[8]{0:T(128)S(1)} %copy-done.37, bf16[128,2560]{1,0:T(8,128)(2,1)S(1)} %copy-done.15, bf16[128,3072]{1,0:T(8,128)(2,1)S(1)} %collective-permute-done.13.refs_1_.refs_9_, bf16[128,3072]{1,0:T(8,128)(2,1)S(1)} %collective-permute-done.14.refs_2_.refs_10_, ...), custom_call_target="tpu_custom_call" | custom-call | flops 671088640 | bytes 3145728 | tf_op jit(solution)/shard_map/pallas_call | solution.py:320
  63.1 11.6 %collective-permute-start.16 = (bf16[1280,512]{1,0:T(8,128)(2,1)}, bf16[1280,512]{1,0:T(8,128)(2,1)}, u32[]{:S(2)}, u32[]{:S(2)}) collective-permute-start(bf16[1280,512]{1,0:T(8,128)(2,1)} %shard_map.82), channel_id=1, source_target_pairs={{0,1},{1,0},{2,3},{3,2},{4,5},{5,4},{6,7},{7,6},{8,9},{9,8},{10,11... | collective-permute-start | bytes 3932168 | tf_op jit(solution)/shard_map/ppermute | solution.py:66
  74.8 2.7 cut_moments.1
  77.5 6.7 %all-to-all-start = ((bf16[8,256,256]{2,1,0:T(8,128)(2,1)}), bf16[8,256,256]{2,1,0:T(8,128)(2,1)S(1)}, u32[]{:S(2)}, u32[]{:S(2)}) async-start(bf16[8,256,256]{2,1,0:T(8,128)(2,1)} %cut_moments.1), calls=%async_computation | async-start | bytes 2097152 | tf_op jit(solution)/shard_map/all_to_all | solution.py:652
  88.7 4.8 %shard_map.83 = (bf16[320,512]{1,0:T(8,128)(2,1)}, bf16[320,512]{1,0:T(8,128)(2,1)}, bf16[320,512]{1,0:T(8,128)(2,1)}, bf16[320,512]{1,0:T(8,128)(2,1)S(1)}) custom-call(s32[8]{0:T(128)S(1)} %copy-done.37, bf16[128,2560]{1,0:T(8,128)(2,1)S(1)} %copy-done.16, bf16[128,3072]{1,0:T(8,128)(2,1)S(1)} %copy-done.4, bf16[128,3072]{1,0:T(8,128)(2,1)S(1)} %copy-done.7, ...), custom_call_target="tpu_custom_call" | custom-call | flops 671088640 | bytes 3145728 | tf_op jit(solution)/shard_map/pallas_call | solution.py:320
  94.2 1.5 collective-permute-start.17
  95.7 2.4 collective-permute-start.18
  98.1 6.4 %shard_map.79 = (bf16[512,512]{1,0:T(8,128)(2,1)}, bf16[512,512]{1,0:T(8,128)(2,1)}, bf16[512,512]{1,0:T(8,128)(2,1)}, bf16[512,512]{1,0:T(8,128)(2,1)}) custom-call(s32[8]{0:T(128)S(1)} %copy-done.37, bf16[128,2048]{1,0:T(8,128)(2,1)S(1)} %copy-done.22, bf16[128,2048]{1,0:T(8,128)(2,1)S(1)} %copy-done.26, ...), custom_call_target="tpu_custom_call" | custom-call | flops 1073741824 | bytes 4718592 | tf_op jit(solution)/shard_map/pallas_call | solution.py:320
  104.5 3.7 %collective-permute-start.7 = (bf16[512,512]{1,0:T(8,128)(2,1)}, bf16[512,512]{1,0:T(8,128)(2,1)}, u32[]{:S(2)}, u32[]{:S(2)}) collective-permute-start(bf16[512,512]{1,0:T(8,128)(2,1)} %get-tuple-element.58), channel_id=1, source_target_pairs={{0,64},{1,5},{2,66},{3,7},{4,68},{5,9},{6,70},{7,11},{8,72},{9,13}... | collective-permute-start | bytes 1572872 | tf_op jit(solution)/shard_map/ppermute | solution.py:66
  108.2 1.6 collective-permute-start.8
  111.5 3.4 %all-to-all-start.1 = ((bf16[8,32,512]{2,1,0:T(8,128)(2,1)}), bf16[8,32,512]{2,1,0:T(8,128)(2,1)S(1)}, u32[]{:S(2)}, u32[]{:S(2)}) async-start(bf16[8,32,512]{2,1,0:T(8,128)(2,1)} %sum_margin.1), calls=%async_computation.1 | async-start | bytes 524288 | tf_op jit(solution)/shard_map/all_to_all | solution.py:654
  115.0 2.6 collective-permute-start.19
  117.6 4.6 %all-to-all-done.1 = bf16[8,32,512]{2,1,0:T(8,128)(2,1)S(1)} async-done(((bf16[8,32,512]{2,1,0:T(8,128)(2,1)}), bf16[8,32,512]{2,1,0:T(8,128)(2,1)S(1)}, u32[]{:S(2)}, u32[]{:S(2)}) %all-to-all-start.1) | async-done | bytes 262176 | tf_op jit(solution)/shard_map/all_to_all | solution.py:654
  122.1 4.8 %collective-permute-start.23 = (bf16[256,512]{1,0:T(8,128)(2,1)S(1)}, bf16[256,512]{1,0:T(8,128)(2,1)S(1)}, u32[]{:S(2)}, u32[]{:S(2)}) collective-permute-start(bf16[256,512]{1,0:T(8,128)(2,1)S(1)} %bitcast.1), channel_id=1, source_target_pairs={{0,1},{1,0},{2,3},{3,2},{4,5},{5,4},{6,7},{7,6},{8,9},{9,8},{10,11... | collective-permute-start | bytes 786440 | tf_op jit(solution)/shard_map/ppermute | solution.py:66
  127.9 2.1 shard_map.84
  130.0 3.9 %collective-permute-start.20 = (bf16[80,512]{1,0:T(8,128)(2,1)}, bf16[80,512]{1,0:T(8,128)(2,1)S(1)}, u32[]{:S(2)}, u32[]{:S(2)}) collective-permute-start(bf16[80,512]{1,0:T(8,128)(2,1)} %get-tuple-element.74), channel_id=1, source_target_pairs={{0,4},{1,5},{2,6},{3,7},{4,8},{5,9},{6,10},{7,11},{8,12},{9,13},{1... | collective-permute-start | bytes 245768 | tf_op jit(solution)/shard_map/ppermute | solution.py:66
  135.0 2.5 shard_map.80
  137.7 2.8 collective-permute-start.11
  140.4 2.0 collective-permute-start.12
  142.4 1.6 collective-permute-start.21
  144.8 3.2 %collective-permute-done.21.refs_6_ = bf16[80,512]{1,0:T(8,128)(2,1)S(1)} collective-permute-done((bf16[80,512]{1,0:T(8,128)(2,1)S(1)}, bf16[80,512]{1,0:T(8,128)(2,1)S(1)}, u32[]{:S(2)}, u32[]{:S(2)}) %collective-permute-start.21) | collective-permute-done | bytes 81952 | tf_op jit(solution)/shard_map/ppermute | solution.py:66
  149.0 1.4 step.1
  150.4 2.8 collective-permute-start.42
  154.7 3.4 %collective-permute-done.41.refs_2_ = bf16[80,512]{1,0:T(8,128)(2,1)S(1)} collective-permute-done((bf16[80,512]{1,0:T(8,128)(2,1)S(1)}, bf16[80,512]{1,0:T(8,128)(2,1)S(1)}, u32[]{:S(2)}, u32[]{:S(2)}) %collective-permute-start.41) | collective-permute-done | bytes 81952 | tf_op jit(solution)/shard_map/ppermute | solution.py:66
  158.1 2.2 collective-permute-done.40.refs_1_
  162.8 2.1 collective-permute-start.25
  164.9 2.0 collective-permute-done.26.refs_3_
  166.9 1.4 collective-permute-start.44
  172.4 2.8 %collective-permute-done.44.refs_2_ = bf16[320,512]{1,0:T(8,128)(2,1)S(1)} collective-permute-done((bf16[320,512]{1,0:T(8,128)(2,1)S(1)}, bf16[320,512]{1,0:T(8,128)(2,1)S(1)}, u32[]{:S(2)}, u32[]{:S(2)}) %collective-permute-start.44) | collective-permute-done | bytes 327712 | tf_op jit(solution)/shard_map/ppermute | solution.py:66
  175.2 9.9 %collective-permute-start.49 = (bf16[320,512]{1,0:T(8,128)(2,1)S(1)}, bf16[320,512]{1,0:T(8,128)(2,1)S(1)}, u32[]{:S(2)}, u32[]{:S(2)}) collective-permute-start(bf16[320,512]{1,0:T(8,128)(2,1)S(1)} %collective-permute-done.45.refs_3_), channel_id=1, source_target_pairs={{0,1},{1,0},{2,3},{3,2},{4,5},{5,4},{6,7},{7,6},{8,9},{9,8},{10,11... | collective-permute-start | bytes 983048 | tf_op jit(solution)/shard_map/ppermute | solution.py:66
  185.1 2.5 collective-permute-start.48
  187.5 2.5 collective-permute-start.30
  190.1 2.2 collective-permute-start.33
  192.2 5.5 %collective-permute-start.32 = (bf16[512,512]{1,0:T(8,128)(2,1)S(1)}, bf16[512,512]{1,0:T(8,128)(2,1)S(1)}, u32[]{:S(2)}, u32[]{:S(2)}) collective-permute-start(bf16[512,512]{1,0:T(8,128)(2,1)S(1)} %collective-permute-done.28.refs_2_), channel_id=1, source_target_pairs={{0,1},{1,0},{2,3},{3,2},{4,5},{5,4},{6,7},{7,6},{8,9},{9,8},{10,11... | collective-permute-start | bytes 1572872 | tf_op jit(solution)/shard_map/ppermute | solution.py:66
  198.3 2.2 collective-permute-done.47.refs_5_
  200.5 8.6 %shard_map.89 = (bf16[128,2560]{1,0:T(8,128)(2,1)}, bf16[128,2560]{1,0:T(8,128)(2,1)S(1)}, bf16[128,2560]{1,0:T(8,128)(2,1)S(1)}, bf16[128,2560]{1,0:T(8,128)(2,1)S(1)}) custom-call(s32[8]{0:T(128)S(1)} %copy-done.37, bf16[320,512]{1,0:T(8,128)(2,1)S(1)} %shard_map.88.refs_0_, bf16[320,512]{1,0:T(8,128)(2,1)S(1)} %collective-permute-done.43.refs_1_, ...), custom_call_target="tpu_custom_call" | custom-call | flops 1342177280 | bytes 5767168 | tf_op jit(solution)/shard_map/pallas_call | solution.py:610
  209.1 1.9 collective-permute-start.50
  212.9 4.6 %shard_map.87 = (bf16[128,2048]{1,0:T(8,128)(2,1)}, bf16[128,2048]{1,0:T(8,128)(2,1)S(1)}, bf16[128,2048]{1,0:T(8,128)(2,1)S(1)}, bf16[128,2048]{1,0:T(8,128)(2,1)S(1)}) custom-call(s32[8]{0:T(128)S(1)} %copy-done.37, bf16[512,512]{1,0:T(8,128)(2,1)S(1)} %shard_map.85.refs_0_, bf16[512,512]{1,0:T(8,128)(2,1)S(1)} %collective-permute-done.27.refs_1_, ...), custom_call_target="tpu_custom_call" | custom-call | flops 1073741824 | bytes 4718592 | tf_op jit(solution)/shard_map/pallas_call | solution.py:610
  217.6 4.5 %shard_map.86 = (bf16[128,2048]{1,0:T(8,128)(2,1)}, bf16[128,2048]{1,0:T(8,128)(2,1)S(1)}, bf16[128,2048]{1,0:T(8,128)(2,1)S(1)}, bf16[128,2048]{1,0:T(8,128)(2,1)S(1)}) custom-call(s32[8]{0:T(128)S(1)} %copy-done.37, bf16[512,512]{1,0:T(8,128)(2,1)S(1)} %shard_map.85.refs_0_, bf16[512,512]{1,0:T(8,128)(2,1)S(1)} %collective-permute-done.27.refs_1_, ...), custom_call_target="tpu_custom_call" | custom-call | flops 1073741824 | bytes 4718592 | tf_op jit(solution)/shard_map/pallas_call | solution.py:610
  222.1 4.6 %collective-permute-done.50.refs_1_ = bf16[128,2560]{1,0:T(8,128)(2,1)S(1)} collective-permute-done((bf16[128,2560]{1,0:T(8,128)(2,1)S(1)}, bf16[128,2560]{1,0:T(8,128)(2,1)S(1)}, u32[]{:S(2)}, u32[]{:S(2)}) %collective-permute-start.50) | collective-permute-done | bytes 655392 | tf_op jit(solution)/shard_map/ppermute | solution.py:66
  227.3 13.3 %collective-permute-start.39 = (bf16[128,2048]{1,0:T(8,128)(2,1)S(1)}, bf16[128,2048]{1,0:T(8,128)(2,1)S(1)}, u32[]{:S(2)}, u32[]{:S(2)}) collective-permute-start(bf16[128,2048]{1,0:T(8,128)(2,1)S(1)} %get-tuple-element.85), channel_id=1, source_target_pairs={{0,8},{1,9},{2,10},{3,11},{4,12},{5,13},{6,14},{7,15},{8,0},{9,1},... | collective-permute-start | bytes 1572872 | tf_op jit(solution)/shard_map/ppermute | solution.py:66
  240.6 1.5 collective-permute-start.36
  243.1 24.6 %all_to_all.15.new = bf16[8,128,256]{2,1,0:T(8,128)(2,1)S(1)} all-to-all(bf16[8,128,256]{2,1,0:T(8,128)(2,1)} %turn_back.1), channel_id=1, replica_groups=mesh['xl'=2,'z'=4,'y'=4,'xh'=2,'core'=2] {'xl','z'}, dimensions={0} | all-to-all | bytes 1048576 | tf_op jit(solution)/shard_map/all_to_all | solution.py:683
  268.8 3.6 %shard_map.90.refs_4_ = bf16[128,26624]{1,0:T(8,128)(2,1)} custom-call(s32[8]{0:T(128)S(1)} %copy-done.37, bf16[128,2560]{1,0:T(8,128)(2,1)S(1)} %copy-done.29, bf16[128,2560]{1,0:T(8,128)(2,1)S(1)} %collective-permute-done.50.refs_1_, bf16[128,2560]{1,0:T(8,128)(2,1)S(1)} %collective-permute-done.51.refs_2_, ...), custom_call_target="tpu_custom_call" | custom-call | bytes 5242880 | tf_op jit(solution)/shard_map/pallas_call | solution.py:227
  272.4 2.5 shard_map.91.refs_4_
  274.9 2.4 shard_map.92
  (156 shorter events, 27.8 us)
Async XLA Ops:
  7.1 15.1 %collective-permute-start = (bf16[128,2048]{1,0:T(8,128)(2,1)S(1)}, bf16[128,2048]{1,0:T(8,128)(2,1)S(1)}, u32[]{:S(2)}, u32[]{:S(2)}) collective-permute-start(bf16[128,2048]{1,0:T(8,128)(2,1)S(1)} %get-tuple-element.50), channel_id=1, source_target_pairs={{0,4},{1,5},{2,6},{3,7},{4,8},{5,9},{6,10},{7,11},{8,12},{9,13},{1... | collective-permute-start | bytes 1572872 | tf_op jit(solution)/shard_map/ppermute | solution.py:66
  12.1 27.3 %collective-permute-start.3 = (bf16[128,2560]{1,0:T(8,128)(2,1)}, bf16[128,2560]{1,0:T(8,128)(2,1)S(1)}, u32[]{:S(2)}, u32[]{:S(2)}) collective-permute-start(bf16[128,2560]{1,0:T(8,128)(2,1)} %get-tuple-element.54), channel_id=1, source_target_pairs={{0,16},{1,17},{2,18},{3,19},{4,20},{5,21},{6,22},{7,23},{8,24},{9,... | collective-permute-start | bytes 1966088 | tf_op jit(solution)/shard_map/ppermute | solution.py:66
  13.8 26.1 %collective-permute-start.4 = (bf16[128,2560]{1,0:T(8,128)(2,1)}, bf16[128,2560]{1,0:T(8,128)(2,1)}, u32[]{:S(2)}, u32[]{:S(2)}) collective-permute-start(bf16[128,2560]{1,0:T(8,128)(2,1)} %get-tuple-element.55), channel_id=1, source_target_pairs={{0,48},{1,49},{2,50},{3,51},{4,52},{5,53},{6,54},{7,55},{8,56},{9,... | collective-permute-start | bytes 1966088 | tf_op jit(solution)/shard_map/ppermute | solution.py:66
  16.0 29.3 %collective-permute-start.5 = (bf16[128,2560]{1,0:T(8,128)(2,1)}, bf16[128,2560]{1,0:T(8,128)(2,1)}, u32[]{:S(2)}, u32[]{:S(2)}) collective-permute-start(bf16[128,2560]{1,0:T(8,128)(2,1)} %get-tuple-element.56), channel_id=1, source_target_pairs={{0,32},{1,33},{2,34},{3,35},{4,36},{5,37},{6,38},{7,39},{8,40},{9,... | collective-permute-start | bytes 1966088 | tf_op jit(solution)/shard_map/ppermute | solution.py:66
  17.2 12.0 %collective-permute-start.1 = (bf16[128,2048]{1,0:T(8,128)(2,1)}, bf16[128,2048]{1,0:T(8,128)(2,1)}, u32[]{:S(2)}, u32[]{:S(2)}) collective-permute-start(bf16[128,2048]{1,0:T(8,128)(2,1)} %get-tuple-element.51), channel_id=1, source_target_pairs={{0,12},{1,13},{2,14},{3,15},{4,0},{5,1},{6,2},{7,3},{8,4},{9,5},{1... | collective-permute-start | bytes 1572872 | tf_op jit(solution)/shard_map/ppermute | solution.py:66
  23.1 22.3 %copy-start.21 = (bf16[128,2048]{1,0:T(8,128)(2,1)S(1)}, bf16[128,2048]{1,0:T(8,128)(2,1)}, u32[]{:S(2)}) copy-start(bf16[128,2048]{1,0:T(8,128)(2,1)} %get-tuple-element.49.refs_0_.refs_8_) | copy-start | bytes 1572868
  23.1 22.3 %copy-start.37 = (s32[8]{0:T(128)S(1)}, s32[8]{0:T(128)}, u32[]{:S(2)}) copy-start(s32[8]{0:T(128)} %copy-done.36) | copy-start | bytes 100
  23.1 14.0 %collective-permute-start.2 = (bf16[128,2048]{1,0:T(8,128)(2,1)}, bf16[128,2048]{1,0:T(8,128)(2,1)}, u32[]{:S(2)}, u32[]{:S(2)}) collective-permute-start(bf16[128,2048]{1,0:T(8,128)(2,1)} %get-tuple-element.52), channel_id=1, source_target_pairs={{0,8},{1,9},{2,10},{3,11},{4,12},{5,13},{6,14},{7,15},{8,0},{9,1},... | collective-permute-start | bytes 1572872 | tf_op jit(solution)/shard_map/ppermute | solution.py:66
  29.3 30.7 %collective-permute-start.13 = (bf16[128,3072]{1,0:T(8,128)(2,1)}, bf16[128,3072]{1,0:T(8,128)(2,1)S(1)}, u32[]{:S(2)}, u32[]{:S(2)}) collective-permute-start(bf16[128,3072]{1,0:T(8,128)(2,1)} %get-tuple-element.66), channel_id=1, source_target_pairs={{0,64},{1,65},{2,66},{3,67},{4,68},{5,69},{6,70},{7,71},{8,72},{9,... | collective-permute-start | bytes 2359304 | tf_op jit(solution)/shard_map/ppermute | solution.py:66
  37.1 22.8 %collective-permute-start.14 = (bf16[128,3072]{1,0:T(8,128)(2,1)}, bf16[128,3072]{1,0:T(8,128)(2,1)S(1)}, u32[]{:S(2)}, u32[]{:S(2)}) collective-permute-start(bf16[128,3072]{1,0:T(8,128)(2,1)} %get-tuple-element.67), channel_id=1, source_target_pairs={{0,66},{1,67},{2,64},{3,65},{4,70},{5,71},{6,68},{7,69},{8,74},{9,... | collective-permute-start | bytes 2359304 | tf_op jit(solution)/shard_map/ppermute | solution.py:66
  39.4 20.6 %collective-permute-start.15 = (bf16[128,2560]{1,0:T(8,128)(2,1)}, bf16[128,2560]{1,0:T(8,128)(2,1)S(1)}, u32[]{:S(2)}, u32[]{:S(2)}) collective-permute-start(bf16[128,2560]{1,0:T(8,128)(2,1)} %get-tuple-element.68), channel_id=1, source_target_pairs={{0,2},{1,3},{2,0},{3,1},{4,6},{5,7},{6,4},{7,5},{8,10},{9,11},{10,... | collective-permute-start | bytes 1966088 | tf_op jit(solution)/shard_map/ppermute | solution.py:66
  51.6 46.5 %collective-permute-start.6 = (bf16[2048,512]{1,0:T(8,128)(2,1)}, bf16[2048,512]{1,0:T(8,128)(2,1)}, u32[]{:S(2)}, u32[]{:S(2)}) collective-permute-start(bf16[2048,512]{1,0:T(8,128)(2,1)} %shard_map.78), channel_id=1, source_target_pairs={{0,1},{1,0},{2,3},{3,2},{4,5},{5,4},{6,7},{7,6},{8,9},{9,8},{10,11... | collective-permute-start | bytes 6291464 | tf_op jit(solution)/shard_map/ppermute | solution.py:66
  63.1 21.1 %collective-permute-start.16 = (bf16[1280,512]{1,0:T(8,128)(2,1)}, bf16[1280,512]{1,0:T(8,128)(2,1)}, u32[]{:S(2)}, u32[]{:S(2)}) collective-permute-start(bf16[1280,512]{1,0:T(8,128)(2,1)} %shard_map.82), channel_id=1, source_target_pairs={{0,1},{1,0},{2,3},{3,2},{4,5},{5,4},{6,7},{7,6},{8,9},{9,8},{10,11... | collective-permute-start | bytes 3932168 | tf_op jit(solution)/shard_map/ppermute | solution.py:66
  77.5 33.3 %all-to-all-start = ((bf16[8,256,256]{2,1,0:T(8,128)(2,1)}), bf16[8,256,256]{2,1,0:T(8,128)(2,1)S(1)}, u32[]{:S(2)}, u32[]{:S(2)}) async-start(bf16[8,256,256]{2,1,0:T(8,128)(2,1)} %cut_moments.1), calls=%async_computation | async-start | bytes 2097152 | tf_op jit(solution)/shard_map/all_to_all | solution.py:652
  94.2 20.8 %collective-permute-start.17 = (bf16[320,512]{1,0:T(8,128)(2,1)}, bf16[320,512]{1,0:T(8,128)(2,1)}, u32[]{:S(2)}, u32[]{:S(2)}) collective-permute-start(bf16[320,512]{1,0:T(8,128)(2,1)} %get-tuple-element.70), channel_id=1, source_target_pairs={{0,16},{1,17},{2,18},{3,19},{4,20},{5,21},{6,22},{7,23},{8,24},{9,... | collective-permute-start | bytes 983048 | tf_op jit(solution)/shard_map/ppermute | solution.py:66
  95.7 26.5 %collective-permute-start.18 = (bf16[320,512]{1,0:T(8,128)(2,1)}, bf16[320,512]{1,0:T(8,128)(2,1)}, u32[]{:S(2)}, u32[]{:S(2)}) collective-permute-start(bf16[320,512]{1,0:T(8,128)(2,1)} %get-tuple-element.71), channel_id=1, source_target_pairs={{0,32},{1,33},{2,34},{3,35},{4,36},{5,37},{6,38},{7,39},{8,40},{9,... | collective-permute-start | bytes 983048 | tf_op jit(solution)/shard_map/ppermute | solution.py:66
  104.5 29.4 %collective-permute-start.7 = (bf16[512,512]{1,0:T(8,128)(2,1)}, bf16[512,512]{1,0:T(8,128)(2,1)}, u32[]{:S(2)}, u32[]{:S(2)}) collective-permute-start(bf16[512,512]{1,0:T(8,128)(2,1)} %get-tuple-element.58), channel_id=1, source_target_pairs={{0,64},{1,5},{2,66},{3,7},{4,68},{5,9},{6,70},{7,11},{8,72},{9,13}... | collective-permute-start | bytes 1572872 | tf_op jit(solution)/shard_map/ppermute | solution.py:66
  108.2 25.7 %collective-permute-start.8 = (bf16[512,512]{1,0:T(8,128)(2,1)}, bf16[512,512]{1,0:T(8,128)(2,1)}, u32[]{:S(2)}, u32[]{:S(2)}) collective-permute-start(bf16[512,512]{1,0:T(8,128)(2,1)} %get-tuple-element.59), channel_id=1, source_target_pairs={{0,2},{1,9},{2,0},{3,11},{4,6},{5,13},{6,4},{7,15},{8,10},{9,1},{1... | collective-permute-start | bytes 1572872 | tf_op jit(solution)/shard_map/ppermute | solution.py:66
  109.9 24.1 %collective-permute-start.9 = (bf16[512,512]{1,0:T(8,128)(2,1)}, bf16[512,512]{1,0:T(8,128)(2,1)}, u32[]{:S(2)}, u32[]{:S(2)}) collective-permute-start(bf16[512,512]{1,0:T(8,128)(2,1)} %get-tuple-element.60), channel_id=1, source_target_pairs={{0,66},{1,13},{2,64},{3,15},{4,70},{5,1},{6,68},{7,3},{8,74},{9,5}... | collective-permute-start | bytes 1572872 | tf_op jit(solution)/shard_map/ppermute | solution.py:66
  111.5 10.6 %all-to-all-start.1 = ((bf16[8,32,512]{2,1,0:T(8,128)(2,1)}), bf16[8,32,512]{2,1,0:T(8,128)(2,1)S(1)}, u32[]{:S(2)}, u32[]{:S(2)}) async-start(bf16[8,32,512]{2,1,0:T(8,128)(2,1)} %sum_margin.1), calls=%async_computation.1 | async-start | bytes 524288 | tf_op jit(solution)/shard_map/all_to_all | solution.py:654
  115.0 11.9 %collective-permute-start.19 = (bf16[320,512]{1,0:T(8,128)(2,1)}, bf16[320,512]{1,0:T(8,128)(2,1)}, u32[]{:S(2)}, u32[]{:S(2)}) collective-permute-start(bf16[320,512]{1,0:T(8,128)(2,1)} %copy-done.40), channel_id=1, source_target_pairs={{0,48},{1,49},{2,50},{3,51},{4,52},{5,53},{6,54},{7,55},{8,56},{9,... | collective-permute-start | bytes 983048 | tf_op jit(solution)/shard_map/ppermute | solution.py:66
  122.1 20.3 %collective-permute-start.23 = (bf16[256,512]{1,0:T(8,128)(2,1)S(1)}, bf16[256,512]{1,0:T(8,128)(2,1)S(1)}, u32[]{:S(2)}, u32[]{:S(2)}) collective-permute-start(bf16[256,512]{1,0:T(8,128)(2,1)S(1)} %bitcast.1), channel_id=1, source_target_pairs={{0,1},{1,0},{2,3},{3,2},{4,5},{5,4},{6,7},{7,6},{8,9},{9,8},{10,11... | collective-permute-start | bytes 786440 | tf_op jit(solution)/shard_map/ppermute | solution.py:66
  130.0 14.0 %collective-permute-start.20 = (bf16[80,512]{1,0:T(8,128)(2,1)}, bf16[80,512]{1,0:T(8,128)(2,1)S(1)}, u32[]{:S(2)}, u32[]{:S(2)}) collective-permute-start(bf16[80,512]{1,0:T(8,128)(2,1)} %get-tuple-element.74), channel_id=1, source_target_pairs={{0,4},{1,5},{2,6},{3,7},{4,8},{5,9},{6,10},{7,11},{8,12},{9,13},{1... | collective-permute-start | bytes 245768 | tf_op jit(solution)/shard_map/ppermute | solution.py:66
  137.5 63.0 %copy-start.5 = (bf16[128,3072]{1,0:T(8,128)(2,1)S(1)}, bf16[128,3072]{1,0:T(8,128)(2,1)}, u32[]{:S(2)}) copy-start(bf16[128,3072]{1,0:T(8,128)(2,1)} %copy-done.3) | copy-start | bytes 2359300
  137.5 63.0 %copy-start.8 = (bf16[128,3072]{1,0:T(8,128)(2,1)S(1)}, bf16[128,3072]{1,0:T(8,128)(2,1)}, u32[]{:S(2)}) copy-start(bf16[128,3072]{1,0:T(8,128)(2,1)} %copy-done.6) | copy-start | bytes 2359300
  137.5 63.0 %copy-start.17 = (bf16[128,2560]{1,0:T(8,128)(2,1)S(1)}, bf16[128,2560]{1,0:T(8,128)(2,1)}, u32[]{:S(2)}) copy-start(bf16[128,2560]{1,0:T(8,128)(2,1)} %get-tuple-element.65.refs_0_.refs_8_) | copy-start | bytes 1966084
  137.6 62.9 %copy-start.20 = (bf16[128,2560]{1,0:T(8,128)(2,1)S(1)}, bf16[128,2560]{1,0:T(8,128)(2,1)}, u32[]{:S(2)}) copy-start(bf16[128,2560]{1,0:T(8,128)(2,1)} %copy-done.18) | copy-start | bytes 1966084
  137.6 10.5 %collective-permute-start.10 = (bf16[128,512]{1,0:T(8,128)(2,1)}, bf16[128,512]{1,0:T(8,128)(2,1)S(1)}, u32[]{:S(2)}, u32[]{:S(2)}) collective-permute-start(bf16[128,512]{1,0:T(8,128)(2,1)} %get-tuple-element.62), channel_id=1, source_target_pairs={{0,16},{1,65},{2,18},{3,67},{4,20},{5,69},{6,22},{7,71},{8,24},{9,... | collective-permute-start | bytes 393224 | tf_op jit(solution)/shard_map/ppermute | solution.py:66
  137.7 10.4 %collective-permute-start.11 = (bf16[128,512]{1,0:T(8,128)(2,1)}, bf16[128,512]{1,0:T(8,128)(2,1)S(1)}, u32[]{:S(2)}, u32[]{:S(2)}) collective-permute-start(bf16[128,512]{1,0:T(8,128)(2,1)} %get-tuple-element.63), channel_id=1, source_target_pairs={{0,32},{1,3},{2,34},{3,1},{4,36},{5,7},{6,38},{7,5},{8,40},{9,11},... | collective-permute-start | bytes 393224 | tf_op jit(solution)/shard_map/ppermute | solution.py:66
  140.4 7.7 %collective-permute-start.12 = (bf16[128,512]{1,0:T(8,128)(2,1)}, bf16[128,512]{1,0:T(8,128)(2,1)S(1)}, u32[]{:S(2)}, u32[]{:S(2)}) collective-permute-start(bf16[128,512]{1,0:T(8,128)(2,1)} %get-tuple-element.64), channel_id=1, source_target_pairs={{0,48},{1,67},{2,50},{3,65},{4,52},{5,71},{6,54},{7,69},{8,56},{9,... | collective-permute-start | bytes 393224 | tf_op jit(solution)/shard_map/ppermute | solution.py:66
  142.4 5.7 %collective-permute-start.21 = (bf16[80,512]{1,0:T(8,128)(2,1)S(1)}, bf16[80,512]{1,0:T(8,128)(2,1)S(1)}, u32[]{:S(2)}, u32[]{:S(2)}) collective-permute-start(bf16[80,512]{1,0:T(8,128)(2,1)S(1)} %copy-done.42), channel_id=1, source_target_pairs={{0,8},{1,9},{2,10},{3,11},{4,12},{5,13},{6,14},{7,15},{8,0},{9,1},... | collective-permute-start | bytes 245768 | tf_op jit(solution)/shard_map/ppermute | solution.py:66
  144.0 4.1 %collective-permute-start.22 = (bf16[80,512]{1,0:T(8,128)(2,1)S(1)}, bf16[80,512]{1,0:T(8,128)(2,1)S(1)}, u32[]{:S(2)}, u32[]{:S(2)}) collective-permute-start(bf16[80,512]{1,0:T(8,128)(2,1)S(1)} %copy-done.41), channel_id=1, source_target_pairs={{0,12},{1,13},{2,14},{3,15},{4,0},{5,1},{6,2},{7,3},{8,4},{9,5},{1... | collective-permute-start | bytes 245768 | tf_op jit(solution)/shard_map/ppermute | solution.py:66
  150.4 4.2 %collective-permute-start.42 = (bf16[80,512]{1,0:T(8,128)(2,1)S(1)}, bf16[80,512]{1,0:T(8,128)(2,1)S(1)}, u32[]{:S(2)}, u32[]{:S(2)}) collective-permute-start(bf16[80,512]{1,0:T(8,128)(2,1)S(1)} %get-tuple-element.86.refs_0_), channel_id=1, source_target_pairs={{0,12},{1,13},{2,14},{3,15},{4,0},{5,1},{6,2},{7,3},{8,4},{9,5},{1... | collective-permute-start | bytes 245768 | tf_op jit(solution)/shard_map/ppermute | solution.py:66
  153.2 4.9 %collective-permute-start.41 = (bf16[80,512]{1,0:T(8,128)(2,1)S(1)}, bf16[80,512]{1,0:T(8,128)(2,1)S(1)}, u32[]{:S(2)}, u32[]{:S(2)}) collective-permute-start(bf16[80,512]{1,0:T(8,128)(2,1)S(1)} %get-tuple-element.86.refs_0_), channel_id=1, source_target_pairs={{0,8},{1,9},{2,10},{3,11},{4,12},{5,13},{6,14},{7,15},{8,0},{9,1},... | collective-permute-start | bytes 245768 | tf_op jit(solution)/shard_map/ppermute | solution.py:66
  153.6 6.7 %collective-permute-start.40 = (bf16[80,512]{1,0:T(8,128)(2,1)S(1)}, bf16[80,512]{1,0:T(8,128)(2,1)S(1)}, u32[]{:S(2)}, u32[]{:S(2)}) collective-permute-start(bf16[80,512]{1,0:T(8,128)(2,1)S(1)} %get-tuple-element.86.refs_0_), channel_id=1, source_target_pairs={{0,4},{1,5},{2,6},{3,7},{4,8},{5,9},{6,10},{7,11},{8,12},{9,13},{1... | collective-permute-start | bytes 245768 | tf_op jit(solution)/shard_map/ppermute | solution.py:66
  160.8 10.7 %collective-permute-start.46 = (bf16[320,512]{1,0:T(8,128)(2,1)S(1)}, bf16[320,512]{1,0:T(8,128)(2,1)S(1)}, u32[]{:S(2)}, u32[]{:S(2)}) collective-permute-start(bf16[320,512]{1,0:T(8,128)(2,1)S(1)} %shard_map.88.refs_0_), channel_id=1, source_target_pairs={{0,1},{1,0},{2,3},{3,2},{4,5},{5,4},{6,7},{7,6},{8,9},{9,8},{10,11... | collective-permute-start | bytes 983048 | tf_op jit(solution)/shard_map/ppermute | solution.py:66
  162.0 9.6 %collective-permute-start.45 = (bf16[320,512]{1,0:T(8,128)(2,1)S(1)}, bf16[320,512]{1,0:T(8,128)(2,1)S(1)}, u32[]{:S(2)}, u32[]{:S(2)}) collective-permute-start(bf16[320,512]{1,0:T(8,128)(2,1)S(1)} %shard_map.88.refs_0_), channel_id=1, source_target_pairs={{0,48},{1,49},{2,50},{3,51},{4,52},{5,53},{6,54},{7,55},{8,56},{9,... | collective-permute-start | bytes 983048 | tf_op jit(solution)/shard_map/ppermute | solution.py:66
  162.8 4.1 %collective-permute-start.26 = (bf16[128,512]{1,0:T(8,128)(2,1)S(1)}, bf16[128,512]{1,0:T(8,128)(2,1)S(1)}, u32[]{:S(2)}, u32[]{:S(2)}) collective-permute-start(bf16[128,512]{1,0:T(8,128)(2,1)S(1)} %get-tuple-element.77.refs_0_), channel_id=1, source_target_pairs={{0,48},{1,67},{2,50},{3,65},{4,52},{5,71},{6,54},{7,69},{8,56},{9,... | collective-permute-start | bytes 393224 | tf_op jit(solution)/shard_map/ppermute | solution.py:66
  162.8 5.4 %collective-permute-start.25 = (bf16[128,512]{1,0:T(8,128)(2,1)S(1)}, bf16[128,512]{1,0:T(8,128)(2,1)S(1)}, u32[]{:S(2)}, u32[]{:S(2)}) collective-permute-start(bf16[128,512]{1,0:T(8,128)(2,1)S(1)} %get-tuple-element.77.refs_0_), channel_id=1, source_target_pairs={{0,32},{1,3},{2,34},{3,1},{4,36},{5,7},{6,38},{7,5},{8,40},{9,11},... | collective-permute-start | bytes 393224 | tf_op jit(solution)/shard_map/ppermute | solution.py:66
  164.9 5.0 %collective-permute-start.24 = (bf16[128,512]{1,0:T(8,128)(2,1)S(1)}, bf16[128,512]{1,0:T(8,128)(2,1)S(1)}, u32[]{:S(2)}, u32[]{:S(2)}) collective-permute-start(bf16[128,512]{1,0:T(8,128)(2,1)S(1)} %get-tuple-element.77.refs_0_), channel_id=1, source_target_pairs={{0,16},{1,65},{2,18},{3,67},{4,20},{5,69},{6,22},{7,71},{8,24},{9,... | collective-permute-start | bytes 393224 | tf_op jit(solution)/shard_map/ppermute | solution.py:66
  166.9 8.3 %collective-permute-start.44 = (bf16[320,512]{1,0:T(8,128)(2,1)S(1)}, bf16[320,512]{1,0:T(8,128)(2,1)S(1)}, u32[]{:S(2)}, u32[]{:S(2)}) collective-permute-start(bf16[320,512]{1,0:T(8,128)(2,1)S(1)} %shard_map.88.refs_0_), channel_id=1, source_target_pairs={{0,32},{1,33},{2,34},{3,35},{4,36},{5,37},{6,38},{7,39},{8,40},{9,... | collective-permute-start | bytes 983048 | tf_op jit(solution)/shard_map/ppermute | solution.py:66
  168.3 16.8 %collective-permute-start.43 = (bf16[320,512]{1,0:T(8,128)(2,1)S(1)}, bf16[320,512]{1,0:T(8,128)(2,1)S(1)}, u32[]{:S(2)}, u32[]{:S(2)}) collective-permute-start(bf16[320,512]{1,0:T(8,128)(2,1)S(1)} %shard_map.88.refs_0_), channel_id=1, source_target_pairs={{0,16},{1,17},{2,18},{3,19},{4,20},{5,21},{6,22},{7,23},{8,24},{9,... | collective-permute-start | bytes 983048 | tf_op jit(solution)/shard_map/ppermute | solution.py:66
  170.5 42.4 %copy-start.23 = (bf16[128,2048]{1,0:T(8,128)(2,1)S(1)}, bf16[128,2048]{1,0:T(8,128)(2,1)}, u32[]{:S(2)}) copy-start(bf16[128,2048]{1,0:T(8,128)(2,1)} %get-tuple-element.49.refs_0_.refs_8_) | copy-start | bytes 1572868
  170.5 42.3 %copy-start.27 = (bf16[128,2048]{1,0:T(8,128)(2,1)S(1)}, bf16[128,2048]{1,0:T(8,128)(2,1)}, u32[]{:S(2)}) copy-start(bf16[128,2048]{1,0:T(8,128)(2,1)} %copy-done.24) | copy-start | bytes 1572868
  170.6 17.0 %collective-permute-start.29 = (bf16[512,512]{1,0:T(8,128)(2,1)S(1)}, bf16[512,512]{1,0:T(8,128)(2,1)S(1)}, u32[]{:S(2)}, u32[]{:S(2)}) collective-permute-start(bf16[512,512]{1,0:T(8,128)(2,1)S(1)} %shard_map.85.refs_0_), channel_id=1, source_target_pairs={{0,66},{1,13},{2,64},{3,15},{4,70},{5,1},{6,68},{7,3},{8,74},{9,5}... | collective-permute-start | bytes 1572872 | tf_op jit(solution)/shard_map/ppermute | solution.py:66
  171.5 18.6 %collective-permute-start.28 = (bf16[512,512]{1,0:T(8,128)(2,1)S(1)}, bf16[512,512]{1,0:T(8,128)(2,1)S(1)}, u32[]{:S(2)}, u32[]{:S(2)}) collective-permute-start(bf16[512,512]{1,0:T(8,128)(2,1)S(1)} %shard_map.85.refs_0_), channel_id=1, source_target_pairs={{0,2},{1,9},{2,0},{3,11},{4,6},{5,13},{6,4},{7,15},{8,10},{9,1},{1... | collective-permute-start | bytes 1572872 | tf_op jit(solution)/shard_map/ppermute | solution.py:66
  171.6 20.6 %collective-permute-start.27 = (bf16[512,512]{1,0:T(8,128)(2,1)S(1)}, bf16[512,512]{1,0:T(8,128)(2,1)S(1)}, u32[]{:S(2)}, u32[]{:S(2)}) collective-permute-start(bf16[512,512]{1,0:T(8,128)(2,1)S(1)} %shard_map.85.refs_0_), channel_id=1, source_target_pairs={{0,64},{1,5},{2,66},{3,7},{4,68},{5,9},{6,70},{7,11},{8,72},{9,13}... | collective-permute-start | bytes 1572872 | tf_op jit(solution)/shard_map/ppermute | solution.py:66
  175.2 22.6 %collective-permute-start.49 = (bf16[320,512]{1,0:T(8,128)(2,1)S(1)}, bf16[320,512]{1,0:T(8,128)(2,1)S(1)}, u32[]{:S(2)}, u32[]{:S(2)}) collective-permute-start(bf16[320,512]{1,0:T(8,128)(2,1)S(1)} %collective-permute-done.45.refs_3_), channel_id=1, source_target_pairs={{0,1},{1,0},{2,3},{3,2},{4,5},{5,4},{6,7},{7,6},{8,9},{9,8},{10,11... | collective-permute-start | bytes 983048 | tf_op jit(solution)/shard_map/ppermute | solution.py:66
  185.1 12.7 %collective-permute-start.48 = (bf16[320,512]{1,0:T(8,128)(2,1)S(1)}, bf16[320,512]{1,0:T(8,128)(2,1)S(1)}, u32[]{:S(2)}, u32[]{:S(2)}) collective-permute-start(bf16[320,512]{1,0:T(8,128)(2,1)S(1)} %collective-permute-done.44.refs_2_), channel_id=1, source_target_pairs={{0,1},{1,0},{2,3},{3,2},{4,5},{5,4},{6,7},{7,6},{8,9},{9,8},{10,11... | collective-permute-start | bytes 983048 | tf_op jit(solution)/shard_map/ppermute | solution.py:66
  187.5 23.5 %collective-permute-start.30 = (bf16[512,512]{1,0:T(8,128)(2,1)S(1)}, bf16[512,512]{1,0:T(8,128)(2,1)S(1)}, u32[]{:S(2)}, u32[]{:S(2)}) collective-permute-start(bf16[512,512]{1,0:T(8,128)(2,1)S(1)} %shard_map.85.refs_0_), channel_id=1, source_target_pairs={{0,1},{1,0},{2,3},{3,2},{4,5},{5,4},{6,7},{7,6},{8,9},{9,8},{10,11... | collective-permute-start | bytes 1572872 | tf_op jit(solution)/shard_map/ppermute | solution.py:66
  190.1 21.8 %collective-permute-start.33 = (bf16[512,512]{1,0:T(8,128)(2,1)S(1)}, bf16[512,512]{1,0:T(8,128)(2,1)S(1)}, u32[]{:S(2)}, u32[]{:S(2)}) collective-permute-start(bf16[512,512]{1,0:T(8,128)(2,1)S(1)} %collective-permute-done.29.refs_3_), channel_id=1, source_target_pairs={{0,1},{1,0},{2,3},{3,2},{4,5},{5,4},{6,7},{7,6},{8,9},{9,8},{10,11... | collective-permute-start | bytes 1572872 | tf_op jit(solution)/shard_map/ppermute | solution.py:66
  192.2 20.7 %collective-permute-start.32 = (bf16[512,512]{1,0:T(8,128)(2,1)S(1)}, bf16[512,512]{1,0:T(8,128)(2,1)S(1)}, u32[]{:S(2)}, u32[]{:S(2)}) collective-permute-start(bf16[512,512]{1,0:T(8,128)(2,1)S(1)} %collective-permute-done.28.refs_2_), channel_id=1, source_target_pairs={{0,1},{1,0},{2,3},{3,2},{4,5},{5,4},{6,7},{7,6},{8,9},{9,8},{10,11... | collective-permute-start | bytes 1572872 | tf_op jit(solution)/shard_map/ppermute | solution.py:66
  197.7 15.1 %collective-permute-start.31 = (bf16[512,512]{1,0:T(8,128)(2,1)S(1)}, bf16[512,512]{1,0:T(8,128)(2,1)S(1)}, u32[]{:S(2)}, u32[]{:S(2)}) collective-permute-start(bf16[512,512]{1,0:T(8,128)(2,1)S(1)} %collective-permute-done.27.refs_1_), channel_id=1, source_target_pairs={{0,1},{1,0},{2,3},{3,2},{4,5},{5,4},{6,7},{7,6},{8,9},{9,8},{10,11... | collective-permute-start | bytes 1572872 | tf_op jit(solution)/shard_map/ppermute | solution.py:66
  197.8 2.7 collective-permute-start.47
  209.1 17.6 %collective-permute-start.50 = (bf16[128,2560]{1,0:T(8,128)(2,1)S(1)}, bf16[128,2560]{1,0:T(8,128)(2,1)S(1)}, u32[]{:S(2)}, u32[]{:S(2)}) collective-permute-start(bf16[128,2560]{1,0:T(8,128)(2,1)S(1)} %get-tuple-element.88), channel_id=1, source_target_pairs={{0,64},{1,65},{2,66},{3,67},{4,68},{5,69},{6,70},{7,71},{8,72},{9,... | collective-permute-start | bytes 1966088 | tf_op jit(solution)/shard_map/ppermute | solution.py:66
  211.0 16.3 %collective-permute-start.51 = (bf16[128,2560]{1,0:T(8,128)(2,1)S(1)}, bf16[128,2560]{1,0:T(8,128)(2,1)S(1)}, u32[]{:S(2)}, u32[]{:S(2)}) collective-permute-start(bf16[128,2560]{1,0:T(8,128)(2,1)S(1)} %get-tuple-element.89), channel_id=1, source_target_pairs={{0,66},{1,67},{2,64},{3,65},{4,70},{5,71},{6,68},{7,69},{8,74},{9,... | collective-permute-start | bytes 1966088 | tf_op jit(solution)/shard_map/ppermute | solution.py:66
  211.9 28.7 %collective-permute-start.52 = (bf16[128,2560]{1,0:T(8,128)(2,1)S(1)}, bf16[128,2560]{1,0:T(8,128)(2,1)S(1)}, u32[]{:S(2)}, u32[]{:S(2)}) collective-permute-start(bf16[128,2560]{1,0:T(8,128)(2,1)S(1)} %get-tuple-element.90), channel_id=1, source_target_pairs={{0,2},{1,3},{2,0},{3,1},{4,6},{5,7},{6,4},{7,5},{8,10},{9,11},{10,... | collective-permute-start | bytes 1966088 | tf_op jit(solution)/shard_map/ppermute | solution.py:66
  217.5 23.1 %collective-permute-start.37 = (bf16[128,2048]{1,0:T(8,128)(2,1)S(1)}, bf16[128,2048]{1,0:T(8,128)(2,1)S(1)}, u32[]{:S(2)}, u32[]{:S(2)}) collective-permute-start(bf16[128,2048]{1,0:T(8,128)(2,1)S(1)} %get-tuple-element.83), channel_id=1, source_target_pairs={{0,4},{1,5},{2,6},{3,7},{4,8},{5,9},{6,10},{7,11},{8,12},{9,13},{1... | collective-permute-start | bytes 1572872 | tf_op jit(solution)/shard_map/ppermute | solution.py:66
  222.0 46.7 %copy-start.29 = (bf16[128,2560]{1,0:T(8,128)(2,1)S(1)}, bf16[128,2560]{1,0:T(8,128)(2,1)}, u32[]{:S(2)}) copy-start(bf16[128,2560]{1,0:T(8,128)(2,1)} %get-tuple-element.87.refs_0_) | copy-start | bytes 1966084
  222.1 52.8 %collective-permute-start.34 = (bf16[128,2048]{1,0:T(8,128)(2,1)S(1)}, bf16[128,2048]{1,0:T(8,128)(2,1)S(1)}, u32[]{:S(2)}, u32[]{:S(2)}) collective-permute-start(bf16[128,2048]{1,0:T(8,128)(2,1)S(1)} %get-tuple-element.79), channel_id=1, source_target_pairs={{0,16},{1,17},{2,18},{3,19},{4,20},{5,21},{6,22},{7,23},{8,24},{9,... | collective-permute-start | bytes 1572872 | tf_op jit(solution)/shard_map/ppermute | solution.py:66
  226.7 45.6 %collective-permute-start.38 = (bf16[128,2048]{1,0:T(8,128)(2,1)S(1)}, bf16[128,2048]{1,0:T(8,128)(2,1)S(1)}, u32[]{:S(2)}, u32[]{:S(2)}) collective-permute-start(bf16[128,2048]{1,0:T(8,128)(2,1)S(1)} %get-tuple-element.84), channel_id=1, source_target_pairs={{0,12},{1,13},{2,14},{3,15},{4,0},{5,1},{6,2},{7,3},{8,4},{9,5},{1... | collective-permute-start | bytes 1572872 | tf_op jit(solution)/shard_map/ppermute | solution.py:66
  227.3 45.0 %collective-permute-start.39 = (bf16[128,2048]{1,0:T(8,128)(2,1)S(1)}, bf16[128,2048]{1,0:T(8,128)(2,1)S(1)}, u32[]{:S(2)}, u32[]{:S(2)}) collective-permute-start(bf16[128,2048]{1,0:T(8,128)(2,1)S(1)} %get-tuple-element.85), channel_id=1, source_target_pairs={{0,8},{1,9},{2,10},{3,11},{4,12},{5,13},{6,14},{7,15},{8,0},{9,1},... | collective-permute-start | bytes 1572872 | tf_op jit(solution)/shard_map/ppermute | solution.py:66
  240.6 34.3 %collective-permute-start.35 = (bf16[128,2048]{1,0:T(8,128)(2,1)S(1)}, bf16[128,2048]{1,0:T(8,128)(2,1)S(1)}, u32[]{:S(2)}, u32[]{:S(2)}) collective-permute-start(bf16[128,2048]{1,0:T(8,128)(2,1)S(1)} %get-tuple-element.80), channel_id=1, source_target_pairs={{0,48},{1,49},{2,50},{3,51},{4,52},{5,53},{6,54},{7,55},{8,56},{9,... | collective-permute-start | bytes 1572872 | tf_op jit(solution)/shard_map/ppermute | solution.py:66
  240.6 34.3 %collective-permute-start.36 = (bf16[128,2048]{1,0:T(8,128)(2,1)S(1)}, bf16[128,2048]{1,0:T(8,128)(2,1)S(1)}, u32[]{:S(2)}, u32[]{:S(2)}) collective-permute-start(bf16[128,2048]{1,0:T(8,128)(2,1)S(1)} %get-tuple-element.81), channel_id=1, source_target_pairs={{0,32},{1,33},{2,34},{3,35},{4,36},{5,37},{6,38},{7,39},{8,40},{9,... | collective-permute-start | bytes 1572872 | tf_op jit(solution)/shard_map/ppermute | solution.py:66
  (34 other events, 227.3 us)

commit v4 on v3

--- a/solution.py
+++ b/solution.py
@@ -21,6 +21,7 @@
 DMA = pltpu.SemaphoreType.DMA
 LIMIT = pltpu.CompilerParams(vmem_limit_bytes=16 * 2**20)
 ALL_OF_IT = pltpu.CompilerParams(vmem_limit_bytes=60 * 1024 * 1024)
+MOST_OF_IT = pltpu.CompilerParams(vmem_limit_bytes=57 * 2**20)
 
 
 def blocks_of(count, shape):
@@ -172,7 +173,7 @@
         out_specs=[ANY] * 4,
         scratch_shapes=[pltpu.VMEM((4, 128, width), BF), DMA((4,)), DMA((4,))]
         + ([pltpu.VMEM((16, 128, 128), BF), DMA((16,))] if ring == "x" else []),
-        compiler_params=ALL_OF_IT if ring == "x" else LIMIT,
+        compiler_params=ALL_OF_IT if ring == "x" else MOST_OF_IT,
         cost_estimate=estimate(0, 4 * 128 * width * 4),
     )(where, grad, basis)
 
@@ -246,59 +247,74 @@
     return base.at[pl.ds(pl.multiple_of((y * 4 + xh * 2 + core) * 128, 128), 128), :]
 
 
-def start_blocks(ring, where, blocks, first, chunk, tile, basis, held, base, in_sem, base_sem):
+def start_basis(ring, where, blocks, basis, base, base_sem):
     for k, step in enumerate(STEPS):
         if with_basis(ring, step):
             source = blocks[k].at[:, pl.ds(WIDTH[ring], 512)]
         else:
             source = basis_rows(ring, where, 4 - step, basis)
         pltpu.make_async_copy(source, base.at[pl.ds(k * 128, 128), :], base_sem).start()
-    for i in range(chunk // tile):
-        for k in range(4):
-            columns = pl.ds(pl.multiple_of(first + i * tile, 128), tile)
-            target = held.at[pl.ds(k * 128, 128), pl.ds(i * tile, tile)]
-            pltpu.make_async_copy(blocks[k].at[:, columns], target, in_sem.at[i]).start()
 
 
 def project_kernel(group, own, where, *refs):
     count = 8 if group == 0 else 4
     blocks, basis, refs = refs[:count], refs[count], refs[count + 1 :]
     if own:
-        other, outs, (held, base, total, in_sem, base_sem, other_sem, out_sem) = refs[0], refs[1:5], refs[5:]
+        other, gathered, outs, (base, total, base_sem, out_sem) = refs[0], refs[1], refs[2:6], refs[6:]
     else:
-        out, held, base, total, in_sem, base_sem, out_sem = refs
+        total, gathered, base, gather, base_sem, out_sem = refs
     chunk, tile = GROUPS[group][0], TILE[group]
     core = place(where, "core")
-    scratch = (chunk, tile, basis, held, base, in_sem, base_sem)
-    if group == 0:
-        on_y = core == (0 if own else 1)
-        for ring, mine, chosen in (("y", blocks[:4], on_y), ("z", blocks[4:], jnp.logical_not(on_y))):
-
-            @pl.when(chosen)
+
+    def multiply(mine, base, first):
+        @pl.loop(0, chunk // tile)
+        def _(i):
+            some = pl.ds(pl.multiple_of(i * tile, tile), tile)
+            columns = pl.ds(pl.multiple_of(first + i * tile, 128), tile)
+            block = jnp.concatenate([ref[:, columns] for ref in mine], axis=0)
+            product = lax.dot_general(block, base[...], (((0,), (0,)), ((), ())), preferred_element_type=F32)
+            if own:
+                product = product + other[some, :].astype(F32)
+            total[some, :] = product.astype(BF)
+
+    if own:
+        if group == 0:
+
+            @pl.when(core == 0)
             def _():
-                start_blocks(ring, where, mine, 0, *scratch)
-
+                start_basis("y", where, blocks[:4], basis, base, base_sem)
+                wait_for(base, base_sem)
+                multiply(blocks[:4], base, 0)
+
+            @pl.when(core == 1)
+            def _():
+                wait_all(start_all([pltpu.make_async_copy(gathered, base, base_sem)]))
+                multiply(blocks[4:], base, 0)
+
+        else:
+            wait_all(start_all([pltpu.make_async_copy(gathered, base, base_sem)]))
+            multiply(blocks, base, core * chunk)
     else:
-        start_blocks("x", where, blocks, (core if own else 1 - core) * chunk, *scratch)
-    if own:
-        copy = pltpu.make_async_copy(other, total, other_sem)
+        ring, mine = ("z", blocks[4:]) if group == 0 else ("x", blocks)
+        start_basis(ring, where, mine, basis, gather, base_sem)
+        wait_for(gather, base_sem)
+        copy = pltpu.make_async_copy(gather, gathered, out_sem)
         copy.start()
+        if group == 0:
+
+            @pl.when(core == 1)
+            def _():
+                start_basis("y", where, blocks[:4], basis, base, base_sem)
+                wait_for(base, base_sem)
+                multiply(blocks[:4], base, 0)
+
+            @pl.when(core == 0)
+            def _():
+                multiply(mine, gather, 0)
+
+        else:
+            multiply(mine, gather, (1 - core) * chunk)
         copy.wait()
-    wait_for(base, base_sem)
-
-    @pl.loop(0, chunk // tile)
-    def _(i):
-        some = pl.ds(pl.multiple_of(i * tile, tile), tile)
-        wait_for(held.at[:, some], in_sem.at[i])
-        product = lax.dot_general(held[:, some], base[...], (((0,), (0,)), ((), ())), preferred_element_type=F32)
-        if own:
-            product = product + total[some, :].astype(F32)
-        total[some, :] = product.astype(BF)
-        if not own:
-            pltpu.make_async_copy(total.at[some, :], out.at[some, :], out_sem).start()
-
-    if not own:
-        wait_for(total, out_sem)
         return
     stores = []
     for j in range(4):
@@ -313,26 +329,26 @@
     wait_all(start_all(stores))
 
 
-def project(group, where, blocks, basis, other=None):
+def project(group, where, blocks, basis, other=None, gathered=None):
     chunk = GROUPS[group][0]
     own = other is not None
-    shapes = blocks_of(4, (chunk // 4, 512)) if own else jax.ShapeDtypeStruct((chunk, 512), BF)
+    shapes = blocks_of(4, (chunk // 4, 512))
+    if not own:
+        shapes = [jax.ShapeDtypeStruct((chunk, 512), BF), pltpu.HBM((512, 512), BF)]
     return pl.pallas_call(
         functools.partial(project_kernel, group, own),
         out_shape=shapes,
-        in_specs=[SMEM] + [ANY] * (len(blocks) + 1 + own),
-        out_specs=[ANY] * 4 if own else ANY,
+        in_specs=[SMEM] + [VMEM] * len(blocks) + [ANY] + ([VMEM, ANY] if own else []),
+        out_specs=[ANY] * 4 if own else [VMEM, ANY],
         scratch_shapes=[
-            pltpu.VMEM((512, chunk), BF),
             pltpu.VMEM((512, 512), BF),
-            pltpu.VMEM((chunk, 512), BF),
-            DMA((4,)),
+            pltpu.VMEM((chunk if own else 512, 512), BF),
             DMA,
-        ]
-        + ([DMA, DMA((4, 8))] if own else [DMA]),
+            DMA((4, 8)) if own else DMA,
+        ],
         compiler_params=LIMIT,
         cost_estimate=estimate(2 * 512 * 512 * chunk, 512 * chunk * 2 + 512 * 1024 + chunk * 1024),
-    )(where, *blocks, basis, *([other] if own else []))
+    )(where, *blocks, basis, *([other, gathered] if own else []))
 
 
 def add_kernel(group, where, a, b, c, d, *refs):
@@ -562,16 +578,15 @@
 
 
 def update_kernel(ring, where, *refs):
-    count = 5
-    own, other, bases, outs = refs[:4], refs[4:8], refs[8 : 8 + count], refs[8 + count : 12 + count]
-    low, base, held, in_sem, other_sem, base_sem, out_sem = refs[12 + count :]
+    own, other, basis, outs = refs[:4], refs[4:8], refs[8], refs[9:13]
+    low, base, held, in_sem, other_sem, base_sem, out_sem = refs[13:]
     core = place(where, "core")
     width = WIDTH[ring]
     for k, step in enumerate(STEPS):
-        if with_basis(ring, step):
-            source = bases[STEPS.index((4 - step) % 4)].at[:, pl.ds(width, 512)]
+        if ring == "y":
+            source = basis_rows(ring, where, step, basis)
         else:
-            source = basis_rows(ring, where, step, bases[4])
+            source = basis.at[pl.ds(STEPS.index((4 - step) % 4) * 128, 128), :]
         pltpu.make_async_copy(source, base.at[pl.ds(k * 128, 128), :], base_sem).start()
     if ring == "x":
         start_all(low_copies(1, where, own, core * 1280, low, in_sem, core))
@@ -605,12 +620,12 @@
         wait_for(held.at[pl.ds(k * 128, 128), :], out_sem.at[k])
 
 
-def update_blocks(ring, where, arrays, bases):
+def update_blocks(ring, where, arrays, basis):
     width = WIDTH[ring]
     return pl.pallas_call(
         functools.partial(update_kernel, ring),
         out_shape=blocks_of(4, (128, width)),
-        in_specs=[SMEM] + [ANY] * (8 + len(bases)),
+        in_specs=[SMEM] + [ANY] * 9,
         out_specs=[ANY] * 4,
         scratch_shapes=[
             pltpu.VMEM((width, 512), BF),
@@ -623,7 +638,7 @@
         ],
         compiler_params=LIMIT,
         cost_estimate=estimate(2 * 512 * 512 * width, 512 * width * 2 + 512 * 1024 + width * 1024),
-    )(where, *arrays, *bases)
+    )(where, *arrays, basis)
 
 
 def exchange(blocks, rings):
@@ -654,11 +669,12 @@
     margin = lax.all_to_all(margin, ROW, 0, 0, tiled=True).reshape(256, 512)
     margin_other = shift(margin, RINGS["core"], 1)
 
-    totals = {}
+    totals, gathered = {}, {"y": basis_new}
     for group, blocks in ((1, arrived["x"]), (0, arrived["y"] + arrived["z"])):
-        other = project(group, where, blocks, basis_new)
+        other, rows = project(group, where, blocks, basis_new)
+        gathered["z" if group == 0 else "x"] = rows
         other = shift(other, RINGS["core"], 1)
-        partial = project(group, where, blocks, basis_new, other)
+        partial = project(group, where, blocks, basis_new, other, rows)
         halves = ordered(partial, U[group])
         rest = add_up(group, where, halves)
         totals[group] = ordered(rest, V[group])
@@ -673,7 +689,7 @@
         whole = ordered([quarter] * 4, U[group])
         whole = whole + [shift(array, RINGS["core"], 1) for array in whole]
         for ring in rings:
-            blocks = update_blocks(ring, where, whole, arrived[ring] + [basis_new])
+            blocks = update_blocks(ring, where, whole, gathered[ring])
             sent[ring] = exchange(blocks, RINGS[ring])
     update = None
     for ring in ("x", "y", "z"):

time: 282 us -> 281 us (level)
  the two profiles are of different devices: /device:TPU:1 before, /device:TPU:38 now
where the time goes in v4:
time: 281 us; the launch traced here: 280 us
  waiting for transfers between devices  100 us (36%)
  starting transfers between devices  71.4 us (25%)
  Pallas kernels  69.2 us (25%)
  blocking collectives  26.4 us (9%)
  local copies, waits for them, and re-layouts  11 us (4%)
    ppermute x53, waiting for transfers between devices, shift(): return lax.ppermute(array, NAMES, pairs)  90.9 us
    ppermute x53, starting transfers between devices, shift(): return lax.ppermute(array, NAMES, pairs)  58.9 us
    all_to_all x1, blocking collectives, compute(): new = lax.all_to_all(new, ROW, 0, 0, tiled=True)  26.4 us
    pallas_call x4, Pallas kernels, project(): pl.pallas_call(functools.partial(project_kernel, group, own), out_shape=s...  18.7 us
    pallas_call x3, Pallas kernels, update_blocks(): pl.pallas_call(functools.partial(update_kernel, ring), out_shape=blocks_o...  17.7 us
    pallas_call x3, Pallas kernels, pack(): pl.pallas_call(functools.partial(pack_kernel, ring), out_shape=[(jax.Shap...  11.5 us
    unnamed x72, local copies, waits for them, and re-layouts  11 us
    all_to_all x1, waiting for transfers between devices, compute(): margin = lax.all_to_all(margin, ROW, 0, 0, tiled=True).reshape(256, 512)  9.17 us
  transfers between devices with their start and end apart: 55, of which 21 were waited for; matrix products, arithmetic and copies ran while one was open for 0% of the time, Pallas kernels for 22%

profile of v4, /device:TPU:38, one launch (start us, length us, event | category | flops | bytes accessed | tf_op | source)
XLA Modules:
  0.0 280.0 jit_solution(6888258111399407244)
XLA Ops:
  1.2 3.2 %shard_map.76 = (bf16[128,2048]{1,0:T(8,128)(2,1)}, bf16[128,2048]{1,0:T(8,128)(2,1)}, bf16[128,2048]{1,0:T(8,128)(2,1)}, bf16[128,2048]{1,0:T(8,128)(2,1)}) custom-call(s32[8]{0:T(128)} %compare_select_fusion.6.where, bf16[128,26624]{1,0:T(8,128)(2,1)} %grad.5, bf16[2048,512]{1,0:T(8,128)(2,1)} %refs_8_.5), custom_call_target="tpu_custom_call" | custom-call | bytes 4194304 | tf_op jit(solution)/shard_map/pallas_call | solution.py:166
  4.4 1.7 collective-permute-start
  6.1 3.7 %shard_map.77 = (bf16[128,2560]{1,0:T(8,128)(2,1)}, bf16[128,2560]{1,0:T(8,128)(2,1)}, bf16[128,2560]{1,0:T(8,128)(2,1)}, bf16[128,2560]{1,0:T(8,128)(2,1)}) custom-call(s32[8]{0:T(128)} %compare_select_fusion.6.where, bf16[128,26624]{1,0:T(8,128)(2,1)} %grad.5, bf16[2048,512]{1,0:T(8,128)(2,1)} %refs_8_.5), custom_call_target="tpu_custom_call" | custom-call | bytes 5242880 | tf_op jit(solution)/shard_map/pallas_call | solution.py:166
  9.8 2.1 collective-permute-start.3
  11.9 3.3 %collective-permute-start.5 = (bf16[128,2560]{1,0:T(8,128)(2,1)}, bf16[128,2560]{1,0:T(8,128)(2,1)}, u32[]{:S(2)}, u32[]{:S(2)}) collective-permute-start(bf16[128,2560]{1,0:T(8,128)(2,1)} %get-tuple-element.60), channel_id=1, source_target_pairs={{0,32},{1,33},{2,34},{3,35},{4,36},{5,37},{6,38},{7,39},{8,40},{9,... | collective-permute-start | bytes 1966088 | tf_op jit(solution)/shard_map/ppermute | solution.py:67
  15.2 1.8 collective-permute-start.1
  17.0 3.0 %collective-permute-done.refs_1_ = bf16[128,2048]{1,0:T(8,128)(2,1)S(1)} collective-permute-done((bf16[128,2048]{1,0:T(8,128)(2,1)}, bf16[128,2048]{1,0:T(8,128)(2,1)S(1)}, u32[]{:S(2)}, u32[]{:S(2)}) %collective-permute-start) | collective-permute-done | bytes 524320 | tf_op jit(solution)/shard_map/ppermute | solution.py:67
  20.8 1.8 collective-permute-start.2
  22.6 4.6 %shard_map.81 = (bf16[128,2560]{1,0:T(8,128)(2,1)}, bf16[128,3072]{1,0:T(8,128)(2,1)}, bf16[128,3072]{1,0:T(8,128)(2,1)}, bf16[128,2560]{1,0:T(8,128)(2,1)}) custom-call(s32[8]{0:T(128)} %compare_select_fusion.6.where, bf16[128,26624]{1,0:T(8,128)(2,1)} %grad.5, bf16[2048,512]{1,0:T(8,128)(2,1)} %refs_8_.5), custom_call_target="tpu_custom_call" | custom-call | bytes 6291456 | tf_op jit(solution)/shard_map/pallas_call | solution.py:166
  27.2 11.7 %collective-permute-done.1.refs_2_ = bf16[128,2048]{1,0:T(8,128)(2,1)} collective-permute-done((bf16[128,2048]{1,0:T(8,128)(2,1)}, bf16[128,2048]{1,0:T(8,128)(2,1)}, u32[]{:S(2)}, u32[]{:S(2)}) %collective-permute-start.1) | collective-permute-done | bytes 524320 | tf_op jit(solution)/shard_map/ppermute | solution.py:67
  39.4 1.5 collective-permute-start.14
  40.9 1.4 collective-permute-start.15
  44.5 5.0 %shard_map.78 = (bf16[2048,512]{1,0:T(8,128)(2,1)}, bf16[512,512]{1,0:T(8,128)(2,1)}) custom-call(s32[8]{0:T(128)S(1)} %copy-done.30, bf16[128,2048]{1,0:T(8,128)(2,1)S(1)} %copy-done.16, bf16[128,2048]{1,0:T(8,128)(2,1)S(1)} %copy-done.19, bf16[128,2048]{1,0:T(8,128)(2,1)} %collective-permute-done.1.refs_2_, ...), custom_call_target="tpu_custom_call" | custom-call | flops 1073741824 | bytes 4718592 | tf_op jit(solution)/shard_map/pallas_call | solution.py:338
  49.6 18.3 %collective-permute-done.15.refs_3_ = bf16[128,2560]{1,0:T(8,128)(2,1)S(1)} collective-permute-done((bf16[128,2560]{1,0:T(8,128)(2,1)}, bf16[128,2560]{1,0:T(8,128)(2,1)S(1)}, u32[]{:S(2)}, u32[]{:S(2)}) %collective-permute-start.15) | collective-permute-done | bytes 655392 | tf_op jit(solution)/shard_map/ppermute | solution.py:67
  67.9 1.2 collective-permute-done.14.refs_2_
  69.1 3.1 %shard_map.82 = (bf16[1280,512]{1,0:T(8,128)(2,1)}, bf16[512,512]{1,0:T(8,128)(2,1)}) custom-call(s32[8]{0:T(128)S(1)} %copy-done.30, bf16[128,2560]{1,0:T(8,128)(2,1)S(1)} %copy-done.9, bf16[128,3072]{1,0:T(8,128)(2,1)S(1)} %collective-permute-done.13.refs_1_, bf16[128,3072]{1,0:T(8,128)(2,1)S(1)} %collective-permute-done.14.refs_2_, ...), custom_call_target="tpu_custom_call" | custom-call | flops 671088640 | bytes 3145728 | tf_op jit(solution)/shard_map/pallas_call | solution.py:338
  72.4 2.8 cut_moments.1
  75.2 6.5 %all-to-all-start = ((bf16[8,256,256]{2,1,0:T(8,128)(2,1)}), bf16[8,256,256]{2,1,0:T(8,128)(2,1)S(1)}, u32[]{:S(2)}, u32[]{:S(2)}) async-start(bf16[8,256,256]{2,1,0:T(8,128)(2,1)} %cut_moments.1), calls=%async_computation | async-start | bytes 2097152 | tf_op jit(solution)/shard_map/all_to_all | solution.py:667
  87.2 3.8 %shard_map.83 = (bf16[320,512]{1,0:T(8,128)(2,1)}, bf16[320,512]{1,0:T(8,128)(2,1)}, bf16[320,512]{1,0:T(8,128)(2,1)}, bf16[320,512]{1,0:T(8,128)(2,1)S(1)}) custom-call(s32[8]{0:T(128)S(1)} %copy-done.30, bf16[128,2560]{1,0:T(8,128)(2,1)S(1)} %copy-done.10, bf16[128,3072]{1,0:T(8,128)(2,1)S(1)} %copy-done.2, bf16[128,3072]{1,0:T(8,128)(2,1)S(1)} %copy-done.4, ...), custom_call_target="tpu_custom_call" | custom-call | flops 671088640 | bytes 3145728 | tf_op jit(solution)/shard_map/pallas_call | solution.py:338
  91.8 1.5 collective-permute-start.17
  93.3 1.2 collective-permute-start.18
  94.5 6.8 %shard_map.79 = (bf16[512,512]{1,0:T(8,128)(2,1)}, bf16[512,512]{1,0:T(8,128)(2,1)}, bf16[512,512]{1,0:T(8,128)(2,1)}, bf16[512,512]{1,0:T(8,128)(2,1)}) custom-call(s32[8]{0:T(128)S(1)} %copy-done.30, bf16[128,2048]{1,0:T(8,128)(2,1)S(1)} %copy-done.17, bf16[128,2048]{1,0:T(8,128)(2,1)S(1)} %copy-done.20, bf16[128,2048]{1,0:T(8,128)(2,1)} %collective-permute-done.1.refs_2_, ...), custom_call_target="tpu_custom_call" | custom-call | flops 1073741824 | bytes 4718592 | tf_op jit(solution)/shard_map/pallas_call | solution.py:338
  101.3 2.1 collective-permute-start.8
  104.7 6.0 %all-to-all-start.1 = ((bf16[8,32,512]{2,1,0:T(8,128)(2,1)}), bf16[8,32,512]{2,1,0:T(8,128)(2,1)S(1)}, u32[]{:S(2)}, u32[]{:S(2)}) async-start(bf16[8,32,512]{2,1,0:T(8,128)(2,1)} %sum_margin.1), calls=%async_computation.1 | async-start | bytes 524288 | tf_op jit(solution)/shard_map/all_to_all | solution.py:669
  111.3 9.2 %all-to-all-done.1 = bf16[8,32,512]{2,1,0:T(8,128)(2,1)S(1)} async-done(((bf16[8,32,512]{2,1,0:T(8,128)(2,1)}), bf16[8,32,512]{2,1,0:T(8,128)(2,1)S(1)}, u32[]{:S(2)}, u32[]{:S(2)}) %all-to-all-start.1) | async-done | bytes 262176 | tf_op jit(solution)/shard_map/all_to_all | solution.py:669
  120.5 2.8 collective-permute-done.19.d
  124.2 2.1 shard_map.84
  126.3 2.4 collective-permute-start.20
  129.9 2.5 shard_map.80
  132.4 1.4 collective-permute-start.10
  133.8 1.6 collective-permute-start.11
  135.5 2.0 collective-permute-start.12
  137.5 2.0 collective-permute-start.21
  140.2 3.2 %collective-permute-done.21.refs_6_ = bf16[80,512]{1,0:T(8,128)(2,1)S(1)} collective-permute-done((bf16[80,512]{1,0:T(8,128)(2,1)S(1)}, bf16[80,512]{1,0:T(8,128)(2,1)S(1)}, u32[]{:S(2)}, u32[]{:S(2)}) %collective-permute-start.21) | collective-permute-done | bytes 81952 | tf_op jit(solution)/shard_map/ppermute | solution.py:67
  144.8 1.4 step.1
  146.2 2.0 collective-permute-start.42
  149.3 1.8 collective-permute-done.42.refs_3_
  151.1 3.1 %collective-permute-done.41.refs_2_ = bf16[80,512]{1,0:T(8,128)(2,1)S(1)} collective-permute-done((bf16[80,512]{1,0:T(8,128)(2,1)S(1)}, bf16[80,512]{1,0:T(8,128)(2,1)S(1)}, u32[]{:S(2)}, u32[]{:S(2)}) %collective-permute-start.41) | collective-permute-done | bytes 81952 | tf_op jit(solution)/shard_map/ppermute | solution.py:67
  155.7 1.1 collective-permute-start.45
  157.4 1.9 collective-permute-start.25
  160.1 12.1 %collective-permute-done.26.refs_3_ = bf16[128,512]{1,0:T(8,128)(2,1)S(1)} collective-permute-done((bf16[128,512]{1,0:T(8,128)(2,1)S(1)}, bf16[128,512]{1,0:T(8,128)(2,1)S(1)}, u32[]{:S(2)}, u32[]{:S(2)}) %collective-permute-start.26) | collective-permute-done | bytes 131104 | tf_op jit(solution)/shard_map/ppermute | solution.py:67
  172.8 2.0 collective-permute-start.29
  174.8 1.8 collective-permute-start.28
  176.6 1.1 collective-permute-start.27
  177.8 3.0 %collective-permute-done.44.refs_2_ = bf16[320,512]{1,0:T(8,128)(2,1)S(1)} collective-permute-done((bf16[320,512]{1,0:T(8,128)(2,1)S(1)}, bf16[320,512]{1,0:T(8,128)(2,1)S(1)}, u32[]{:S(2)}, u32[]{:S(2)}) %collective-permute-start.44) | collective-permute-done | bytes 327712 | tf_op jit(solution)/shard_map/ppermute | solution.py:67
  180.7 1.7 collective-permute-done.43.refs_1_
  183.2 6.2 %collective-permute-done.28.refs_2_ = bf16[512,512]{1,0:T(8,128)(2,1)S(1)} collective-permute-done((bf16[512,512]{1,0:T(8,128)(2,1)S(1)}, bf16[512,512]{1,0:T(8,128)(2,1)S(1)}, u32[]{:S(2)}, u32[]{:S(2)}) %collective-permute-start.28) | collective-permute-done | bytes 524320 | tf_op jit(solution)/shard_map/ppermute | solution.py:67
  190.4 2.8 %collective-permute-done.47.refs_5_ = bf16[320,512]{1,0:T(8,128)(2,1)S(1)} collective-permute-done((bf16[320,512]{1,0:T(8,128)(2,1)S(1)}, bf16[320,512]{1,0:T(8,128)(2,1)S(1)}, u32[]{:S(2)}, u32[]{:S(2)}) %collective-permute-start.47) | collective-permute-done | bytes 327712 | tf_op jit(solution)/shard_map/ppermute | solution.py:67
  193.3 8.8 %shard_map.89 = (bf16[128,2560]{1,0:T(8,128)(2,1)}, bf16[128,2560]{1,0:T(8,128)(2,1)S(1)}, bf16[128,2560]{1,0:T(8,128)(2,1)S(1)}, bf16[128,2560]{1,0:T(8,128)(2,1)S(1)}) custom-call(s32[8]{0:T(128)S(1)} %copy-done.30, bf16[320,512]{1,0:T(8,128)(2,1)S(1)} %shard_map.88.refs_0_, bf16[320,512]{1,0:T(8,128)(2,1)S(1)} %collective-permute-done.43.refs_1_, ...), custom_call_target="tpu_custom_call" | custom-call | flops 1342177280 | bytes 5767168 | tf_op jit(solution)/shard_map/pallas_call | solution.py:625
  202.1 2.3 collective-permute-start.50
  204.4 1.7 collective-permute-start.52
  206.1 4.3 %shard_map.87 = (bf16[128,2048]{1,0:T(8,128)(2,1)}, bf16[128,2048]{1,0:T(8,128)(2,1)S(1)}, bf16[128,2048]{1,0:T(8,128)(2,1)S(1)}, bf16[128,2048]{1,0:T(8,128)(2,1)S(1)}) custom-call(s32[8]{0:T(128)S(1)} %copy-done.30, bf16[512,512]{1,0:T(8,128)(2,1)S(1)} %shard_map.85.refs_0_, bf16[512,512]{1,0:T(8,128)(2,1)S(1)} %collective-permute-done.27.refs_1_, ...), custom_call_target="tpu_custom_call" | custom-call | flops 1073741824 | bytes 4718592 | tf_op jit(solution)/shard_map/pallas_call | solution.py:625
  210.4 2.0 collective-permute-start.37
  212.5 4.5 %shard_map.86 = (bf16[128,2048]{1,0:T(8,128)(2,1)}, bf16[128,2048]{1,0:T(8,128)(2,1)S(1)}, bf16[128,2048]{1,0:T(8,128)(2,1)S(1)}, bf16[128,2048]{1,0:T(8,128)(2,1)S(1)}) custom-call(s32[8]{0:T(128)S(1)} %copy-done.30, bf16[512,512]{1,0:T(8,128)(2,1)S(1)} %shard_map.85.refs_0_, bf16[512,512]{1,0:T(8,128)(2,1)S(1)} %collective-permute-done.27.refs_1_, ...), custom_call_target="tpu_custom_call" | custom-call | flops 1073741824 | bytes 4718592 | tf_op jit(solution)/shard_map/pallas_call | solution.py:625
  217.0 2.1 collective-permute-start.34
  219.1 13.7 %collective-permute-done.50.refs_1_ = bf16[128,2560]{1,0:T(8,128)(2,1)S(1)} collective-permute-done((bf16[128,2560]{1,0:T(8,128)(2,1)S(1)}, bf16[128,2560]{1,0:T(8,128)(2,1)S(1)}, u32[]{:S(2)}, u32[]{:S(2)}) %collective-permute-start.50) | collective-permute-done | bytes 655392 | tf_op jit(solution)/shard_map/ppermute | solution.py:67
  233.3 2.8 %collective-permute-done.51.refs_2_ = bf16[128,2560]{1,0:T(8,128)(2,1)S(1)} collective-permute-done((bf16[128,2560]{1,0:T(8,128)(2,1)S(1)}, bf16[128,2560]{1,0:T(8,128)(2,1)S(1)}, u32[]{:S(2)}, u32[]{:S(2)}) %collective-permute-start.51) | collective-permute-done | bytes 655392 | tf_op jit(solution)/shard_map/ppermute | solution.py:67
  236.1 1.1 collective-permute-start.39
  237.3 2.0 collective-permute-start.35
  239.3 3.5 %collective-permute-start.36 = (bf16[128,2048]{1,0:T(8,128)(2,1)S(1)}, bf16[128,2048]{1,0:T(8,128)(2,1)S(1)}, u32[]{:S(2)}, u32[]{:S(2)}) collective-permute-start(bf16[128,2048]{1,0:T(8,128)(2,1)S(1)} %get-tuple-element.89), channel_id=1, source_target_pairs={{0,32},{1,33},{2,34},{3,35},{4,36},{5,37},{6,38},{7,39},{8,40},{9,... | collective-permute-start | bytes 1572872 | tf_op jit(solution)/shard_map/ppermute | solution.py:67
  243.9 26.4 %all_to_all.15.new = bf16[8,128,256]{2,1,0:T(8,128)(2,1)S(1)} all-to-all(bf16[8,128,256]{2,1,0:T(8,128)(2,1)} %turn_back.1), channel_id=1, replica_groups=mesh['xl'=2,'z'=4,'y'=4,'xh'=2,'core'=2] {'xl','z'}, dimensions={0} | all-to-all | bytes 1048576 | tf_op jit(solution)/shard_map/all_to_all | solution.py:699
  271.2 3.6 %shard_map.90.refs_4_ = bf16[128,26624]{1,0:T(8,128)(2,1)} custom-call(s32[8]{0:T(128)S(1)} %copy-done.30, bf16[128,2560]{1,0:T(8,128)(2,1)S(1)} %copy-done.21, bf16[128,2560]{1,0:T(8,128)(2,1)S(1)} %collective-permute-done.50.refs_1_, bf16[128,2560]{1,0:T(8,128)(2,1)S(1)} %collective-permute-done.51.refs_2_, ...), custom_call_target="tpu_custom_call" | custom-call | bytes 5242880 | tf_op jit(solution)/shard_map/pallas_call | solution.py:228
  274.9 2.5 shard_map.91.refs_4_
  277.4 2.4 shard_map.92
  (142 shorter events, 25.4 us)
Async XLA Ops:
  4.4 15.6 %collective-permute-start = (bf16[128,2048]{1,0:T(8,128)(2,1)}, bf16[128,2048]{1,0:T(8,128)(2,1)S(1)}, u32[]{:S(2)}, u32[]{:S(2)}) collective-permute-start(bf16[128,2048]{1,0:T(8,128)(2,1)} %get-tuple-element.54), channel_id=1, source_target_pairs={{0,4},{1,5},{2,6},{3,7},{4,8},{5,9},{6,10},{7,11},{8,12},{9,13},{1... | collective-permute-start | bytes 1572872 | tf_op jit(solution)/shard_map/ppermute | solution.py:67
  9.8 31.1 %collective-permute-start.3 = (bf16[128,2560]{1,0:T(8,128)(2,1)}, bf16[128,2560]{1,0:T(8,128)(2,1)S(1)}, u32[]{:S(2)}, u32[]{:S(2)}) collective-permute-start(bf16[128,2560]{1,0:T(8,128)(2,1)} %get-tuple-element.58), channel_id=1, source_target_pairs={{0,16},{1,17},{2,18},{3,19},{4,20},{5,21},{6,22},{7,23},{8,24},{9,... | collective-permute-start | bytes 1966088 | tf_op jit(solution)/shard_map/ppermute | solution.py:67
  11.9 30.4 %collective-permute-start.4 = (bf16[128,2560]{1,0:T(8,128)(2,1)}, bf16[128,2560]{1,0:T(8,128)(2,1)}, u32[]{:S(2)}, u32[]{:S(2)}) collective-permute-start(bf16[128,2560]{1,0:T(8,128)(2,1)} %get-tuple-element.59), channel_id=1, source_target_pairs={{0,48},{1,49},{2,50},{3,51},{4,52},{5,53},{6,54},{7,55},{8,56},{9,... | collective-permute-start | bytes 1966088 | tf_op jit(solution)/shard_map/ppermute | solution.py:67
  11.9 31.5 %collective-permute-start.5 = (bf16[128,2560]{1,0:T(8,128)(2,1)}, bf16[128,2560]{1,0:T(8,128)(2,1)}, u32[]{:S(2)}, u32[]{:S(2)}) collective-permute-start(bf16[128,2560]{1,0:T(8,128)(2,1)} %get-tuple-element.60), channel_id=1, source_target_pairs={{0,32},{1,33},{2,34},{3,35},{4,36},{5,37},{6,38},{7,39},{8,40},{9,... | collective-permute-start | bytes 1966088 | tf_op jit(solution)/shard_map/ppermute | solution.py:67
  15.2 23.7 %collective-permute-start.1 = (bf16[128,2048]{1,0:T(8,128)(2,1)}, bf16[128,2048]{1,0:T(8,128)(2,1)}, u32[]{:S(2)}, u32[]{:S(2)}) collective-permute-start(bf16[128,2048]{1,0:T(8,128)(2,1)} %get-tuple-element.55), channel_id=1, source_target_pairs={{0,12},{1,13},{2,14},{3,15},{4,0},{5,1},{6,2},{7,3},{8,4},{9,5},{1... | collective-permute-start | bytes 1572872 | tf_op jit(solution)/shard_map/ppermute | solution.py:67
  20.8 22.7 %copy-start = (bf16[2048,512]{1,0:T(8,128)(2,1)S(1)}, bf16[2048,512]{1,0:T(8,128)(2,1)}, u32[]{:S(2)}) copy-start(bf16[2048,512]{1,0:T(8,128)(2,1)} %refs_8_.5) | copy-start | bytes 6291460
  20.8 22.7 %copy-start.5 = (bf16[128,2560]{1,0:T(8,128)(2,1)S(1)}, bf16[128,2560]{1,0:T(8,128)(2,1)}, u32[]{:S(2)}) copy-start(bf16[128,2560]{1,0:T(8,128)(2,1)} %get-tuple-element.57.refs_4_) | copy-start | bytes 1966084
  20.8 22.7 %copy-start.16 = (bf16[128,2048]{1,0:T(8,128)(2,1)S(1)}, bf16[128,2048]{1,0:T(8,128)(2,1)}, u32[]{:S(2)}) copy-start(bf16[128,2048]{1,0:T(8,128)(2,1)} %get-tuple-element.53.refs_0_) | copy-start | bytes 1572868
  20.8 22.7 %copy-start.30 = (s32[8]{0:T(128)S(1)}, s32[8]{0:T(128)}, u32[]{:S(2)}) copy-start(s32[8]{0:T(128)} %compare_select_fusion.6.where) | copy-start | bytes 100
  20.8 18.6 %collective-permute-start.2 = (bf16[128,2048]{1,0:T(8,128)(2,1)}, bf16[128,2048]{1,0:T(8,128)(2,1)}, u32[]{:S(2)}, u32[]{:S(2)}) collective-permute-start(bf16[128,2048]{1,0:T(8,128)(2,1)} %get-tuple-element.56), channel_id=1, source_target_pairs={{0,8},{1,9},{2,10},{3,11},{4,12},{5,13},{6,14},{7,15},{8,0},{9,1},... | collective-permute-start | bytes 1572872 | tf_op jit(solution)/shard_map/ppermute | solution.py:67
  38.9 29.0 %collective-permute-start.13 = (bf16[128,3072]{1,0:T(8,128)(2,1)}, bf16[128,3072]{1,0:T(8,128)(2,1)S(1)}, u32[]{:S(2)}, u32[]{:S(2)}) collective-permute-start(bf16[128,3072]{1,0:T(8,128)(2,1)} %get-tuple-element.72), channel_id=1, source_target_pairs={{0,64},{1,65},{2,66},{3,67},{4,68},{5,69},{6,70},{7,71},{8,72},{9,... | collective-permute-start | bytes 2359304 | tf_op jit(solution)/shard_map/ppermute | solution.py:67
  39.4 29.7 %collective-permute-start.14 = (bf16[128,3072]{1,0:T(8,128)(2,1)}, bf16[128,3072]{1,0:T(8,128)(2,1)S(1)}, u32[]{:S(2)}, u32[]{:S(2)}) collective-permute-start(bf16[128,3072]{1,0:T(8,128)(2,1)} %get-tuple-element.73), channel_id=1, source_target_pairs={{0,66},{1,67},{2,64},{3,65},{4,70},{5,71},{6,68},{7,69},{8,74},{9,... | collective-permute-start | bytes 2359304 | tf_op jit(solution)/shard_map/ppermute | solution.py:67
  40.9 26.9 %collective-permute-start.15 = (bf16[128,2560]{1,0:T(8,128)(2,1)}, bf16[128,2560]{1,0:T(8,128)(2,1)S(1)}, u32[]{:S(2)}, u32[]{:S(2)}) collective-permute-start(bf16[128,2560]{1,0:T(8,128)(2,1)} %get-tuple-element.74), channel_id=1, source_target_pairs={{0,2},{1,3},{2,0},{3,1},{4,6},{5,7},{6,4},{7,5},{8,10},{9,11},{10,... | collective-permute-start | bytes 1966088 | tf_op jit(solution)/shard_map/ppermute | solution.py:67
  44.5 24.6 %copy-start.9 = (bf16[128,2560]{1,0:T(8,128)(2,1)S(1)}, bf16[128,2560]{1,0:T(8,128)(2,1)}, u32[]{:S(2)}) copy-start(bf16[128,2560]{1,0:T(8,128)(2,1)} %get-tuple-element.71.refs_0_) | copy-start | bytes 1966084
  49.5 44.9 %collective-permute-start.6 = (bf16[2048,512]{1,0:T(8,128)(2,1)}, bf16[2048,512]{1,0:T(8,128)(2,1)}, u32[]{:S(2)}, u32[]{:S(2)}) collective-permute-start(bf16[2048,512]{1,0:T(8,128)(2,1)} %get-tuple-element.61), channel_id=1, source_target_pairs={{0,1},{1,0},{2,3},{3,2},{4,5},{5,4},{6,7},{7,6},{8,9},{9,8},{10,11... | collective-permute-start | bytes 6291464 | tf_op jit(solution)/shard_map/ppermute | solution.py:67
  72.3 9.4 %collective-permute-start.16 = (bf16[1280,512]{1,0:T(8,128)(2,1)}, bf16[1280,512]{1,0:T(8,128)(2,1)}, u32[]{:S(2)}, u32[]{:S(2)}) collective-permute-start(bf16[1280,512]{1,0:T(8,128)(2,1)} %get-tuple-element.75), channel_id=1, source_target_pairs={{0,1},{1,0},{2,3},{3,2},{4,5},{5,4},{6,7},{7,6},{8,9},{9,8},{10,11... | collective-permute-start | bytes 3932168 | tf_op jit(solution)/shard_map/ppermute | solution.py:67
  75.2 28.7 %all-to-all-start = ((bf16[8,256,256]{2,1,0:T(8,128)(2,1)}), bf16[8,256,256]{2,1,0:T(8,128)(2,1)S(1)}, u32[]{:S(2)}, u32[]{:S(2)}) async-start(bf16[8,256,256]{2,1,0:T(8,128)(2,1)} %cut_moments.1), calls=%async_computation | async-start | bytes 2097152 | tf_op jit(solution)/shard_map/all_to_all | solution.py:667
  91.8 18.9 %collective-permute-start.17 = (bf16[320,512]{1,0:T(8,128)(2,1)}, bf16[320,512]{1,0:T(8,128)(2,1)}, u32[]{:S(2)}, u32[]{:S(2)}) collective-permute-start(bf16[320,512]{1,0:T(8,128)(2,1)} %get-tuple-element.78), channel_id=1, source_target_pairs={{0,16},{1,17},{2,18},{3,19},{4,20},{5,21},{6,22},{7,23},{8,24},{9,... | collective-permute-start | bytes 983048 | tf_op jit(solution)/shard_map/ppermute | solution.py:67
  93.3 27.2 %collective-permute-start.18 = (bf16[320,512]{1,0:T(8,128)(2,1)}, bf16[320,512]{1,0:T(8,128)(2,1)}, u32[]{:S(2)}, u32[]{:S(2)}) collective-permute-start(bf16[320,512]{1,0:T(8,128)(2,1)} %get-tuple-element.79), channel_id=1, source_target_pairs={{0,32},{1,33},{2,34},{3,35},{4,36},{5,37},{6,38},{7,39},{8,40},{9,... | collective-permute-start | bytes 983048 | tf_op jit(solution)/shard_map/ppermute | solution.py:67
  101.3 27.5 %collective-permute-start.7 = (bf16[512,512]{1,0:T(8,128)(2,1)}, bf16[512,512]{1,0:T(8,128)(2,1)}, u32[]{:S(2)}, u32[]{:S(2)}) collective-permute-start(bf16[512,512]{1,0:T(8,128)(2,1)} %get-tuple-element.64), channel_id=1, source_target_pairs={{0,64},{1,5},{2,66},{3,7},{4,68},{5,9},{6,70},{7,11},{8,72},{9,13}... | collective-permute-start | bytes 1572872 | tf_op jit(solution)/shard_map/ppermute | solution.py:67
  101.3 27.5 %collective-permute-start.8 = (bf16[512,512]{1,0:T(8,128)(2,1)}, bf16[512,512]{1,0:T(8,128)(2,1)}, u32[]{:S(2)}, u32[]{:S(2)}) collective-permute-start(bf16[512,512]{1,0:T(8,128)(2,1)} %get-tuple-element.65), channel_id=1, source_target_pairs={{0,2},{1,9},{2,0},{3,11},{4,6},{5,13},{6,4},{7,15},{8,10},{9,1},{1... | collective-permute-start | bytes 1572872 | tf_op jit(solution)/shard_map/ppermute | solution.py:67
  103.4 25.4 %collective-permute-start.9 = (bf16[512,512]{1,0:T(8,128)(2,1)}, bf16[512,512]{1,0:T(8,128)(2,1)}, u32[]{:S(2)}, u32[]{:S(2)}) collective-permute-start(bf16[512,512]{1,0:T(8,128)(2,1)} %get-tuple-element.66), channel_id=1, source_target_pairs={{0,66},{1,13},{2,64},{3,15},{4,70},{5,1},{6,68},{7,3},{8,74},{9,5}... | collective-permute-start | bytes 1572872 | tf_op jit(solution)/shard_map/ppermute | solution.py:67
  104.7 15.8 %all-to-all-start.1 = ((bf16[8,32,512]{2,1,0:T(8,128)(2,1)}), bf16[8,32,512]{2,1,0:T(8,128)(2,1)S(1)}, u32[]{:S(2)}, u32[]{:S(2)}) async-start(bf16[8,32,512]{2,1,0:T(8,128)(2,1)} %sum_margin.1), calls=%async_computation.1 | async-start | bytes 524288 | tf_op jit(solution)/shard_map/all_to_all | solution.py:669
  110.7 12.5 %collective-permute-start.19 = (bf16[320,512]{1,0:T(8,128)(2,1)}, bf16[320,512]{1,0:T(8,128)(2,1)}, u32[]{:S(2)}, u32[]{:S(2)}) collective-permute-start(bf16[320,512]{1,0:T(8,128)(2,1)} %copy-done.33), channel_id=1, source_target_pairs={{0,48},{1,49},{2,50},{3,51},{4,52},{5,53},{6,54},{7,55},{8,56},{9,... | collective-permute-start | bytes 983048 | tf_op jit(solution)/shard_map/ppermute | solution.py:67
  120.5 17.0 %collective-permute-start.23 = (bf16[256,512]{1,0:T(8,128)(2,1)S(1)}, bf16[256,512]{1,0:T(8,128)(2,1)S(1)}, u32[]{:S(2)}, u32[]{:S(2)}) collective-permute-start(bf16[256,512]{1,0:T(8,128)(2,1)S(1)} %bitcast.1), channel_id=1, source_target_pairs={{0,1},{1,0},{2,3},{3,2},{4,5},{5,4},{6,7},{7,6},{8,9},{9,8},{10,11... | collective-permute-start | bytes 786440 | tf_op jit(solution)/shard_map/ppermute | solution.py:67
  126.3 13.1 %collective-permute-start.20 = (bf16[80,512]{1,0:T(8,128)(2,1)}, bf16[80,512]{1,0:T(8,128)(2,1)S(1)}, u32[]{:S(2)}, u32[]{:S(2)}) collective-permute-start(bf16[80,512]{1,0:T(8,128)(2,1)} %get-tuple-element.82), channel_id=1, source_target_pairs={{0,4},{1,5},{2,6},{3,7},{4,8},{5,9},{6,10},{7,11},{8,12},{9,13},{1... | collective-permute-start | bytes 245768 | tf_op jit(solution)/shard_map/ppermute | solution.py:67
  129.8 9.6 %copy-start.34 = (bf16[80,512]{1,0:T(8,128)(2,1)S(1)}, bf16[80,512]{1,0:T(8,128)(2,1)}, u32[]{:S(2)}) copy-start(bf16[80,512]{1,0:T(8,128)(2,1)} %get-tuple-element.84) | copy-start | bytes 245764
  129.9 14.0 %copy-start.32 = (bf16[80,512]{1,0:T(8,128)(2,1)S(1)}, bf16[80,512]{1,0:T(8,128)(2,1)}, u32[]{:S(2)}) copy-start(bf16[80,512]{1,0:T(8,128)(2,1)} %get-tuple-element.81.refs_4_) | copy-start | bytes 245764
  132.4 60.9 %copy-start.26 = (bf16[512,512]{1,0:T(8,128)(2,1)S(1)}, bf16[512,512]{1,0:T(8,128)(2,1)}, u32[]{:S(2)}) copy-start(bf16[512,512]{1,0:T(8,128)(2,1)} %get-tuple-element.76.refs_6_.refs_8_) | copy-start | bytes 1572868
  132.4 11.5 %collective-permute-start.10 = (bf16[128,512]{1,0:T(8,128)(2,1)}, bf16[128,512]{1,0:T(8,128)(2,1)S(1)}, u32[]{:S(2)}, u32[]{:S(2)}) collective-permute-start(bf16[128,512]{1,0:T(8,128)(2,1)} %get-tuple-element.68), channel_id=1, source_target_pairs={{0,16},{1,65},{2,18},{3,67},{4,20},{5,69},{6,22},{7,71},{8,24},{9,... | collective-permute-start | bytes 393224 | tf_op jit(solution)/shard_map/ppermute | solution.py:67
  133.8 10.1 %collective-permute-start.11 = (bf16[128,512]{1,0:T(8,128)(2,1)}, bf16[128,512]{1,0:T(8,128)(2,1)S(1)}, u32[]{:S(2)}, u32[]{:S(2)}) collective-permute-start(bf16[128,512]{1,0:T(8,128)(2,1)} %get-tuple-element.69), channel_id=1, source_target_pairs={{0,32},{1,3},{2,34},{3,1},{4,36},{5,7},{6,38},{7,5},{8,40},{9,11},... | collective-permute-start | bytes 393224 | tf_op jit(solution)/shard_map/ppermute | solution.py:67
  135.5 8.4 %collective-permute-start.12 = (bf16[128,512]{1,0:T(8,128)(2,1)}, bf16[128,512]{1,0:T(8,128)(2,1)S(1)}, u32[]{:S(2)}, u32[]{:S(2)}) collective-permute-start(bf16[128,512]{1,0:T(8,128)(2,1)} %get-tuple-element.70), channel_id=1, source_target_pairs={{0,48},{1,67},{2,50},{3,65},{4,52},{5,71},{6,54},{7,69},{8,56},{9,... | collective-permute-start | bytes 393224 | tf_op jit(solution)/shard_map/ppermute | solution.py:67
  137.5 5.9 %collective-permute-start.21 = (bf16[80,512]{1,0:T(8,128)(2,1)S(1)}, bf16[80,512]{1,0:T(8,128)(2,1)S(1)}, u32[]{:S(2)}, u32[]{:S(2)}) collective-permute-start(bf16[80,512]{1,0:T(8,128)(2,1)S(1)} %copy-done.35), channel_id=1, source_target_pairs={{0,8},{1,9},{2,10},{3,11},{4,12},{5,13},{6,14},{7,15},{8,0},{9,1},... | collective-permute-start | bytes 245768 | tf_op jit(solution)/shard_map/ppermute | solution.py:67
  139.4 4.4 %collective-permute-start.22 = (bf16[80,512]{1,0:T(8,128)(2,1)S(1)}, bf16[80,512]{1,0:T(8,128)(2,1)S(1)}, u32[]{:S(2)}, u32[]{:S(2)}) collective-permute-start(bf16[80,512]{1,0:T(8,128)(2,1)S(1)} %copy-done.34), channel_id=1, source_target_pairs={{0,12},{1,13},{2,14},{3,15},{4,0},{5,1},{6,2},{7,3},{8,4},{9,5},{1... | collective-permute-start | bytes 245768 | tf_op jit(solution)/shard_map/ppermute | solution.py:67
  146.2 4.9 %collective-permute-start.42 = (bf16[80,512]{1,0:T(8,128)(2,1)S(1)}, bf16[80,512]{1,0:T(8,128)(2,1)S(1)}, u32[]{:S(2)}, u32[]{:S(2)}) collective-permute-start(bf16[80,512]{1,0:T(8,128)(2,1)S(1)} %get-tuple-element.94.refs_0_), channel_id=1, source_target_pairs={{0,12},{1,13},{2,14},{3,15},{4,0},{5,1},{6,2},{7,3},{8,4},{9,5},{1... | collective-permute-start | bytes 245768 | tf_op jit(solution)/shard_map/ppermute | solution.py:67
  148.2 6.0 %collective-permute-start.41 = (bf16[80,512]{1,0:T(8,128)(2,1)S(1)}, bf16[80,512]{1,0:T(8,128)(2,1)S(1)}, u32[]{:S(2)}, u32[]{:S(2)}) collective-permute-start(bf16[80,512]{1,0:T(8,128)(2,1)S(1)} %get-tuple-element.94.refs_0_), channel_id=1, source_target_pairs={{0,8},{1,9},{2,10},{3,11},{4,12},{5,13},{6,14},{7,15},{8,0},{9,1},... | collective-permute-start | bytes 245768 | tf_op jit(solution)/shard_map/ppermute | solution.py:67
  148.8 6.2 %collective-permute-start.40 = (bf16[80,512]{1,0:T(8,128)(2,1)S(1)}, bf16[80,512]{1,0:T(8,128)(2,1)S(1)}, u32[]{:S(2)}, u32[]{:S(2)}) collective-permute-start(bf16[80,512]{1,0:T(8,128)(2,1)S(1)} %get-tuple-element.94.refs_0_), channel_id=1, source_target_pairs={{0,4},{1,5},{2,6},{3,7},{4,8},{5,9},{6,10},{7,11},{8,12},{9,13},{1... | collective-permute-start | bytes 245768 | tf_op jit(solution)/shard_map/ppermute | solution.py:67
  155.6 19.2 %collective-permute-start.46 = (bf16[320,512]{1,0:T(8,128)(2,1)S(1)}, bf16[320,512]{1,0:T(8,128)(2,1)S(1)}, u32[]{:S(2)}, u32[]{:S(2)}) collective-permute-start(bf16[320,512]{1,0:T(8,128)(2,1)S(1)} %shard_map.88.refs_0_), channel_id=1, source_target_pairs={{0,1},{1,0},{2,3},{3,2},{4,5},{5,4},{6,7},{7,6},{8,9},{9,8},{10,11... | collective-permute-start | bytes 983048 | tf_op jit(solution)/shard_map/ppermute | solution.py:67
  155.7 20.9 %collective-permute-start.45 = (bf16[320,512]{1,0:T(8,128)(2,1)S(1)}, bf16[320,512]{1,0:T(8,128)(2,1)S(1)}, u32[]{:S(2)}, u32[]{:S(2)}) collective-permute-start(bf16[320,512]{1,0:T(8,128)(2,1)S(1)} %shard_map.88.refs_0_), channel_id=1, source_target_pairs={{0,48},{1,49},{2,50},{3,51},{4,52},{5,53},{6,54},{7,55},{8,56},{9,... | collective-permute-start | bytes 983048 | tf_op jit(solution)/shard_map/ppermute | solution.py:67
  156.9 15.3 %collective-permute-start.26 = (bf16[128,512]{1,0:T(8,128)(2,1)S(1)}, bf16[128,512]{1,0:T(8,128)(2,1)S(1)}, u32[]{:S(2)}, u32[]{:S(2)}) collective-permute-start(bf16[128,512]{1,0:T(8,128)(2,1)S(1)} %get-tuple-element.85.refs_0_), channel_id=1, source_target_pairs={{0,48},{1,67},{2,50},{3,65},{4,52},{5,71},{6,54},{7,69},{8,56},{9,... | collective-permute-start | bytes 393224 | tf_op jit(solution)/shard_map/ppermute | solution.py:67
  157.4 14.8 %collective-permute-start.25 = (bf16[128,512]{1,0:T(8,128)(2,1)S(1)}, bf16[128,512]{1,0:T(8,128)(2,1)S(1)}, u32[]{:S(2)}, u32[]{:S(2)}) collective-permute-start(bf16[128,512]{1,0:T(8,128)(2,1)S(1)} %get-tuple-element.85.refs_0_), channel_id=1, source_target_pairs={{0,32},{1,3},{2,34},{3,1},{4,36},{5,7},{6,38},{7,5},{8,40},{9,11},... | collective-permute-start | bytes 393224 | tf_op jit(solution)/shard_map/ppermute | solution.py:67
  159.3 12.9 %collective-permute-start.24 = (bf16[128,512]{1,0:T(8,128)(2,1)S(1)}, bf16[128,512]{1,0:T(8,128)(2,1)S(1)}, u32[]{:S(2)}, u32[]{:S(2)}) collective-permute-start(bf16[128,512]{1,0:T(8,128)(2,1)S(1)} %get-tuple-element.85.refs_0_), channel_id=1, source_target_pairs={{0,16},{1,65},{2,18},{3,67},{4,20},{5,69},{6,22},{7,71},{8,24},{9,... | collective-permute-start | bytes 393224 | tf_op jit(solution)/shard_map/ppermute | solution.py:67
  172.2 8.6 %collective-permute-start.44 = (bf16[320,512]{1,0:T(8,128)(2,1)S(1)}, bf16[320,512]{1,0:T(8,128)(2,1)S(1)}, u32[]{:S(2)}, u32[]{:S(2)}) collective-permute-start(bf16[320,512]{1,0:T(8,128)(2,1)S(1)} %shard_map.88.refs_0_), channel_id=1, source_target_pairs={{0,32},{1,33},{2,34},{3,35},{4,36},{5,37},{6,38},{7,39},{8,40},{9,... | collective-permute-start | bytes 983048 | tf_op jit(solution)/shard_map/ppermute | solution.py:67
  172.2 10.2 %collective-permute-start.43 = (bf16[320,512]{1,0:T(8,128)(2,1)S(1)}, bf16[320,512]{1,0:T(8,128)(2,1)S(1)}, u32[]{:S(2)}, u32[]{:S(2)}) collective-permute-start(bf16[320,512]{1,0:T(8,128)(2,1)S(1)} %shard_map.88.refs_0_), channel_id=1, source_target_pairs={{0,16},{1,17},{2,18},{3,19},{4,20},{5,21},{6,22},{7,23},{8,24},{9,... | collective-permute-start | bytes 983048 | tf_op jit(solution)/shard_map/ppermute | solution.py:67
  172.8 10.5 %collective-permute-start.29 = (bf16[512,512]{1,0:T(8,128)(2,1)S(1)}, bf16[512,512]{1,0:T(8,128)(2,1)S(1)}, u32[]{:S(2)}, u32[]{:S(2)}) collective-permute-start(bf16[512,512]{1,0:T(8,128)(2,1)S(1)} %shard_map.85.refs_0_), channel_id=1, source_target_pairs={{0,66},{1,13},{2,64},{3,15},{4,70},{5,1},{6,68},{7,3},{8,74},{9,5}... | collective-permute-start | bytes 1572872 | tf_op jit(solution)/shard_map/ppermute | solution.py:67
  174.8 14.6 %collective-permute-start.28 = (bf16[512,512]{1,0:T(8,128)(2,1)S(1)}, bf16[512,512]{1,0:T(8,128)(2,1)S(1)}, u32[]{:S(2)}, u32[]{:S(2)}) collective-permute-start(bf16[512,512]{1,0:T(8,128)(2,1)S(1)} %shard_map.85.refs_0_), channel_id=1, source_target_pairs={{0,2},{1,9},{2,0},{3,11},{4,6},{5,13},{6,4},{7,15},{8,10},{9,1},{1... | collective-permute-start | bytes 1572872 | tf_op jit(solution)/shard_map/ppermute | solution.py:67
  176.6 13.1 %collective-permute-start.27 = (bf16[512,512]{1,0:T(8,128)(2,1)S(1)}, bf16[512,512]{1,0:T(8,128)(2,1)S(1)}, u32[]{:S(2)}, u32[]{:S(2)}) collective-permute-start(bf16[512,512]{1,0:T(8,128)(2,1)S(1)} %shard_map.85.refs_0_), channel_id=1, source_target_pairs={{0,64},{1,5},{2,66},{3,7},{4,68},{5,9},{6,70},{7,11},{8,72},{9,13}... | collective-permute-start | bytes 1572872 | tf_op jit(solution)/shard_map/ppermute | solution.py:67
  180.7 9.2 %collective-permute-start.49 = (bf16[320,512]{1,0:T(8,128)(2,1)S(1)}, bf16[320,512]{1,0:T(8,128)(2,1)S(1)}, u32[]{:S(2)}, u32[]{:S(2)}) collective-permute-start(bf16[320,512]{1,0:T(8,128)(2,1)S(1)} %collective-permute-done.45.refs_3_), channel_id=1, source_target_pairs={{0,1},{1,0},{2,3},{3,2},{4,5},{5,4},{6,7},{7,6},{8,9},{9,8},{10,11... | collective-permute-start | bytes 983048 | tf_op jit(solution)/shard_map/ppermute | solution.py:67
  182.4 7.9 %collective-permute-start.48 = (bf16[320,512]{1,0:T(8,128)(2,1)S(1)}, bf16[320,512]{1,0:T(8,128)(2,1)S(1)}, u32[]{:S(2)}, u32[]{:S(2)}) collective-permute-start(bf16[320,512]{1,0:T(8,128)(2,1)S(1)} %collective-permute-done.44.refs_2_), channel_id=1, source_target_pairs={{0,1},{1,0},{2,3},{3,2},{4,5},{5,4},{6,7},{7,6},{8,9},{9,8},{10,11... | collective-permute-start | bytes 983048 | tf_op jit(solution)/shard_map/ppermute | solution.py:67
  183.2 21.2 %collective-permute-start.30 = (bf16[512,512]{1,0:T(8,128)(2,1)S(1)}, bf16[512,512]{1,0:T(8,128)(2,1)S(1)}, u32[]{:S(2)}, u32[]{:S(2)}) collective-permute-start(bf16[512,512]{1,0:T(8,128)(2,1)S(1)} %shard_map.85.refs_0_), channel_id=1, source_target_pairs={{0,1},{1,0},{2,3},{3,2},{4,5},{5,4},{6,7},{7,6},{8,9},{9,8},{10,11... | collective-permute-start | bytes 1572872 | tf_op jit(solution)/shard_map/ppermute | solution.py:67
  189.4 15.0 %collective-permute-start.33 = (bf16[512,512]{1,0:T(8,128)(2,1)S(1)}, bf16[512,512]{1,0:T(8,128)(2,1)S(1)}, u32[]{:S(2)}, u32[]{:S(2)}) collective-permute-start(bf16[512,512]{1,0:T(8,128)(2,1)S(1)} %collective-permute-done.29.refs_3_), channel_id=1, source_target_pairs={{0,1},{1,0},{2,3},{3,2},{4,5},{5,4},{6,7},{7,6},{8,9},{9,8},{10,11... | collective-permute-start | bytes 1572872 | tf_op jit(solution)/shard_map/ppermute | solution.py:67
  189.8 16.3 %collective-permute-start.32 = (bf16[512,512]{1,0:T(8,128)(2,1)S(1)}, bf16[512,512]{1,0:T(8,128)(2,1)S(1)}, u32[]{:S(2)}, u32[]{:S(2)}) collective-permute-start(bf16[512,512]{1,0:T(8,128)(2,1)S(1)} %collective-permute-done.28.refs_2_), channel_id=1, source_target_pairs={{0,1},{1,0},{2,3},{3,2},{4,5},{5,4},{6,7},{7,6},{8,9},{9,8},{10,11... | collective-permute-start | bytes 1572872 | tf_op jit(solution)/shard_map/ppermute | solution.py:67
  189.9 16.2 %collective-permute-start.31 = (bf16[512,512]{1,0:T(8,128)(2,1)S(1)}, bf16[512,512]{1,0:T(8,128)(2,1)S(1)}, u32[]{:S(2)}, u32[]{:S(2)}) collective-permute-start(bf16[512,512]{1,0:T(8,128)(2,1)S(1)} %collective-permute-done.27.refs_1_), channel_id=1, source_target_pairs={{0,1},{1,0},{2,3},{3,2},{4,5},{5,4},{6,7},{7,6},{8,9},{9,8},{10,11... | collective-permute-start | bytes 1572872 | tf_op jit(solution)/shard_map/ppermute | solution.py:67
  190.3 3.0 %collective-permute-start.47 = (bf16[320,512]{1,0:T(8,128)(2,1)S(1)}, bf16[320,512]{1,0:T(8,128)(2,1)S(1)}, u32[]{:S(2)}, u32[]{:S(2)}) collective-permute-start(bf16[320,512]{1,0:T(8,128)(2,1)S(1)} %collective-permute-done.43.refs_1_), channel_id=1, source_target_pairs={{0,1},{1,0},{2,3},{3,2},{4,5},{5,4},{6,7},{7,6},{8,9},{9,8},{10,11... | collective-permute-start | bytes 983048 | tf_op jit(solution)/shard_map/ppermute | solution.py:67
  202.1 30.7 %collective-permute-start.50 = (bf16[128,2560]{1,0:T(8,128)(2,1)S(1)}, bf16[128,2560]{1,0:T(8,128)(2,1)S(1)}, u32[]{:S(2)}, u32[]{:S(2)}) collective-permute-start(bf16[128,2560]{1,0:T(8,128)(2,1)S(1)} %get-tuple-element.96), channel_id=1, source_target_pairs={{0,64},{1,65},{2,66},{3,67},{4,68},{5,69},{6,70},{7,71},{8,72},{9,... | collective-permute-start | bytes 1966088 | tf_op jit(solution)/shard_map/ppermute | solution.py:67
  204.4 31.7 %collective-permute-start.51 = (bf16[128,2560]{1,0:T(8,128)(2,1)S(1)}, bf16[128,2560]{1,0:T(8,128)(2,1)S(1)}, u32[]{:S(2)}, u32[]{:S(2)}) collective-permute-start(bf16[128,2560]{1,0:T(8,128)(2,1)S(1)} %get-tuple-element.97), channel_id=1, source_target_pairs={{0,66},{1,67},{2,64},{3,65},{4,70},{5,71},{6,68},{7,69},{8,74},{9,... | collective-permute-start | bytes 1966088 | tf_op jit(solution)/shard_map/ppermute | solution.py:67
  204.4 32.9 %collective-permute-start.52 = (bf16[128,2560]{1,0:T(8,128)(2,1)S(1)}, bf16[128,2560]{1,0:T(8,128)(2,1)S(1)}, u32[]{:S(2)}, u32[]{:S(2)}) collective-permute-start(bf16[128,2560]{1,0:T(8,128)(2,1)S(1)} %get-tuple-element.98), channel_id=1, source_target_pairs={{0,2},{1,3},{2,0},{3,1},{4,6},{5,7},{6,4},{7,5},{8,10},{9,11},{10,... | collective-permute-start | bytes 1966088 | tf_op jit(solution)/shard_map/ppermute | solution.py:67
  210.4 28.9 %collective-permute-start.37 = (bf16[128,2048]{1,0:T(8,128)(2,1)S(1)}, bf16[128,2048]{1,0:T(8,128)(2,1)S(1)}, u32[]{:S(2)}, u32[]{:S(2)}) collective-permute-start(bf16[128,2048]{1,0:T(8,128)(2,1)S(1)} %get-tuple-element.91), channel_id=1, source_target_pairs={{0,4},{1,5},{2,6},{3,7},{4,8},{5,9},{6,10},{7,11},{8,12},{9,13},{1... | collective-permute-start | bytes 1572872 | tf_op jit(solution)/shard_map/ppermute | solution.py:67
  217.0 54.2 %copy-start.21 = (bf16[128,2560]{1,0:T(8,128)(2,1)S(1)}, bf16[128,2560]{1,0:T(8,128)(2,1)}, u32[]{:S(2)}) copy-start(bf16[128,2560]{1,0:T(8,128)(2,1)} %get-tuple-element.95.refs_0_) | copy-start | bytes 1966084
  217.0 60.3 %collective-permute-start.34 = (bf16[128,2048]{1,0:T(8,128)(2,1)S(1)}, bf16[128,2048]{1,0:T(8,128)(2,1)S(1)}, u32[]{:S(2)}, u32[]{:S(2)}) collective-permute-start(bf16[128,2048]{1,0:T(8,128)(2,1)S(1)} %get-tuple-element.87), channel_id=1, source_target_pairs={{0,16},{1,17},{2,18},{3,19},{4,20},{5,21},{6,22},{7,23},{8,24},{9,... | collective-permute-start | bytes 1572872 | tf_op jit(solution)/shard_map/ppermute | solution.py:67
  232.8 42.1 %collective-permute-start.38 = (bf16[128,2048]{1,0:T(8,128)(2,1)S(1)}, bf16[128,2048]{1,0:T(8,128)(2,1)S(1)}, u32[]{:S(2)}, u32[]{:S(2)}) collective-permute-start(bf16[128,2048]{1,0:T(8,128)(2,1)S(1)} %get-tuple-element.92), channel_id=1, source_target_pairs={{0,12},{1,13},{2,14},{3,15},{4,0},{5,1},{6,2},{7,3},{8,4},{9,5},{1... | collective-permute-start | bytes 1572872 | tf_op jit(solution)/shard_map/ppermute | solution.py:67
  236.1 38.7 %collective-permute-start.39 = (bf16[128,2048]{1,0:T(8,128)(2,1)S(1)}, bf16[128,2048]{1,0:T(8,128)(2,1)S(1)}, u32[]{:S(2)}, u32[]{:S(2)}) collective-permute-start(bf16[128,2048]{1,0:T(8,128)(2,1)S(1)} %get-tuple-element.93), channel_id=1, source_target_pairs={{0,8},{1,9},{2,10},{3,11},{4,12},{5,13},{6,14},{7,15},{8,0},{9,1},... | collective-permute-start | bytes 1572872 | tf_op jit(solution)/shard_map/ppermute | solution.py:67
  237.3 40.1 %collective-permute-start.35 = (bf16[128,2048]{1,0:T(8,128)(2,1)S(1)}, bf16[128,2048]{1,0:T(8,128)(2,1)S(1)}, u32[]{:S(2)}, u32[]{:S(2)}) collective-permute-start(bf16[128,2048]{1,0:T(8,128)(2,1)S(1)} %get-tuple-element.88), channel_id=1, source_target_pairs={{0,48},{1,49},{2,50},{3,51},{4,52},{5,53},{6,54},{7,55},{8,56},{9,... | collective-permute-start | bytes 1572872 | tf_op jit(solution)/shard_map/ppermute | solution.py:67
  239.3 38.0 %collective-permute-start.36 = (bf16[128,2048]{1,0:T(8,128)(2,1)S(1)}, bf16[128,2048]{1,0:T(8,128)(2,1)S(1)}, u32[]{:S(2)}, u32[]{:S(2)}) collective-permute-start(bf16[128,2048]{1,0:T(8,128)(2,1)S(1)} %get-tuple-element.89), channel_id=1, source_target_pairs={{0,32},{1,33},{2,34},{3,35},{4,36},{5,37},{6,38},{7,39},{8,40},{9,... | collective-permute-start | bytes 1572872 | tf_op jit(solution)/shard_map/ppermute | solution.py:67
  (27 other events, 99.5 us)

commit v5 on v4

--- a/solution.py
+++ b/solution.py
@@ -20,8 +20,6 @@
 HBM = pl.BlockSpec(memory_space=pltpu.HBM)
 DMA = pltpu.SemaphoreType.DMA
 LIMIT = pltpu.CompilerParams(vmem_limit_bytes=16 * 2**20)
-ALL_OF_IT = pltpu.CompilerParams(vmem_limit_bytes=60 * 1024 * 1024)
-MOST_OF_IT = pltpu.CompilerParams(vmem_limit_bytes=57 * 2**20)
 
 
 def blocks_of(count, shape):
@@ -93,6 +91,10 @@
     if group == 0:
         return [(u_at * 512, 512)]
     return [one for v in range(4) for one in ((v * 256 + u_at * 64, 64), (1024 + v * 64 + u_at * 16, 16))]
+
+
+def in_hbm(array):
+    return pltpu.with_memory_space_constraint(array, pltpu.HBM)
 
 
 def rows_at(first, count):
@@ -173,9 +175,9 @@
         out_specs=[ANY] * 4,
         scratch_shapes=[pltpu.VMEM((4, 128, width), BF), DMA((4,)), DMA((4,))]
         + ([pltpu.VMEM((16, 128, 128), BF), DMA((16,))] if ring == "x" else []),
-        compiler_params=ALL_OF_IT if ring == "x" else MOST_OF_IT,
+        compiler_params=LIMIT,
         cost_estimate=estimate(0, 4 * 128 * width * 4),
-    )(where, grad, basis)
+    )(where, in_hbm(grad), basis)
 
 
 def unpack_kernel(ring, where, *refs):
@@ -258,75 +260,87 @@
 
 def project_kernel(group, own, where, *refs):
     count = 8 if group == 0 else 4
-    blocks, basis, refs = refs[:count], refs[count], refs[count + 1 :]
+    blocks, basis, refs = list(refs[:count]), refs[count], refs[count + 1 :]
     if own:
-        other, gathered, outs, (base, total, base_sem, out_sem) = refs[0], refs[1], refs[2:6], refs[6:]
+        other, gathered, outs, (base, total, mine, base_sem, out_sem, in_sem) = refs[0], refs[1], refs[2:6], refs[6:]
     else:
-        total, gathered, base, gather, base_sem, out_sem = refs
+        total, gathered, base, gather, mine, base_sem, out_sem, in_sem = refs
     chunk, tile = GROUPS[group][0], TILE[group]
-    core = place(where, "core")
-
-    def multiply(mine, base, first):
+    core, u = place(where, "core"), place(where, "u%d" % group)
+
+    def fetch(block, first):
+        copy = pltpu.make_async_copy(block.at[:, pl.ds(pl.multiple_of(first, 128), chunk)], mine, in_sem)
+        copy.start()
+        return copy
+
+    def multiply(far, base, first):
         @pl.loop(0, chunk // tile)
         def _(i):
             some = pl.ds(pl.multiple_of(i * tile, tile), tile)
             columns = pl.ds(pl.multiple_of(first + i * tile, 128), tile)
-            block = jnp.concatenate([ref[:, columns] for ref in mine], axis=0)
+            block = jnp.concatenate([mine[:, some]] + [ref[:, columns] for ref in far], axis=0)
             product = lax.dot_general(block, base[...], (((0,), (0,)), ((), ())), preferred_element_type=F32)
             if own:
                 product = product + other[some, :].astype(F32)
             total[some, :] = product.astype(BF)
+            if own and group == 0:
+                for j in range(4):
+
+                    @pl.when((u + j) % 4 == i)
+                    def _():
+                        pltpu.make_async_copy(total.at[some, :], outs[j], out_sem.at[j]).start()
+
+    def with_y():
+        copy = fetch(blocks[0], 0)
+        start_basis("y", where, blocks[:4], basis, base, base_sem)
+        wait_for(base, base_sem)
+        copy.wait()
+        multiply(blocks[1:4], base, 0)
 
     if own:
+
+        def with_gathered(four, first):
+            copy = fetch(four[0], first)
+            wait_all(start_all([pltpu.make_async_copy(gathered, base, base_sem)]))
+            copy.wait()
+            multiply(four[1:], base, first)
+
         if group == 0:
-
-            @pl.when(core == 0)
-            def _():
-                start_basis("y", where, blocks[:4], basis, base, base_sem)
-                wait_for(base, base_sem)
-                multiply(blocks[:4], base, 0)
-
-            @pl.when(core == 1)
-            def _():
-                wait_all(start_all([pltpu.make_async_copy(gathered, base, base_sem)]))
-                multiply(blocks[4:], base, 0)
-
+            pl.when(core == 0)(with_y)
+            pl.when(core == 1)(lambda: with_gathered(blocks[4:], 0))
+            for j in range(4):
+                wait_for(outs[j], out_sem.at[j])
+            return
+        with_gathered(blocks, core * chunk)
+    else:
+        ring, four = ("z", blocks[4:]) if group == 0 else ("x", blocks)
+        start_basis(ring, where, four, basis, gather, base_sem)
+
+        def with_gather(first):
+            fetch(four[0], first).wait()
+            multiply(four[1:], gather, first)
+
+        wait_for(gather, base_sem)
+        out_copy = pltpu.make_async_copy(gather, gathered, out_sem)
+        out_copy.start()
+        if group == 0:
+            pl.when(core == 1)(with_y)
+            pl.when(core == 0)(lambda: with_gather(0))
         else:
-            wait_all(start_all([pltpu.make_async_copy(gathered, base, base_sem)]))
-            multiply(blocks, base, core * chunk)
-    else:
-        ring, mine = ("z", blocks[4:]) if group == 0 else ("x", blocks)
-        start_basis(ring, where, mine, basis, gather, base_sem)
-        wait_for(gather, base_sem)
-        copy = pltpu.make_async_copy(gather, gathered, out_sem)
-        copy.start()
-        if group == 0:
-
-            @pl.when(core == 1)
-            def _():
-                start_basis("y", where, blocks[:4], basis, base, base_sem)
-                wait_for(base, base_sem)
-                multiply(blocks[:4], base, 0)
-
-            @pl.when(core == 0)
-            def _():
-                multiply(mine, gather, 0)
-
-        else:
-            multiply(mine, gather, (1 - core) * chunk)
-        copy.wait()
+            with_gather((1 - core) * chunk)
+        out_copy.wait()
         return
     stores = []
     for j in range(4):
         done = 0
-        for i, (first, size) in enumerate(pieces(group, (place(where, "u%d" % group) + j) % 4)):
+        for first, size in pieces(group, (u + j) % 4):
             stores.append(
-                pltpu.make_async_copy(
-                    total.at[rows_at(first, size), :], outs[j].at[pl.ds(done, size), :], out_sem.at[j, i]
-                )
+                pltpu.make_async_copy(total.at[rows_at(first, size), :], outs[j].at[pl.ds(done, size), :], out_sem.at[j])
             )
             done += size
-    wait_all(start_all(stores))
+    start_all(stores)
+    for j in range(4):
+        wait_for(outs[j], out_sem.at[j])
 
 
 def project(group, where, blocks, basis, other=None, gathered=None):
@@ -338,22 +352,30 @@
     return pl.pallas_call(
         functools.partial(project_kernel, group, own),
         out_shape=shapes,
-        in_specs=[SMEM] + [VMEM] * len(blocks) + [ANY] + ([VMEM, ANY] if own else []),
+        in_specs=[SMEM] + ([ANY] + [VMEM] * 3) * (len(blocks) // 4) + [ANY] + ([VMEM, ANY] if own else []),
         out_specs=[ANY] * 4 if own else [VMEM, ANY],
         scratch_shapes=[
             pltpu.VMEM((512, 512), BF),
             pltpu.VMEM((chunk if own else 512, 512), BF),
+            pltpu.VMEM((128, chunk), BF),
             DMA,
-            DMA((4, 8)) if own else DMA,
+            DMA((4,)) if own else DMA,
+            DMA,
         ],
         compiler_params=LIMIT,
         cost_estimate=estimate(2 * 512 * 512 * chunk, 512 * chunk * 2 + 512 * 1024 + chunk * 1024),
-    )(where, *blocks, basis, *([other, gathered] if own else []))
-
-
-def add_kernel(group, where, a, b, c, d, *refs):
-    outs, total, sem = refs[:4], refs[4], refs[5]
+    )(
+        where,
+        *(in_hbm(block) if i % 4 == 0 else block for i, block in enumerate(blocks)),
+        basis,
+        *([other, in_hbm(gathered)] if own else []),
+    )
+
+
+def add_kernel(group, where, mine, b, c, d, *refs):
+    outs, total, a, sem, in_sem = refs[:4], refs[4], refs[5], refs[6], refs[7]
     piece = GROUPS[group][1]
+    wait_all(start_all([pltpu.make_async_copy(mine, a, in_sem)]))
     total[...] = (
         (a[...].astype(F32) + b[...].astype(F32)) + (c[...].astype(F32) + d[...].astype(F32))
     ).astype(BF)
@@ -369,12 +391,12 @@
     return pl.pallas_call(
         functools.partial(add_kernel, group),
         out_shape=[pltpu.HBM((piece, 512), BF)] * 4,
-        in_specs=[SMEM] + [VMEM] * 4,
+        in_specs=[SMEM, ANY] + [VMEM] * 3,
         out_specs=[ANY] * 4,
-        scratch_shapes=[pltpu.VMEM((chunk // 4, 512), BF), DMA((4,))],
+        scratch_shapes=[pltpu.VMEM((chunk // 4, 512), BF)] * 2 + [DMA((4,)), DMA],
         compiler_params=LIMIT,
         cost_estimate=estimate(3 * chunk * 128, 5 * chunk * 256),
-    )(where, *arrays)
+    )(where, in_hbm(arrays[0]), *arrays[1:])
 
 
 def moments_kernel(where, first, second, new, old, result, half, old_held, out, sem):
@@ -418,7 +440,7 @@
         compiler_params=LIMIT,
         cost_estimate=estimate(2 * 2048 * 256 * 512, 6 * 2**20),
         name="cut_moments",
-    )(where, first, second, new, old)
+    )(where, first, second, new, in_hbm(old))
 
 
 def margin_kernel(moments, out, held, sem):
@@ -449,19 +471,25 @@
 
 def step_kernel(where, *refs):
     sums, (own, other, moments), lows = refs[:8], refs[8:11], refs[11:13]
-    first_out, second_out, margin = refs[13:]
+    first_out, second_out, margin, mine, in_sem = refs[13:]
     core = place(where, "core")
+    copies = [
+        pltpu.make_async_copy(sums[0], mine.at[pl.ds(0, 128), :], in_sem.at[0]),
+        pltpu.make_async_copy(sums[4], mine.at[pl.ds(128, 80), :], in_sem.at[1]),
+    ]
+    start_all(copies)
     margin[rows_at(core * 256, 256), :] = own[...]
     margin[rows_at(256 - core * 256, 256), :] = other[...]
-    projected = jnp.concatenate(
-        [sum(ref[...].astype(F32) for ref in sums[4 * g : 4 * g + 4]) for g in range(2)], axis=0
-    )
     contract = (((0,), (1,)), ((), ()))
     one, one_low, two = (moments[:, i * 64 : i * 64 + 64, :].reshape(512, 256) for i in range(3))
     rotated_one = lax.dot_general(one, margin[...], contract, preferred_element_type=F32)
     rotated_one = rotated_one + lax.dot_general(one_low, margin[...], contract, preferred_element_type=F32)
     wide = margin[...].astype(F32)
     rotated_two = lax.dot_general(two, (wide * wide).astype(BF), contract, preferred_element_type=F32)
+    wait_all(copies)
+    projected = mine[...].astype(F32) + jnp.concatenate(
+        [sum(ref[...].astype(F32) for ref in sums[4 * g + 1 : 4 * g + 4]) for g in range(2)], axis=0
+    )
     first_new = 0.9 * rotated_one[:208] + 0.1 * projected
     second_new = 0.999 * rotated_two[:208] + 0.001 * projected * projected
     low_step = (
@@ -480,13 +508,13 @@
         step_kernel,
         out_shape=[jax.ShapeDtypeStruct((piece, 512), BF) for _, piece in GROUPS]
         + [jax.ShapeDtypeStruct((208, 512), F32)] * 2,
-        in_specs=[SMEM] + [VMEM] * 11,
+        in_specs=[SMEM] + ([ANY] + [VMEM] * 3) * 2 + [VMEM] * 3,
         out_specs=[VMEM] * 4,
-        scratch_shapes=[pltpu.VMEM((512, 512), BF)],
+        scratch_shapes=[pltpu.VMEM((512, 512), BF), pltpu.VMEM((208, 512), BF), DMA((2,))],
         compiler_params=LIMIT,
         cost_estimate=estimate(6 * 208 * 512 * 512, 4 * 2**20),
         name="step",
-    )(where, *sums, *rest)
+    )(where, in_hbm(sums[0]), *sums[1:4], in_hbm(sums[4]), *sums[5:], *rest)
 
 
 def turn_kernel(first, second, result, wide, out, sem):
@@ -638,7 +666,7 @@
         ],
         compiler_params=LIMIT,
         cost_estimate=estimate(2 * 512 * 512 * width, 512 * width * 2 + 512 * 1024 + width * 1024),
-    )(where, *arrays, basis)
+    )(where, *arrays, basis if ring == "y" else in_hbm(basis))
 
 
 def exchange(blocks, rings):

time: 281 us -> 280 us (level)
  the two profiles are of different devices: /device:TPU:38 before, /device:TPU:1 now
where the time goes in v5:
time: 280 us; the launch traced here: 275 us
  starting transfers between devices  112 us (40%)
  Pallas kernels  71.2 us (25%)
  waiting for transfers between devices  61.3 us (22%)
  blocking collectives  23.2 us (8%)
  local copies, waits for them, and re-layouts  5.04 us (2%)
    ppermute x53, starting transfers between devices, shift(): return lax.ppermute(array, NAMES, pairs)  102 us
    ppermute x53, waiting for transfers between devices, shift(): return lax.ppermute(array, NAMES, pairs)  56.7 us
    all_to_all x1, blocking collectives, compute(): new = lax.all_to_all(new, ROW, 0, 0, tiled=True)  23.2 us
    pallas_call x4, Pallas kernels, project(): pl.pallas_call(functools.partial(project_kernel, group, own), out_shape=s...  20.8 us
    pallas_call x3, Pallas kernels, update_blocks(): pl.pallas_call(functools.partial(update_kernel, ring), out_shape=blocks_o...  17 us
    pallas_call x3, Pallas kernels, unpack(): pl.pallas_call(functools.partial(unpack_kernel, ring), out_shape=jax.Shap...  8.48 us
    pallas_call x3, Pallas kernels, pack(): pl.pallas_call(functools.partial(pack_kernel, ring), out_shape=[(jax.Shap...  8.01 us
    all_to_all x1, starting transfers between devices, compute(): moments = lax.all_to_all(moments, ROW, 0, 0, tiled=True)  6.82 us
  transfers between devices with their start and end apart: 55, of which 17 were waited for; matrix products, arithmetic and copies ran while one was open for 0% of the time, Pallas kernels for 23%

profile of v5, /device:TPU:1, one launch (start us, length us, event | category | flops | bytes accessed | tf_op | source)
XLA Modules:
  0.0 274.6 jit_solution(6054645822767294427)
XLA Ops:
  0.7 1.6 copy-done
  2.3 2.5 shard_map.76
  4.7 2.3 collective-permute-start
  7.1 2.6 shard_map.77
  9.6 1.8 collective-permute-start.3
  11.5 2.6 collective-permute-start.4
  15.2 1.8 collective-permute-start.1
  16.9 3.5 %collective-permute-done.refs_1_ = bf16[128,2048]{1,0:T(8,128)(2,1)S(1)} collective-permute-done((bf16[128,2048]{1,0:T(8,128)(2,1)S(1)}, bf16[128,2048]{1,0:T(8,128)(2,1)S(1)}, u32[]{:S(2)}, u32[]{:S(2)}) %collective-permute-start) | collective-permute-done | bytes 524320 | tf_op jit(solution)/shard_map/ppermute | solution.py:65
  20.5 1.2 collective-permute-start.2
  21.7 3.0 %shard_map.81 = (bf16[128,2560]{1,0:T(8,128)(2,1)}, bf16[128,3072]{1,0:T(8,128)(2,1)S(1)}, bf16[128,3072]{1,0:T(8,128)(2,1)S(1)}, bf16[128,2560]{1,0:T(8,128)(2,1)S(1)}) custom-call(s32[8]{0:T(128)S(1)} %compare_select_fusion.6.where, bf16[128,26624]{1,0:T(8,128)(2,1)} %grad.5, bf16[2048,512]{1,0:T(8,128)(2,1)S(1)} %copy-done), custom_call_target="tpu_custom_call" | custom-call | bytes 6291456 | tf_op jit(solution)/shard_map/pallas_call | solution.py:168
  24.6 2.5 collective-permute-done.1.refs_2_
  27.1 1.2 collective-permute-start.13
  28.3 5.9 %collective-permute-done.2.refs_3_ = bf16[128,2048]{1,0:T(8,128)(2,1)S(1)} collective-permute-done((bf16[128,2048]{1,0:T(8,128)(2,1)S(1)}, bf16[128,2048]{1,0:T(8,128)(2,1)S(1)}, u32[]{:S(2)}, u32[]{:S(2)}) %collective-permute-start.2) | collective-permute-done | bytes 524320 | tf_op jit(solution)/shard_map/ppermute | solution.py:65
  34.2 2.5 collective-permute-start.14
  37.2 5.9 %collective-permute-done.5.refs_7_ = bf16[128,2560]{1,0:T(8,128)(2,1)S(1)} collective-permute-done((bf16[128,2560]{1,0:T(8,128)(2,1)S(1)}, bf16[128,2560]{1,0:T(8,128)(2,1)S(1)}, u32[]{:S(2)}, u32[]{:S(2)}) %collective-permute-start.5) | collective-permute-done | bytes 655392 | tf_op jit(solution)/shard_map/ppermute | solution.py:65
  43.1 6.0 %shard_map.78 = (bf16[2048,512]{1,0:T(8,128)(2,1)}, bf16[512,512]{1,0:T(8,128)(2,1)}) custom-call(s32[8]{0:T(128)S(1)} %compare_select_fusion.6.where, bf16[128,2048]{1,0:T(8,128)(2,1)} %get-tuple-element.53.refs_0_, bf16[128,2048]{1,0:T(8,128)(2,1)S(1)} %collective-permute-done.refs_1_, bf16[128,2048]{1,0:T(8,128)(2,1)S(1)} %collective-permute-done.1.refs_2_, ...), custom_call_target="tpu_custom_call" | custom-call | flops 1073741824 | bytes 4718592 | tf_op jit(solution)/shard_map/pallas_call | solution.py:352
  49.2 2.4 collective-permute-start.6
  51.6 4.4 %shard_map.82 = (bf16[1280,512]{1,0:T(8,128)(2,1)}, bf16[512,512]{1,0:T(8,128)(2,1)}) custom-call(s32[8]{0:T(128)S(1)} %compare_select_fusion.6.where, bf16[128,2560]{1,0:T(8,128)(2,1)} %get-tuple-element.71.refs_0_, bf16[128,3072]{1,0:T(8,128)(2,1)S(1)} %collective-permute-done.13.refs_1_, bf16[128,3072]{1,0:T(8,128)(2,1)S(1)} %collective-permute-done.14.refs_2_, ...), custom_call_target="tpu_custom_call" | custom-call | flops 671088640 | bytes 3145728 | tf_op jit(solution)/shard_map/pallas_call | solution.py:352
  56.1 16.9 %collective-permute-start.16 = (bf16[1280,512]{1,0:T(8,128)(2,1)}, bf16[1280,512]{1,0:T(8,128)(2,1)}, u32[]{:S(2)}, u32[]{:S(2)}) collective-permute-start(bf16[1280,512]{1,0:T(8,128)(2,1)} %get-tuple-element.75), channel_id=1, source_target_pairs={{0,1},{1,0},{2,3},{3,2},{4,5},{5,4},{6,7},{7,6},{8,9},{9,8},{10,11... | collective-permute-start | bytes 3932168 | tf_op jit(solution)/shard_map/ppermute | solution.py:65
  72.9 4.1 %cut_moments.1 = bf16[8,256,256]{2,1,0:T(8,128)(2,1)} custom-call(s32[8]{0:T(128)S(1)} %compare_select_fusion.6.where, f32[64,1664]{1,0:T(8,128)S(1)} %copy-done.23, f32[64,1664]{1,0:T(8,128)S(1)} %copy-done.24, bf16[2048,512]{1,0:T(8,128)(2,1)S(1)} %copy-done, bf16[2048,512]{1,0:T(8,128)(2,1)} %old.1), custom_call_target="tpu_custom_call" | custom-call | flops 536870912 | bytes 6291456 | tf_op jit(solution)/shard_map/cut_moments/pallas_call | solution.py:429
  77.0 6.8 %all-to-all-start = ((bf16[8,256,256]{2,1,0:T(8,128)(2,1)}), bf16[8,256,256]{2,1,0:T(8,128)(2,1)S(1)}, u32[]{:S(2)}, u32[]{:S(2)}) async-start(bf16[8,256,256]{2,1,0:T(8,128)(2,1)} %cut_moments.1), calls=%async_computation | async-start | bytes 2097152 | tf_op jit(solution)/shard_map/all_to_all | solution.py:695
  87.2 4.7 %shard_map.83 = (bf16[320,512]{1,0:T(8,128)(2,1)}, bf16[320,512]{1,0:T(8,128)(2,1)}, bf16[320,512]{1,0:T(8,128)(2,1)}, bf16[320,512]{1,0:T(8,128)(2,1)S(1)}) custom-call(s32[8]{0:T(128)S(1)} %compare_select_fusion.6.where, bf16[128,2560]{1,0:T(8,128)(2,1)} %get-tuple-element.71.refs_0_, bf16[128,3072]{1,0:T(8,128)(2,1)S(1)} %copy-done.3, ...), custom_call_target="tpu_custom_call" | custom-call | flops 671088640 | bytes 3145728 | tf_op jit(solution)/shard_map/pallas_call | solution.py:352
  91.9 1.5 collective-permute-start.17
  93.5 2.4 collective-permute-start.18
  95.9 5.7 %shard_map.79 = (bf16[512,512]{1,0:T(8,128)(2,1)}, bf16[512,512]{1,0:T(8,128)(2,1)}, bf16[512,512]{1,0:T(8,128)(2,1)}, bf16[512,512]{1,0:T(8,128)(2,1)}) custom-call(s32[8]{0:T(128)S(1)} %compare_select_fusion.6.where, bf16[128,2048]{1,0:T(8,128)(2,1)} %get-tuple-element.53.refs_0_, bf16[128,2048]{1,0:T(8,128)(2,1)S(1)} %copy-done.15, ...), custom_call_target="tpu_custom_call" | custom-call | flops 1073741824 | bytes 4718592 | tf_op jit(solution)/shard_map/pallas_call | solution.py:352
  101.6 4.7 %collective-permute-start.7 = (bf16[512,512]{1,0:T(8,128)(2,1)}, bf16[512,512]{1,0:T(8,128)(2,1)}, u32[]{:S(2)}, u32[]{:S(2)}) collective-permute-start(bf16[512,512]{1,0:T(8,128)(2,1)} %get-tuple-element.64), channel_id=1, source_target_pairs={{0,64},{1,5},{2,66},{3,7},{4,68},{5,9},{6,70},{7,11},{8,72},{9,13}... | collective-permute-start | bytes 1572872 | tf_op jit(solution)/shard_map/ppermute | solution.py:65
  106.3 1.2 collective-permute-start.8
  107.5 1.2 collective-permute-start.9
  109.6 3.4 %all-to-all-start.1 = ((bf16[8,32,512]{2,1,0:T(8,128)(2,1)}), bf16[8,32,512]{2,1,0:T(8,128)(2,1)S(1)}, u32[]{:S(2)}, u32[]{:S(2)}) async-start(bf16[8,32,512]{2,1,0:T(8,128)(2,1)} %sum_margin.1), calls=%async_computation.1 | async-start | bytes 524288 | tf_op jit(solution)/shard_map/all_to_all | solution.py:697
  113.0 2.6 collective-permute-start.19
  115.6 4.6 %all-to-all-done.1 = bf16[8,32,512]{2,1,0:T(8,128)(2,1)S(1)} async-done(((bf16[8,32,512]{2,1,0:T(8,128)(2,1)}), bf16[8,32,512]{2,1,0:T(8,128)(2,1)S(1)}, u32[]{:S(2)}, u32[]{:S(2)}) %all-to-all-start.1) | async-done | bytes 262176 | tf_op jit(solution)/shard_map/all_to_all | solution.py:697
  120.2 3.0 %collective-permute-start.23 = (bf16[256,512]{1,0:T(8,128)(2,1)S(1)}, bf16[256,512]{1,0:T(8,128)(2,1)S(1)}, u32[]{:S(2)}, u32[]{:S(2)}) collective-permute-start(bf16[256,512]{1,0:T(8,128)(2,1)S(1)} %bitcast.1), channel_id=1, source_target_pairs={{0,1},{1,0},{2,3},{3,2},{4,5},{5,4},{6,7},{7,6},{8,9},{9,8},{10,11... | collective-permute-start | bytes 786440 | tf_op jit(solution)/shard_map/ppermute | solution.py:65
  123.2 2.3 collective-permute-done.19.d
  125.5 3.1 %shard_map.84 = (bf16[80,512]{1,0:T(8,128)(2,1)}, bf16[80,512]{1,0:T(8,128)(2,1)}, bf16[80,512]{1,0:T(8,128)(2,1)}, bf16[80,512]{1,0:T(8,128)(2,1)}) custom-call(s32[8]{0:T(128)S(1)} %compare_select_fusion.6.where, bf16[320,512]{1,0:T(8,128)(2,1)} %get-tuple-element.77.mine, bf16[320,512]{1,0:T(8,128)(2,1)} %collective-permute-done.17.b, ...), custom_call_target="tpu_custom_call" | custom-call | flops 491520 | bytes 1638400 | tf_op jit(solution)/shard_map/pallas_call | solution.py:391
  128.6 2.4 collective-permute-start.20
  131.0 3.5 %shard_map.80 = (bf16[128,512]{1,0:T(8,128)(2,1)}, bf16[128,512]{1,0:T(8,128)(2,1)}, bf16[128,512]{1,0:T(8,128)(2,1)}, bf16[128,512]{1,0:T(8,128)(2,1)}) custom-call(s32[8]{0:T(128)S(1)} %compare_select_fusion.6.where, bf16[512,512]{1,0:T(8,128)(2,1)} %get-tuple-element.63.mine, bf16[512,512]{1,0:T(8,128)(2,1)} %collective-permute-done.7.b, ...), custom_call_target="tpu_custom_call" | custom-call | flops 786432 | bytes 2621440 | tf_op jit(solution)/shard_map/pallas_call | solution.py:391
  134.8 2.7 collective-permute-start.11
  137.4 2.0 collective-permute-start.12
  139.4 1.3 collective-permute-start.21
  140.7 1.1 collective-permute-start.22
  141.9 3.1 %collective-permute-done.21.refs_6_ = bf16[80,512]{1,0:T(8,128)(2,1)S(1)} collective-permute-done((bf16[80,512]{1,0:T(8,128)(2,1)S(1)}, bf16[80,512]{1,0:T(8,128)(2,1)S(1)}, u32[]{:S(2)}, u32[]{:S(2)}) %collective-permute-start.21) | collective-permute-done | bytes 81952 | tf_op jit(solution)/shard_map/ppermute | solution.py:65
  145.2 2.3 step.1
  147.5 3.1 %collective-permute-start.42 = (bf16[80,512]{1,0:T(8,128)(2,1)S(1)}, bf16[80,512]{1,0:T(8,128)(2,1)S(1)}, u32[]{:S(2)}, u32[]{:S(2)}) collective-permute-start(bf16[80,512]{1,0:T(8,128)(2,1)S(1)} %get-tuple-element.94.refs_0_), channel_id=1, source_target_pairs={{0,12},{1,13},{2,14},{3,15},{4,0},{5,1},{6,2},{7,3},{8,4},{9,5},{1... | collective-permute-start | bytes 245768 | tf_op jit(solution)/shard_map/ppermute | solution.py:65
  152.3 3.2 %collective-permute-done.41.refs_2_ = bf16[80,512]{1,0:T(8,128)(2,1)S(1)} collective-permute-done((bf16[80,512]{1,0:T(8,128)(2,1)S(1)}, bf16[80,512]{1,0:T(8,128)(2,1)S(1)}, u32[]{:S(2)}, u32[]{:S(2)}) %collective-permute-start.41) | collective-permute-done | bytes 81952 | tf_op jit(solution)/shard_map/ppermute | solution.py:65
  157.0 2.0 collective-permute-start.46
  161.6 2.5 collective-permute-done.26.refs_3_
  169.5 2.9 %collective-permute-done.44.refs_2_ = bf16[320,512]{1,0:T(8,128)(2,1)S(1)} collective-permute-done((bf16[320,512]{1,0:T(8,128)(2,1)S(1)}, bf16[320,512]{1,0:T(8,128)(2,1)S(1)}, u32[]{:S(2)}, u32[]{:S(2)}) %collective-permute-start.44) | collective-permute-done | bytes 327712 | tf_op jit(solution)/shard_map/ppermute | solution.py:65
  172.4 8.8 %collective-permute-start.49 = (bf16[320,512]{1,0:T(8,128)(2,1)S(1)}, bf16[320,512]{1,0:T(8,128)(2,1)S(1)}, u32[]{:S(2)}, u32[]{:S(2)}) collective-permute-start(bf16[320,512]{1,0:T(8,128)(2,1)S(1)} %collective-permute-done.45.refs_3_), channel_id=1, source_target_pairs={{0,1},{1,0},{2,3},{3,2},{4,5},{5,4},{6,7},{7,6},{8,9},{9,8},{10,11... | collective-permute-start | bytes 983048 | tf_op jit(solution)/shard_map/ppermute | solution.py:65
  181.2 3.4 %collective-permute-start.48 = (bf16[320,512]{1,0:T(8,128)(2,1)S(1)}, bf16[320,512]{1,0:T(8,128)(2,1)S(1)}, u32[]{:S(2)}, u32[]{:S(2)}) collective-permute-start(bf16[320,512]{1,0:T(8,128)(2,1)S(1)} %collective-permute-done.44.refs_2_), channel_id=1, source_target_pairs={{0,1},{1,0},{2,3},{3,2},{4,5},{5,4},{6,7},{7,6},{8,9},{9,8},{10,11... | collective-permute-start | bytes 983048 | tf_op jit(solution)/shard_map/ppermute | solution.py:65
  184.7 1.3 collective-permute-start.30
  185.9 3.0 %collective-permute-start.33 = (bf16[512,512]{1,0:T(8,128)(2,1)S(1)}, bf16[512,512]{1,0:T(8,128)(2,1)S(1)}, u32[]{:S(2)}, u32[]{:S(2)}) collective-permute-start(bf16[512,512]{1,0:T(8,128)(2,1)S(1)} %collective-permute-done.29.refs_3_), channel_id=1, source_target_pairs={{0,1},{1,0},{2,3},{3,2},{4,5},{5,4},{6,7},{7,6},{8,9},{9,8},{10,11... | collective-permute-start | bytes 1572872 | tf_op jit(solution)/shard_map/ppermute | solution.py:65
  188.9 5.5 %collective-permute-start.32 = (bf16[512,512]{1,0:T(8,128)(2,1)S(1)}, bf16[512,512]{1,0:T(8,128)(2,1)S(1)}, u32[]{:S(2)}, u32[]{:S(2)}) collective-permute-start(bf16[512,512]{1,0:T(8,128)(2,1)S(1)} %collective-permute-done.28.refs_2_), channel_id=1, source_target_pairs={{0,1},{1,0},{2,3},{3,2},{4,5},{5,4},{6,7},{7,6},{8,9},{9,8},{10,11... | collective-permute-start | bytes 1572872 | tf_op jit(solution)/shard_map/ppermute | solution.py:65
  194.9 2.2 collective-permute-done.47.refs_5_
  197.2 8.1 %shard_map.89 = (bf16[128,2560]{1,0:T(8,128)(2,1)}, bf16[128,2560]{1,0:T(8,128)(2,1)S(1)}, bf16[128,2560]{1,0:T(8,128)(2,1)S(1)}, bf16[128,2560]{1,0:T(8,128)(2,1)S(1)}) custom-call(s32[8]{0:T(128)S(1)} %compare_select_fusion.6.where, bf16[320,512]{1,0:T(8,128)(2,1)S(1)} %shard_map.88.refs_0_, bf16[320,512]{1,0:T(8,128)(2,1)S(1)} %collective-permute-done.43.refs_1_, ...), custom_call_target="tpu_custom_call" | custom-call | flops 1342177280 | bytes 5767168 | tf_op jit(solution)/shard_map/pallas_call | solution.py:653
  205.4 2.7 collective-permute-start.51
  208.2 4.3 %shard_map.87 = (bf16[128,2048]{1,0:T(8,128)(2,1)}, bf16[128,2048]{1,0:T(8,128)(2,1)S(1)}, bf16[128,2048]{1,0:T(8,128)(2,1)S(1)}, bf16[128,2048]{1,0:T(8,128)(2,1)S(1)}) custom-call(s32[8]{0:T(128)S(1)} %compare_select_fusion.6.where, bf16[512,512]{1,0:T(8,128)(2,1)S(1)} %shard_map.85.refs_0_, bf16[512,512]{1,0:T(8,128)(2,1)S(1)} %collective-permute-done.27.refs_1_, ...), custom_call_target="tpu_custom_call" | custom-call | flops 1073741824 | bytes 4718592 | tf_op jit(solution)/shard_map/pallas_call | solution.py:653
  212.7 4.5 %shard_map.86 = (bf16[128,2048]{1,0:T(8,128)(2,1)}, bf16[128,2048]{1,0:T(8,128)(2,1)S(1)}, bf16[128,2048]{1,0:T(8,128)(2,1)S(1)}, bf16[128,2048]{1,0:T(8,128)(2,1)S(1)}) custom-call(s32[8]{0:T(128)S(1)} %compare_select_fusion.6.where, bf16[512,512]{1,0:T(8,128)(2,1)S(1)} %shard_map.85.refs_0_, bf16[512,512]{1,0:T(8,128)(2,1)S(1)} %collective-permute-done.27.refs_1_, ...), custom_call_target="tpu_custom_call" | custom-call | flops 1073741824 | bytes 4718592 | tf_op jit(solution)/shard_map/pallas_call | solution.py:653
  217.3 19.2 %collective-permute-done.50.refs_1_ = bf16[128,2560]{1,0:T(8,128)(2,1)S(1)} collective-permute-done((bf16[128,2560]{1,0:T(8,128)(2,1)S(1)}, bf16[128,2560]{1,0:T(8,128)(2,1)S(1)}, u32[]{:S(2)}, u32[]{:S(2)}) %collective-permute-start.50) | collective-permute-done | bytes 655392 | tf_op jit(solution)/shard_map/ppermute | solution.py:65
  237.2 2.0 collective-permute-start.35
  239.2 1.4 collective-permute-start.36
  241.6 23.2 %all_to_all.15.new = bf16[8,128,256]{2,1,0:T(8,128)(2,1)S(1)} all-to-all(bf16[8,128,256]{2,1,0:T(8,128)(2,1)} %turn_back.1), channel_id=1, replica_groups=mesh['xl'=2,'z'=4,'y'=4,'xh'=2,'core'=2] {'xl','z'}, dimensions={0} | all-to-all | bytes 1048576 | tf_op jit(solution)/shard_map/all_to_all | solution.py:727
  265.8 3.6 %shard_map.90.refs_4_ = bf16[128,26624]{1,0:T(8,128)(2,1)} custom-call(s32[8]{0:T(128)S(1)} %compare_select_fusion.6.where, bf16[128,2560]{1,0:T(8,128)(2,1)S(1)} %copy-done.20, bf16[128,2560]{1,0:T(8,128)(2,1)S(1)} %collective-permute-done.50.refs_1_, bf16[128,2560]{1,0:T(8,128)(2,1)S(1)} %collective-permute-done.51.refs_2_, ...), custom_call_target="tpu_custom_call" | custom-call | bytes 5242880 | tf_op jit(solution)/shard_map/pallas_call | solution.py:230
  269.4 2.5 shard_map.91.refs_4_
  272.0 2.4 shard_map.92
  (126 shorter events, 21.2 us)
Async XLA Ops:
  4.7 15.7 %collective-permute-start = (bf16[128,2048]{1,0:T(8,128)(2,1)S(1)}, bf16[128,2048]{1,0:T(8,128)(2,1)S(1)}, u32[]{:S(2)}, u32[]{:S(2)}) collective-permute-start(bf16[128,2048]{1,0:T(8,128)(2,1)S(1)} %get-tuple-element.54), channel_id=1, source_target_pairs={{0,4},{1,5},{2,6},{3,7},{4,8},{5,9},{6,10},{7,11},{8,12},{9,13},{1... | collective-permute-start | bytes 1572872 | tf_op jit(solution)/shard_map/ppermute | solution.py:65
  9.6 27.0 %collective-permute-start.3 = (bf16[128,2560]{1,0:T(8,128)(2,1)S(1)}, bf16[128,2560]{1,0:T(8,128)(2,1)S(1)}, u32[]{:S(2)}, u32[]{:S(2)}) collective-permute-start(bf16[128,2560]{1,0:T(8,128)(2,1)S(1)} %get-tuple-element.58), channel_id=1, source_target_pairs={{0,16},{1,17},{2,18},{3,19},{4,20},{5,21},{6,22},{7,23},{8,24},{9,... | collective-permute-start | bytes 1966088 | tf_op jit(solution)/shard_map/ppermute | solution.py:65
  11.5 25.7 %collective-permute-start.4 = (bf16[128,2560]{1,0:T(8,128)(2,1)S(1)}, bf16[128,2560]{1,0:T(8,128)(2,1)S(1)}, u32[]{:S(2)}, u32[]{:S(2)}) collective-permute-start(bf16[128,2560]{1,0:T(8,128)(2,1)S(1)} %get-tuple-element.59), channel_id=1, source_target_pairs={{0,48},{1,49},{2,50},{3,51},{4,52},{5,53},{6,54},{7,55},{8,56},{9,... | collective-permute-start | bytes 1966088 | tf_op jit(solution)/shard_map/ppermute | solution.py:65
  14.0 29.0 %collective-permute-start.5 = (bf16[128,2560]{1,0:T(8,128)(2,1)S(1)}, bf16[128,2560]{1,0:T(8,128)(2,1)S(1)}, u32[]{:S(2)}, u32[]{:S(2)}) collective-permute-start(bf16[128,2560]{1,0:T(8,128)(2,1)S(1)} %get-tuple-element.60), channel_id=1, source_target_pairs={{0,32},{1,33},{2,34},{3,35},{4,36},{5,37},{6,38},{7,39},{8,40},{9,... | collective-permute-start | bytes 1966088 | tf_op jit(solution)/shard_map/ppermute | solution.py:65
  15.2 12.0 %collective-permute-start.1 = (bf16[128,2048]{1,0:T(8,128)(2,1)S(1)}, bf16[128,2048]{1,0:T(8,128)(2,1)S(1)}, u32[]{:S(2)}, u32[]{:S(2)}) collective-permute-start(bf16[128,2048]{1,0:T(8,128)(2,1)S(1)} %get-tuple-element.55), channel_id=1, source_target_pairs={{0,12},{1,13},{2,14},{3,15},{4,0},{5,1},{6,2},{7,3},{8,4},{9,5},{1... | collective-permute-start | bytes 1572872 | tf_op jit(solution)/shard_map/ppermute | solution.py:65
  20.5 22.6 %copy-start.14 = (bf16[128,2048]{1,0:T(8,128)(2,1)}, bf16[128,2048]{1,0:T(8,128)(2,1)S(1)}, u32[]{:S(2)}) copy-start(bf16[128,2048]{1,0:T(8,128)(2,1)S(1)} %collective-permute-done.refs_1_) | copy-start | bytes 1572868
  20.5 13.7 %collective-permute-start.2 = (bf16[128,2048]{1,0:T(8,128)(2,1)S(1)}, bf16[128,2048]{1,0:T(8,128)(2,1)S(1)}, u32[]{:S(2)}, u32[]{:S(2)}) collective-permute-start(bf16[128,2048]{1,0:T(8,128)(2,1)S(1)} %get-tuple-element.56), channel_id=1, source_target_pairs={{0,8},{1,9},{2,10},{3,11},{4,12},{5,13},{6,14},{7,15},{8,0},{9,1},... | collective-permute-start | bytes 1572872 | tf_op jit(solution)/shard_map/ppermute | solution.py:65
  27.1 22.0 %copy-start.16 = (bf16[128,2048]{1,0:T(8,128)(2,1)}, bf16[128,2048]{1,0:T(8,128)(2,1)S(1)}, u32[]{:S(2)}) copy-start(bf16[128,2048]{1,0:T(8,128)(2,1)S(1)} %collective-permute-done.1.refs_2_) | copy-start | bytes 1572868
  27.1 24.5 %collective-permute-start.13 = (bf16[128,3072]{1,0:T(8,128)(2,1)S(1)}, bf16[128,3072]{1,0:T(8,128)(2,1)S(1)}, u32[]{:S(2)}, u32[]{:S(2)}) collective-permute-start(bf16[128,3072]{1,0:T(8,128)(2,1)S(1)} %get-tuple-element.72), channel_id=1, source_target_pairs={{0,64},{1,65},{2,66},{3,67},{4,68},{5,69},{6,70},{7,71},{8,72},{9,... | collective-permute-start | bytes 2359304 | tf_op jit(solution)/shard_map/ppermute | solution.py:65
  34.2 14.9 %copy-start.18 = (bf16[128,2048]{1,0:T(8,128)(2,1)}, bf16[128,2048]{1,0:T(8,128)(2,1)S(1)}, u32[]{:S(2)}) copy-start(bf16[128,2048]{1,0:T(8,128)(2,1)S(1)} %collective-permute-done.2.refs_3_) | copy-start | bytes 1572868
  34.2 17.4 %collective-permute-start.14 = (bf16[128,3072]{1,0:T(8,128)(2,1)S(1)}, bf16[128,3072]{1,0:T(8,128)(2,1)S(1)}, u32[]{:S(2)}, u32[]{:S(2)}) collective-permute-start(bf16[128,3072]{1,0:T(8,128)(2,1)S(1)} %get-tuple-element.73), channel_id=1, source_target_pairs={{0,66},{1,67},{2,64},{3,65},{4,70},{5,71},{6,68},{7,69},{8,74},{9,... | collective-permute-start | bytes 2359304 | tf_op jit(solution)/shard_map/ppermute | solution.py:65
  36.7 12.5 %copy-start.6 = (bf16[128,2560]{1,0:T(8,128)(2,1)}, bf16[128,2560]{1,0:T(8,128)(2,1)S(1)}, u32[]{:S(2)}) copy-start(bf16[128,2560]{1,0:T(8,128)(2,1)S(1)} %collective-permute-done.3.refs_5_) | copy-start | bytes 1966084
  36.7 14.9 %collective-permute-start.15 = (bf16[128,2560]{1,0:T(8,128)(2,1)S(1)}, bf16[128,2560]{1,0:T(8,128)(2,1)S(1)}, u32[]{:S(2)}, u32[]{:S(2)}) collective-permute-start(bf16[128,2560]{1,0:T(8,128)(2,1)S(1)} %get-tuple-element.74), channel_id=1, source_target_pairs={{0,2},{1,3},{2,0},{3,1},{4,6},{5,7},{6,4},{7,5},{8,10},{9,11},{10,... | collective-permute-start | bytes 1966088 | tf_op jit(solution)/shard_map/ppermute | solution.py:65
  37.2 11.9 %copy-start.8 = (bf16[128,2560]{1,0:T(8,128)(2,1)}, bf16[128,2560]{1,0:T(8,128)(2,1)S(1)}, u32[]{:S(2)}) copy-start(bf16[128,2560]{1,0:T(8,128)(2,1)S(1)} %collective-permute-done.4.refs_6_) | copy-start | bytes 1966084
  49.2 46.7 %collective-permute-start.6 = (bf16[2048,512]{1,0:T(8,128)(2,1)}, bf16[2048,512]{1,0:T(8,128)(2,1)}, u32[]{:S(2)}, u32[]{:S(2)}) collective-permute-start(bf16[2048,512]{1,0:T(8,128)(2,1)} %get-tuple-element.61), channel_id=1, source_target_pairs={{0,1},{1,0},{2,3},{3,2},{4,5},{5,4},{6,7},{7,6},{8,9},{9,8},{10,11... | collective-permute-start | bytes 6291464 | tf_op jit(solution)/shard_map/ppermute | solution.py:65
  51.6 21.3 %copy-start.23 = (f32[64,1664]{1,0:T(8,128)S(1)}, f32[64,1664]{1,0:T(8,128)}, u32[]{:S(2)}) copy-start(f32[64,1664]{1,0:T(8,128)} %first.1) | copy-start | bytes 1277956
  51.6 21.3 %copy-start.24 = (f32[64,1664]{1,0:T(8,128)S(1)}, f32[64,1664]{1,0:T(8,128)}, u32[]{:S(2)}) copy-start(f32[64,1664]{1,0:T(8,128)} %second.1) | copy-start | bytes 1277956
  56.1 27.8 %collective-permute-start.16 = (bf16[1280,512]{1,0:T(8,128)(2,1)}, bf16[1280,512]{1,0:T(8,128)(2,1)}, u32[]{:S(2)}, u32[]{:S(2)}) collective-permute-start(bf16[1280,512]{1,0:T(8,128)(2,1)} %get-tuple-element.75), channel_id=1, source_target_pairs={{0,1},{1,0},{2,3},{3,2},{4,5},{5,4},{6,7},{7,6},{8,9},{9,8},{10,11... | collective-permute-start | bytes 3932168 | tf_op jit(solution)/shard_map/ppermute | solution.py:65
  77.0 31.7 %all-to-all-start = ((bf16[8,256,256]{2,1,0:T(8,128)(2,1)}), bf16[8,256,256]{2,1,0:T(8,128)(2,1)S(1)}, u32[]{:S(2)}, u32[]{:S(2)}) async-start(bf16[8,256,256]{2,1,0:T(8,128)(2,1)} %cut_moments.1), calls=%async_computation | async-start | bytes 2097152 | tf_op jit(solution)/shard_map/all_to_all | solution.py:695
  91.9 21.0 %collective-permute-start.17 = (bf16[320,512]{1,0:T(8,128)(2,1)}, bf16[320,512]{1,0:T(8,128)(2,1)}, u32[]{:S(2)}, u32[]{:S(2)}) collective-permute-start(bf16[320,512]{1,0:T(8,128)(2,1)} %get-tuple-element.78), channel_id=1, source_target_pairs={{0,16},{1,17},{2,18},{3,19},{4,20},{5,21},{6,22},{7,23},{8,24},{9,... | collective-permute-start | bytes 983048 | tf_op jit(solution)/shard_map/ppermute | solution.py:65
  93.5 26.7 %collective-permute-start.18 = (bf16[320,512]{1,0:T(8,128)(2,1)}, bf16[320,512]{1,0:T(8,128)(2,1)}, u32[]{:S(2)}, u32[]{:S(2)}) collective-permute-start(bf16[320,512]{1,0:T(8,128)(2,1)} %get-tuple-element.79), channel_id=1, source_target_pairs={{0,32},{1,33},{2,34},{3,35},{4,36},{5,37},{6,38},{7,39},{8,40},{9,... | collective-permute-start | bytes 983048 | tf_op jit(solution)/shard_map/ppermute | solution.py:65
  101.6 29.4 %collective-permute-start.7 = (bf16[512,512]{1,0:T(8,128)(2,1)}, bf16[512,512]{1,0:T(8,128)(2,1)}, u32[]{:S(2)}, u32[]{:S(2)}) collective-permute-start(bf16[512,512]{1,0:T(8,128)(2,1)} %get-tuple-element.64), channel_id=1, source_target_pairs={{0,64},{1,5},{2,66},{3,7},{4,68},{5,9},{6,70},{7,11},{8,72},{9,13}... | collective-permute-start | bytes 1572872 | tf_op jit(solution)/shard_map/ppermute | solution.py:65
  106.3 24.7 %collective-permute-start.8 = (bf16[512,512]{1,0:T(8,128)(2,1)}, bf16[512,512]{1,0:T(8,128)(2,1)}, u32[]{:S(2)}, u32[]{:S(2)}) collective-permute-start(bf16[512,512]{1,0:T(8,128)(2,1)} %get-tuple-element.65), channel_id=1, source_target_pairs={{0,2},{1,9},{2,0},{3,11},{4,6},{5,13},{6,4},{7,15},{8,10},{9,1},{1... | collective-permute-start | bytes 1572872 | tf_op jit(solution)/shard_map/ppermute | solution.py:65
  107.5 23.5 %collective-permute-start.9 = (bf16[512,512]{1,0:T(8,128)(2,1)}, bf16[512,512]{1,0:T(8,128)(2,1)}, u32[]{:S(2)}, u32[]{:S(2)}) collective-permute-start(bf16[512,512]{1,0:T(8,128)(2,1)} %get-tuple-element.66), channel_id=1, source_target_pairs={{0,66},{1,13},{2,64},{3,15},{4,70},{5,1},{6,68},{7,3},{8,74},{9,5}... | collective-permute-start | bytes 1572872 | tf_op jit(solution)/shard_map/ppermute | solution.py:65
  109.6 10.6 %all-to-all-start.1 = ((bf16[8,32,512]{2,1,0:T(8,128)(2,1)}), bf16[8,32,512]{2,1,0:T(8,128)(2,1)S(1)}, u32[]{:S(2)}, u32[]{:S(2)}) async-start(bf16[8,32,512]{2,1,0:T(8,128)(2,1)} %sum_margin.1), calls=%async_computation.1 | async-start | bytes 524288 | tf_op jit(solution)/shard_map/all_to_all | solution.py:697
  113.0 12.5 %collective-permute-start.19 = (bf16[320,512]{1,0:T(8,128)(2,1)}, bf16[320,512]{1,0:T(8,128)(2,1)}, u32[]{:S(2)}, u32[]{:S(2)}) collective-permute-start(bf16[320,512]{1,0:T(8,128)(2,1)} %copy-done.25), channel_id=1, source_target_pairs={{0,48},{1,49},{2,50},{3,51},{4,52},{5,53},{6,54},{7,55},{8,56},{9,... | collective-permute-start | bytes 983048 | tf_op jit(solution)/shard_map/ppermute | solution.py:65
  120.2 19.3 %collective-permute-start.23 = (bf16[256,512]{1,0:T(8,128)(2,1)S(1)}, bf16[256,512]{1,0:T(8,128)(2,1)S(1)}, u32[]{:S(2)}, u32[]{:S(2)}) collective-permute-start(bf16[256,512]{1,0:T(8,128)(2,1)S(1)} %bitcast.1), channel_id=1, source_target_pairs={{0,1},{1,0},{2,3},{3,2},{4,5},{5,4},{6,7},{7,6},{8,9},{9,8},{10,11... | collective-permute-start | bytes 786440 | tf_op jit(solution)/shard_map/ppermute | solution.py:65
  128.6 12.1 %copy-start.26 = (bf16[80,512]{1,0:T(8,128)(2,1)S(1)}, bf16[80,512]{1,0:T(8,128)(2,1)}, u32[]{:S(2)}) copy-start(bf16[80,512]{1,0:T(8,128)(2,1)} %get-tuple-element.84) | copy-start | bytes 245764
  128.6 12.1 %collective-permute-start.20 = (bf16[80,512]{1,0:T(8,128)(2,1)}, bf16[80,512]{1,0:T(8,128)(2,1)S(1)}, u32[]{:S(2)}, u32[]{:S(2)}) collective-permute-start(bf16[80,512]{1,0:T(8,128)(2,1)} %get-tuple-element.82), channel_id=1, source_target_pairs={{0,4},{1,5},{2,6},{3,7},{4,8},{5,9},{6,10},{7,11},{8,12},{9,13},{1... | collective-permute-start | bytes 245768 | tf_op jit(solution)/shard_map/ppermute | solution.py:65
  134.5 10.7 %collective-permute-start.10 = (bf16[128,512]{1,0:T(8,128)(2,1)}, bf16[128,512]{1,0:T(8,128)(2,1)S(1)}, u32[]{:S(2)}, u32[]{:S(2)}) collective-permute-start(bf16[128,512]{1,0:T(8,128)(2,1)} %get-tuple-element.68), channel_id=1, source_target_pairs={{0,16},{1,65},{2,18},{3,67},{4,20},{5,69},{6,22},{7,71},{8,24},{9,... | collective-permute-start | bytes 393224 | tf_op jit(solution)/shard_map/ppermute | solution.py:65
  134.8 10.4 %collective-permute-start.11 = (bf16[128,512]{1,0:T(8,128)(2,1)}, bf16[128,512]{1,0:T(8,128)(2,1)S(1)}, u32[]{:S(2)}, u32[]{:S(2)}) collective-permute-start(bf16[128,512]{1,0:T(8,128)(2,1)} %get-tuple-element.69), channel_id=1, source_target_pairs={{0,32},{1,3},{2,34},{3,1},{4,36},{5,7},{6,38},{7,5},{8,40},{9,11},... | collective-permute-start | bytes 393224 | tf_op jit(solution)/shard_map/ppermute | solution.py:65
  137.4 7.7 %collective-permute-start.12 = (bf16[128,512]{1,0:T(8,128)(2,1)}, bf16[128,512]{1,0:T(8,128)(2,1)S(1)}, u32[]{:S(2)}, u32[]{:S(2)}) collective-permute-start(bf16[128,512]{1,0:T(8,128)(2,1)} %get-tuple-element.70), channel_id=1, source_target_pairs={{0,48},{1,67},{2,50},{3,65},{4,52},{5,71},{6,54},{7,69},{8,56},{9,... | collective-permute-start | bytes 393224 | tf_op jit(solution)/shard_map/ppermute | solution.py:65
  139.4 5.6 %collective-permute-start.21 = (bf16[80,512]{1,0:T(8,128)(2,1)S(1)}, bf16[80,512]{1,0:T(8,128)(2,1)S(1)}, u32[]{:S(2)}, u32[]{:S(2)}) collective-permute-start(bf16[80,512]{1,0:T(8,128)(2,1)S(1)} %copy-done.27), channel_id=1, source_target_pairs={{0,8},{1,9},{2,10},{3,11},{4,12},{5,13},{6,14},{7,15},{8,0},{9,1},... | collective-permute-start | bytes 245768 | tf_op jit(solution)/shard_map/ppermute | solution.py:65
  140.7 4.5 %collective-permute-start.22 = (bf16[80,512]{1,0:T(8,128)(2,1)S(1)}, bf16[80,512]{1,0:T(8,128)(2,1)S(1)}, u32[]{:S(2)}, u32[]{:S(2)}) collective-permute-start(bf16[80,512]{1,0:T(8,128)(2,1)S(1)} %copy-done.26), channel_id=1, source_target_pairs={{0,12},{1,13},{2,14},{3,15},{4,0},{5,1},{6,2},{7,3},{8,4},{9,5},{1... | collective-permute-start | bytes 245768 | tf_op jit(solution)/shard_map/ppermute | solution.py:65
  147.5 4.8 %collective-permute-start.42 = (bf16[80,512]{1,0:T(8,128)(2,1)S(1)}, bf16[80,512]{1,0:T(8,128)(2,1)S(1)}, u32[]{:S(2)}, u32[]{:S(2)}) collective-permute-start(bf16[80,512]{1,0:T(8,128)(2,1)S(1)} %get-tuple-element.94.refs_0_), channel_id=1, source_target_pairs={{0,12},{1,13},{2,14},{3,15},{4,0},{5,1},{6,2},{7,3},{8,4},{9,5},{1... | collective-permute-start | bytes 245768 | tf_op jit(solution)/shard_map/ppermute | solution.py:65
  150.6 4.9 %collective-permute-start.41 = (bf16[80,512]{1,0:T(8,128)(2,1)S(1)}, bf16[80,512]{1,0:T(8,128)(2,1)S(1)}, u32[]{:S(2)}, u32[]{:S(2)}) collective-permute-start(bf16[80,512]{1,0:T(8,128)(2,1)S(1)} %get-tuple-element.94.refs_0_), channel_id=1, source_target_pairs={{0,8},{1,9},{2,10},{3,11},{4,12},{5,13},{6,14},{7,15},{8,0},{9,1},... | collective-permute-start | bytes 245768 | tf_op jit(solution)/shard_map/ppermute | solution.py:65
  150.6 5.9 %collective-permute-start.40 = (bf16[80,512]{1,0:T(8,128)(2,1)S(1)}, bf16[80,512]{1,0:T(8,128)(2,1)S(1)}, u32[]{:S(2)}, u32[]{:S(2)}) collective-permute-start(bf16[80,512]{1,0:T(8,128)(2,1)S(1)} %get-tuple-element.94.refs_0_), channel_id=1, source_target_pairs={{0,4},{1,5},{2,6},{3,7},{4,8},{5,9},{6,10},{7,11},{8,12},{9,13},{1... | collective-permute-start | bytes 245768 | tf_op jit(solution)/shard_map/ppermute | solution.py:65
  157.0 11.3 %collective-permute-start.46 = (bf16[320,512]{1,0:T(8,128)(2,1)S(1)}, bf16[320,512]{1,0:T(8,128)(2,1)S(1)}, u32[]{:S(2)}, u32[]{:S(2)}) collective-permute-start(bf16[320,512]{1,0:T(8,128)(2,1)S(1)} %shard_map.88.refs_0_), channel_id=1, source_target_pairs={{0,1},{1,0},{2,3},{3,2},{4,5},{5,4},{6,7},{7,6},{8,9},{9,8},{10,11... | collective-permute-start | bytes 983048 | tf_op jit(solution)/shard_map/ppermute | solution.py:65
  159.1 9.7 %collective-permute-start.45 = (bf16[320,512]{1,0:T(8,128)(2,1)S(1)}, bf16[320,512]{1,0:T(8,128)(2,1)S(1)}, u32[]{:S(2)}, u32[]{:S(2)}) collective-permute-start(bf16[320,512]{1,0:T(8,128)(2,1)S(1)} %shard_map.88.refs_0_), channel_id=1, source_target_pairs={{0,48},{1,49},{2,50},{3,51},{4,52},{5,53},{6,54},{7,55},{8,56},{9,... | collective-permute-start | bytes 983048 | tf_op jit(solution)/shard_map/ppermute | solution.py:65
  160.0 4.1 %collective-permute-start.26 = (bf16[128,512]{1,0:T(8,128)(2,1)S(1)}, bf16[128,512]{1,0:T(8,128)(2,1)S(1)}, u32[]{:S(2)}, u32[]{:S(2)}) collective-permute-start(bf16[128,512]{1,0:T(8,128)(2,1)S(1)} %get-tuple-element.85.refs_0_), channel_id=1, source_target_pairs={{0,48},{1,67},{2,50},{3,65},{4,52},{5,71},{6,54},{7,69},{8,56},{9,... | collective-permute-start | bytes 393224 | tf_op jit(solution)/shard_map/ppermute | solution.py:65
  160.4 5.6 %collective-permute-start.25 = (bf16[128,512]{1,0:T(8,128)(2,1)S(1)}, bf16[128,512]{1,0:T(8,128)(2,1)S(1)}, u32[]{:S(2)}, u32[]{:S(2)}) collective-permute-start(bf16[128,512]{1,0:T(8,128)(2,1)S(1)} %get-tuple-element.85.refs_0_), channel_id=1, source_target_pairs={{0,32},{1,3},{2,34},{3,1},{4,36},{5,7},{6,38},{7,5},{8,40},{9,11},... | collective-permute-start | bytes 393224 | tf_op jit(solution)/shard_map/ppermute | solution.py:65
  161.1 6.0 %collective-permute-start.24 = (bf16[128,512]{1,0:T(8,128)(2,1)S(1)}, bf16[128,512]{1,0:T(8,128)(2,1)S(1)}, u32[]{:S(2)}, u32[]{:S(2)}) collective-permute-start(bf16[128,512]{1,0:T(8,128)(2,1)S(1)} %get-tuple-element.85.refs_0_), channel_id=1, source_target_pairs={{0,16},{1,65},{2,18},{3,67},{4,20},{5,69},{6,22},{7,71},{8,24},{9,... | collective-permute-start | bytes 393224 | tf_op jit(solution)/shard_map/ppermute | solution.py:65
  164.1 8.3 %collective-permute-start.44 = (bf16[320,512]{1,0:T(8,128)(2,1)S(1)}, bf16[320,512]{1,0:T(8,128)(2,1)S(1)}, u32[]{:S(2)}, u32[]{:S(2)}) collective-permute-start(bf16[320,512]{1,0:T(8,128)(2,1)S(1)} %shard_map.88.refs_0_), channel_id=1, source_target_pairs={{0,32},{1,33},{2,34},{3,35},{4,36},{5,37},{6,38},{7,39},{8,40},{9,... | collective-permute-start | bytes 983048 | tf_op jit(solution)/shard_map/ppermute | solution.py:65
  166.0 15.2 %collective-permute-start.43 = (bf16[320,512]{1,0:T(8,128)(2,1)S(1)}, bf16[320,512]{1,0:T(8,128)(2,1)S(1)}, u32[]{:S(2)}, u32[]{:S(2)}) collective-permute-start(bf16[320,512]{1,0:T(8,128)(2,1)S(1)} %shard_map.88.refs_0_), channel_id=1, source_target_pairs={{0,16},{1,17},{2,18},{3,19},{4,20},{5,21},{6,22},{7,23},{8,24},{9,... | collective-permute-start | bytes 983048 | tf_op jit(solution)/shard_map/ppermute | solution.py:65
  167.7 16.9 %collective-permute-start.29 = (bf16[512,512]{1,0:T(8,128)(2,1)S(1)}, bf16[512,512]{1,0:T(8,128)(2,1)S(1)}, u32[]{:S(2)}, u32[]{:S(2)}) collective-permute-start(bf16[512,512]{1,0:T(8,128)(2,1)S(1)} %shard_map.85.refs_0_), channel_id=1, source_target_pairs={{0,66},{1,13},{2,64},{3,15},{4,70},{5,1},{6,68},{7,3},{8,74},{9,5}... | collective-permute-start | bytes 1572872 | tf_op jit(solution)/shard_map/ppermute | solution.py:65
  168.4 17.5 %collective-permute-start.28 = (bf16[512,512]{1,0:T(8,128)(2,1)S(1)}, bf16[512,512]{1,0:T(8,128)(2,1)S(1)}, u32[]{:S(2)}, u32[]{:S(2)}) collective-permute-start(bf16[512,512]{1,0:T(8,128)(2,1)S(1)} %shard_map.85.refs_0_), channel_id=1, source_target_pairs={{0,2},{1,9},{2,0},{3,11},{4,6},{5,13},{6,4},{7,15},{8,10},{9,1},{1... | collective-permute-start | bytes 1572872 | tf_op jit(solution)/shard_map/ppermute | solution.py:65
  168.8 20.1 %collective-permute-start.27 = (bf16[512,512]{1,0:T(8,128)(2,1)S(1)}, bf16[512,512]{1,0:T(8,128)(2,1)S(1)}, u32[]{:S(2)}, u32[]{:S(2)}) collective-permute-start(bf16[512,512]{1,0:T(8,128)(2,1)S(1)} %shard_map.85.refs_0_), channel_id=1, source_target_pairs={{0,64},{1,5},{2,66},{3,7},{4,68},{5,9},{6,70},{7,11},{8,72},{9,13}... | collective-permute-start | bytes 1572872 | tf_op jit(solution)/shard_map/ppermute | solution.py:65
  172.4 22.0 %collective-permute-start.49 = (bf16[320,512]{1,0:T(8,128)(2,1)S(1)}, bf16[320,512]{1,0:T(8,128)(2,1)S(1)}, u32[]{:S(2)}, u32[]{:S(2)}) collective-permute-start(bf16[320,512]{1,0:T(8,128)(2,1)S(1)} %collective-permute-done.45.refs_3_), channel_id=1, source_target_pairs={{0,1},{1,0},{2,3},{3,2},{4,5},{5,4},{6,7},{7,6},{8,9},{9,8},{10,11... | collective-permute-start | bytes 983048 | tf_op jit(solution)/shard_map/ppermute | solution.py:65
  181.2 13.2 %collective-permute-start.48 = (bf16[320,512]{1,0:T(8,128)(2,1)S(1)}, bf16[320,512]{1,0:T(8,128)(2,1)S(1)}, u32[]{:S(2)}, u32[]{:S(2)}) collective-permute-start(bf16[320,512]{1,0:T(8,128)(2,1)S(1)} %collective-permute-done.44.refs_2_), channel_id=1, source_target_pairs={{0,1},{1,0},{2,3},{3,2},{4,5},{5,4},{6,7},{7,6},{8,9},{9,8},{10,11... | collective-permute-start | bytes 983048 | tf_op jit(solution)/shard_map/ppermute | solution.py:65
  184.7 20.7 %collective-permute-start.30 = (bf16[512,512]{1,0:T(8,128)(2,1)S(1)}, bf16[512,512]{1,0:T(8,128)(2,1)S(1)}, u32[]{:S(2)}, u32[]{:S(2)}) collective-permute-start(bf16[512,512]{1,0:T(8,128)(2,1)S(1)} %shard_map.85.refs_0_), channel_id=1, source_target_pairs={{0,1},{1,0},{2,3},{3,2},{4,5},{5,4},{6,7},{7,6},{8,9},{9,8},{10,11... | collective-permute-start | bytes 1572872 | tf_op jit(solution)/shard_map/ppermute | solution.py:65
  185.9 22.1 %collective-permute-start.33 = (bf16[512,512]{1,0:T(8,128)(2,1)S(1)}, bf16[512,512]{1,0:T(8,128)(2,1)S(1)}, u32[]{:S(2)}, u32[]{:S(2)}) collective-permute-start(bf16[512,512]{1,0:T(8,128)(2,1)S(1)} %collective-permute-done.29.refs_3_), channel_id=1, source_target_pairs={{0,1},{1,0},{2,3},{3,2},{4,5},{5,4},{6,7},{7,6},{8,9},{9,8},{10,11... | collective-permute-start | bytes 1572872 | tf_op jit(solution)/shard_map/ppermute | solution.py:65
  188.9 19.3 %collective-permute-start.32 = (bf16[512,512]{1,0:T(8,128)(2,1)S(1)}, bf16[512,512]{1,0:T(8,128)(2,1)S(1)}, u32[]{:S(2)}, u32[]{:S(2)}) collective-permute-start(bf16[512,512]{1,0:T(8,128)(2,1)S(1)} %collective-permute-done.28.refs_2_), channel_id=1, source_target_pairs={{0,1},{1,0},{2,3},{3,2},{4,5},{5,4},{6,7},{7,6},{8,9},{9,8},{10,11... | collective-permute-start | bytes 1572872 | tf_op jit(solution)/shard_map/ppermute | solution.py:65
  194.4 13.8 %collective-permute-start.31 = (bf16[512,512]{1,0:T(8,128)(2,1)S(1)}, bf16[512,512]{1,0:T(8,128)(2,1)S(1)}, u32[]{:S(2)}, u32[]{:S(2)}) collective-permute-start(bf16[512,512]{1,0:T(8,128)(2,1)S(1)} %collective-permute-done.27.refs_1_), channel_id=1, source_target_pairs={{0,1},{1,0},{2,3},{3,2},{4,5},{5,4},{6,7},{7,6},{8,9},{9,8},{10,11... | collective-permute-start | bytes 1572872 | tf_op jit(solution)/shard_map/ppermute | solution.py:65
  194.4 2.7 collective-permute-start.47
  205.3 31.2 %collective-permute-start.50 = (bf16[128,2560]{1,0:T(8,128)(2,1)S(1)}, bf16[128,2560]{1,0:T(8,128)(2,1)S(1)}, u32[]{:S(2)}, u32[]{:S(2)}) collective-permute-start(bf16[128,2560]{1,0:T(8,128)(2,1)S(1)} %get-tuple-element.96), channel_id=1, source_target_pairs={{0,64},{1,65},{2,66},{3,67},{4,68},{5,69},{6,70},{7,71},{8,72},{9,... | collective-permute-start | bytes 1966088 | tf_op jit(solution)/shard_map/ppermute | solution.py:65
  205.4 31.1 %collective-permute-start.51 = (bf16[128,2560]{1,0:T(8,128)(2,1)S(1)}, bf16[128,2560]{1,0:T(8,128)(2,1)S(1)}, u32[]{:S(2)}, u32[]{:S(2)}) collective-permute-start(bf16[128,2560]{1,0:T(8,128)(2,1)S(1)} %get-tuple-element.97), channel_id=1, source_target_pairs={{0,66},{1,67},{2,64},{3,65},{4,70},{5,71},{6,68},{7,69},{8,74},{9,... | collective-permute-start | bytes 1966088 | tf_op jit(solution)/shard_map/ppermute | solution.py:65
  208.1 29.2 %collective-permute-start.52 = (bf16[128,2560]{1,0:T(8,128)(2,1)S(1)}, bf16[128,2560]{1,0:T(8,128)(2,1)S(1)}, u32[]{:S(2)}, u32[]{:S(2)}) collective-permute-start(bf16[128,2560]{1,0:T(8,128)(2,1)S(1)} %get-tuple-element.98), channel_id=1, source_target_pairs={{0,2},{1,3},{2,0},{3,1},{4,6},{5,7},{6,4},{7,5},{8,10},{9,11},{10,... | collective-permute-start | bytes 1966088 | tf_op jit(solution)/shard_map/ppermute | solution.py:65
  212.6 26.6 %collective-permute-start.37 = (bf16[128,2048]{1,0:T(8,128)(2,1)S(1)}, bf16[128,2048]{1,0:T(8,128)(2,1)S(1)}, u32[]{:S(2)}, u32[]{:S(2)}) collective-permute-start(bf16[128,2048]{1,0:T(8,128)(2,1)S(1)} %get-tuple-element.91), channel_id=1, source_target_pairs={{0,4},{1,5},{2,6},{3,7},{4,8},{5,9},{6,10},{7,11},{8,12},{9,13},{1... | collective-permute-start | bytes 1572872 | tf_op jit(solution)/shard_map/ppermute | solution.py:65
  217.2 48.6 %copy-start.20 = (bf16[128,2560]{1,0:T(8,128)(2,1)S(1)}, bf16[128,2560]{1,0:T(8,128)(2,1)}, u32[]{:S(2)}) copy-start(bf16[128,2560]{1,0:T(8,128)(2,1)} %get-tuple-element.95.refs_0_) | copy-start | bytes 1966084
  217.2 54.7 %collective-permute-start.34 = (bf16[128,2048]{1,0:T(8,128)(2,1)S(1)}, bf16[128,2048]{1,0:T(8,128)(2,1)S(1)}, u32[]{:S(2)}, u32[]{:S(2)}) collective-permute-start(bf16[128,2048]{1,0:T(8,128)(2,1)S(1)} %get-tuple-element.87), channel_id=1, source_target_pairs={{0,16},{1,17},{2,18},{3,19},{4,20},{5,21},{6,22},{7,23},{8,24},{9,... | collective-permute-start | bytes 1572872 | tf_op jit(solution)/shard_map/ppermute | solution.py:65
  236.5 32.9 %collective-permute-start.38 = (bf16[128,2048]{1,0:T(8,128)(2,1)S(1)}, bf16[128,2048]{1,0:T(8,128)(2,1)S(1)}, u32[]{:S(2)}, u32[]{:S(2)}) collective-permute-start(bf16[128,2048]{1,0:T(8,128)(2,1)S(1)} %get-tuple-element.92), channel_id=1, source_target_pairs={{0,12},{1,13},{2,14},{3,15},{4,0},{5,1},{6,2},{7,3},{8,4},{9,5},{1... | collective-permute-start | bytes 1572872 | tf_op jit(solution)/shard_map/ppermute | solution.py:65
  236.5 32.9 %collective-permute-start.39 = (bf16[128,2048]{1,0:T(8,128)(2,1)S(1)}, bf16[128,2048]{1,0:T(8,128)(2,1)S(1)}, u32[]{:S(2)}, u32[]{:S(2)}) collective-permute-start(bf16[128,2048]{1,0:T(8,128)(2,1)S(1)} %get-tuple-element.93), channel_id=1, source_target_pairs={{0,8},{1,9},{2,10},{3,11},{4,12},{5,13},{6,14},{7,15},{8,0},{9,1},... | collective-permute-start | bytes 1572872 | tf_op jit(solution)/shard_map/ppermute | solution.py:65
  237.2 34.7 %collective-permute-start.35 = (bf16[128,2048]{1,0:T(8,128)(2,1)S(1)}, bf16[128,2048]{1,0:T(8,128)(2,1)S(1)}, u32[]{:S(2)}, u32[]{:S(2)}) collective-permute-start(bf16[128,2048]{1,0:T(8,128)(2,1)S(1)} %get-tuple-element.88), channel_id=1, source_target_pairs={{0,48},{1,49},{2,50},{3,51},{4,52},{5,53},{6,54},{7,55},{8,56},{9,... | collective-permute-start | bytes 1572872 | tf_op jit(solution)/shard_map/ppermute | solution.py:65
  239.2 32.7 %collective-permute-start.36 = (bf16[128,2048]{1,0:T(8,128)(2,1)S(1)}, bf16[128,2048]{1,0:T(8,128)(2,1)S(1)}, u32[]{:S(2)}, u32[]{:S(2)}) collective-permute-start(bf16[128,2048]{1,0:T(8,128)(2,1)S(1)} %get-tuple-element.89), channel_id=1, source_target_pairs={{0,32},{1,33},{2,34},{3,35},{4,36},{5,37},{6,38},{7,39},{8,40},{9,... | collective-permute-start | bytes 1572872 | tf_op jit(solution)/shard_map/ppermute | solution.py:65
  (19 other events, 109.9 us)

commit v6 on v5

--- a/solution.py
+++ b/solution.py
@@ -264,7 +264,7 @@
     if own:
         other, gathered, outs, (base, total, mine, base_sem, out_sem, in_sem) = refs[0], refs[1], refs[2:6], refs[6:]
     else:
-        total, gathered, base, gather, mine, base_sem, out_sem, in_sem = refs
+        total, gathered, base, gather, mine, base_sem, out_sem, in_sem, y_sem = refs
     chunk, tile = GROUPS[group][0], TILE[group]
     core, u = place(where, "core"), place(where, "u%d" % group)
 
@@ -315,19 +315,36 @@
     else:
         ring, four = ("z", blocks[4:]) if group == 0 else ("x", blocks)
         start_basis(ring, where, four, basis, gather, base_sem)
-
-        def with_gather(first):
-            fetch(four[0], first).wait()
-            multiply(four[1:], gather, first)
-
+        if group == 0:
+
+            @pl.when(core == 1)
+            def _():
+                fetch(blocks[0], 0)
+                start_basis("y", where, blocks[:4], basis, base, y_sem)
+
+            @pl.when(core == 0)
+            def _():
+                fetch(blocks[4], 0)
+
+        else:
+            fetch(blocks[0], (1 - core) * chunk)
         wait_for(gather, base_sem)
         out_copy = pltpu.make_async_copy(gather, gathered, out_sem)
         out_copy.start()
+        wait_for(mine, in_sem)
         if group == 0:
-            pl.when(core == 1)(with_y)
-            pl.when(core == 0)(lambda: with_gather(0))
+
+            @pl.when(core == 1)
+            def _():
+                wait_for(base, y_sem)
+                multiply(blocks[1:4], base, 0)
+
+            @pl.when(core == 0)
+            def _():
+                multiply(blocks[5:], gather, 0)
+
         else:
-            with_gather((1 - core) * chunk)
+            multiply(blocks[1:], gather, (1 - core) * chunk)
         out_copy.wait()
         return
     stores = []
@@ -361,7 +378,8 @@
             DMA,
             DMA((4,)) if own else DMA,
             DMA,
-        ],
+        ]
+        + ([] if own else [DMA]),
         compiler_params=LIMIT,
         cost_estimate=estimate(2 * 512 * 512 * chunk, 512 * chunk * 2 + 512 * 1024 + chunk * 1024),
     )(
@@ -373,12 +391,12 @@
 
 
 def add_kernel(group, where, mine, b, c, d, *refs):
-    outs, total, a, sem, in_sem = refs[:4], refs[4], refs[5], refs[6], refs[7]
+    outs, total, a, far, sem, in_sem = refs[:4], refs[4], refs[5], refs[6], refs[7], refs[8]
     piece = GROUPS[group][1]
-    wait_all(start_all([pltpu.make_async_copy(mine, a, in_sem)]))
-    total[...] = (
-        (a[...].astype(F32) + b[...].astype(F32)) + (c[...].astype(F32) + d[...].astype(F32))
-    ).astype(BF)
+    loads = start_all([pltpu.make_async_copy(mine, a, in_sem)])
+    far[...] = b[...].astype(F32) + (c[...].astype(F32) + d[...].astype(F32))
+    wait_all(loads)
+    total[...] = (a[...].astype(F32) + far[...]).astype(BF)
     copies = []
     for j in range(4):
         at = (place(where, "v%d" % group) + j) % 4
@@ -393,7 +411,7 @@
         out_shape=[pltpu.HBM((piece, 512), BF)] * 4,
         in_specs=[SMEM, ANY] + [VMEM] * 3,
         out_specs=[ANY] * 4,
-        scratch_shapes=[pltpu.VMEM((chunk // 4, 512), BF)] * 2 + [DMA((4,)), DMA],
+        scratch_shapes=[pltpu.VMEM((chunk // 4, 512), BF)] * 2 + [pltpu.VMEM((chunk // 4, 512), F32), DMA((4,)), DMA],
         compiler_params=LIMIT,
         cost_estimate=estimate(3 * chunk * 128, 5 * chunk * 256),
     )(where, in_hbm(arrays[0]), *arrays[1:])

time: 280 us -> 280 us (level)
  no operation moved by 1% of the time
where the time goes in v6:
time: 280 us; the launch traced here: 274 us
  starting transfers between devices  113 us (40%)
  Pallas kernels  70.2 us (25%)
  waiting for transfers between devices  61 us (22%)
  blocking collectives  23.2 us (8%)
  local copies, waits for them, and re-layouts  5.04 us (2%)
    ppermute x53, starting transfers between devices, shift(): return lax.ppermute(array, NAMES, pairs)  103 us
    ppermute x53, waiting for transfers between devices, shift(): return lax.ppermute(array, NAMES, pairs)  56.4 us
    all_to_all x1, blocking collectives, compute(): new = lax.all_to_all(new, ROW, 0, 0, tiled=True)  23.2 us
    pallas_call x4, Pallas kernels, project(): pl.pallas_call(functools.partial(project_kernel, group, own), out_shape=s...  19.8 us
    pallas_call x3, Pallas kernels, update_blocks(): pl.pallas_call(functools.partial(update_kernel, ring), out_shape=blocks_o...  17.2 us
    pallas_call x3, Pallas kernels, unpack(): pl.pallas_call(functools.partial(unpack_kernel, ring), out_shape=jax.Shap...  8.48 us
    pallas_call x3, Pallas kernels, pack(): pl.pallas_call(functools.partial(pack_kernel, ring), out_shape=[(jax.Shap...  8.01 us
    all_to_all x1, starting transfers between devices, compute(): moments = lax.all_to_all(moments, ROW, 0, 0, tiled=True)  6.82 us
  transfers between devices with their start and end apart: 55, of which 17 were waited for; matrix products, arithmetic and copies ran while one was open for 0% of the time, Pallas kernels for 23%

profile of v6, /device:TPU:1, one launch (start us, length us, event | category | flops | bytes accessed | tf_op | source)
XLA Modules:
  0.0 274.3 jit_solution(17985585936735129079)
XLA Ops:
  0.7 1.6 copy-done
  2.3 2.5 shard_map.76
  4.7 2.3 collective-permute-start
  7.1 2.6 shard_map.77
  9.6 1.8 collective-permute-start.3
  11.5 2.6 collective-permute-start.4
  15.2 1.8 collective-permute-start.1
  16.9 3.5 %collective-permute-done.refs_1_ = bf16[128,2048]{1,0:T(8,128)(2,1)S(1)} collective-permute-done((bf16[128,2048]{1,0:T(8,128)(2,1)S(1)}, bf16[128,2048]{1,0:T(8,128)(2,1)S(1)}, u32[]{:S(2)}, u32[]{:S(2)}) %collective-permute-start) | collective-permute-done | bytes 524320 | tf_op jit(solution)/shard_map/ppermute | solution.py:65
  20.5 1.2 collective-permute-start.2
  21.7 3.0 %shard_map.81 = (bf16[128,2560]{1,0:T(8,128)(2,1)}, bf16[128,3072]{1,0:T(8,128)(2,1)S(1)}, bf16[128,3072]{1,0:T(8,128)(2,1)S(1)}, bf16[128,2560]{1,0:T(8,128)(2,1)S(1)}) custom-call(s32[8]{0:T(128)S(1)} %compare_select_fusion.6.where, bf16[128,26624]{1,0:T(8,128)(2,1)} %grad.5, bf16[2048,512]{1,0:T(8,128)(2,1)S(1)} %copy-done), custom_call_target="tpu_custom_call" | custom-call | bytes 6291456 | tf_op jit(solution)/shard_map/pallas_call | solution.py:168
  24.6 2.5 collective-permute-done.1.refs_2_
  27.1 1.2 collective-permute-start.13
  28.3 5.9 %collective-permute-done.2.refs_3_ = bf16[128,2048]{1,0:T(8,128)(2,1)S(1)} collective-permute-done((bf16[128,2048]{1,0:T(8,128)(2,1)S(1)}, bf16[128,2048]{1,0:T(8,128)(2,1)S(1)}, u32[]{:S(2)}, u32[]{:S(2)}) %collective-permute-start.2) | collective-permute-done | bytes 524320 | tf_op jit(solution)/shard_map/ppermute | solution.py:65
  34.2 2.5 collective-permute-start.14
  37.2 5.9 %collective-permute-done.5.refs_7_ = bf16[128,2560]{1,0:T(8,128)(2,1)S(1)} collective-permute-done((bf16[128,2560]{1,0:T(8,128)(2,1)S(1)}, bf16[128,2560]{1,0:T(8,128)(2,1)S(1)}, u32[]{:S(2)}, u32[]{:S(2)}) %collective-permute-start.5) | collective-permute-done | bytes 655392 | tf_op jit(solution)/shard_map/ppermute | solution.py:65
  43.1 5.0 %shard_map.78 = (bf16[2048,512]{1,0:T(8,128)(2,1)}, bf16[512,512]{1,0:T(8,128)(2,1)}) custom-call(s32[8]{0:T(128)S(1)} %compare_select_fusion.6.where, bf16[128,2048]{1,0:T(8,128)(2,1)} %get-tuple-element.53.refs_0_, bf16[128,2048]{1,0:T(8,128)(2,1)S(1)} %collective-permute-done.refs_1_, bf16[128,2048]{1,0:T(8,128)(2,1)S(1)} %collective-permute-done.1.refs_2_, ...), custom_call_target="tpu_custom_call" | custom-call | flops 1073741824 | bytes 4718592 | tf_op jit(solution)/shard_map/pallas_call | solution.py:369
  48.2 2.4 collective-permute-start.6
  50.6 4.4 %shard_map.82 = (bf16[1280,512]{1,0:T(8,128)(2,1)}, bf16[512,512]{1,0:T(8,128)(2,1)}) custom-call(s32[8]{0:T(128)S(1)} %compare_select_fusion.6.where, bf16[128,2560]{1,0:T(8,128)(2,1)} %get-tuple-element.71.refs_0_, bf16[128,3072]{1,0:T(8,128)(2,1)S(1)} %collective-permute-done.13.refs_1_, bf16[128,3072]{1,0:T(8,128)(2,1)S(1)} %collective-permute-done.14.refs_2_, ...), custom_call_target="tpu_custom_call" | custom-call | flops 671088640 | bytes 3145728 | tf_op jit(solution)/shard_map/pallas_call | solution.py:369
  55.1 17.9 %collective-permute-start.16 = (bf16[1280,512]{1,0:T(8,128)(2,1)}, bf16[1280,512]{1,0:T(8,128)(2,1)}, u32[]{:S(2)}, u32[]{:S(2)}) collective-permute-start(bf16[1280,512]{1,0:T(8,128)(2,1)} %get-tuple-element.75), channel_id=1, source_target_pairs={{0,1},{1,0},{2,3},{3,2},{4,5},{5,4},{6,7},{7,6},{8,9},{9,8},{10,11... | collective-permute-start | bytes 3932168 | tf_op jit(solution)/shard_map/ppermute | solution.py:65
  72.9 4.1 %cut_moments.1 = bf16[8,256,256]{2,1,0:T(8,128)(2,1)} custom-call(s32[8]{0:T(128)S(1)} %compare_select_fusion.6.where, f32[64,1664]{1,0:T(8,128)S(1)} %copy-done.23, f32[64,1664]{1,0:T(8,128)S(1)} %copy-done.24, bf16[2048,512]{1,0:T(8,128)(2,1)S(1)} %copy-done, bf16[2048,512]{1,0:T(8,128)(2,1)} %old.1), custom_call_target="tpu_custom_call" | custom-call | flops 536870912 | bytes 6291456 | tf_op jit(solution)/shard_map/cut_moments/pallas_call | solution.py:447
  77.0 6.8 %all-to-all-start = ((bf16[8,256,256]{2,1,0:T(8,128)(2,1)}), bf16[8,256,256]{2,1,0:T(8,128)(2,1)S(1)}, u32[]{:S(2)}, u32[]{:S(2)}) async-start(bf16[8,256,256]{2,1,0:T(8,128)(2,1)} %cut_moments.1), calls=%async_computation | async-start | bytes 2097152 | tf_op jit(solution)/shard_map/all_to_all | solution.py:713
  87.2 4.7 %shard_map.83 = (bf16[320,512]{1,0:T(8,128)(2,1)}, bf16[320,512]{1,0:T(8,128)(2,1)}, bf16[320,512]{1,0:T(8,128)(2,1)}, bf16[320,512]{1,0:T(8,128)(2,1)S(1)}) custom-call(s32[8]{0:T(128)S(1)} %compare_select_fusion.6.where, bf16[128,2560]{1,0:T(8,128)(2,1)} %get-tuple-element.71.refs_0_, bf16[128,3072]{1,0:T(8,128)(2,1)S(1)} %copy-done.3, ...), custom_call_target="tpu_custom_call" | custom-call | flops 671088640 | bytes 3145728 | tf_op jit(solution)/shard_map/pallas_call | solution.py:369
  91.9 1.5 collective-permute-start.17
  93.5 2.4 collective-permute-start.18
  95.9 5.7 %shard_map.79 = (bf16[512,512]{1,0:T(8,128)(2,1)}, bf16[512,512]{1,0:T(8,128)(2,1)}, bf16[512,512]{1,0:T(8,128)(2,1)}, bf16[512,512]{1,0:T(8,128)(2,1)}) custom-call(s32[8]{0:T(128)S(1)} %compare_select_fusion.6.where, bf16[128,2048]{1,0:T(8,128)(2,1)} %get-tuple-element.53.refs_0_, bf16[128,2048]{1,0:T(8,128)(2,1)S(1)} %copy-done.15, ...), custom_call_target="tpu_custom_call" | custom-call | flops 1073741824 | bytes 4718592 | tf_op jit(solution)/shard_map/pallas_call | solution.py:369
  101.6 4.6 %collective-permute-start.7 = (bf16[512,512]{1,0:T(8,128)(2,1)}, bf16[512,512]{1,0:T(8,128)(2,1)}, u32[]{:S(2)}, u32[]{:S(2)}) collective-permute-start(bf16[512,512]{1,0:T(8,128)(2,1)} %get-tuple-element.64), channel_id=1, source_target_pairs={{0,64},{1,5},{2,66},{3,7},{4,68},{5,9},{6,70},{7,11},{8,72},{9,13}... | collective-permute-start | bytes 1572872 | tf_op jit(solution)/shard_map/ppermute | solution.py:65
  106.3 1.2 collective-permute-start.8
  107.5 1.2 collective-permute-start.9
  109.6 3.4 %all-to-all-start.1 = ((bf16[8,32,512]{2,1,0:T(8,128)(2,1)}), bf16[8,32,512]{2,1,0:T(8,128)(2,1)S(1)}, u32[]{:S(2)}, u32[]{:S(2)}) async-start(bf16[8,32,512]{2,1,0:T(8,128)(2,1)} %sum_margin.1), calls=%async_computation.1 | async-start | bytes 524288 | tf_op jit(solution)/shard_map/all_to_all | solution.py:715
  113.0 2.6 collective-permute-start.19
  115.6 4.6 %all-to-all-done.1 = bf16[8,32,512]{2,1,0:T(8,128)(2,1)S(1)} async-done(((bf16[8,32,512]{2,1,0:T(8,128)(2,1)}), bf16[8,32,512]{2,1,0:T(8,128)(2,1)S(1)}, u32[]{:S(2)}, u32[]{:S(2)}) %all-to-all-start.1) | async-done | bytes 262176 | tf_op jit(solution)/shard_map/all_to_all | solution.py:715
  120.2 3.0 %collective-permute-start.23 = (bf16[256,512]{1,0:T(8,128)(2,1)S(1)}, bf16[256,512]{1,0:T(8,128)(2,1)S(1)}, u32[]{:S(2)}, u32[]{:S(2)}) collective-permute-start(bf16[256,512]{1,0:T(8,128)(2,1)S(1)} %bitcast.1), channel_id=1, source_target_pairs={{0,1},{1,0},{2,3},{3,2},{4,5},{5,4},{6,7},{7,6},{8,9},{9,8},{10,11... | collective-permute-start | bytes 786440 | tf_op jit(solution)/shard_map/ppermute | solution.py:65
  123.2 2.3 collective-permute-done.19.d
  125.5 3.0 %shard_map.84 = (bf16[80,512]{1,0:T(8,128)(2,1)}, bf16[80,512]{1,0:T(8,128)(2,1)}, bf16[80,512]{1,0:T(8,128)(2,1)}, bf16[80,512]{1,0:T(8,128)(2,1)}) custom-call(s32[8]{0:T(128)S(1)} %compare_select_fusion.6.where, bf16[320,512]{1,0:T(8,128)(2,1)} %get-tuple-element.77.mine, bf16[320,512]{1,0:T(8,128)(2,1)} %collective-permute-done.17.b, ...), custom_call_target="tpu_custom_call" | custom-call | flops 491520 | bytes 1638400 | tf_op jit(solution)/shard_map/pallas_call | solution.py:409
  128.5 2.6 collective-permute-start.20
  131.1 3.3 %shard_map.80 = (bf16[128,512]{1,0:T(8,128)(2,1)}, bf16[128,512]{1,0:T(8,128)(2,1)}, bf16[128,512]{1,0:T(8,128)(2,1)}, bf16[128,512]{1,0:T(8,128)(2,1)}) custom-call(s32[8]{0:T(128)S(1)} %compare_select_fusion.6.where, bf16[512,512]{1,0:T(8,128)(2,1)} %get-tuple-element.63.mine, bf16[512,512]{1,0:T(8,128)(2,1)} %collective-permute-done.7.b, ...), custom_call_target="tpu_custom_call" | custom-call | flops 786432 | bytes 2621440 | tf_op jit(solution)/shard_map/pallas_call | solution.py:409
  134.5 2.7 collective-permute-start.11
  137.2 2.0 collective-permute-start.12
  139.2 1.3 collective-permute-start.21
  140.5 1.1 collective-permute-start.22
  141.6 3.1 %collective-permute-done.21.refs_6_ = bf16[80,512]{1,0:T(8,128)(2,1)S(1)} collective-permute-done((bf16[80,512]{1,0:T(8,128)(2,1)S(1)}, bf16[80,512]{1,0:T(8,128)(2,1)S(1)}, u32[]{:S(2)}, u32[]{:S(2)}) %collective-permute-start.21) | collective-permute-done | bytes 81952 | tf_op jit(solution)/shard_map/ppermute | solution.py:65
  144.9 2.3 step.1
  147.2 3.1 %collective-permute-start.42 = (bf16[80,512]{1,0:T(8,128)(2,1)S(1)}, bf16[80,512]{1,0:T(8,128)(2,1)S(1)}, u32[]{:S(2)}, u32[]{:S(2)}) collective-permute-start(bf16[80,512]{1,0:T(8,128)(2,1)S(1)} %get-tuple-element.94.refs_0_), channel_id=1, source_target_pairs={{0,12},{1,13},{2,14},{3,15},{4,0},{5,1},{6,2},{7,3},{8,4},{9,5},{1... | collective-permute-start | bytes 245768 | tf_op jit(solution)/shard_map/ppermute | solution.py:65
  152.1 3.2 %collective-permute-done.41.refs_2_ = bf16[80,512]{1,0:T(8,128)(2,1)S(1)} collective-permute-done((bf16[80,512]{1,0:T(8,128)(2,1)S(1)}, bf16[80,512]{1,0:T(8,128)(2,1)S(1)}, u32[]{:S(2)}, u32[]{:S(2)}) %collective-permute-start.41) | collective-permute-done | bytes 81952 | tf_op jit(solution)/shard_map/ppermute | solution.py:65
  156.8 2.1 collective-permute-start.46
  161.3 2.5 collective-permute-done.26.refs_3_
  169.3 2.8 %collective-permute-done.44.refs_2_ = bf16[320,512]{1,0:T(8,128)(2,1)S(1)} collective-permute-done((bf16[320,512]{1,0:T(8,128)(2,1)S(1)}, bf16[320,512]{1,0:T(8,128)(2,1)S(1)}, u32[]{:S(2)}, u32[]{:S(2)}) %collective-permute-start.44) | collective-permute-done | bytes 327712 | tf_op jit(solution)/shard_map/ppermute | solution.py:65
  172.1 8.8 %collective-permute-start.49 = (bf16[320,512]{1,0:T(8,128)(2,1)S(1)}, bf16[320,512]{1,0:T(8,128)(2,1)S(1)}, u32[]{:S(2)}, u32[]{:S(2)}) collective-permute-start(bf16[320,512]{1,0:T(8,128)(2,1)S(1)} %collective-permute-done.45.refs_3_), channel_id=1, source_target_pairs={{0,1},{1,0},{2,3},{3,2},{4,5},{5,4},{6,7},{7,6},{8,9},{9,8},{10,11... | collective-permute-start | bytes 983048 | tf_op jit(solution)/shard_map/ppermute | solution.py:65
  181.0 3.4 %collective-permute-start.48 = (bf16[320,512]{1,0:T(8,128)(2,1)S(1)}, bf16[320,512]{1,0:T(8,128)(2,1)S(1)}, u32[]{:S(2)}, u32[]{:S(2)}) collective-permute-start(bf16[320,512]{1,0:T(8,128)(2,1)S(1)} %collective-permute-done.44.refs_2_), channel_id=1, source_target_pairs={{0,1},{1,0},{2,3},{3,2},{4,5},{5,4},{6,7},{7,6},{8,9},{9,8},{10,11... | collective-permute-start | bytes 983048 | tf_op jit(solution)/shard_map/ppermute | solution.py:65
  184.4 1.3 collective-permute-start.30
  185.7 3.0 %collective-permute-start.33 = (bf16[512,512]{1,0:T(8,128)(2,1)S(1)}, bf16[512,512]{1,0:T(8,128)(2,1)S(1)}, u32[]{:S(2)}, u32[]{:S(2)}) collective-permute-start(bf16[512,512]{1,0:T(8,128)(2,1)S(1)} %collective-permute-done.29.refs_3_), channel_id=1, source_target_pairs={{0,1},{1,0},{2,3},{3,2},{4,5},{5,4},{6,7},{7,6},{8,9},{9,8},{10,11... | collective-permute-start | bytes 1572872 | tf_op jit(solution)/shard_map/ppermute | solution.py:65
  188.6 5.5 %collective-permute-start.32 = (bf16[512,512]{1,0:T(8,128)(2,1)S(1)}, bf16[512,512]{1,0:T(8,128)(2,1)S(1)}, u32[]{:S(2)}, u32[]{:S(2)}) collective-permute-start(bf16[512,512]{1,0:T(8,128)(2,1)S(1)} %collective-permute-done.28.refs_2_), channel_id=1, source_target_pairs={{0,1},{1,0},{2,3},{3,2},{4,5},{5,4},{6,7},{7,6},{8,9},{9,8},{10,11... | collective-permute-start | bytes 1572872 | tf_op jit(solution)/shard_map/ppermute | solution.py:65
  194.7 2.2 collective-permute-done.47.refs_5_
  196.9 8.1 %shard_map.89 = (bf16[128,2560]{1,0:T(8,128)(2,1)}, bf16[128,2560]{1,0:T(8,128)(2,1)S(1)}, bf16[128,2560]{1,0:T(8,128)(2,1)S(1)}, bf16[128,2560]{1,0:T(8,128)(2,1)S(1)}) custom-call(s32[8]{0:T(128)S(1)} %compare_select_fusion.6.where, bf16[320,512]{1,0:T(8,128)(2,1)S(1)} %shard_map.88.refs_0_, bf16[320,512]{1,0:T(8,128)(2,1)S(1)} %collective-permute-done.43.refs_1_, ...), custom_call_target="tpu_custom_call" | custom-call | flops 1342177280 | bytes 5767168 | tf_op jit(solution)/shard_map/pallas_call | solution.py:671
  205.1 2.7 collective-permute-start.51
  208.0 4.6 %shard_map.87 = (bf16[128,2048]{1,0:T(8,128)(2,1)}, bf16[128,2048]{1,0:T(8,128)(2,1)S(1)}, bf16[128,2048]{1,0:T(8,128)(2,1)S(1)}, bf16[128,2048]{1,0:T(8,128)(2,1)S(1)}) custom-call(s32[8]{0:T(128)S(1)} %compare_select_fusion.6.where, bf16[512,512]{1,0:T(8,128)(2,1)S(1)} %shard_map.85.refs_0_, bf16[512,512]{1,0:T(8,128)(2,1)S(1)} %collective-permute-done.27.refs_1_, ...), custom_call_target="tpu_custom_call" | custom-call | flops 1073741824 | bytes 4718592 | tf_op jit(solution)/shard_map/pallas_call | solution.py:671
  212.6 4.5 %shard_map.86 = (bf16[128,2048]{1,0:T(8,128)(2,1)}, bf16[128,2048]{1,0:T(8,128)(2,1)S(1)}, bf16[128,2048]{1,0:T(8,128)(2,1)S(1)}, bf16[128,2048]{1,0:T(8,128)(2,1)S(1)}) custom-call(s32[8]{0:T(128)S(1)} %compare_select_fusion.6.where, bf16[512,512]{1,0:T(8,128)(2,1)S(1)} %shard_map.85.refs_0_, bf16[512,512]{1,0:T(8,128)(2,1)S(1)} %collective-permute-done.27.refs_1_, ...), custom_call_target="tpu_custom_call" | custom-call | flops 1073741824 | bytes 4718592 | tf_op jit(solution)/shard_map/pallas_call | solution.py:671
  217.3 19.0 %collective-permute-done.50.refs_1_ = bf16[128,2560]{1,0:T(8,128)(2,1)S(1)} collective-permute-done((bf16[128,2560]{1,0:T(8,128)(2,1)S(1)}, bf16[128,2560]{1,0:T(8,128)(2,1)S(1)}, u32[]{:S(2)}, u32[]{:S(2)}) %collective-permute-start.50) | collective-permute-done | bytes 655392 | tf_op jit(solution)/shard_map/ppermute | solution.py:65
  237.0 2.0 collective-permute-start.35
  238.9 1.4 collective-permute-start.36
  241.3 23.2 %all_to_all.15.new = bf16[8,128,256]{2,1,0:T(8,128)(2,1)S(1)} all-to-all(bf16[8,128,256]{2,1,0:T(8,128)(2,1)} %turn_back.1), channel_id=1, replica_groups=mesh['xl'=2,'z'=4,'y'=4,'xh'=2,'core'=2] {'xl','z'}, dimensions={0} | all-to-all | bytes 1048576 | tf_op jit(solution)/shard_map/all_to_all | solution.py:745
  265.6 3.6 %shard_map.90.refs_4_ = bf16[128,26624]{1,0:T(8,128)(2,1)} custom-call(s32[8]{0:T(128)S(1)} %compare_select_fusion.6.where, bf16[128,2560]{1,0:T(8,128)(2,1)S(1)} %copy-done.20, bf16[128,2560]{1,0:T(8,128)(2,1)S(1)} %collective-permute-done.50.refs_1_, bf16[128,2560]{1,0:T(8,128)(2,1)S(1)} %collective-permute-done.51.refs_2_, ...), custom_call_target="tpu_custom_call" | custom-call | bytes 5242880 | tf_op jit(solution)/shard_map/pallas_call | solution.py:230
  269.2 2.5 shard_map.91.refs_4_
  271.7 2.4 shard_map.92
  (126 shorter events, 21.1 us)
Async XLA Ops:
  4.7 15.7 %collective-permute-start = (bf16[128,2048]{1,0:T(8,128)(2,1)S(1)}, bf16[128,2048]{1,0:T(8,128)(2,1)S(1)}, u32[]{:S(2)}, u32[]{:S(2)}) collective-permute-start(bf16[128,2048]{1,0:T(8,128)(2,1)S(1)} %get-tuple-element.54), channel_id=1, source_target_pairs={{0,4},{1,5},{2,6},{3,7},{4,8},{5,9},{6,10},{7,11},{8,12},{9,13},{1... | collective-permute-start | bytes 1572872 | tf_op jit(solution)/shard_map/ppermute | solution.py:65
  9.6 27.0 %collective-permute-start.3 = (bf16[128,2560]{1,0:T(8,128)(2,1)S(1)}, bf16[128,2560]{1,0:T(8,128)(2,1)S(1)}, u32[]{:S(2)}, u32[]{:S(2)}) collective-permute-start(bf16[128,2560]{1,0:T(8,128)(2,1)S(1)} %get-tuple-element.58), channel_id=1, source_target_pairs={{0,16},{1,17},{2,18},{3,19},{4,20},{5,21},{6,22},{7,23},{8,24},{9,... | collective-permute-start | bytes 1966088 | tf_op jit(solution)/shard_map/ppermute | solution.py:65
  11.5 25.7 %collective-permute-start.4 = (bf16[128,2560]{1,0:T(8,128)(2,1)S(1)}, bf16[128,2560]{1,0:T(8,128)(2,1)S(1)}, u32[]{:S(2)}, u32[]{:S(2)}) collective-permute-start(bf16[128,2560]{1,0:T(8,128)(2,1)S(1)} %get-tuple-element.59), channel_id=1, source_target_pairs={{0,48},{1,49},{2,50},{3,51},{4,52},{5,53},{6,54},{7,55},{8,56},{9,... | collective-permute-start | bytes 1966088 | tf_op jit(solution)/shard_map/ppermute | solution.py:65
  14.0 29.0 %collective-permute-start.5 = (bf16[128,2560]{1,0:T(8,128)(2,1)S(1)}, bf16[128,2560]{1,0:T(8,128)(2,1)S(1)}, u32[]{:S(2)}, u32[]{:S(2)}) collective-permute-start(bf16[128,2560]{1,0:T(8,128)(2,1)S(1)} %get-tuple-element.60), channel_id=1, source_target_pairs={{0,32},{1,33},{2,34},{3,35},{4,36},{5,37},{6,38},{7,39},{8,40},{9,... | collective-permute-start | bytes 1966088 | tf_op jit(solution)/shard_map/ppermute | solution.py:65
  15.2 12.0 %collective-permute-start.1 = (bf16[128,2048]{1,0:T(8,128)(2,1)S(1)}, bf16[128,2048]{1,0:T(8,128)(2,1)S(1)}, u32[]{:S(2)}, u32[]{:S(2)}) collective-permute-start(bf16[128,2048]{1,0:T(8,128)(2,1)S(1)} %get-tuple-element.55), channel_id=1, source_target_pairs={{0,12},{1,13},{2,14},{3,15},{4,0},{5,1},{6,2},{7,3},{8,4},{9,5},{1... | collective-permute-start | bytes 1572872 | tf_op jit(solution)/shard_map/ppermute | solution.py:65
  20.5 22.6 %copy-start.14 = (bf16[128,2048]{1,0:T(8,128)(2,1)}, bf16[128,2048]{1,0:T(8,128)(2,1)S(1)}, u32[]{:S(2)}) copy-start(bf16[128,2048]{1,0:T(8,128)(2,1)S(1)} %collective-permute-done.refs_1_) | copy-start | bytes 1572868
  20.5 13.7 %collective-permute-start.2 = (bf16[128,2048]{1,0:T(8,128)(2,1)S(1)}, bf16[128,2048]{1,0:T(8,128)(2,1)S(1)}, u32[]{:S(2)}, u32[]{:S(2)}) collective-permute-start(bf16[128,2048]{1,0:T(8,128)(2,1)S(1)} %get-tuple-element.56), channel_id=1, source_target_pairs={{0,8},{1,9},{2,10},{3,11},{4,12},{5,13},{6,14},{7,15},{8,0},{9,1},... | collective-permute-start | bytes 1572872 | tf_op jit(solution)/shard_map/ppermute | solution.py:65
  27.1 21.0 %copy-start.16 = (bf16[128,2048]{1,0:T(8,128)(2,1)}, bf16[128,2048]{1,0:T(8,128)(2,1)S(1)}, u32[]{:S(2)}) copy-start(bf16[128,2048]{1,0:T(8,128)(2,1)S(1)} %collective-permute-done.1.refs_2_) | copy-start | bytes 1572868
  27.1 23.5 %collective-permute-start.13 = (bf16[128,3072]{1,0:T(8,128)(2,1)S(1)}, bf16[128,3072]{1,0:T(8,128)(2,1)S(1)}, u32[]{:S(2)}, u32[]{:S(2)}) collective-permute-start(bf16[128,3072]{1,0:T(8,128)(2,1)S(1)} %get-tuple-element.72), channel_id=1, source_target_pairs={{0,64},{1,65},{2,66},{3,67},{4,68},{5,69},{6,70},{7,71},{8,72},{9,... | collective-permute-start | bytes 2359304 | tf_op jit(solution)/shard_map/ppermute | solution.py:65
  34.2 13.9 %copy-start.18 = (bf16[128,2048]{1,0:T(8,128)(2,1)}, bf16[128,2048]{1,0:T(8,128)(2,1)S(1)}, u32[]{:S(2)}) copy-start(bf16[128,2048]{1,0:T(8,128)(2,1)S(1)} %collective-permute-done.2.refs_3_) | copy-start | bytes 1572868
  34.2 16.4 %collective-permute-start.14 = (bf16[128,3072]{1,0:T(8,128)(2,1)S(1)}, bf16[128,3072]{1,0:T(8,128)(2,1)S(1)}, u32[]{:S(2)}, u32[]{:S(2)}) collective-permute-start(bf16[128,3072]{1,0:T(8,128)(2,1)S(1)} %get-tuple-element.73), channel_id=1, source_target_pairs={{0,66},{1,67},{2,64},{3,65},{4,70},{5,71},{6,68},{7,69},{8,74},{9,... | collective-permute-start | bytes 2359304 | tf_op jit(solution)/shard_map/ppermute | solution.py:65
  36.7 11.5 %copy-start.6 = (bf16[128,2560]{1,0:T(8,128)(2,1)}, bf16[128,2560]{1,0:T(8,128)(2,1)S(1)}, u32[]{:S(2)}) copy-start(bf16[128,2560]{1,0:T(8,128)(2,1)S(1)} %collective-permute-done.3.refs_5_) | copy-start | bytes 1966084
  36.7 13.9 %collective-permute-start.15 = (bf16[128,2560]{1,0:T(8,128)(2,1)S(1)}, bf16[128,2560]{1,0:T(8,128)(2,1)S(1)}, u32[]{:S(2)}, u32[]{:S(2)}) collective-permute-start(bf16[128,2560]{1,0:T(8,128)(2,1)S(1)} %get-tuple-element.74), channel_id=1, source_target_pairs={{0,2},{1,3},{2,0},{3,1},{4,6},{5,7},{6,4},{7,5},{8,10},{9,11},{10,... | collective-permute-start | bytes 1966088 | tf_op jit(solution)/shard_map/ppermute | solution.py:65
  37.2 10.9 %copy-start.8 = (bf16[128,2560]{1,0:T(8,128)(2,1)}, bf16[128,2560]{1,0:T(8,128)(2,1)S(1)}, u32[]{:S(2)}) copy-start(bf16[128,2560]{1,0:T(8,128)(2,1)S(1)} %collective-permute-done.4.refs_6_) | copy-start | bytes 1966084
  48.2 47.7 %collective-permute-start.6 = (bf16[2048,512]{1,0:T(8,128)(2,1)}, bf16[2048,512]{1,0:T(8,128)(2,1)}, u32[]{:S(2)}, u32[]{:S(2)}) collective-permute-start(bf16[2048,512]{1,0:T(8,128)(2,1)} %get-tuple-element.61), channel_id=1, source_target_pairs={{0,1},{1,0},{2,3},{3,2},{4,5},{5,4},{6,7},{7,6},{8,9},{9,8},{10,11... | collective-permute-start | bytes 6291464 | tf_op jit(solution)/shard_map/ppermute | solution.py:65
  50.6 22.3 %copy-start.23 = (f32[64,1664]{1,0:T(8,128)S(1)}, f32[64,1664]{1,0:T(8,128)}, u32[]{:S(2)}) copy-start(f32[64,1664]{1,0:T(8,128)} %first.1) | copy-start | bytes 1277956
  50.6 22.3 %copy-start.24 = (f32[64,1664]{1,0:T(8,128)S(1)}, f32[64,1664]{1,0:T(8,128)}, u32[]{:S(2)}) copy-start(f32[64,1664]{1,0:T(8,128)} %second.1) | copy-start | bytes 1277956
  55.1 28.8 %collective-permute-start.16 = (bf16[1280,512]{1,0:T(8,128)(2,1)}, bf16[1280,512]{1,0:T(8,128)(2,1)}, u32[]{:S(2)}, u32[]{:S(2)}) collective-permute-start(bf16[1280,512]{1,0:T(8,128)(2,1)} %get-tuple-element.75), channel_id=1, source_target_pairs={{0,1},{1,0},{2,3},{3,2},{4,5},{5,4},{6,7},{7,6},{8,9},{9,8},{10,11... | collective-permute-start | bytes 3932168 | tf_op jit(solution)/shard_map/ppermute | solution.py:65
  77.0 31.7 %all-to-all-start = ((bf16[8,256,256]{2,1,0:T(8,128)(2,1)}), bf16[8,256,256]{2,1,0:T(8,128)(2,1)S(1)}, u32[]{:S(2)}, u32[]{:S(2)}) async-start(bf16[8,256,256]{2,1,0:T(8,128)(2,1)} %cut_moments.1), calls=%async_computation | async-start | bytes 2097152 | tf_op jit(solution)/shard_map/all_to_all | solution.py:713
  91.9 21.0 %collective-permute-start.17 = (bf16[320,512]{1,0:T(8,128)(2,1)}, bf16[320,512]{1,0:T(8,128)(2,1)}, u32[]{:S(2)}, u32[]{:S(2)}) collective-permute-start(bf16[320,512]{1,0:T(8,128)(2,1)} %get-tuple-element.78), channel_id=1, source_target_pairs={{0,16},{1,17},{2,18},{3,19},{4,20},{5,21},{6,22},{7,23},{8,24},{9,... | collective-permute-start | bytes 983048 | tf_op jit(solution)/shard_map/ppermute | solution.py:65
  93.5 26.7 %collective-permute-start.18 = (bf16[320,512]{1,0:T(8,128)(2,1)}, bf16[320,512]{1,0:T(8,128)(2,1)}, u32[]{:S(2)}, u32[]{:S(2)}) collective-permute-start(bf16[320,512]{1,0:T(8,128)(2,1)} %get-tuple-element.79), channel_id=1, source_target_pairs={{0,32},{1,33},{2,34},{3,35},{4,36},{5,37},{6,38},{7,39},{8,40},{9,... | collective-permute-start | bytes 983048 | tf_op jit(solution)/shard_map/ppermute | solution.py:65
  101.6 29.4 %collective-permute-start.7 = (bf16[512,512]{1,0:T(8,128)(2,1)}, bf16[512,512]{1,0:T(8,128)(2,1)}, u32[]{:S(2)}, u32[]{:S(2)}) collective-permute-start(bf16[512,512]{1,0:T(8,128)(2,1)} %get-tuple-element.64), channel_id=1, source_target_pairs={{0,64},{1,5},{2,66},{3,7},{4,68},{5,9},{6,70},{7,11},{8,72},{9,13}... | collective-permute-start | bytes 1572872 | tf_op jit(solution)/shard_map/ppermute | solution.py:65
  106.3 24.8 %collective-permute-start.8 = (bf16[512,512]{1,0:T(8,128)(2,1)}, bf16[512,512]{1,0:T(8,128)(2,1)}, u32[]{:S(2)}, u32[]{:S(2)}) collective-permute-start(bf16[512,512]{1,0:T(8,128)(2,1)} %get-tuple-element.65), channel_id=1, source_target_pairs={{0,2},{1,9},{2,0},{3,11},{4,6},{5,13},{6,4},{7,15},{8,10},{9,1},{1... | collective-permute-start | bytes 1572872 | tf_op jit(solution)/shard_map/ppermute | solution.py:65
  107.5 23.6 %collective-permute-start.9 = (bf16[512,512]{1,0:T(8,128)(2,1)}, bf16[512,512]{1,0:T(8,128)(2,1)}, u32[]{:S(2)}, u32[]{:S(2)}) collective-permute-start(bf16[512,512]{1,0:T(8,128)(2,1)} %get-tuple-element.66), channel_id=1, source_target_pairs={{0,66},{1,13},{2,64},{3,15},{4,70},{5,1},{6,68},{7,3},{8,74},{9,5}... | collective-permute-start | bytes 1572872 | tf_op jit(solution)/shard_map/ppermute | solution.py:65
  109.6 10.6 %all-to-all-start.1 = ((bf16[8,32,512]{2,1,0:T(8,128)(2,1)}), bf16[8,32,512]{2,1,0:T(8,128)(2,1)S(1)}, u32[]{:S(2)}, u32[]{:S(2)}) async-start(bf16[8,32,512]{2,1,0:T(8,128)(2,1)} %sum_margin.1), calls=%async_computation.1 | async-start | bytes 524288 | tf_op jit(solution)/shard_map/all_to_all | solution.py:715
  113.0 12.5 %collective-permute-start.19 = (bf16[320,512]{1,0:T(8,128)(2,1)}, bf16[320,512]{1,0:T(8,128)(2,1)}, u32[]{:S(2)}, u32[]{:S(2)}) collective-permute-start(bf16[320,512]{1,0:T(8,128)(2,1)} %copy-done.25), channel_id=1, source_target_pairs={{0,48},{1,49},{2,50},{3,51},{4,52},{5,53},{6,54},{7,55},{8,56},{9,... | collective-permute-start | bytes 983048 | tf_op jit(solution)/shard_map/ppermute | solution.py:65
  120.2 19.0 %collective-permute-start.23 = (bf16[256,512]{1,0:T(8,128)(2,1)S(1)}, bf16[256,512]{1,0:T(8,128)(2,1)S(1)}, u32[]{:S(2)}, u32[]{:S(2)}) collective-permute-start(bf16[256,512]{1,0:T(8,128)(2,1)S(1)} %bitcast.1), channel_id=1, source_target_pairs={{0,1},{1,0},{2,3},{3,2},{4,5},{5,4},{6,7},{7,6},{8,9},{9,8},{10,11... | collective-permute-start | bytes 786440 | tf_op jit(solution)/shard_map/ppermute | solution.py:65
  128.5 12.0 %copy-start.26 = (bf16[80,512]{1,0:T(8,128)(2,1)S(1)}, bf16[80,512]{1,0:T(8,128)(2,1)}, u32[]{:S(2)}) copy-start(bf16[80,512]{1,0:T(8,128)(2,1)} %get-tuple-element.84) | copy-start | bytes 245764
  128.5 12.0 %collective-permute-start.20 = (bf16[80,512]{1,0:T(8,128)(2,1)}, bf16[80,512]{1,0:T(8,128)(2,1)S(1)}, u32[]{:S(2)}, u32[]{:S(2)}) collective-permute-start(bf16[80,512]{1,0:T(8,128)(2,1)} %get-tuple-element.82), channel_id=1, source_target_pairs={{0,4},{1,5},{2,6},{3,7},{4,8},{5,9},{6,10},{7,11},{8,12},{9,13},{1... | collective-permute-start | bytes 245768 | tf_op jit(solution)/shard_map/ppermute | solution.py:65
  134.4 10.5 %collective-permute-start.10 = (bf16[128,512]{1,0:T(8,128)(2,1)}, bf16[128,512]{1,0:T(8,128)(2,1)S(1)}, u32[]{:S(2)}, u32[]{:S(2)}) collective-permute-start(bf16[128,512]{1,0:T(8,128)(2,1)} %get-tuple-element.68), channel_id=1, source_target_pairs={{0,16},{1,65},{2,18},{3,67},{4,20},{5,69},{6,22},{7,71},{8,24},{9,... | collective-permute-start | bytes 393224 | tf_op jit(solution)/shard_map/ppermute | solution.py:65
  134.5 10.4 %collective-permute-start.11 = (bf16[128,512]{1,0:T(8,128)(2,1)}, bf16[128,512]{1,0:T(8,128)(2,1)S(1)}, u32[]{:S(2)}, u32[]{:S(2)}) collective-permute-start(bf16[128,512]{1,0:T(8,128)(2,1)} %get-tuple-element.69), channel_id=1, source_target_pairs={{0,32},{1,3},{2,34},{3,1},{4,36},{5,7},{6,38},{7,5},{8,40},{9,11},... | collective-permute-start | bytes 393224 | tf_op jit(solution)/shard_map/ppermute | solution.py:65
  137.2 7.8 %collective-permute-start.12 = (bf16[128,512]{1,0:T(8,128)(2,1)}, bf16[128,512]{1,0:T(8,128)(2,1)S(1)}, u32[]{:S(2)}, u32[]{:S(2)}) collective-permute-start(bf16[128,512]{1,0:T(8,128)(2,1)} %get-tuple-element.70), channel_id=1, source_target_pairs={{0,48},{1,67},{2,50},{3,65},{4,52},{5,71},{6,54},{7,69},{8,56},{9,... | collective-permute-start | bytes 393224 | tf_op jit(solution)/shard_map/ppermute | solution.py:65
  139.2 5.6 %collective-permute-start.21 = (bf16[80,512]{1,0:T(8,128)(2,1)S(1)}, bf16[80,512]{1,0:T(8,128)(2,1)S(1)}, u32[]{:S(2)}, u32[]{:S(2)}) collective-permute-start(bf16[80,512]{1,0:T(8,128)(2,1)S(1)} %copy-done.27), channel_id=1, source_target_pairs={{0,8},{1,9},{2,10},{3,11},{4,12},{5,13},{6,14},{7,15},{8,0},{9,1},... | collective-permute-start | bytes 245768 | tf_op jit(solution)/shard_map/ppermute | solution.py:65
  140.5 4.5 %collective-permute-start.22 = (bf16[80,512]{1,0:T(8,128)(2,1)S(1)}, bf16[80,512]{1,0:T(8,128)(2,1)S(1)}, u32[]{:S(2)}, u32[]{:S(2)}) collective-permute-start(bf16[80,512]{1,0:T(8,128)(2,1)S(1)} %copy-done.26), channel_id=1, source_target_pairs={{0,12},{1,13},{2,14},{3,15},{4,0},{5,1},{6,2},{7,3},{8,4},{9,5},{1... | collective-permute-start | bytes 245768 | tf_op jit(solution)/shard_map/ppermute | solution.py:65
  147.2 4.8 %collective-permute-start.42 = (bf16[80,512]{1,0:T(8,128)(2,1)S(1)}, bf16[80,512]{1,0:T(8,128)(2,1)S(1)}, u32[]{:S(2)}, u32[]{:S(2)}) collective-permute-start(bf16[80,512]{1,0:T(8,128)(2,1)S(1)} %get-tuple-element.94.refs_0_), channel_id=1, source_target_pairs={{0,12},{1,13},{2,14},{3,15},{4,0},{5,1},{6,2},{7,3},{8,4},{9,5},{1... | collective-permute-start | bytes 245768 | tf_op jit(solution)/shard_map/ppermute | solution.py:65
  150.3 4.9 %collective-permute-start.41 = (bf16[80,512]{1,0:T(8,128)(2,1)S(1)}, bf16[80,512]{1,0:T(8,128)(2,1)S(1)}, u32[]{:S(2)}, u32[]{:S(2)}) collective-permute-start(bf16[80,512]{1,0:T(8,128)(2,1)S(1)} %get-tuple-element.94.refs_0_), channel_id=1, source_target_pairs={{0,8},{1,9},{2,10},{3,11},{4,12},{5,13},{6,14},{7,15},{8,0},{9,1},... | collective-permute-start | bytes 245768 | tf_op jit(solution)/shard_map/ppermute | solution.py:65
  150.3 5.8 %collective-permute-start.40 = (bf16[80,512]{1,0:T(8,128)(2,1)S(1)}, bf16[80,512]{1,0:T(8,128)(2,1)S(1)}, u32[]{:S(2)}, u32[]{:S(2)}) collective-permute-start(bf16[80,512]{1,0:T(8,128)(2,1)S(1)} %get-tuple-element.94.refs_0_), channel_id=1, source_target_pairs={{0,4},{1,5},{2,6},{3,7},{4,8},{5,9},{6,10},{7,11},{8,12},{9,13},{1... | collective-permute-start | bytes 245768 | tf_op jit(solution)/shard_map/ppermute | solution.py:65
  156.8 11.4 %collective-permute-start.46 = (bf16[320,512]{1,0:T(8,128)(2,1)S(1)}, bf16[320,512]{1,0:T(8,128)(2,1)S(1)}, u32[]{:S(2)}, u32[]{:S(2)}) collective-permute-start(bf16[320,512]{1,0:T(8,128)(2,1)S(1)} %shard_map.88.refs_0_), channel_id=1, source_target_pairs={{0,1},{1,0},{2,3},{3,2},{4,5},{5,4},{6,7},{7,6},{8,9},{9,8},{10,11... | collective-permute-start | bytes 983048 | tf_op jit(solution)/shard_map/ppermute | solution.py:65
  158.8 9.7 %collective-permute-start.45 = (bf16[320,512]{1,0:T(8,128)(2,1)S(1)}, bf16[320,512]{1,0:T(8,128)(2,1)S(1)}, u32[]{:S(2)}, u32[]{:S(2)}) collective-permute-start(bf16[320,512]{1,0:T(8,128)(2,1)S(1)} %shard_map.88.refs_0_), channel_id=1, source_target_pairs={{0,48},{1,49},{2,50},{3,51},{4,52},{5,53},{6,54},{7,55},{8,56},{9,... | collective-permute-start | bytes 983048 | tf_op jit(solution)/shard_map/ppermute | solution.py:65
  159.7 4.1 %collective-permute-start.26 = (bf16[128,512]{1,0:T(8,128)(2,1)S(1)}, bf16[128,512]{1,0:T(8,128)(2,1)S(1)}, u32[]{:S(2)}, u32[]{:S(2)}) collective-permute-start(bf16[128,512]{1,0:T(8,128)(2,1)S(1)} %get-tuple-element.85.refs_0_), channel_id=1, source_target_pairs={{0,48},{1,67},{2,50},{3,65},{4,52},{5,71},{6,54},{7,69},{8,56},{9,... | collective-permute-start | bytes 393224 | tf_op jit(solution)/shard_map/ppermute | solution.py:65
  160.2 5.6 %collective-permute-start.25 = (bf16[128,512]{1,0:T(8,128)(2,1)S(1)}, bf16[128,512]{1,0:T(8,128)(2,1)S(1)}, u32[]{:S(2)}, u32[]{:S(2)}) collective-permute-start(bf16[128,512]{1,0:T(8,128)(2,1)S(1)} %get-tuple-element.85.refs_0_), channel_id=1, source_target_pairs={{0,32},{1,3},{2,34},{3,1},{4,36},{5,7},{6,38},{7,5},{8,40},{9,11},... | collective-permute-start | bytes 393224 | tf_op jit(solution)/shard_map/ppermute | solution.py:65
  160.9 6.0 %collective-permute-start.24 = (bf16[128,512]{1,0:T(8,128)(2,1)S(1)}, bf16[128,512]{1,0:T(8,128)(2,1)S(1)}, u32[]{:S(2)}, u32[]{:S(2)}) collective-permute-start(bf16[128,512]{1,0:T(8,128)(2,1)S(1)} %get-tuple-element.85.refs_0_), channel_id=1, source_target_pairs={{0,16},{1,65},{2,18},{3,67},{4,20},{5,69},{6,22},{7,71},{8,24},{9,... | collective-permute-start | bytes 393224 | tf_op jit(solution)/shard_map/ppermute | solution.py:65
  163.9 8.3 %collective-permute-start.44 = (bf16[320,512]{1,0:T(8,128)(2,1)S(1)}, bf16[320,512]{1,0:T(8,128)(2,1)S(1)}, u32[]{:S(2)}, u32[]{:S(2)}) collective-permute-start(bf16[320,512]{1,0:T(8,128)(2,1)S(1)} %shard_map.88.refs_0_), channel_id=1, source_target_pairs={{0,32},{1,33},{2,34},{3,35},{4,36},{5,37},{6,38},{7,39},{8,40},{9,... | collective-permute-start | bytes 983048 | tf_op jit(solution)/shard_map/ppermute | solution.py:65
  165.8 15.2 %collective-permute-start.43 = (bf16[320,512]{1,0:T(8,128)(2,1)S(1)}, bf16[320,512]{1,0:T(8,128)(2,1)S(1)}, u32[]{:S(2)}, u32[]{:S(2)}) collective-permute-start(bf16[320,512]{1,0:T(8,128)(2,1)S(1)} %shard_map.88.refs_0_), channel_id=1, source_target_pairs={{0,16},{1,17},{2,18},{3,19},{4,20},{5,21},{6,22},{7,23},{8,24},{9,... | collective-permute-start | bytes 983048 | tf_op jit(solution)/shard_map/ppermute | solution.py:65
  167.5 16.9 %collective-permute-start.29 = (bf16[512,512]{1,0:T(8,128)(2,1)S(1)}, bf16[512,512]{1,0:T(8,128)(2,1)S(1)}, u32[]{:S(2)}, u32[]{:S(2)}) collective-permute-start(bf16[512,512]{1,0:T(8,128)(2,1)S(1)} %shard_map.85.refs_0_), channel_id=1, source_target_pairs={{0,66},{1,13},{2,64},{3,15},{4,70},{5,1},{6,68},{7,3},{8,74},{9,5}... | collective-permute-start | bytes 1572872 | tf_op jit(solution)/shard_map/ppermute | solution.py:65
  168.1 17.5 %collective-permute-start.28 = (bf16[512,512]{1,0:T(8,128)(2,1)S(1)}, bf16[512,512]{1,0:T(8,128)(2,1)S(1)}, u32[]{:S(2)}, u32[]{:S(2)}) collective-permute-start(bf16[512,512]{1,0:T(8,128)(2,1)S(1)} %shard_map.85.refs_0_), channel_id=1, source_target_pairs={{0,2},{1,9},{2,0},{3,11},{4,6},{5,13},{6,4},{7,15},{8,10},{9,1},{1... | collective-permute-start | bytes 1572872 | tf_op jit(solution)/shard_map/ppermute | solution.py:65
  168.5 20.1 %collective-permute-start.27 = (bf16[512,512]{1,0:T(8,128)(2,1)S(1)}, bf16[512,512]{1,0:T(8,128)(2,1)S(1)}, u32[]{:S(2)}, u32[]{:S(2)}) collective-permute-start(bf16[512,512]{1,0:T(8,128)(2,1)S(1)} %shard_map.85.refs_0_), channel_id=1, source_target_pairs={{0,64},{1,5},{2,66},{3,7},{4,68},{5,9},{6,70},{7,11},{8,72},{9,13}... | collective-permute-start | bytes 1572872 | tf_op jit(solution)/shard_map/ppermute | solution.py:65
  172.1 22.0 %collective-permute-start.49 = (bf16[320,512]{1,0:T(8,128)(2,1)S(1)}, bf16[320,512]{1,0:T(8,128)(2,1)S(1)}, u32[]{:S(2)}, u32[]{:S(2)}) collective-permute-start(bf16[320,512]{1,0:T(8,128)(2,1)S(1)} %collective-permute-done.45.refs_3_), channel_id=1, source_target_pairs={{0,1},{1,0},{2,3},{3,2},{4,5},{5,4},{6,7},{7,6},{8,9},{9,8},{10,11... | collective-permute-start | bytes 983048 | tf_op jit(solution)/shard_map/ppermute | solution.py:65
  181.0 13.2 %collective-permute-start.48 = (bf16[320,512]{1,0:T(8,128)(2,1)S(1)}, bf16[320,512]{1,0:T(8,128)(2,1)S(1)}, u32[]{:S(2)}, u32[]{:S(2)}) collective-permute-start(bf16[320,512]{1,0:T(8,128)(2,1)S(1)} %collective-permute-done.44.refs_2_), channel_id=1, source_target_pairs={{0,1},{1,0},{2,3},{3,2},{4,5},{5,4},{6,7},{7,6},{8,9},{9,8},{10,11... | collective-permute-start | bytes 983048 | tf_op jit(solution)/shard_map/ppermute | solution.py:65
  184.4 20.7 %collective-permute-start.30 = (bf16[512,512]{1,0:T(8,128)(2,1)S(1)}, bf16[512,512]{1,0:T(8,128)(2,1)S(1)}, u32[]{:S(2)}, u32[]{:S(2)}) collective-permute-start(bf16[512,512]{1,0:T(8,128)(2,1)S(1)} %shard_map.85.refs_0_), channel_id=1, source_target_pairs={{0,1},{1,0},{2,3},{3,2},{4,5},{5,4},{6,7},{7,6},{8,9},{9,8},{10,11... | collective-permute-start | bytes 1572872 | tf_op jit(solution)/shard_map/ppermute | solution.py:65
  185.7 22.1 %collective-permute-start.33 = (bf16[512,512]{1,0:T(8,128)(2,1)S(1)}, bf16[512,512]{1,0:T(8,128)(2,1)S(1)}, u32[]{:S(2)}, u32[]{:S(2)}) collective-permute-start(bf16[512,512]{1,0:T(8,128)(2,1)S(1)} %collective-permute-done.29.refs_3_), channel_id=1, source_target_pairs={{0,1},{1,0},{2,3},{3,2},{4,5},{5,4},{6,7},{7,6},{8,9},{9,8},{10,11... | collective-permute-start | bytes 1572872 | tf_op jit(solution)/shard_map/ppermute | solution.py:65
  188.6 19.3 %collective-permute-start.32 = (bf16[512,512]{1,0:T(8,128)(2,1)S(1)}, bf16[512,512]{1,0:T(8,128)(2,1)S(1)}, u32[]{:S(2)}, u32[]{:S(2)}) collective-permute-start(bf16[512,512]{1,0:T(8,128)(2,1)S(1)} %collective-permute-done.28.refs_2_), channel_id=1, source_target_pairs={{0,1},{1,0},{2,3},{3,2},{4,5},{5,4},{6,7},{7,6},{8,9},{9,8},{10,11... | collective-permute-start | bytes 1572872 | tf_op jit(solution)/shard_map/ppermute | solution.py:65
  194.2 13.8 %collective-permute-start.31 = (bf16[512,512]{1,0:T(8,128)(2,1)S(1)}, bf16[512,512]{1,0:T(8,128)(2,1)S(1)}, u32[]{:S(2)}, u32[]{:S(2)}) collective-permute-start(bf16[512,512]{1,0:T(8,128)(2,1)S(1)} %collective-permute-done.27.refs_1_), channel_id=1, source_target_pairs={{0,1},{1,0},{2,3},{3,2},{4,5},{5,4},{6,7},{7,6},{8,9},{9,8},{10,11... | collective-permute-start | bytes 1572872 | tf_op jit(solution)/shard_map/ppermute | solution.py:65
  194.2 2.7 %collective-permute-start.47 = (bf16[320,512]{1,0:T(8,128)(2,1)S(1)}, bf16[320,512]{1,0:T(8,128)(2,1)S(1)}, u32[]{:S(2)}, u32[]{:S(2)}) collective-permute-start(bf16[320,512]{1,0:T(8,128)(2,1)S(1)} %collective-permute-done.43.refs_1_), channel_id=1, source_target_pairs={{0,1},{1,0},{2,3},{3,2},{4,5},{5,4},{6,7},{7,6},{8,9},{9,8},{10,11... | collective-permute-start | bytes 983048 | tf_op jit(solution)/shard_map/ppermute | solution.py:65
  205.0 31.2 %collective-permute-start.50 = (bf16[128,2560]{1,0:T(8,128)(2,1)S(1)}, bf16[128,2560]{1,0:T(8,128)(2,1)S(1)}, u32[]{:S(2)}, u32[]{:S(2)}) collective-permute-start(bf16[128,2560]{1,0:T(8,128)(2,1)S(1)} %get-tuple-element.96), channel_id=1, source_target_pairs={{0,64},{1,65},{2,66},{3,67},{4,68},{5,69},{6,70},{7,71},{8,72},{9,... | collective-permute-start | bytes 1966088 | tf_op jit(solution)/shard_map/ppermute | solution.py:65
  205.1 31.2 %collective-permute-start.51 = (bf16[128,2560]{1,0:T(8,128)(2,1)S(1)}, bf16[128,2560]{1,0:T(8,128)(2,1)S(1)}, u32[]{:S(2)}, u32[]{:S(2)}) collective-permute-start(bf16[128,2560]{1,0:T(8,128)(2,1)S(1)} %get-tuple-element.97), channel_id=1, source_target_pairs={{0,66},{1,67},{2,64},{3,65},{4,70},{5,71},{6,68},{7,69},{8,74},{9,... | collective-permute-start | bytes 1966088 | tf_op jit(solution)/shard_map/ppermute | solution.py:65
  207.8 29.2 %collective-permute-start.52 = (bf16[128,2560]{1,0:T(8,128)(2,1)S(1)}, bf16[128,2560]{1,0:T(8,128)(2,1)S(1)}, u32[]{:S(2)}, u32[]{:S(2)}) collective-permute-start(bf16[128,2560]{1,0:T(8,128)(2,1)S(1)} %get-tuple-element.98), channel_id=1, source_target_pairs={{0,2},{1,3},{2,0},{3,1},{4,6},{5,7},{6,4},{7,5},{8,10},{9,11},{10,... | collective-permute-start | bytes 1966088 | tf_op jit(solution)/shard_map/ppermute | solution.py:65
  212.5 26.4 %collective-permute-start.37 = (bf16[128,2048]{1,0:T(8,128)(2,1)S(1)}, bf16[128,2048]{1,0:T(8,128)(2,1)S(1)}, u32[]{:S(2)}, u32[]{:S(2)}) collective-permute-start(bf16[128,2048]{1,0:T(8,128)(2,1)S(1)} %get-tuple-element.91), channel_id=1, source_target_pairs={{0,4},{1,5},{2,6},{3,7},{4,8},{5,9},{6,10},{7,11},{8,12},{9,13},{1... | collective-permute-start | bytes 1572872 | tf_op jit(solution)/shard_map/ppermute | solution.py:65
  217.2 48.4 %copy-start.20 = (bf16[128,2560]{1,0:T(8,128)(2,1)S(1)}, bf16[128,2560]{1,0:T(8,128)(2,1)}, u32[]{:S(2)}) copy-start(bf16[128,2560]{1,0:T(8,128)(2,1)} %get-tuple-element.95.refs_0_) | copy-start | bytes 1966084
  217.2 54.5 %collective-permute-start.34 = (bf16[128,2048]{1,0:T(8,128)(2,1)S(1)}, bf16[128,2048]{1,0:T(8,128)(2,1)S(1)}, u32[]{:S(2)}, u32[]{:S(2)}) collective-permute-start(bf16[128,2048]{1,0:T(8,128)(2,1)S(1)} %get-tuple-element.87), channel_id=1, source_target_pairs={{0,16},{1,17},{2,18},{3,19},{4,20},{5,21},{6,22},{7,23},{8,24},{9,... | collective-permute-start | bytes 1572872 | tf_op jit(solution)/shard_map/ppermute | solution.py:65
  236.3 32.9 %collective-permute-start.38 = (bf16[128,2048]{1,0:T(8,128)(2,1)S(1)}, bf16[128,2048]{1,0:T(8,128)(2,1)S(1)}, u32[]{:S(2)}, u32[]{:S(2)}) collective-permute-start(bf16[128,2048]{1,0:T(8,128)(2,1)S(1)} %get-tuple-element.92), channel_id=1, source_target_pairs={{0,12},{1,13},{2,14},{3,15},{4,0},{5,1},{6,2},{7,3},{8,4},{9,5},{1... | collective-permute-start | bytes 1572872 | tf_op jit(solution)/shard_map/ppermute | solution.py:65
  236.3 32.9 %collective-permute-start.39 = (bf16[128,2048]{1,0:T(8,128)(2,1)S(1)}, bf16[128,2048]{1,0:T(8,128)(2,1)S(1)}, u32[]{:S(2)}, u32[]{:S(2)}) collective-permute-start(bf16[128,2048]{1,0:T(8,128)(2,1)S(1)} %get-tuple-element.93), channel_id=1, source_target_pairs={{0,8},{1,9},{2,10},{3,11},{4,12},{5,13},{6,14},{7,15},{8,0},{9,1},... | collective-permute-start | bytes 1572872 | tf_op jit(solution)/shard_map/ppermute | solution.py:65
  237.0 34.7 %collective-permute-start.35 = (bf16[128,2048]{1,0:T(8,128)(2,1)S(1)}, bf16[128,2048]{1,0:T(8,128)(2,1)S(1)}, u32[]{:S(2)}, u32[]{:S(2)}) collective-permute-start(bf16[128,2048]{1,0:T(8,128)(2,1)S(1)} %get-tuple-element.88), channel_id=1, source_target_pairs={{0,48},{1,49},{2,50},{3,51},{4,52},{5,53},{6,54},{7,55},{8,56},{9,... | collective-permute-start | bytes 1572872 | tf_op jit(solution)/shard_map/ppermute | solution.py:65
  238.9 32.7 %collective-permute-start.36 = (bf16[128,2048]{1,0:T(8,128)(2,1)S(1)}, bf16[128,2048]{1,0:T(8,128)(2,1)S(1)}, u32[]{:S(2)}, u32[]{:S(2)}) collective-permute-start(bf16[128,2048]{1,0:T(8,128)(2,1)S(1)} %get-tuple-element.89), channel_id=1, source_target_pairs={{0,32},{1,33},{2,34},{3,35},{4,36},{5,37},{6,38},{7,39},{8,40},{9,... | collective-permute-start | bytes 1572872 | tf_op jit(solution)/shard_map/ppermute | solution.py:65
  (19 other events, 108.7 us)

commit v7 on v6

--- a/solution.py
+++ b/solution.py
@@ -177,7 +177,7 @@
         + ([pltpu.VMEM((16, 128, 128), BF), DMA((16,))] if ring == "x" else []),
         compiler_params=LIMIT,
         cost_estimate=estimate(0, 4 * 128 * width * 4),
-    )(where, in_hbm(grad), basis)
+    )(where, in_hbm(grad), in_hbm(basis))
 
 
 def unpack_kernel(ring, where, *refs):
@@ -623,11 +623,8 @@
     return copies
 
 
-def update_kernel(ring, where, *refs):
-    own, other, basis, outs = refs[:4], refs[4:8], refs[8], refs[9:13]
-    low, base, held, in_sem, other_sem, base_sem, out_sem = refs[13:]
+def start_update(ring, where, own, other, basis, low, base, in_sem, other_sem, base_sem):
     core = place(where, "core")
-    width = WIDTH[ring]
     for k, step in enumerate(STEPS):
         if ring == "y":
             source = basis_rows(ring, where, step, basis)
@@ -637,20 +634,23 @@
     if ring == "x":
         start_all(low_copies(1, where, own, core * 1280, low, in_sem, core))
         start_all(low_copies(1, where, other, (1 - core) * 1280, low, other_sem, 1 - core))
+        return
+    part_core = 0 if ring == "y" else 1
+    for arrays, chosen in ((own, core == part_core), (other, core != part_core)):
+
+        @pl.when(chosen)
+        def _():
+            start_all(low_copies(0, where, arrays, 0, low, in_sem, jnp.int32(part_core)))
+
+
+def end_update(ring, outs, low, base, held, in_sem, other_sem, base_sem, out_sem):
+    if ring == "x":
         for at in range(4):
             wait_for(low.at[pl.ds(0, 320), :], in_sem.at[at])
             wait_for(low.at[pl.ds(0, 320), :], other_sem.at[at])
-    else:
-        part_core = 0 if ring == "y" else 1
-        for arrays, chosen in ((own, core == part_core), (other, core != part_core)):
-
-            @pl.when(chosen)
-            def _():
-                start_all(low_copies(0, where, arrays, 0, low, in_sem, jnp.int32(part_core)))
-
     wait_for(base, base_sem)
 
-    @pl.loop(0, width // 512)
+    @pl.loop(0, WIDTH[ring] // 512)
     def _(i):
         columns = pl.ds(pl.multiple_of(i * 512, 512), 512)
         if ring != "x":
@@ -662,29 +662,45 @@
                 held.at[pl.ds(k * 128, 128), columns], outs[k].at[:, columns], out_sem.at[k]
             ).start()
 
-    for k in range(4):
-        wait_for(held.at[pl.ds(k * 128, 128), :], out_sem.at[k])
-
-
-def update_blocks(ring, where, arrays, basis):
-    width = WIDTH[ring]
-    return pl.pallas_call(
-        functools.partial(update_kernel, ring),
-        out_shape=blocks_of(4, (128, width)),
-        in_specs=[SMEM] + [ANY] * 9,
-        out_specs=[ANY] * 4,
+
+def update_kernel(rings, where, *refs):
+    n = len(rings)
+    own, other, bases, outs, refs = refs[:4], refs[4:8], refs[8 : 8 + n], refs[8 + n : 8 + 5 * n], refs[8 + 5 * n :]
+    scratch = [refs[7 * i : 7 * i + 7] for i in range(n)]
+    for i, ring in enumerate(rings):
+        low, base, _, in_sem, other_sem, base_sem, _ = scratch[i]
+        start_update(ring, where, own, other, bases[i], low, base, in_sem, other_sem, base_sem)
+    for i, ring in enumerate(rings):
+        end_update(ring, outs[4 * i : 4 * i + 4], *scratch[i])
+    for i in range(n):
+        for k in range(4):
+            wait_for(scratch[i][2].at[pl.ds(k * 128, 128), :], scratch[i][6].at[k])
+
+
+def update_blocks(rings, where, arrays, bases):
+    widths = [WIDTH[ring] for ring in rings]
+    out = pl.pallas_call(
+        functools.partial(update_kernel, rings),
+        out_shape=[shape for width in widths for shape in blocks_of(4, (128, width))],
+        in_specs=[SMEM] + [ANY] * (8 + len(rings)),
+        out_specs=[ANY] * (4 * len(rings)),
         scratch_shapes=[
-            pltpu.VMEM((width, 512), BF),
-            pltpu.VMEM((512, 512), BF),
-            pltpu.VMEM((512, width), BF),
-            DMA((4,)),
-            DMA((4,)),
-            DMA,
-            DMA((4,)),
+            shape
+            for width in widths
+            for shape in (
+                pltpu.VMEM((width, 512), BF),
+                pltpu.VMEM((512, 512), BF),
+                pltpu.VMEM((512, width), BF),
+                DMA((4,)),
+                DMA((4,)),
+                DMA,
+                DMA((4,)),
+            )
         ],
         compiler_params=LIMIT,
-        cost_estimate=estimate(2 * 512 * 512 * width, 512 * width * 2 + 512 * 1024 + width * 1024),
-    )(where, *arrays, basis if ring == "y" else in_hbm(basis))
+        cost_estimate=estimate(2 * 512 * 512 * sum(widths), sum(512 * w * 2 + 512 * 1024 + w * 1024 for w in widths)),
+    )(where, *arrays, *(basis if ring == "y" else in_hbm(basis) for ring, basis in zip(rings, bases)))
+    return [out[4 * i : 4 * i + 4] for i in range(len(rings))]
 
 
 def exchange(blocks, rings):
@@ -728,15 +744,15 @@
     *lows, first_new, second_new = take_step(where, totals[0] + totals[1], margin, margin_other, moments)
 
     sent = {}
-    for group, rings in ((1, ("x",)), (0, ("y", "z"))):
+    for group, rings in ((1, "x"), (0, "yz")):
         low = lows[group]
         quarters = ordered([low] * 4, V[group])
         quarter = join(group, where, quarters)
         whole = ordered([quarter] * 4, U[group])
         whole = whole + [shift(array, RINGS["core"], 1) for array in whole]
-        for ring in rings:
-            blocks = update_blocks(ring, where, whole, gathered[ring])
-            sent[ring] = exchange(blocks, RINGS[ring])
+        blocks = update_blocks(rings, where, whole, [gathered[ring] for ring in rings])
+        for i, ring in enumerate(rings):
+            sent[ring] = exchange(blocks[i], RINGS[ring])
     update = None
     for ring in ("x", "y", "z"):
         update = unpack(ring, where, sent[ring], update, grad.shape[1])

time: 280 us -> 278 us (level)
    pallas_call x3 -> x2, Pallas kernels: 17.2 us -> 15.2 us  [update_blocks(): pl.pallas_call(functools.partial(update_kernel, rings), out_shape=[shape...]
  transfers between devices with their start and end apart: 55 -> 55, of which waited for: 17 -> 16; matrix products, arithmetic and copies ran while one was open for 0% -> 0% of each run, Pallas kernels for 23% -> 22%
where the time goes in v7:
time: 278 us; the launch traced here: 273 us
  starting transfers between devices  114 us (41%)
  Pallas kernels  69.1 us (25%)
  waiting for transfers between devices  62.3 us (22%)
  blocking collectives  23.2 us (8%)
  local copies, waits for them, and re-layouts  3.45 us (1%)
    ppermute x53, starting transfers between devices, shift(): return lax.ppermute(array, NAMES, pairs)  103 us
    ppermute x53, waiting for transfers between devices, shift(): return lax.ppermute(array, NAMES, pairs)  57.8 us
    all_to_all x1, blocking collectives, compute(): new = lax.all_to_all(new, ROW, 0, 0, tiled=True)  23.2 us
    pallas_call x4, Pallas kernels, project(): pl.pallas_call(functools.partial(project_kernel, group, own), out_shape=s...  19.8 us
    pallas_call x2, Pallas kernels, update_blocks(): pl.pallas_call(functools.partial(update_kernel, rings), out_shape=[shape...  15.2 us
    pallas_call x3, Pallas kernels, pack(): pl.pallas_call(functools.partial(pack_kernel, ring), out_shape=[(jax.Shap...  9.06 us
    pallas_call x3, Pallas kernels, unpack(): pl.pallas_call(functools.partial(unpack_kernel, ring), out_shape=jax.Shap...  8.48 us
    all_to_all x1, starting transfers between devices, compute(): moments = lax.all_to_all(moments, ROW, 0, 0, tiled=True)  6.69 us
  transfers between devices with their start and end apart: 55, of which 16 were waited for; matrix products, arithmetic and copies ran while one was open for 0% of the time, Pallas kernels for 22%

profile of v7, /device:TPU:1, one launch (start us, length us, event | category | flops | bytes accessed | tf_op | source)
XLA Modules:
  0.0 273.1 jit_solution(10194871396872181716)
XLA Ops:
  0.7 2.4 shard_map.76
  3.1 2.3 collective-permute-start
  5.5 3.0 %shard_map.77 = (bf16[128,2560]{1,0:T(8,128)(2,1)}, bf16[128,2560]{1,0:T(8,128)(2,1)S(1)}, bf16[128,2560]{1,0:T(8,128)(2,1)S(1)}, bf16[128,2560]{1,0:T(8,128)(2,1)S(1)}) custom-call(s32[8]{0:T(128)S(1)} %compare_select_fusion.6.where, bf16[128,26624]{1,0:T(8,128)(2,1)} %grad.5, bf16[2048,512]{1,0:T(8,128)(2,1)} %refs_8_.5), custom_call_target="tpu_custom_call" | custom-call | bytes 5242880 | tf_op jit(solution)/shard_map/pallas_call | solution.py:168
  8.4 1.8 collective-permute-start.3
  10.2 2.5 collective-permute-start.4
  13.8 1.8 collective-permute-start.1
  15.6 3.2 %collective-permute-done.refs_1_ = bf16[128,2048]{1,0:T(8,128)(2,1)S(1)} collective-permute-done((bf16[128,2048]{1,0:T(8,128)(2,1)S(1)}, bf16[128,2048]{1,0:T(8,128)(2,1)S(1)}, u32[]{:S(2)}, u32[]{:S(2)}) %collective-permute-start) | collective-permute-done | bytes 524320 | tf_op jit(solution)/shard_map/ppermute | solution.py:65
  18.8 1.2 collective-permute-start.2
  20.0 3.7 %shard_map.81 = (bf16[128,2560]{1,0:T(8,128)(2,1)}, bf16[128,3072]{1,0:T(8,128)(2,1)S(1)}, bf16[128,3072]{1,0:T(8,128)(2,1)S(1)}, bf16[128,2560]{1,0:T(8,128)(2,1)S(1)}) custom-call(s32[8]{0:T(128)S(1)} %compare_select_fusion.6.where, bf16[128,26624]{1,0:T(8,128)(2,1)} %grad.5, bf16[2048,512]{1,0:T(8,128)(2,1)} %refs_8_.5), custom_call_target="tpu_custom_call" | custom-call | bytes 6291456 | tf_op jit(solution)/shard_map/pallas_call | solution.py:168
  23.7 2.1 collective-permute-done.1.refs_2_
  25.9 1.2 collective-permute-start.13
  27.1 5.5 %collective-permute-done.2.refs_3_ = bf16[128,2048]{1,0:T(8,128)(2,1)S(1)} collective-permute-done((bf16[128,2048]{1,0:T(8,128)(2,1)S(1)}, bf16[128,2048]{1,0:T(8,128)(2,1)S(1)}, u32[]{:S(2)}, u32[]{:S(2)}) %collective-permute-start.2) | collective-permute-done | bytes 524320 | tf_op jit(solution)/shard_map/ppermute | solution.py:65
  32.6 2.5 collective-permute-start.14
  35.6 6.2 %collective-permute-done.5.refs_7_ = bf16[128,2560]{1,0:T(8,128)(2,1)S(1)} collective-permute-done((bf16[128,2560]{1,0:T(8,128)(2,1)S(1)}, bf16[128,2560]{1,0:T(8,128)(2,1)S(1)}, u32[]{:S(2)}, u32[]{:S(2)}) %collective-permute-start.5) | collective-permute-done | bytes 655392 | tf_op jit(solution)/shard_map/ppermute | solution.py:65
  41.8 5.0 %shard_map.78 = (bf16[2048,512]{1,0:T(8,128)(2,1)}, bf16[512,512]{1,0:T(8,128)(2,1)}) custom-call(s32[8]{0:T(128)S(1)} %compare_select_fusion.6.where, bf16[128,2048]{1,0:T(8,128)(2,1)} %get-tuple-element.53.refs_0_, bf16[128,2048]{1,0:T(8,128)(2,1)S(1)} %collective-permute-done.refs_1_, bf16[128,2048]{1,0:T(8,128)(2,1)S(1)} %collective-permute-done.1.refs_2_, ...), custom_call_target="tpu_custom_call" | custom-call | flops 1073741824 | bytes 4718592 | tf_op jit(solution)/shard_map/pallas_call | solution.py:369
  46.9 2.4 collective-permute-start.6
  49.3 4.4 %shard_map.82 = (bf16[1280,512]{1,0:T(8,128)(2,1)}, bf16[512,512]{1,0:T(8,128)(2,1)}) custom-call(s32[8]{0:T(128)S(1)} %compare_select_fusion.6.where, bf16[128,2560]{1,0:T(8,128)(2,1)} %get-tuple-element.71.refs_0_, bf16[128,3072]{1,0:T(8,128)(2,1)S(1)} %collective-permute-done.13.refs_1_, bf16[128,3072]{1,0:T(8,128)(2,1)S(1)} %collective-permute-done.14.refs_2_, ...), custom_call_target="tpu_custom_call" | custom-call | flops 671088640 | bytes 3145728 | tf_op jit(solution)/shard_map/pallas_call | solution.py:369
  53.8 17.6 %collective-permute-start.16 = (bf16[1280,512]{1,0:T(8,128)(2,1)}, bf16[1280,512]{1,0:T(8,128)(2,1)}, u32[]{:S(2)}, u32[]{:S(2)}) collective-permute-start(bf16[1280,512]{1,0:T(8,128)(2,1)} %get-tuple-element.75), channel_id=1, source_target_pairs={{0,1},{1,0},{2,3},{3,2},{4,5},{5,4},{6,7},{7,6},{8,9},{9,8},{10,11... | collective-permute-start | bytes 3932168 | tf_op jit(solution)/shard_map/ppermute | solution.py:65
  71.3 4.1 %cut_moments.1 = bf16[8,256,256]{2,1,0:T(8,128)(2,1)} custom-call(s32[8]{0:T(128)S(1)} %compare_select_fusion.6.where, f32[64,1664]{1,0:T(8,128)S(1)} %copy-done.22, f32[64,1664]{1,0:T(8,128)S(1)} %copy-done.23, bf16[2048,512]{1,0:T(8,128)(2,1)S(1)} %copy-done, bf16[2048,512]{1,0:T(8,128)(2,1)} %old.1), custom_call_target="tpu_custom_call" | custom-call | flops 536870912 | bytes 6291456 | tf_op jit(solution)/shard_map/cut_moments/pallas_call | solution.py:447
  75.4 6.7 %all-to-all-start = ((bf16[8,256,256]{2,1,0:T(8,128)(2,1)}), bf16[8,256,256]{2,1,0:T(8,128)(2,1)S(1)}, u32[]{:S(2)}, u32[]{:S(2)}) async-start(bf16[8,256,256]{2,1,0:T(8,128)(2,1)} %cut_moments.1), calls=%async_computation | async-start | bytes 2097152 | tf_op jit(solution)/shard_map/all_to_all | solution.py:729
  85.5 4.7 %shard_map.83 = (bf16[320,512]{1,0:T(8,128)(2,1)}, bf16[320,512]{1,0:T(8,128)(2,1)}, bf16[320,512]{1,0:T(8,128)(2,1)}, bf16[320,512]{1,0:T(8,128)(2,1)S(1)}) custom-call(s32[8]{0:T(128)S(1)} %compare_select_fusion.6.where, bf16[128,2560]{1,0:T(8,128)(2,1)} %get-tuple-element.71.refs_0_, bf16[128,3072]{1,0:T(8,128)(2,1)S(1)} %copy-done.2, ...), custom_call_target="tpu_custom_call" | custom-call | flops 671088640 | bytes 3145728 | tf_op jit(solution)/shard_map/pallas_call | solution.py:369
  90.2 1.5 collective-permute-start.17
  91.7 2.4 collective-permute-start.18
  94.2 5.7 %shard_map.79 = (bf16[512,512]{1,0:T(8,128)(2,1)}, bf16[512,512]{1,0:T(8,128)(2,1)}, bf16[512,512]{1,0:T(8,128)(2,1)}, bf16[512,512]{1,0:T(8,128)(2,1)}) custom-call(s32[8]{0:T(128)S(1)} %compare_select_fusion.6.where, bf16[128,2048]{1,0:T(8,128)(2,1)} %get-tuple-element.53.refs_0_, bf16[128,2048]{1,0:T(8,128)(2,1)S(1)} %copy-done.14, ...), custom_call_target="tpu_custom_call" | custom-call | flops 1073741824 | bytes 4718592 | tf_op jit(solution)/shard_map/pallas_call | solution.py:369
  99.8 5.0 %collective-permute-start.7 = (bf16[512,512]{1,0:T(8,128)(2,1)}, bf16[512,512]{1,0:T(8,128)(2,1)}, u32[]{:S(2)}, u32[]{:S(2)}) collective-permute-start(bf16[512,512]{1,0:T(8,128)(2,1)} %get-tuple-element.64), channel_id=1, source_target_pairs={{0,64},{1,5},{2,66},{3,7},{4,68},{5,9},{6,70},{7,11},{8,72},{9,13}... | collective-permute-start | bytes 1572872 | tf_op jit(solution)/shard_map/ppermute | solution.py:65
  104.8 1.3 collective-permute-start.8
  106.1 1.2 collective-permute-start.9
  108.1 3.4 %all-to-all-start.1 = ((bf16[8,32,512]{2,1,0:T(8,128)(2,1)}), bf16[8,32,512]{2,1,0:T(8,128)(2,1)S(1)}, u32[]{:S(2)}, u32[]{:S(2)}) async-start(bf16[8,32,512]{2,1,0:T(8,128)(2,1)} %sum_margin.1), calls=%async_computation.1 | async-start | bytes 524288 | tf_op jit(solution)/shard_map/all_to_all | solution.py:731
  111.5 2.6 collective-permute-start.19
  114.1 4.6 %all-to-all-done.1 = bf16[8,32,512]{2,1,0:T(8,128)(2,1)S(1)} async-done(((bf16[8,32,512]{2,1,0:T(8,128)(2,1)}), bf16[8,32,512]{2,1,0:T(8,128)(2,1)S(1)}, u32[]{:S(2)}, u32[]{:S(2)}) %all-to-all-start.1) | async-done | bytes 262176 | tf_op jit(solution)/shard_map/all_to_all | solution.py:731
  118.7 2.7 %collective-permute-start.23 = (bf16[256,512]{1,0:T(8,128)(2,1)S(1)}, bf16[256,512]{1,0:T(8,128)(2,1)S(1)}, u32[]{:S(2)}, u32[]{:S(2)}) collective-permute-start(bf16[256,512]{1,0:T(8,128)(2,1)S(1)} %bitcast.1), channel_id=1, source_target_pairs={{0,1},{1,0},{2,3},{3,2},{4,5},{5,4},{6,7},{7,6},{8,9},{9,8},{10,11... | collective-permute-start | bytes 786440 | tf_op jit(solution)/shard_map/ppermute | solution.py:65
  121.4 2.1 collective-permute-done.19.d
  123.5 3.0 %shard_map.84 = (bf16[80,512]{1,0:T(8,128)(2,1)}, bf16[80,512]{1,0:T(8,128)(2,1)}, bf16[80,512]{1,0:T(8,128)(2,1)}, bf16[80,512]{1,0:T(8,128)(2,1)}) custom-call(s32[8]{0:T(128)S(1)} %compare_select_fusion.6.where, bf16[320,512]{1,0:T(8,128)(2,1)} %get-tuple-element.77.mine, bf16[320,512]{1,0:T(8,128)(2,1)} %collective-permute-done.17.b, ...), custom_call_target="tpu_custom_call" | custom-call | flops 491520 | bytes 1638400 | tf_op jit(solution)/shard_map/pallas_call | solution.py:409
  126.6 2.9 %collective-permute-start.20 = (bf16[80,512]{1,0:T(8,128)(2,1)}, bf16[80,512]{1,0:T(8,128)(2,1)S(1)}, u32[]{:S(2)}, u32[]{:S(2)}) collective-permute-start(bf16[80,512]{1,0:T(8,128)(2,1)} %get-tuple-element.82), channel_id=1, source_target_pairs={{0,4},{1,5},{2,6},{3,7},{4,8},{5,9},{6,10},{7,11},{8,12},{9,13},{1... | collective-permute-start | bytes 245768 | tf_op jit(solution)/shard_map/ppermute | solution.py:65
  129.4 3.3 %shard_map.80 = (bf16[128,512]{1,0:T(8,128)(2,1)}, bf16[128,512]{1,0:T(8,128)(2,1)}, bf16[128,512]{1,0:T(8,128)(2,1)}, bf16[128,512]{1,0:T(8,128)(2,1)}) custom-call(s32[8]{0:T(128)S(1)} %compare_select_fusion.6.where, bf16[512,512]{1,0:T(8,128)(2,1)} %get-tuple-element.63.mine, bf16[512,512]{1,0:T(8,128)(2,1)} %collective-permute-done.7.b, ...), custom_call_target="tpu_custom_call" | custom-call | flops 786432 | bytes 2621440 | tf_op jit(solution)/shard_map/pallas_call | solution.py:409
  133.0 2.7 collective-permute-start.11
  135.7 2.0 collective-permute-start.12
  137.7 1.3 collective-permute-start.21
  139.0 1.2 collective-permute-start.22
  140.1 3.2 %collective-permute-done.21.refs_6_ = bf16[80,512]{1,0:T(8,128)(2,1)S(1)} collective-permute-done((bf16[80,512]{1,0:T(8,128)(2,1)S(1)}, bf16[80,512]{1,0:T(8,128)(2,1)S(1)}, u32[]{:S(2)}, u32[]{:S(2)}) %collective-permute-start.21) | collective-permute-done | bytes 81952 | tf_op jit(solution)/shard_map/ppermute | solution.py:65
  143.3 2.3 step.1
  145.6 2.7 collective-permute-start.42
  149.8 3.4 %collective-permute-done.41.refs_2_ = bf16[80,512]{1,0:T(8,128)(2,1)S(1)} collective-permute-done((bf16[80,512]{1,0:T(8,128)(2,1)S(1)}, bf16[80,512]{1,0:T(8,128)(2,1)S(1)}, u32[]{:S(2)}, u32[]{:S(2)}) %collective-permute-start.41) | collective-permute-done | bytes 81952 | tf_op jit(solution)/shard_map/ppermute | solution.py:65
  153.1 2.0 collective-permute-done.40.refs_1_
  155.7 1.3 collective-permute-start.46
  159.8 2.5 collective-permute-done.26.refs_3_
  162.3 1.2 collective-permute-start.44
  167.8 2.8 %collective-permute-done.44.refs_2_ = bf16[320,512]{1,0:T(8,128)(2,1)S(1)} collective-permute-done((bf16[320,512]{1,0:T(8,128)(2,1)S(1)}, bf16[320,512]{1,0:T(8,128)(2,1)S(1)}, u32[]{:S(2)}, u32[]{:S(2)}) %collective-permute-start.44) | collective-permute-done | bytes 327712 | tf_op jit(solution)/shard_map/ppermute | solution.py:65
  170.6 8.6 %collective-permute-start.49 = (bf16[320,512]{1,0:T(8,128)(2,1)S(1)}, bf16[320,512]{1,0:T(8,128)(2,1)S(1)}, u32[]{:S(2)}, u32[]{:S(2)}) collective-permute-start(bf16[320,512]{1,0:T(8,128)(2,1)S(1)} %collective-permute-done.45.refs_3_), channel_id=1, source_target_pairs={{0,1},{1,0},{2,3},{3,2},{4,5},{5,4},{6,7},{7,6},{8,9},{9,8},{10,11... | collective-permute-start | bytes 983048 | tf_op jit(solution)/shard_map/ppermute | solution.py:65
  179.1 3.5 %collective-permute-start.48 = (bf16[320,512]{1,0:T(8,128)(2,1)S(1)}, bf16[320,512]{1,0:T(8,128)(2,1)S(1)}, u32[]{:S(2)}, u32[]{:S(2)}) collective-permute-start(bf16[320,512]{1,0:T(8,128)(2,1)S(1)} %collective-permute-done.44.refs_2_), channel_id=1, source_target_pairs={{0,1},{1,0},{2,3},{3,2},{4,5},{5,4},{6,7},{7,6},{8,9},{9,8},{10,11... | collective-permute-start | bytes 983048 | tf_op jit(solution)/shard_map/ppermute | solution.py:65
  182.6 1.6 collective-permute-start.30
  184.2 2.9 %collective-permute-start.33 = (bf16[512,512]{1,0:T(8,128)(2,1)S(1)}, bf16[512,512]{1,0:T(8,128)(2,1)S(1)}, u32[]{:S(2)}, u32[]{:S(2)}) collective-permute-start(bf16[512,512]{1,0:T(8,128)(2,1)S(1)} %collective-permute-done.29.refs_3_), channel_id=1, source_target_pairs={{0,1},{1,0},{2,3},{3,2},{4,5},{5,4},{6,7},{7,6},{8,9},{9,8},{10,11... | collective-permute-start | bytes 1572872 | tf_op jit(solution)/shard_map/ppermute | solution.py:65
  187.1 5.5 %collective-permute-start.32 = (bf16[512,512]{1,0:T(8,128)(2,1)S(1)}, bf16[512,512]{1,0:T(8,128)(2,1)S(1)}, u32[]{:S(2)}, u32[]{:S(2)}) collective-permute-start(bf16[512,512]{1,0:T(8,128)(2,1)S(1)} %collective-permute-done.28.refs_2_), channel_id=1, source_target_pairs={{0,1},{1,0},{2,3},{3,2},{4,5},{5,4},{6,7},{7,6},{8,9},{9,8},{10,11... | collective-permute-start | bytes 1572872 | tf_op jit(solution)/shard_map/ppermute | solution.py:65
  193.2 2.2 collective-permute-done.47.refs_5_
  195.4 8.1 %shard_map.88 = (bf16[128,2560]{1,0:T(8,128)(2,1)}, bf16[128,2560]{1,0:T(8,128)(2,1)S(1)}, bf16[128,2560]{1,0:T(8,128)(2,1)S(1)}, bf16[128,2560]{1,0:T(8,128)(2,1)S(1)}) custom-call(s32[8]{0:T(128)S(1)} %compare_select_fusion.6.where, bf16[320,512]{1,0:T(8,128)(2,1)S(1)} %shard_map.87.refs_0_, bf16[320,512]{1,0:T(8,128)(2,1)S(1)} %collective-permute-done.43.refs_1_, ...), custom_call_target="tpu_custom_call" | custom-call | flops 1342177280 | bytes 5767168 | tf_op jit(solution)/shard_map/pallas_call | solution.py:682
  203.6 2.7 collective-permute-start.51
  206.3 7.1 %shard_map.86 = (bf16[128,2048]{1,0:T(8,128)(2,1)}, bf16[128,2048]{1,0:T(8,128)(2,1)S(1)}, bf16[128,2048]{1,0:T(8,128)(2,1)S(1)}, bf16[128,2048]{1,0:T(8,128)(2,...) custom-call(s32[8]{0:T(128)S(1)} %compare_select_fusion.6.where, ...), custom_call_target="tpu_custom_call" | custom-call | flops 2147483648 | bytes 9437184 | tf_op jit(solution)/shard_map/pallas_call | solution.py:682
  213.5 21.2 %collective-permute-done.50.refs_1_ = bf16[128,2560]{1,0:T(8,128)(2,1)S(1)} collective-permute-done((bf16[128,2560]{1,0:T(8,128)(2,1)S(1)}, bf16[128,2560]{1,0:T(8,128)(2,1)S(1)}, u32[]{:S(2)}, u32[]{:S(2)}) %collective-permute-start.50) | collective-permute-done | bytes 655392 | tf_op jit(solution)/shard_map/ppermute | solution.py:65
  235.6 2.0 collective-permute-start.35
  237.7 1.4 collective-permute-start.36
  240.1 23.2 %all_to_all.15.new = bf16[8,128,256]{2,1,0:T(8,128)(2,1)S(1)} all-to-all(bf16[8,128,256]{2,1,0:T(8,128)(2,1)} %turn_back.1), channel_id=1, replica_groups=mesh['xl'=2,'z'=4,'y'=4,'xh'=2,'core'=2] {'xl','z'}, dimensions={0} | all-to-all | bytes 1048576 | tf_op jit(solution)/shard_map/all_to_all | solution.py:761
  264.4 3.6 %shard_map.89.refs_4_ = bf16[128,26624]{1,0:T(8,128)(2,1)} custom-call(s32[8]{0:T(128)S(1)} %compare_select_fusion.6.where, bf16[128,2560]{1,0:T(8,128)(2,1)S(1)} %copy-done.19, bf16[128,2560]{1,0:T(8,128)(2,1)S(1)} %collective-permute-done.50.refs_1_, bf16[128,2560]{1,0:T(8,128)(2,1)S(1)} %collective-permute-done.51.refs_2_, ...), custom_call_target="tpu_custom_call" | custom-call | bytes 5242880 | tf_op jit(solution)/shard_map/pallas_call | solution.py:230
  268.0 2.5 shard_map.90.refs_4_
  270.5 2.4 shard_map.91
  (123 shorter events, 18.9 us)
Async XLA Ops:
  3.1 15.7 %collective-permute-start = (bf16[128,2048]{1,0:T(8,128)(2,1)S(1)}, bf16[128,2048]{1,0:T(8,128)(2,1)S(1)}, u32[]{:S(2)}, u32[]{:S(2)}) collective-permute-start(bf16[128,2048]{1,0:T(8,128)(2,1)S(1)} %get-tuple-element.54), channel_id=1, source_target_pairs={{0,4},{1,5},{2,6},{3,7},{4,8},{5,9},{6,10},{7,11},{8,12},{9,13},{1... | collective-permute-start | bytes 1572872 | tf_op jit(solution)/shard_map/ppermute | solution.py:65
  8.4 26.7 %collective-permute-start.3 = (bf16[128,2560]{1,0:T(8,128)(2,1)S(1)}, bf16[128,2560]{1,0:T(8,128)(2,1)S(1)}, u32[]{:S(2)}, u32[]{:S(2)}) collective-permute-start(bf16[128,2560]{1,0:T(8,128)(2,1)S(1)} %get-tuple-element.58), channel_id=1, source_target_pairs={{0,16},{1,17},{2,18},{3,19},{4,20},{5,21},{6,22},{7,23},{8,24},{9,... | collective-permute-start | bytes 1966088 | tf_op jit(solution)/shard_map/ppermute | solution.py:65
  10.2 25.4 %collective-permute-start.4 = (bf16[128,2560]{1,0:T(8,128)(2,1)S(1)}, bf16[128,2560]{1,0:T(8,128)(2,1)S(1)}, u32[]{:S(2)}, u32[]{:S(2)}) collective-permute-start(bf16[128,2560]{1,0:T(8,128)(2,1)S(1)} %get-tuple-element.59), channel_id=1, source_target_pairs={{0,48},{1,49},{2,50},{3,51},{4,52},{5,53},{6,54},{7,55},{8,56},{9,... | collective-permute-start | bytes 1966088 | tf_op jit(solution)/shard_map/ppermute | solution.py:65
  12.7 29.0 %collective-permute-start.5 = (bf16[128,2560]{1,0:T(8,128)(2,1)S(1)}, bf16[128,2560]{1,0:T(8,128)(2,1)S(1)}, u32[]{:S(2)}, u32[]{:S(2)}) collective-permute-start(bf16[128,2560]{1,0:T(8,128)(2,1)S(1)} %get-tuple-element.60), channel_id=1, source_target_pairs={{0,32},{1,33},{2,34},{3,35},{4,36},{5,37},{6,38},{7,39},{8,40},{9,... | collective-permute-start | bytes 1966088 | tf_op jit(solution)/shard_map/ppermute | solution.py:65
  13.8 12.0 %collective-permute-start.1 = (bf16[128,2048]{1,0:T(8,128)(2,1)S(1)}, bf16[128,2048]{1,0:T(8,128)(2,1)S(1)}, u32[]{:S(2)}, u32[]{:S(2)}) collective-permute-start(bf16[128,2048]{1,0:T(8,128)(2,1)S(1)} %get-tuple-element.55), channel_id=1, source_target_pairs={{0,12},{1,13},{2,14},{3,15},{4,0},{5,1},{6,2},{7,3},{8,4},{9,5},{1... | collective-permute-start | bytes 1572872 | tf_op jit(solution)/shard_map/ppermute | solution.py:65
  18.8 22.9 %copy-start.13 = (bf16[128,2048]{1,0:T(8,128)(2,1)}, bf16[128,2048]{1,0:T(8,128)(2,1)S(1)}, u32[]{:S(2)}) copy-start(bf16[128,2048]{1,0:T(8,128)(2,1)S(1)} %collective-permute-done.refs_1_) | copy-start | bytes 1572868
  18.8 22.9 %copy-start = (bf16[2048,512]{1,0:T(8,128)(2,1)S(1)}, bf16[2048,512]{1,0:T(8,128)(2,1)}, u32[]{:S(2)}) copy-start(bf16[2048,512]{1,0:T(8,128)(2,1)} %refs_8_.5) | copy-start | bytes 6291460
  18.8 13.7 %collective-permute-start.2 = (bf16[128,2048]{1,0:T(8,128)(2,1)S(1)}, bf16[128,2048]{1,0:T(8,128)(2,1)S(1)}, u32[]{:S(2)}, u32[]{:S(2)}) collective-permute-start(bf16[128,2048]{1,0:T(8,128)(2,1)S(1)} %get-tuple-element.56), channel_id=1, source_target_pairs={{0,8},{1,9},{2,10},{3,11},{4,12},{5,13},{6,14},{7,15},{8,0},{9,1},... | collective-permute-start | bytes 1572872 | tf_op jit(solution)/shard_map/ppermute | solution.py:65
  25.9 21.0 %copy-start.15 = (bf16[128,2048]{1,0:T(8,128)(2,1)}, bf16[128,2048]{1,0:T(8,128)(2,1)S(1)}, u32[]{:S(2)}) copy-start(bf16[128,2048]{1,0:T(8,128)(2,1)S(1)} %collective-permute-done.1.refs_2_) | copy-start | bytes 1572868
  25.9 23.4 %collective-permute-start.13 = (bf16[128,3072]{1,0:T(8,128)(2,1)S(1)}, bf16[128,3072]{1,0:T(8,128)(2,1)S(1)}, u32[]{:S(2)}, u32[]{:S(2)}) collective-permute-start(bf16[128,3072]{1,0:T(8,128)(2,1)S(1)} %get-tuple-element.72), channel_id=1, source_target_pairs={{0,64},{1,65},{2,66},{3,67},{4,68},{5,69},{6,70},{7,71},{8,72},{9,... | collective-permute-start | bytes 2359304 | tf_op jit(solution)/shard_map/ppermute | solution.py:65
  32.6 14.2 %copy-start.17 = (bf16[128,2048]{1,0:T(8,128)(2,1)}, bf16[128,2048]{1,0:T(8,128)(2,1)S(1)}, u32[]{:S(2)}) copy-start(bf16[128,2048]{1,0:T(8,128)(2,1)S(1)} %collective-permute-done.2.refs_3_) | copy-start | bytes 1572868
  32.6 16.7 %collective-permute-start.14 = (bf16[128,3072]{1,0:T(8,128)(2,1)S(1)}, bf16[128,3072]{1,0:T(8,128)(2,1)S(1)}, u32[]{:S(2)}, u32[]{:S(2)}) collective-permute-start(bf16[128,3072]{1,0:T(8,128)(2,1)S(1)} %get-tuple-element.73), channel_id=1, source_target_pairs={{0,66},{1,67},{2,64},{3,65},{4,70},{5,71},{6,68},{7,69},{8,74},{9,... | collective-permute-start | bytes 2359304 | tf_op jit(solution)/shard_map/ppermute | solution.py:65
  35.1 11.8 %copy-start.5 = (bf16[128,2560]{1,0:T(8,128)(2,1)}, bf16[128,2560]{1,0:T(8,128)(2,1)S(1)}, u32[]{:S(2)}) copy-start(bf16[128,2560]{1,0:T(8,128)(2,1)S(1)} %collective-permute-done.3.refs_5_) | copy-start | bytes 1966084
  35.1 14.2 %collective-permute-start.15 = (bf16[128,2560]{1,0:T(8,128)(2,1)S(1)}, bf16[128,2560]{1,0:T(8,128)(2,1)S(1)}, u32[]{:S(2)}, u32[]{:S(2)}) collective-permute-start(bf16[128,2560]{1,0:T(8,128)(2,1)S(1)} %get-tuple-element.74), channel_id=1, source_target_pairs={{0,2},{1,3},{2,0},{3,1},{4,6},{5,7},{6,4},{7,5},{8,10},{9,11},{10,... | collective-permute-start | bytes 1966088 | tf_op jit(solution)/shard_map/ppermute | solution.py:65
  46.9 47.2 %collective-permute-start.6 = (bf16[2048,512]{1,0:T(8,128)(2,1)}, bf16[2048,512]{1,0:T(8,128)(2,1)}, u32[]{:S(2)}, u32[]{:S(2)}) collective-permute-start(bf16[2048,512]{1,0:T(8,128)(2,1)} %get-tuple-element.61), channel_id=1, source_target_pairs={{0,1},{1,0},{2,3},{3,2},{4,5},{5,4},{6,7},{7,6},{8,9},{9,8},{10,11... | collective-permute-start | bytes 6291464 | tf_op jit(solution)/shard_map/ppermute | solution.py:65
  49.3 22.0 %copy-start.22 = (f32[64,1664]{1,0:T(8,128)S(1)}, f32[64,1664]{1,0:T(8,128)}, u32[]{:S(2)}) copy-start(f32[64,1664]{1,0:T(8,128)} %first.1) | copy-start | bytes 1277956
  49.3 22.0 %copy-start.23 = (f32[64,1664]{1,0:T(8,128)S(1)}, f32[64,1664]{1,0:T(8,128)}, u32[]{:S(2)}) copy-start(f32[64,1664]{1,0:T(8,128)} %second.1) | copy-start | bytes 1277956
  53.8 28.3 %collective-permute-start.16 = (bf16[1280,512]{1,0:T(8,128)(2,1)}, bf16[1280,512]{1,0:T(8,128)(2,1)}, u32[]{:S(2)}, u32[]{:S(2)}) collective-permute-start(bf16[1280,512]{1,0:T(8,128)(2,1)} %get-tuple-element.75), channel_id=1, source_target_pairs={{0,1},{1,0},{2,3},{3,2},{4,5},{5,4},{6,7},{7,6},{8,9},{9,8},{10,11... | collective-permute-start | bytes 3932168 | tf_op jit(solution)/shard_map/ppermute | solution.py:65
  75.4 31.9 %all-to-all-start = ((bf16[8,256,256]{2,1,0:T(8,128)(2,1)}), bf16[8,256,256]{2,1,0:T(8,128)(2,1)S(1)}, u32[]{:S(2)}, u32[]{:S(2)}) async-start(bf16[8,256,256]{2,1,0:T(8,128)(2,1)} %cut_moments.1), calls=%async_computation | async-start | bytes 2097152 | tf_op jit(solution)/shard_map/all_to_all | solution.py:729
  90.2 21.3 %collective-permute-start.17 = (bf16[320,512]{1,0:T(8,128)(2,1)}, bf16[320,512]{1,0:T(8,128)(2,1)}, u32[]{:S(2)}, u32[]{:S(2)}) collective-permute-start(bf16[320,512]{1,0:T(8,128)(2,1)} %get-tuple-element.78), channel_id=1, source_target_pairs={{0,16},{1,17},{2,18},{3,19},{4,20},{5,21},{6,22},{7,23},{8,24},{9,... | collective-permute-start | bytes 983048 | tf_op jit(solution)/shard_map/ppermute | solution.py:65
  91.7 27.0 %collective-permute-start.18 = (bf16[320,512]{1,0:T(8,128)(2,1)}, bf16[320,512]{1,0:T(8,128)(2,1)}, u32[]{:S(2)}, u32[]{:S(2)}) collective-permute-start(bf16[320,512]{1,0:T(8,128)(2,1)} %get-tuple-element.79), channel_id=1, source_target_pairs={{0,32},{1,33},{2,34},{3,35},{4,36},{5,37},{6,38},{7,39},{8,40},{9,... | collective-permute-start | bytes 983048 | tf_op jit(solution)/shard_map/ppermute | solution.py:65
  99.8 29.6 %collective-permute-start.7 = (bf16[512,512]{1,0:T(8,128)(2,1)}, bf16[512,512]{1,0:T(8,128)(2,1)}, u32[]{:S(2)}, u32[]{:S(2)}) collective-permute-start(bf16[512,512]{1,0:T(8,128)(2,1)} %get-tuple-element.64), channel_id=1, source_target_pairs={{0,64},{1,5},{2,66},{3,7},{4,68},{5,9},{6,70},{7,11},{8,72},{9,13}... | collective-permute-start | bytes 1572872 | tf_op jit(solution)/shard_map/ppermute | solution.py:65
  104.8 24.6 %collective-permute-start.8 = (bf16[512,512]{1,0:T(8,128)(2,1)}, bf16[512,512]{1,0:T(8,128)(2,1)}, u32[]{:S(2)}, u32[]{:S(2)}) collective-permute-start(bf16[512,512]{1,0:T(8,128)(2,1)} %get-tuple-element.65), channel_id=1, source_target_pairs={{0,2},{1,9},{2,0},{3,11},{4,6},{5,13},{6,4},{7,15},{8,10},{9,1},{1... | collective-permute-start | bytes 1572872 | tf_op jit(solution)/shard_map/ppermute | solution.py:65
  106.1 23.4 %collective-permute-start.9 = (bf16[512,512]{1,0:T(8,128)(2,1)}, bf16[512,512]{1,0:T(8,128)(2,1)}, u32[]{:S(2)}, u32[]{:S(2)}) collective-permute-start(bf16[512,512]{1,0:T(8,128)(2,1)} %get-tuple-element.66), channel_id=1, source_target_pairs={{0,66},{1,13},{2,64},{3,15},{4,70},{5,1},{6,68},{7,3},{8,74},{9,5}... | collective-permute-start | bytes 1572872 | tf_op jit(solution)/shard_map/ppermute | solution.py:65
  108.1 10.6 %all-to-all-start.1 = ((bf16[8,32,512]{2,1,0:T(8,128)(2,1)}), bf16[8,32,512]{2,1,0:T(8,128)(2,1)S(1)}, u32[]{:S(2)}, u32[]{:S(2)}) async-start(bf16[8,32,512]{2,1,0:T(8,128)(2,1)} %sum_margin.1), calls=%async_computation.1 | async-start | bytes 524288 | tf_op jit(solution)/shard_map/all_to_all | solution.py:731
  111.5 12.0 %collective-permute-start.19 = (bf16[320,512]{1,0:T(8,128)(2,1)}, bf16[320,512]{1,0:T(8,128)(2,1)}, u32[]{:S(2)}, u32[]{:S(2)}) collective-permute-start(bf16[320,512]{1,0:T(8,128)(2,1)} %copy-done.24), channel_id=1, source_target_pairs={{0,48},{1,49},{2,50},{3,51},{4,52},{5,53},{6,54},{7,55},{8,56},{9,... | collective-permute-start | bytes 983048 | tf_op jit(solution)/shard_map/ppermute | solution.py:65
  118.7 19.0 %collective-permute-start.23 = (bf16[256,512]{1,0:T(8,128)(2,1)S(1)}, bf16[256,512]{1,0:T(8,128)(2,1)S(1)}, u32[]{:S(2)}, u32[]{:S(2)}) collective-permute-start(bf16[256,512]{1,0:T(8,128)(2,1)S(1)} %bitcast.1), channel_id=1, source_target_pairs={{0,1},{1,0},{2,3},{3,2},{4,5},{5,4},{6,7},{7,6},{8,9},{9,8},{10,11... | collective-permute-start | bytes 786440 | tf_op jit(solution)/shard_map/ppermute | solution.py:65
  126.5 12.4 %copy-start.25 = (bf16[80,512]{1,0:T(8,128)(2,1)S(1)}, bf16[80,512]{1,0:T(8,128)(2,1)}, u32[]{:S(2)}) copy-start(bf16[80,512]{1,0:T(8,128)(2,1)} %get-tuple-element.84) | copy-start | bytes 245764
  126.6 12.4 %collective-permute-start.20 = (bf16[80,512]{1,0:T(8,128)(2,1)}, bf16[80,512]{1,0:T(8,128)(2,1)S(1)}, u32[]{:S(2)}, u32[]{:S(2)}) collective-permute-start(bf16[80,512]{1,0:T(8,128)(2,1)} %get-tuple-element.82), channel_id=1, source_target_pairs={{0,4},{1,5},{2,6},{3,7},{4,8},{5,9},{6,10},{7,11},{8,12},{9,13},{1... | collective-permute-start | bytes 245768 | tf_op jit(solution)/shard_map/ppermute | solution.py:65
  132.8 10.5 %collective-permute-start.10 = (bf16[128,512]{1,0:T(8,128)(2,1)}, bf16[128,512]{1,0:T(8,128)(2,1)S(1)}, u32[]{:S(2)}, u32[]{:S(2)}) collective-permute-start(bf16[128,512]{1,0:T(8,128)(2,1)} %get-tuple-element.68), channel_id=1, source_target_pairs={{0,16},{1,65},{2,18},{3,67},{4,20},{5,69},{6,22},{7,71},{8,24},{9,... | collective-permute-start | bytes 393224 | tf_op jit(solution)/shard_map/ppermute | solution.py:65
  133.0 10.3 %collective-permute-start.11 = (bf16[128,512]{1,0:T(8,128)(2,1)}, bf16[128,512]{1,0:T(8,128)(2,1)S(1)}, u32[]{:S(2)}, u32[]{:S(2)}) collective-permute-start(bf16[128,512]{1,0:T(8,128)(2,1)} %get-tuple-element.69), channel_id=1, source_target_pairs={{0,32},{1,3},{2,34},{3,1},{4,36},{5,7},{6,38},{7,5},{8,40},{9,11},... | collective-permute-start | bytes 393224 | tf_op jit(solution)/shard_map/ppermute | solution.py:65
  135.7 7.6 %collective-permute-start.12 = (bf16[128,512]{1,0:T(8,128)(2,1)}, bf16[128,512]{1,0:T(8,128)(2,1)S(1)}, u32[]{:S(2)}, u32[]{:S(2)}) collective-permute-start(bf16[128,512]{1,0:T(8,128)(2,1)} %get-tuple-element.70), channel_id=1, source_target_pairs={{0,48},{1,67},{2,50},{3,65},{4,52},{5,71},{6,54},{7,69},{8,56},{9,... | collective-permute-start | bytes 393224 | tf_op jit(solution)/shard_map/ppermute | solution.py:65
  137.7 5.6 %collective-permute-start.21 = (bf16[80,512]{1,0:T(8,128)(2,1)S(1)}, bf16[80,512]{1,0:T(8,128)(2,1)S(1)}, u32[]{:S(2)}, u32[]{:S(2)}) collective-permute-start(bf16[80,512]{1,0:T(8,128)(2,1)S(1)} %copy-done.26), channel_id=1, source_target_pairs={{0,8},{1,9},{2,10},{3,11},{4,12},{5,13},{6,14},{7,15},{8,0},{9,1},... | collective-permute-start | bytes 245768 | tf_op jit(solution)/shard_map/ppermute | solution.py:65
  139.0 4.3 %collective-permute-start.22 = (bf16[80,512]{1,0:T(8,128)(2,1)S(1)}, bf16[80,512]{1,0:T(8,128)(2,1)S(1)}, u32[]{:S(2)}, u32[]{:S(2)}) collective-permute-start(bf16[80,512]{1,0:T(8,128)(2,1)S(1)} %copy-done.25), channel_id=1, source_target_pairs={{0,12},{1,13},{2,14},{3,15},{4,0},{5,1},{6,2},{7,3},{8,4},{9,5},{1... | collective-permute-start | bytes 245768 | tf_op jit(solution)/shard_map/ppermute | solution.py:65
  145.6 4.2 %collective-permute-start.42 = (bf16[80,512]{1,0:T(8,128)(2,1)S(1)}, bf16[80,512]{1,0:T(8,128)(2,1)S(1)}, u32[]{:S(2)}, u32[]{:S(2)}) collective-permute-start(bf16[80,512]{1,0:T(8,128)(2,1)S(1)} %get-tuple-element.94.refs_0_), channel_id=1, source_target_pairs={{0,12},{1,13},{2,14},{3,15},{4,0},{5,1},{6,2},{7,3},{8,4},{9,5},{1... | collective-permute-start | bytes 245768 | tf_op jit(solution)/shard_map/ppermute | solution.py:65
  148.3 4.9 %collective-permute-start.41 = (bf16[80,512]{1,0:T(8,128)(2,1)S(1)}, bf16[80,512]{1,0:T(8,128)(2,1)S(1)}, u32[]{:S(2)}, u32[]{:S(2)}) collective-permute-start(bf16[80,512]{1,0:T(8,128)(2,1)S(1)} %get-tuple-element.94.refs_0_), channel_id=1, source_target_pairs={{0,8},{1,9},{2,10},{3,11},{4,12},{5,13},{6,14},{7,15},{8,0},{9,1},... | collective-permute-start | bytes 245768 | tf_op jit(solution)/shard_map/ppermute | solution.py:65
  148.8 6.3 %collective-permute-start.40 = (bf16[80,512]{1,0:T(8,128)(2,1)S(1)}, bf16[80,512]{1,0:T(8,128)(2,1)S(1)}, u32[]{:S(2)}, u32[]{:S(2)}) collective-permute-start(bf16[80,512]{1,0:T(8,128)(2,1)S(1)} %get-tuple-element.94.refs_0_), channel_id=1, source_target_pairs={{0,4},{1,5},{2,6},{3,7},{4,8},{5,9},{6,10},{7,11},{8,12},{9,13},{1... | collective-permute-start | bytes 245768 | tf_op jit(solution)/shard_map/ppermute | solution.py:65
  155.7 10.4 %collective-permute-start.46 = (bf16[320,512]{1,0:T(8,128)(2,1)S(1)}, bf16[320,512]{1,0:T(8,128)(2,1)S(1)}, u32[]{:S(2)}, u32[]{:S(2)}) collective-permute-start(bf16[320,512]{1,0:T(8,128)(2,1)S(1)} %shard_map.87.refs_0_), channel_id=1, source_target_pairs={{0,1},{1,0},{2,3},{3,2},{4,5},{5,4},{6,7},{7,6},{8,9},{9,8},{10,11... | collective-permute-start | bytes 983048 | tf_op jit(solution)/shard_map/ppermute | solution.py:65
  157.1 10.0 %collective-permute-start.45 = (bf16[320,512]{1,0:T(8,128)(2,1)S(1)}, bf16[320,512]{1,0:T(8,128)(2,1)S(1)}, u32[]{:S(2)}, u32[]{:S(2)}) collective-permute-start(bf16[320,512]{1,0:T(8,128)(2,1)S(1)} %shard_map.87.refs_0_), channel_id=1, source_target_pairs={{0,48},{1,49},{2,50},{3,51},{4,52},{5,53},{6,54},{7,55},{8,56},{9,... | collective-permute-start | bytes 983048 | tf_op jit(solution)/shard_map/ppermute | solution.py:65
  158.2 4.1 %collective-permute-start.26 = (bf16[128,512]{1,0:T(8,128)(2,1)S(1)}, bf16[128,512]{1,0:T(8,128)(2,1)S(1)}, u32[]{:S(2)}, u32[]{:S(2)}) collective-permute-start(bf16[128,512]{1,0:T(8,128)(2,1)S(1)} %get-tuple-element.85.refs_0_), channel_id=1, source_target_pairs={{0,48},{1,67},{2,50},{3,65},{4,52},{5,71},{6,54},{7,69},{8,56},{9,... | collective-permute-start | bytes 393224 | tf_op jit(solution)/shard_map/ppermute | solution.py:65
  158.4 5.6 %collective-permute-start.25 = (bf16[128,512]{1,0:T(8,128)(2,1)S(1)}, bf16[128,512]{1,0:T(8,128)(2,1)S(1)}, u32[]{:S(2)}, u32[]{:S(2)}) collective-permute-start(bf16[128,512]{1,0:T(8,128)(2,1)S(1)} %get-tuple-element.85.refs_0_), channel_id=1, source_target_pairs={{0,32},{1,3},{2,34},{3,1},{4,36},{5,7},{6,38},{7,5},{8,40},{9,11},... | collective-permute-start | bytes 393224 | tf_op jit(solution)/shard_map/ppermute | solution.py:65
  159.4 5.8 %collective-permute-start.24 = (bf16[128,512]{1,0:T(8,128)(2,1)S(1)}, bf16[128,512]{1,0:T(8,128)(2,1)S(1)}, u32[]{:S(2)}, u32[]{:S(2)}) collective-permute-start(bf16[128,512]{1,0:T(8,128)(2,1)S(1)} %get-tuple-element.85.refs_0_), channel_id=1, source_target_pairs={{0,16},{1,65},{2,18},{3,67},{4,20},{5,69},{6,22},{7,71},{8,24},{9,... | collective-permute-start | bytes 393224 | tf_op jit(solution)/shard_map/ppermute | solution.py:65
  162.3 8.3 %collective-permute-start.44 = (bf16[320,512]{1,0:T(8,128)(2,1)S(1)}, bf16[320,512]{1,0:T(8,128)(2,1)S(1)}, u32[]{:S(2)}, u32[]{:S(2)}) collective-permute-start(bf16[320,512]{1,0:T(8,128)(2,1)S(1)} %shard_map.87.refs_0_), channel_id=1, source_target_pairs={{0,32},{1,33},{2,34},{3,35},{4,36},{5,37},{6,38},{7,39},{8,40},{9,... | collective-permute-start | bytes 983048 | tf_op jit(solution)/shard_map/ppermute | solution.py:65
  164.0 15.1 %collective-permute-start.43 = (bf16[320,512]{1,0:T(8,128)(2,1)S(1)}, bf16[320,512]{1,0:T(8,128)(2,1)S(1)}, u32[]{:S(2)}, u32[]{:S(2)}) collective-permute-start(bf16[320,512]{1,0:T(8,128)(2,1)S(1)} %shard_map.87.refs_0_), channel_id=1, source_target_pairs={{0,16},{1,17},{2,18},{3,19},{4,20},{5,21},{6,22},{7,23},{8,24},{9,... | collective-permute-start | bytes 983048 | tf_op jit(solution)/shard_map/ppermute | solution.py:65
  165.7 16.9 %collective-permute-start.29 = (bf16[512,512]{1,0:T(8,128)(2,1)S(1)}, bf16[512,512]{1,0:T(8,128)(2,1)S(1)}, u32[]{:S(2)}, u32[]{:S(2)}) collective-permute-start(bf16[512,512]{1,0:T(8,128)(2,1)S(1)} %shard_map.85.refs_0_), channel_id=1, source_target_pairs={{0,66},{1,13},{2,64},{3,15},{4,70},{5,1},{6,68},{7,3},{8,74},{9,5}... | collective-permute-start | bytes 1572872 | tf_op jit(solution)/shard_map/ppermute | solution.py:65
  166.1 18.1 %collective-permute-start.28 = (bf16[512,512]{1,0:T(8,128)(2,1)S(1)}, bf16[512,512]{1,0:T(8,128)(2,1)S(1)}, u32[]{:S(2)}, u32[]{:S(2)}) collective-permute-start(bf16[512,512]{1,0:T(8,128)(2,1)S(1)} %shard_map.85.refs_0_), channel_id=1, source_target_pairs={{0,2},{1,9},{2,0},{3,11},{4,6},{5,13},{6,4},{7,15},{8,10},{9,1},{1... | collective-permute-start | bytes 1572872 | tf_op jit(solution)/shard_map/ppermute | solution.py:65
  167.0 20.1 %collective-permute-start.27 = (bf16[512,512]{1,0:T(8,128)(2,1)S(1)}, bf16[512,512]{1,0:T(8,128)(2,1)S(1)}, u32[]{:S(2)}, u32[]{:S(2)}) collective-permute-start(bf16[512,512]{1,0:T(8,128)(2,1)S(1)} %shard_map.85.refs_0_), channel_id=1, source_target_pairs={{0,64},{1,5},{2,66},{3,7},{4,68},{5,9},{6,70},{7,11},{8,72},{9,13}... | collective-permute-start | bytes 1572872 | tf_op jit(solution)/shard_map/ppermute | solution.py:65
  170.6 22.1 %collective-permute-start.49 = (bf16[320,512]{1,0:T(8,128)(2,1)S(1)}, bf16[320,512]{1,0:T(8,128)(2,1)S(1)}, u32[]{:S(2)}, u32[]{:S(2)}) collective-permute-start(bf16[320,512]{1,0:T(8,128)(2,1)S(1)} %collective-permute-done.45.refs_3_), channel_id=1, source_target_pairs={{0,1},{1,0},{2,3},{3,2},{4,5},{5,4},{6,7},{7,6},{8,9},{9,8},{10,11... | collective-permute-start | bytes 983048 | tf_op jit(solution)/shard_map/ppermute | solution.py:65
  179.1 13.5 %collective-permute-start.48 = (bf16[320,512]{1,0:T(8,128)(2,1)S(1)}, bf16[320,512]{1,0:T(8,128)(2,1)S(1)}, u32[]{:S(2)}, u32[]{:S(2)}) collective-permute-start(bf16[320,512]{1,0:T(8,128)(2,1)S(1)} %collective-permute-done.44.refs_2_), channel_id=1, source_target_pairs={{0,1},{1,0},{2,3},{3,2},{4,5},{5,4},{6,7},{7,6},{8,9},{9,8},{10,11... | collective-permute-start | bytes 983048 | tf_op jit(solution)/shard_map/ppermute | solution.py:65
  182.6 21.0 %collective-permute-start.30 = (bf16[512,512]{1,0:T(8,128)(2,1)S(1)}, bf16[512,512]{1,0:T(8,128)(2,1)S(1)}, u32[]{:S(2)}, u32[]{:S(2)}) collective-permute-start(bf16[512,512]{1,0:T(8,128)(2,1)S(1)} %shard_map.85.refs_0_), channel_id=1, source_target_pairs={{0,1},{1,0},{2,3},{3,2},{4,5},{5,4},{6,7},{7,6},{8,9},{9,8},{10,11... | collective-permute-start | bytes 1572872 | tf_op jit(solution)/shard_map/ppermute | solution.py:65
  184.2 22.0 %collective-permute-start.33 = (bf16[512,512]{1,0:T(8,128)(2,1)S(1)}, bf16[512,512]{1,0:T(8,128)(2,1)S(1)}, u32[]{:S(2)}, u32[]{:S(2)}) collective-permute-start(bf16[512,512]{1,0:T(8,128)(2,1)S(1)} %collective-permute-done.29.refs_3_), channel_id=1, source_target_pairs={{0,1},{1,0},{2,3},{3,2},{4,5},{5,4},{6,7},{7,6},{8,9},{9,8},{10,11... | collective-permute-start | bytes 1572872 | tf_op jit(solution)/shard_map/ppermute | solution.py:65
  187.1 19.2 %collective-permute-start.32 = (bf16[512,512]{1,0:T(8,128)(2,1)S(1)}, bf16[512,512]{1,0:T(8,128)(2,1)S(1)}, u32[]{:S(2)}, u32[]{:S(2)}) collective-permute-start(bf16[512,512]{1,0:T(8,128)(2,1)S(1)} %collective-permute-done.28.refs_2_), channel_id=1, source_target_pairs={{0,1},{1,0},{2,3},{3,2},{4,5},{5,4},{6,7},{7,6},{8,9},{9,8},{10,11... | collective-permute-start | bytes 1572872 | tf_op jit(solution)/shard_map/ppermute | solution.py:65
  192.6 13.6 %collective-permute-start.31 = (bf16[512,512]{1,0:T(8,128)(2,1)S(1)}, bf16[512,512]{1,0:T(8,128)(2,1)S(1)}, u32[]{:S(2)}, u32[]{:S(2)}) collective-permute-start(bf16[512,512]{1,0:T(8,128)(2,1)S(1)} %collective-permute-done.27.refs_1_), channel_id=1, source_target_pairs={{0,1},{1,0},{2,3},{3,2},{4,5},{5,4},{6,7},{7,6},{8,9},{9,8},{10,11... | collective-permute-start | bytes 1572872 | tf_op jit(solution)/shard_map/ppermute | solution.py:65
  192.6 2.7 %collective-permute-start.47 = (bf16[320,512]{1,0:T(8,128)(2,1)S(1)}, bf16[320,512]{1,0:T(8,128)(2,1)S(1)}, u32[]{:S(2)}, u32[]{:S(2)}) collective-permute-start(bf16[320,512]{1,0:T(8,128)(2,1)S(1)} %collective-permute-done.43.refs_1_), channel_id=1, source_target_pairs={{0,1},{1,0},{2,3},{3,2},{4,5},{5,4},{6,7},{7,6},{8,9},{9,8},{10,11... | collective-permute-start | bytes 983048 | tf_op jit(solution)/shard_map/ppermute | solution.py:65
  203.5 31.2 %collective-permute-start.50 = (bf16[128,2560]{1,0:T(8,128)(2,1)S(1)}, bf16[128,2560]{1,0:T(8,128)(2,1)S(1)}, u32[]{:S(2)}, u32[]{:S(2)}) collective-permute-start(bf16[128,2560]{1,0:T(8,128)(2,1)S(1)} %get-tuple-element.96), channel_id=1, source_target_pairs={{0,64},{1,65},{2,66},{3,67},{4,68},{5,69},{6,70},{7,71},{8,72},{9,... | collective-permute-start | bytes 1966088 | tf_op jit(solution)/shard_map/ppermute | solution.py:65
  203.6 31.4 %collective-permute-start.51 = (bf16[128,2560]{1,0:T(8,128)(2,1)S(1)}, bf16[128,2560]{1,0:T(8,128)(2,1)S(1)}, u32[]{:S(2)}, u32[]{:S(2)}) collective-permute-start(bf16[128,2560]{1,0:T(8,128)(2,1)S(1)} %get-tuple-element.97), channel_id=1, source_target_pairs={{0,66},{1,67},{2,64},{3,65},{4,70},{5,71},{6,68},{7,69},{8,74},{9,... | collective-permute-start | bytes 1966088 | tf_op jit(solution)/shard_map/ppermute | solution.py:65
  206.3 29.4 %collective-permute-start.52 = (bf16[128,2560]{1,0:T(8,128)(2,1)S(1)}, bf16[128,2560]{1,0:T(8,128)(2,1)S(1)}, u32[]{:S(2)}, u32[]{:S(2)}) collective-permute-start(bf16[128,2560]{1,0:T(8,128)(2,1)S(1)} %get-tuple-element.98), channel_id=1, source_target_pairs={{0,2},{1,3},{2,0},{3,1},{4,6},{5,7},{6,4},{7,5},{8,10},{9,11},{10,... | collective-permute-start | bytes 1966088 | tf_op jit(solution)/shard_map/ppermute | solution.py:65
  213.4 51.0 %copy-start.19 = (bf16[128,2560]{1,0:T(8,128)(2,1)S(1)}, bf16[128,2560]{1,0:T(8,128)(2,1)}, u32[]{:S(2)}) copy-start(bf16[128,2560]{1,0:T(8,128)(2,1)} %get-tuple-element.95.refs_0_) | copy-start | bytes 1966084
  213.4 24.3 %collective-permute-start.37 = (bf16[128,2048]{1,0:T(8,128)(2,1)S(1)}, bf16[128,2048]{1,0:T(8,128)(2,1)S(1)}, u32[]{:S(2)}, u32[]{:S(2)}) collective-permute-start(bf16[128,2048]{1,0:T(8,128)(2,1)S(1)} %get-tuple-element.91), channel_id=1, source_target_pairs={{0,4},{1,5},{2,6},{3,7},{4,8},{5,9},{6,10},{7,11},{8,12},{9,13},{1... | collective-permute-start | bytes 1572872 | tf_op jit(solution)/shard_map/ppermute | solution.py:65
  213.5 57.0 %collective-permute-start.34 = (bf16[128,2048]{1,0:T(8,128)(2,1)S(1)}, bf16[128,2048]{1,0:T(8,128)(2,1)S(1)}, u32[]{:S(2)}, u32[]{:S(2)}) collective-permute-start(bf16[128,2048]{1,0:T(8,128)(2,1)S(1)} %get-tuple-element.87), channel_id=1, source_target_pairs={{0,16},{1,17},{2,18},{3,19},{4,20},{5,21},{6,22},{7,23},{8,24},{9,... | collective-permute-start | bytes 1572872 | tf_op jit(solution)/shard_map/ppermute | solution.py:65
  234.8 33.2 %collective-permute-start.38 = (bf16[128,2048]{1,0:T(8,128)(2,1)S(1)}, bf16[128,2048]{1,0:T(8,128)(2,1)S(1)}, u32[]{:S(2)}, u32[]{:S(2)}) collective-permute-start(bf16[128,2048]{1,0:T(8,128)(2,1)S(1)} %get-tuple-element.92), channel_id=1, source_target_pairs={{0,12},{1,13},{2,14},{3,15},{4,0},{5,1},{6,2},{7,3},{8,4},{9,5},{1... | collective-permute-start | bytes 1572872 | tf_op jit(solution)/shard_map/ppermute | solution.py:65
  235.0 32.9 %collective-permute-start.39 = (bf16[128,2048]{1,0:T(8,128)(2,1)S(1)}, bf16[128,2048]{1,0:T(8,128)(2,1)S(1)}, u32[]{:S(2)}, u32[]{:S(2)}) collective-permute-start(bf16[128,2048]{1,0:T(8,128)(2,1)S(1)} %get-tuple-element.93), channel_id=1, source_target_pairs={{0,8},{1,9},{2,10},{3,11},{4,12},{5,13},{6,14},{7,15},{8,0},{9,1},... | collective-permute-start | bytes 1572872 | tf_op jit(solution)/shard_map/ppermute | solution.py:65
  235.6 34.8 %collective-permute-start.35 = (bf16[128,2048]{1,0:T(8,128)(2,1)S(1)}, bf16[128,2048]{1,0:T(8,128)(2,1)S(1)}, u32[]{:S(2)}, u32[]{:S(2)}) collective-permute-start(bf16[128,2048]{1,0:T(8,128)(2,1)S(1)} %get-tuple-element.88), channel_id=1, source_target_pairs={{0,48},{1,49},{2,50},{3,51},{4,52},{5,53},{6,54},{7,55},{8,56},{9,... | collective-permute-start | bytes 1572872 | tf_op jit(solution)/shard_map/ppermute | solution.py:65
  237.7 32.8 %collective-permute-start.36 = (bf16[128,2048]{1,0:T(8,128)(2,1)S(1)}, bf16[128,2048]{1,0:T(8,128)(2,1)S(1)}, u32[]{:S(2)}, u32[]{:S(2)}) collective-permute-start(bf16[128,2048]{1,0:T(8,128)(2,1)S(1)} %get-tuple-element.89), channel_id=1, source_target_pairs={{0,32},{1,33},{2,34},{3,35},{4,36},{5,37},{6,38},{7,39},{8,40},{9,... | collective-permute-start | bytes 1572872 | tf_op jit(solution)/shard_map/ppermute | solution.py:65
  (18 other events, 111.9 us)
